TPU v7x, 32 devices: a whole 2x2x4 slice. The times are simulated.
32 devices in a mesh: mod: 2 (over x), page: 16 (over z, y, core).
Axes of the slice: x: 2, y: 2, z: 4, core: 2. Of those that a mesh axis runs over, the one named last changes fastest.
Arguments:
- states: bfloat16 [2, 16, 512, 768], P('mod', 'page'), may hold values from -6 to 6
- cotangent: bfloat16 [2, 16, 512, 768], P('mod', 'page'), may hold values from -6 to 6
- segments: int32 [16, 512], P('page'), may hold values from 0 to 7, never falling along the last dimension, each value on 1 to 128 neighbouring positions
- box_x: int32 [16, 512], P('page'), may hold values from 0 to 31
- box_y: int32 [16, 512], P('page'), may hold values from 0 to 31
- conv_weight: float32 [3, 768], replicated, may hold values from -3 to 3
- conv_bias: float32 [768], replicated, may hold values from -2 to 2
- w_query: bfloat16 [768, 768], P('page'), may hold values from -0.21875 to 0.21875
- b_query: float32 [768], replicated, may hold values from -3 to 3
- w_key: bfloat16 [768, 768], P('page'), may hold values from -0.21875 to 0.21875
- w_value: bfloat16 [768, 768], P('page'), may hold values from -0.21875 to 0.21875
- b_value: float32 [768], replicated, may hold values from -3 to 3
- w_out: bfloat16 [768, 768], P('page'), may hold values from -0.875 to 0.875
- b_out: float32 [768], replicated, may hold values from -2 to 2
- table_pos: float32 [12, 127], replicated, may hold values from -3 to 3
- table_x: float32 [12, 63], replicated, may hold values from -3 to 3
- table_y: float32 [12, 63], replicated, may hold values from -3 to 3
- gain_one: float32 [768], replicated, may hold values from 0.5 to 1.5
- bias_one: float32 [768], replicated, may hold values from -2 to 2
- w_up: bfloat16 [768, 3072], P('page'), may hold values from -0.21875 to 0.21875
- b_up: float32 [3072], replicated, may hold values from -3 to 3
- w_down: bfloat16 [3072, 768], P('page'), may hold values from -0.109375 to 0.109375
- b_down: float32 [768], replicated, may hold values from -2 to 2
- gain_two: float32 [768], replicated, may hold values from 0.5 to 1.5
- bias_two: float32 [768], replicated, may hold values from -2 to 2
Outputs:
- output: bfloat16 [2, 16, 512, 768], P('mod', 'page')
- grad_states: bfloat16 [2, 16, 512, 768], P('mod', 'page')
- grad_conv_weight: float32 [3, 768], replicated
- grad_conv_bias: float32 [768], replicated
- grad_w_query: float32 [768, 768], P('page')
- grad_b_query: float32 [768], replicated
- grad_w_key: float32 [768, 768], P('page')
- grad_w_value: float32 [768, 768], P('page')
- grad_b_value: float32 [768], replicated
- grad_w_out: float32 [768, 768], P('page')
- grad_b_out: float32 [768], replicated
- grad_table_pos: float32 [12, 127], replicated
- grad_table_x: float32 [12, 63], replicated
- grad_table_y: float32 [12, 63], replicated
- grad_gain_one: float32 [768], replicated
- grad_bias_one: float32 [768], replicated
- grad_w_up: float32 [768, 3072], P('page')
- grad_b_up: float32 [3072], replicated
- grad_w_down: float32 [3072, 768], P('page')
- grad_b_down: float32 [768], replicated
- grad_gain_two: float32 [768], replicated
- grad_bias_two: float32 [768], replicated
Inputs may be any that keep to these rules, and one draw needn't show every extreme that they name: `segments`: in each row the page ids never fall and each of the 8 pages has 1 to 128 text tokens, one page exactly 128.
All inputs are finite; a program needn't handle non-finite values.
Results may differ from a plain program's by a relative error of at most 0.017.
The roundings to bfloat16 on the way count: a program that leaves them out, or rounds other values in their place, can miss the bound.
Values may be sent and summed in bfloat16 or wider, within the bound.
No kernel may reach another device: no remote copies, remote signals or barrier semaphores. Data moves between devices by JAX's collectives and lax.ppermute only.
A program may use at most 192 MiB of HBM per device.

v0:
```python
import jax
import jax.numpy as jnp
import numpy as np
from jax import lax
from jax.sharding import PartitionSpec as P

HEADS = 12
HEAD = 64
GRID = 8
POS_BINS = 64
BOX_BINS = 32
PATCH = 64
TEXT = 512


dilation = 2
norm_eps = 1e-05
mask_fill = -1000000000.0
highest = lax.Precision.HIGHEST


def shifted(values, offset, fill_value):
    padding = jnp.full((abs(offset),) + values.shape[1:], fill_value, values.dtype)
    if offset > 0:
        return jnp.concatenate([values[offset:], padding], axis=0)
    return jnp.concatenate([padding, values[:offset]], axis=0)


def dilated_mix(inputs, page_ids, conv_weight, conv_bias):
    summed = inputs + conv_bias + conv_weight[1] * inputs
    for tap_index, offset in ((0, -dilation), (2, dilation)):
        moved_rows = shifted(inputs, offset, 0.0)
        moved_pages = shifted(page_ids, offset, -1)
        same_page = (moved_pages == page_ids)[:, None]
        summed = summed + conv_weight[tap_index] * jnp.where(same_page, moved_rows, 0.0)
    return summed


def bias_blocks(table_pos, table_x, table_y):
    head_count = table_pos.shape[0]
    width_all = POS_BINS + 2 * BOX_BINS
    rows_list = []
    offset_col = 0
    for rel_table, bin_count in ((table_pos, POS_BINS), (table_x, BOX_BINS), (table_y, BOX_BINS)):
        index_grid = np.arange(bin_count)[None, :] - np.arange(bin_count)[:, None] + bin_count - 1
        one_block = jnp.take(rel_table, jnp.asarray(index_grid, dtype=jnp.int32), axis=1)
        left_zero = jnp.zeros((head_count, bin_count, offset_col), one_block.dtype)
        right_zero = jnp.zeros(
            (head_count, bin_count, width_all - offset_col - bin_count), one_block.dtype
        )
        rows_list.append(jnp.concatenate([left_zero, one_block, right_zero], axis=2))
        offset_col = offset_col + bin_count
    return jnp.concatenate(rows_list, axis=1)


def bin_features(pos_bins, bins_x, bins_y):
    return jnp.concatenate(
        [
            jax.nn.one_hot(pos_bins, POS_BINS, dtype=jnp.float32),
            jax.nn.one_hot(bins_x, BOX_BINS, dtype=jnp.float32),
            jax.nn.one_hot(bins_y, BOX_BINS, dtype=jnp.float32),
        ],
        axis=1,
    )


def token_ids(text_pages, text_x, text_y):
    text_index = jnp.arange(TEXT, dtype=jnp.int32)
    text_pos = text_index * POS_BINS // TEXT
    patch_pos = text_index % PATCH * POS_BINS // PATCH
    patch_page = text_index // PATCH
    patch_x = text_index % GRID * BOX_BINS // GRID
    patch_y = text_index // GRID % GRID * BOX_BINS // GRID
    page_ids = jnp.stack([text_pages, patch_page])
    pos_bins = jnp.stack([text_pos, patch_pos])
    bins_x = jnp.stack([text_x, patch_x])
    bins_y = jnp.stack([text_y, patch_y])
    return (page_ids, pos_bins, bins_x, bins_y)


def layer_norm(values, gain_vec, bias_vec):
    centered = values - jnp.mean(values, axis=-1, keepdims=True)
    variance = jnp.mean(centered * centered, axis=-1, keepdims=True)
    return centered * lax.rsqrt(variance + norm_eps) * gain_vec + bias_vec


def exact_gelu(values):
    return jax.nn.gelu(values, approximate=False)


def plain_dot(left_side, right_side):
    return jnp.dot(left_side, right_side, preferred_element_type=jnp.float32)


def dot_left_t(left_side, right_side):
    return lax.dot_general(
        left_side, right_side, (((0,), (0,)), ((), ())), preferred_element_type=jnp.float32
    )


def dot_right_t(left_side, right_side):
    return lax.dot_general(
        left_side, right_side, (((1,), (1,)), ((), ())), preferred_element_type=jnp.float32
    )


def column_sum(values):
    return jnp.sum(values, axis=0, dtype=jnp.float32)


def local(
    states,
    cotangent,
    segments,
    box_x,
    box_y,
    conv_weight,
    conv_bias,
    w_query,
    b_query,
    w_key,
    w_value,
    b_value,
    w_out,
    b_out,
    table_pos,
    table_x,
    table_y,
    gain_one,
    bias_one,
    w_up,
    b_up,
    w_down,
    b_down,
    gain_two,
    bias_two,
):
    bf16 = jnp.bfloat16
    f32 = jnp.float32
    is_text = lax.axis_index("mod") == 0
    full_query, full_key, full_value, full_out, full_up, full_down = (
        lax.all_gather(w_query, "page", axis=0, tiled=True),
        lax.all_gather(w_key, "page", axis=0, tiled=True),
        lax.all_gather(w_value, "page", axis=0, tiled=True),
        lax.all_gather(w_out, "page", axis=0, tiled=True),
        lax.all_gather(w_up, "page", axis=0, tiled=True),
        lax.all_gather(w_down, "page", axis=0, tiled=True),
    )
    blocks_low = bias_blocks(table_pos.astype(bf16), table_x.astype(bf16), table_y.astype(bf16))
    unused_blocks, blocks_pull = jax.vjp(bias_blocks, table_pos, table_x, table_y)
    text_len = states.shape[2]
    d_model = states.shape[3]
    score_scale = HEAD ** (-0.5)
    own_states = states[0, 0].astype(f32)
    page_ids, pos_bins, bins_x, bins_y = token_ids(segments[0], box_x[0], box_y[0])
    own_pages = jnp.where(is_text, page_ids[0], page_ids[1])
    key_pages = page_ids.reshape(-1)
    key_feats = bin_features(pos_bins.reshape(-1), bins_x.reshape(-1), bins_y.reshape(-1))
    own_feats = jnp.where(is_text, key_feats[:text_len], key_feats[text_len:])
    key_feats_low = key_feats.astype(bf16)

    def mix_fn(inputs_f, weight_f, bias_f):
        return dilated_mix(inputs_f, own_pages, weight_f, bias_f)

    mixed, mix_pull = jax.vjp(mix_fn, own_states, conv_weight, conv_bias)
    mixed_low = mixed.astype(bf16)
    queries = (plain_dot(mixed_low, full_query) + b_query).astype(bf16)
    own_keys = plain_dot(mixed_low, full_key).astype(bf16)
    own_values = (plain_dot(mixed_low, full_value) + b_value).astype(bf16)
    keys_all = lax.all_gather(own_keys, "mod", axis=0, tiled=True)
    values_all = lax.all_gather(own_values, "mod", axis=0, tiled=True)
    head_q = queries.reshape(text_len, HEADS, HEAD)
    head_k = keys_all.reshape(2 * text_len, HEADS, HEAD)
    head_v = values_all.reshape(2 * text_len, HEADS, HEAD)
    lookup = jnp.einsum(
        "qa,hab->hqb", own_feats.astype(bf16), blocks_low, preferred_element_type=f32
    ).astype(bf16)
    same_page = own_pages[:, None] == key_pages[None, :]

    def scores_of():
        raw_scores = (
            jnp.einsum("qhd,khd->hqk", head_q, head_k, preferred_element_type=f32) * score_scale
        )
        raw_scores = raw_scores + jnp.einsum(
            "hqb,kb->hqk", lookup, key_feats_low, preferred_element_type=f32
        )
        return jnp.where(same_page[None], raw_scores, mask_fill)

    scores = scores_of()
    row_max = jnp.max(scores, axis=-1, keepdims=True)
    log_total = row_max + jnp.log(jnp.sum(jnp.exp(scores - row_max), axis=-1, keepdims=True))
    attn_prob = jnp.exp(scores - log_total)
    context = (
        jnp.einsum("hqk,khd->qhd", attn_prob.astype(bf16), head_v, preferred_element_type=f32)
        .reshape(text_len, d_model)
        .astype(bf16)
    )
    first_sum = mixed + plain_dot(context, full_out) + b_out
    normed, norm_one_pull = jax.vjp(layer_norm, first_sum, gain_one, bias_one)
    normed_low = normed.astype(bf16)
    hidden = plain_dot(normed_low, full_up) + b_up
    active, gelu_pull = jax.vjp(exact_gelu, hidden)
    active_low = active.astype(bf16)
    ffn_out = plain_dot(active_low, full_down) + b_down
    output_row, norm_two_pull = jax.vjp(layer_norm, normed + ffn_out, gain_two, bias_two)
    out_rows = [output_row.astype(bf16)]
    grad_out = cotangent[0, 0].astype(f32)
    grad_sum_two, grad_gain_two, grad_bias_two = norm_two_pull(grad_out)
    grad_ffn = grad_sum_two.astype(bf16)
    grad_w_down = dot_left_t(active_low, grad_ffn)
    grad_b_down = column_sum(grad_ffn)
    (grad_hidden_f,) = gelu_pull(dot_right_t(grad_ffn, full_down))
    grad_hidden = grad_hidden_f.astype(bf16)
    grad_w_up = dot_left_t(normed_low, grad_hidden)
    grad_b_up = column_sum(grad_hidden)
    grad_normed = grad_sum_two + dot_right_t(grad_hidden, full_up)
    grad_first, grad_gain_one, grad_bias_one = norm_one_pull(grad_normed)
    grad_branch = grad_first.astype(bf16)
    grad_w_out = dot_left_t(context, grad_branch)
    grad_b_out = column_sum(grad_branch)
    grad_context = dot_right_t(grad_branch, full_out).astype(bf16).reshape(text_len, HEADS, HEAD)
    scores = scores_of()
    attn_prob = jnp.exp(scores - log_total)
    grad_prob = jnp.einsum("qhd,khd->hqk", grad_context, head_v, preferred_element_type=f32)
    grad_values = jnp.einsum(
        "hqk,qhd->khd", attn_prob.astype(bf16), grad_context, preferred_element_type=f32
    ).reshape(2 * text_len, d_model)
    grad_scores = (
        attn_prob * (grad_prob - jnp.sum(attn_prob * grad_prob, axis=-1, keepdims=True))
    ).astype(bf16)
    grad_queries = (
        (jnp.einsum("hqk,khd->qhd", grad_scores, head_k, preferred_element_type=f32) * score_scale)
        .reshape(text_len, d_model)
        .astype(bf16)
    )
    grad_keys = (
        jnp.einsum("hqk,qhd->khd", grad_scores, head_q, preferred_element_type=f32) * score_scale
    ).reshape(2 * text_len, d_model)
    grad_lookup = jnp.einsum("hqk,kb->hqb", grad_scores, key_feats_low, preferred_element_type=f32)
    grad_blocks = jnp.einsum("qa,hqb->hab", own_feats, grad_lookup, precision=highest)
    own_grad_keys = lax.psum_scatter(
        grad_keys.astype(jnp.bfloat16), "mod", scatter_dimension=0, tiled=True
    ).astype(jnp.float32)
    own_grad_values = lax.psum_scatter(
        grad_values.astype(jnp.bfloat16), "mod", scatter_dimension=0, tiled=True
    ).astype(jnp.float32)
    own_grad_keys = own_grad_keys.astype(bf16)
    own_grad_values = own_grad_values.astype(bf16)
    grad_w_query = dot_left_t(mixed_low, grad_queries)
    grad_b_query = column_sum(grad_queries)
    grad_w_key = dot_left_t(mixed_low, own_grad_keys)
    grad_w_value = dot_left_t(mixed_low, own_grad_values)
    grad_b_value = column_sum(own_grad_values)
    grad_mixed = (
        grad_first
        + dot_right_t(grad_queries, full_query)
        + dot_right_t(own_grad_keys, full_key)
        + dot_right_t(own_grad_values, full_value)
    )
    grad_in, grad_conv_w, grad_conv_b = mix_pull(grad_mixed)
    grad_rows = [grad_in.astype(bf16)]
    row_grads = (
        grad_conv_w,
        grad_conv_b,
        grad_w_query,
        grad_b_query,
        grad_w_key,
        grad_w_value,
        grad_b_value,
        grad_w_out,
        grad_b_out,
        grad_blocks,
        grad_gain_one,
        grad_bias_one,
        grad_w_up,
        grad_b_up,
        grad_w_down,
        grad_b_down,
        grad_gain_two,
        grad_bias_two,
    )
    (
        g_conv_w,
        g_conv_b,
        g_wq,
        g_bq,
        g_wk,
        g_wv,
        g_bv,
        g_wo,
        g_bo,
        g_blocks,
        g_gain1,
        g_bias1,
        g_wup,
        g_bup,
        g_wdown,
        g_bdown,
        g_gain2,
        g_bias2,
    ) = row_grads
    g_tpos, g_tx, g_ty = blocks_pull(g_blocks)
    (
        g_conv_w,
        g_conv_b,
        g_bq,
        g_bv,
        g_bo,
        g_tpos,
        g_tx,
        g_ty,
        g_gain1,
        g_bias1,
        g_bup,
        g_bdown,
        g_gain2,
        g_bias2,
    ) = lax.psum(
        (
            g_conv_w,
            g_conv_b,
            g_bq,
            g_bv,
            g_bo,
            g_tpos,
            g_tx,
            g_ty,
            g_gain1,
            g_bias1,
            g_bup,
            g_bdown,
            g_gain2,
            g_bias2,
        ),
        ("mod", "page"),
    )
    shard_wq, shard_wk, shard_wv, shard_wo, shard_wup, shard_wdown = (
        lax.psum_scatter(g_wq, "page", scatter_dimension=0, tiled=True),
        lax.psum_scatter(g_wk, "page", scatter_dimension=0, tiled=True),
        lax.psum_scatter(g_wv, "page", scatter_dimension=0, tiled=True),
        lax.psum_scatter(g_wo, "page", scatter_dimension=0, tiled=True),
        lax.psum_scatter(g_wup, "page", scatter_dimension=0, tiled=True),
        lax.psum_scatter(g_wdown, "page", scatter_dimension=0, tiled=True),
    )
    shard_wq, shard_wk, shard_wv, shard_wo, shard_wup, shard_wdown = (
        lax.psum(shard_wq.astype(jnp.bfloat16), "mod").astype(jnp.float32),
        lax.psum(shard_wk.astype(jnp.bfloat16), "mod").astype(jnp.float32),
        lax.psum(shard_wv.astype(jnp.bfloat16), "mod").astype(jnp.float32),
        lax.psum(shard_wo.astype(jnp.bfloat16), "mod").astype(jnp.float32),
        lax.psum(shard_wup.astype(jnp.bfloat16), "mod").astype(jnp.float32),
        lax.psum(shard_wdown.astype(jnp.bfloat16), "mod").astype(jnp.float32),
    )
    output = jnp.stack(out_rows)[None]
    grad_states = jnp.stack(grad_rows)[None]
    return (
        output,
        grad_states,
        g_conv_w,
        g_conv_b,
        shard_wq,
        g_bq,
        shard_wk,
        shard_wv,
        g_bv,
        shard_wo,
        g_bo,
        g_tpos,
        g_tx,
        g_ty,
        g_gain1,
        g_bias1,
        shard_wup,
        g_bup,
        shard_wdown,
        g_bdown,
        g_gain2,
        g_bias2,
    )


def solution(mesh):
    return jax.shard_map(
        local,
        mesh=mesh,
        in_specs=(
            P("mod", "page", None, None),
            P("mod", "page", None, None),
            P("page", None),
            P("page", None),
            P("page", None),
            P(),
            P(),
            P("page", None),
            P(),
            P("page", None),
            P("page", None),
            P(),
            P("page", None),
            P(),
            P(),
            P(),
            P(),
            P(),
            P(),
            P("page", None),
            P(),
            P("page", None),
            P(),
            P(),
            P(),
        ),
        out_specs=(
            P("mod", "page", None, None),
            P("mod", "page", None, None),
            P(),
            P(),
            P("page", None),
            P(),
            P("page", None),
            P("page", None),
            P(),
            P("page", None),
            P(),
            P(),
            P(),
            P(),
            P(),
            P(),
            P("page", None),
            P(),
            P("page", None),
            P(),
            P(),
            P(),
        ),
        check_vma=False,
    )
```

profile of v0, /device:TPU:0, one launch (start us, length us, event | category | flops | bytes accessed | tf_op | source)
XLA Modules:
  0.0 1007.3 jit_solution(7655687598830141367)
XLA Ops:
  14.8 36.6 %all-gather.15.cloned.1.call-done = bf16[768,768]{1,0:T(8,128)(2,1)} async-done(((bf16[48,768]{1,0:T(8,128)(2,1)}), bf16[768,768]{1,0:T(8,128)(2,1)}) %all-gather.15.cloned.1.call-update) | async-done | bytes 1179664 | tf_op jit(solution)/shard_map/all_gather | solution.py:143
  51.4 3.0 convolution_convert_fusion.2
  54.5 36.5 %all-gather.9.cloned.1.call-done = bf16[768,768]{1,0:T(8,128)(2,1)} async-done(((bf16[48,768]{1,0:T(8,128)(2,1)}), bf16[768,768]{1,0:T(8,128)(2,1)}) %all-gather.9.cloned.1.call-update) | async-done | bytes 1179664 | tf_op jit(solution)/shard_map/all_gather | solution.py:144
  91.0 2.9 add_convert_fusion.4
  97.7 3.5 gather_fusion.1
  101.5 3.2 gather_fusion.2
  106.1 12.1 %gather_fusion = bf16[4096,12]{1,0:T(8,128)(2,1)S(1)} fusion(bf16[12,127]{0,1:T(8,128)(2,1)S(1)} %copy.108, s32[4096]{0:T(1024)S(1)} %broadcast_clamp_fusion), kind=kCustom, calls=%fused_computation.2 | custom fusion | bytes 212992 | tf_op jit(solution)/shard_map/jit(_take)/gather | solution.py:46
  120.2 10.4 %all-gather.13.cloned.1.call-done = bf16[768,768]{1,0:T(8,128)(2,1)} async-done(((bf16[48,768]{1,0:T(8,128)(2,1)}), bf16[768,768]{1,0:T(8,128)(2,1)}) %all-gather.13.cloned.1.call-update) | async-done | bytes 1179664 | tf_op jit(solution)/shard_map/all_gather | solution.py:142
  130.6 2.9 add_convert_fusion.3
  135.0 23.2 %all-gather.17.cloned.1.call-done = bf16[1024,768]{1,0:T(8,128)(2,1)} async-done(((bf16[512,768]{1,0:T(8,128)(2,1)}), bf16[1024,768]{1,0:T(8,128)(2,1)}) %all-gather.17.cloned.1.call-update) | async-done | bytes 1572880 | tf_op jit(solution)/shard_map/all_gather | solution.py:170
  159.9 10.6 %fusion.113 = f32[12,512,1024]{2,1,0:T(8,128)} fusion(bf16[512,12,64]{0,2,1:T(8,128)(2,1)S(1)} %bitcast.158, bf16[1024,12,64]{0,2,1:T(8,128)(2,1)S(1)} %bitcast.154), kind=kOutput, calls=%fused_computation.205 | convolution fusion | flops 805306368 | bytes 27525120 | tf_op jit(solution)/shard_map/qhd,khd->hqk/dot_general | solution.py:182
  170.5 16.8 %all-gather.11.cloned.1.call-done = bf16[1024,768]{1,0:T(8,128)(2,1)} async-done(((bf16[512,768]{1,0:T(8,128)(2,1)}), bf16[1024,768]{1,0:T(8,128)(2,1)}) %all-gather.11.cloned.1.call-update) | async-done | bytes 1572880 | tf_op jit(solution)/shard_map/all_gather | solution.py:171
  189.1 20.5 %fusion.106 = (f32[12,512]{1,0:T(8,128)S(1)}, f32[12,512,1024]{2,1,0:T(8,128)}) fusion(f32[1024,128]{1,0:T(8,128)S(1)} %add_convert_fusion.7, bf16[12,32,32]{2,1,0:T(8,128)(2,1)S(1)} %bitcast.176, bf16[12,64,64]{2,1,0:T(8,128)(2,1)S(1)} %bitcast.170, bf16[12,32,32]{2,1,0:T(8,128)(2,1)S(1)} %bitcast.175, bf16[128,128]{1,0:T(8,128)(2,1)S(1)} %pad.38.clone, ...), kind=kOutput, calls=%fused_computation.202 | convolution fusion | flops 1840834560 | bytes 52125696 | tf_op jit(solution)/shard_map/hqb,kb->hqk/dot_general | solution.py:184
  209.6 11.0 %exponential_reduce_fusion = f32[12,512]{1,0:T(8,128)S(1)} fusion(f32[12,512,1024]{2,1,0:T(8,128)} %get-tuple-element.170, f32[12,512]{1,0:T(8,128)S(1)} %get-tuple-element.169), kind=kLoop, calls=%fused_computation.9 | loop fusion | flops 12576768 | bytes 25214976 | tf_op jit(solution)/shard_map/reduce_sum | solution.py:191
  220.7 11.3 %fusion.27 = bf16[12,64,512]{2,1,0:T(8,128)(2,1)} fusion(bf16[1024,12,64]{0,2,1:T(8,128)(2,1)S(1)} %bitcast.156, f32[12,512,1024]{2,1,0:T(8,128)} %get-tuple-element.170, f32[12,512]{1,0:T(8,128)S(1)} %log_add_fusion), kind=kOutput, calls=%fused_computation.85 | convolution fusion | flops 818282496 | bytes 27549696 | tf_op jit(solution)/shard_map/hqk,khd->qhd/dot_general | solution.py:194
  232.0 2.9 fusion.111
  235.3 47.3 %all-gather.21.cloned.1.call-done = bf16[768,3072]{1,0:T(8,128)(2,1)} async-done(((bf16[48,3072]{1,0:T(8,128)(2,1)}), bf16[768,3072]{1,0:T(8,128)(2,1)}) %all-gather.21.cloned.1.call-update) | async-done | bytes 4718608 | tf_op jit(solution)/shard_map/all_gather | solution.py:146
  282.6 20.2 %multiply_convert_fusion.1 = (bf16[512,3072]{1,0:T(8,128)(2,1)}, f32[512,3072]{1,0:T(8,128)}, f32[512,3072]{1,0:T(8,128)}) fusion(f32[3072]{0:T(1024)S(1)} %copy-done.76, bf16[768,3072]{1,0:T(8,128)(2,1)} %all-gather.21.cloned.1.call-done, f32[512,768]{1,0:T(8,128)S(1)} %get-tuple-element.172, f32[768]{0:T(1024)S(1)} %copy-done.81, f32[768]{0:T(1024)S(1)} %copy-done.69, ...), kind=kOutput, calls=%fused_computation.16 | convolution fusion | flops 2521694208 | bytes 22042624 | tf_op jit(solution)/shard_map/dot_general | solution.py:92
  302.7 34.1 %all-gather.23.cloned.1.call-done = bf16[3072,768]{1,0:T(8,128)(2,1)} async-done(((bf16[192,768]{1,0:T(8,128)(2,1)}), bf16[3072,768]{1,0:T(8,128)(2,1)}) %all-gather.23.cloned.1.call-update) | async-done | bytes 4718608 | tf_op jit(solution)/shard_map/all_gather | solution.py:147
  336.8 6.0 fusion.112
  347.4 9.0 convert_reduce_fusion
  356.4 3.7 multiply_reduce_fusion.1
  365.4 2.3 copy.116
  367.7 11.9 %fusion.15 = bf16[12,64,1024]{2,1,0:T(8,128)(2,1)} fusion(bf16[512,12,64]{0,2,1:T(8,128)(2,1)} %bitcast.161, f32[12,512,1024]{2,1,0:T(8,128)} %get-tuple-element.170, f32[12,512]{1,0:T(8,128)S(1)} %log_add_fusion), kind=kOutput, calls=%fused_computation.42 | convolution fusion | flops 818675712 | bytes 27549696 | tf_op jit(solution)/shard_map/hqk,qhd->khd/dot_general | solution.py:225
  379.7 17.1 %multiply_reduce_fusion = (f32[12,512]{1,0:T(8,128)S(1)}, f32[12,512,1024]{2,1,0:T(8,128)}) fusion(f32[12,512,1024]{2,1,0:T(8,128)} %get-tuple-element.170, f32[12,512]{1,0:T(8,128)S(1)} %log_add_fusion, bf16[512,12,64]{0,2,1:T(8,128)(2,1)} %bitcast.162, bf16[1024,12,64]{0,2,1:T(8,128)(2,1)S(1)} %bitcast.157), kind=kOutput, calls=%fused_computation.7 | convolution fusion | flops 824174592 | bytes 52740096 | tf_op jit(solution)/shard_map/qhd,khd->hqk/dot_general | solution.py:224
  396.8 16.7 %multiply_convert_fusion = bf16[12,512,1024]{2,1,0:T(8,128)(2,1)S(1)} fusion(f32[12,512,1024]{2,1,0:T(8,128)} %get-tuple-element.178, f32[12,512,1024]{2,1,0:T(8,128)} %get-tuple-element.170, f32[12,512]{1,0:T(8,128)S(1)} %get-tuple-element.177, f32[12,512]{1,0:T(8,128)S(1)} %log_add_fusion), kind=kLoop, calls=%fused_computation.6 | loop fusion | flops 25165824 | bytes 62963712 | tf_op jit(solution)/shard_map/convert_element_type | solution.py:230
  413.5 4.1 multiply_convert_fusion.2
  423.5 8.7 convert_reduce_fusion.5
  433.1 2.2 fusion.116
  436.4 3.4 fusion.118
  439.9 3.6 reduce-scatter.9.cloned.1.call-done
  443.5 3.3 fusion.117
  448.2 7.2 fusion.95
  456.6 8.3 fusion.120
  467.5 9.0 fusion.56
  476.5 2.6 convolution_bitcast_fusion
  481.1 7.0 scatter_custom_fusion.2
  488.1 6.9 scatter_custom_fusion.1
  495.0 3.0 copy.130
  497.9 22.7 %scatter_custom_fusion = f32[12,127]{0,1:T(8,128)S(1)} fusion(s32[4096]{0:T(1024)} %constant.301, f32[4096,12]{1,0:T(8,128)} %bitcast.168, f32[]{:T(128)} %constant.196.clone.1), kind=kCustom, calls=%fused_computation.123 | custom fusion | flops 49152 | bytes 6608 | tf_op jit(solution)/shard_map/transpose(jvp(jit(_take)))/scatter-add | solution.py:46
  520.6 2.3 fusion.114
  527.2 49.2 %reduce-scatter.13.cloned.1.call-done = f32[48,768]{1,0:T(8,128)} async-done(((f32[768,768]{1,0:T(8,128)}), f32[48,768]{1,0:T(8,128)}) %reduce-scatter.13.cloned.1.call-update) | async-done | bytes 147472 | tf_op jit(solution)/shard_map/reduce_scatter | solution.py:338
  577.9 64.2 %reduce-scatter.17.cloned.1.call-done = f32[48,768]{1,0:T(8,128)} async-done(((f32[768,768]{1,0:T(8,128)}), f32[48,768]{1,0:T(8,128)}) %reduce-scatter.17.cloned.1.call-update) | async-done | bytes 147472 | tf_op jit(solution)/shard_map/reduce_scatter | solution.py:340
  643.7 64.5 %reduce-scatter.15.cloned.1.call-done = f32[48,768]{1,0:T(8,128)} async-done(((f32[768,768]{1,0:T(8,128)}), f32[48,768]{1,0:T(8,128)}) %reduce-scatter.15.cloned.1.call-update) | async-done | bytes 147472 | tf_op jit(solution)/shard_map/reduce_scatter | solution.py:339
  709.8 112.8 %reduce-scatter.21.cloned.1.call-done = f32[48,3072]{1,0:T(8,128)} async-done(((f32[768,3072]{1,0:T(8,128)}), f32[48,3072]{1,0:T(8,128)}) %reduce-scatter.21.cloned.1.call-update) | async-done | bytes 589840 | tf_op jit(solution)/shard_map/reduce_scatter | solution.py:342
  824.4 113.8 %reduce-scatter.23.cloned.1.call-done = f32[192,768]{1,0:T(8,128)} async-done(((f32[3072,768]{1,0:T(8,128)}), f32[192,768]{1,0:T(8,128)}) %reduce-scatter.23.cloned.1.call-update) | async-done | bytes 589840 | tf_op jit(solution)/shard_map/reduce_scatter | solution.py:343
  942.3 2.4 fusion.99
  945.0 44.6 %all-reduce.11 = (f32[3,768]{1,0:T(4,128)}, f32[768]{0:T(1024)}, f32[768]{0:T(1024)}, f32[768]{0:T(1024)}, f32[768]{0:T(1024)}, /*index=5*/f32[12,127]{0,1:T(8,1...) all-reduce(f32[3,768]{1,0:T(4,128)S(1)} %pad_add_fusion, ...), channel_id=1, replica_groups=mesh['mod'=2,'page'=16] {'mod','page'}, use_global_device_ids=true, to_apply=%region_16.18 | all-reduce | flops 15324 | bytes 122592 | tf_op jit(solution)/shard_map/psum | solution.py:318
  (298 shorter events, 70.6 us)
Async XLA Ops:
  7.2 44.2 %all-gather.15.cloned.1.call-start = ((), (), s32[]{:S(2)}) async-start(), calls=%async_computation.11 | async-start | bytes 1253376 | tf_op jit(solution)/shard_map/all_gather | solution.py:143
  7.9 83.0 %all-gather.9.cloned.1.call-start = ((), (), s32[]{:S(2)}) async-start(), calls=%async_computation.8 | async-start | bytes 1253376 | tf_op jit(solution)/shard_map/all_gather | solution.py:144
  8.7 121.9 %all-gather.13.cloned.1.call-start = ((), (), s32[]{:S(2)}) async-start(), calls=%async_computation.10 | async-start | bytes 1253376 | tf_op jit(solution)/shard_map/all_gather | solution.py:142
  9.4 148.8 %all-gather.17.cloned.1.call-start = ((), (), s32[]{:S(2)}) async-start(), calls=%async_computation.12 | async-start | bytes 2359296 | tf_op jit(solution)/shard_map/all_gather | solution.py:170
  14.8 115.8 %copy-start.9 = (bf16[512,768]{1,0:T(8,128)(2,1)}, bf16[512,768]{1,0:T(8,128)(2,1)S(1)}, u32[]{:S(2)}) copy-start(bf16[512,768]{1,0:T(8,128)(2,1)S(1)} %get-tuple-element.155) | copy-start | bytes 2359300
  51.4 39.6 %copy-start.77 = (f32[768]{0:T(1024)S(1)}, f32[768]{0:T(1024)}, u32[]{:S(2)}) copy-start(f32[768]{0:T(1024)} %param.44) | copy-start | bytes 9220
  54.4 41.8 %copy-start.70 = (s32[1,512]{1,0:T(1,128)S(1)}, s32[1,512]{1,0:T(1,128)}, u32[]{:S(2)}) copy-start(s32[1,512]{1,0:T(1,128)} %param.36) | copy-start | bytes 6148
  54.4 41.8 %copy-start.71 = (s32[1,512]{1,0:T(1,128)S(1)}, s32[1,512]{1,0:T(1,128)}, u32[]{:S(2)}) copy-start(s32[1,512]{1,0:T(1,128)} %param.37) | copy-start | bytes 6148
  54.4 41.9 %copy-start.67 = (s32[1024]{0:T(1024)S(1)}, s32[1024]{0:T(1024)}, u32[]{:S(2)}) copy-start(s32[1024]{0:T(1024)} %constant.303) | copy-start | bytes 12292
  54.4 41.9 %copy-start.55 = (f32[12,127]{1,0:T(8,128)S(1)}, f32[12,127]{1,0:T(8,128)}, u32[]{:S(2)}) copy-start(f32[12,127]{1,0:T(8,128)} %param.47) | copy-start | bytes 18292
  54.4 41.9 %copy-start.56 = (f32[12,63]{1,0:T(8,128)S(1)}, f32[12,63]{1,0:T(8,128)}, u32[]{:S(2)}) copy-start(f32[12,63]{1,0:T(8,128)} %param.48) | copy-start | bytes 9076
  54.4 41.9 %copy-start.57 = (f32[12,63]{1,0:T(8,128)S(1)}, f32[12,63]{1,0:T(8,128)}, u32[]{:S(2)}) copy-start(f32[12,63]{1,0:T(8,128)} %param.49) | copy-start | bytes 9076
  54.5 132.9 %all-gather.11.cloned.1.call-start = ((), (), s32[]{:S(2)}) async-start(), calls=%async_computation.9 | async-start | bytes 2359296 | tf_op jit(solution)/shard_map/all_gather | solution.py:171
  93.9 138.0 %all-gather.19.cloned.1.call-start = ((), (), s32[]{:S(2)}) async-start(), calls=%async_computation.13 | async-start | bytes 1253376 | tf_op jit(solution)/shard_map/all_gather | solution.py:145
  94.5 188.0 %all-gather.21.cloned.1.call-start = ((), (), s32[]{:S(2)}) async-start(), calls=%async_computation.14 | async-start | bytes 5013504 | tf_op jit(solution)/shard_map/all_gather | solution.py:146
  95.3 241.5 %all-gather.23.cloned.1.call-start = ((), (), s32[]{:S(2)}) async-start(), calls=%async_computation.15 | async-start | bytes 5013504 | tf_op jit(solution)/shard_map/all_gather | solution.py:147
  96.0 339.4 %reduce-scatter.11.cloned.1.call-start = ((), (), s32[]{:S(2)}) async-start(), calls=%async_computation.17 | async-start | bytes 2359296 | tf_op jit(solution)/shard_map/reduce_scatter | solution.py:244
  97.7 22.1 %copy-start.27 = (pred[1024,64]{1,0:T(32,128)(4,1)}, pred[1024,64]{1,0:T(32,128)(4,1)S(1)}, u32[]{:S(2)}) copy-start(pred[1024,64]{1,0:T(32,128)(4,1)S(1)} %iota_compare_fusion.4) | copy-start | bytes 196612
  118.2 12.4 %copy-start.78 = (f32[768]{0:T(1024)S(1)}, f32[768]{0:T(1024)}, u32[]{:S(2)}) copy-start(f32[768]{0:T(1024)} %param.41) | copy-start | bytes 9220
  119.8 10.8 %copy-start.29 = (pred[1024,32]{1,0:T(32,128)(4,1)}, pred[1024,32]{1,0:T(32,128)(4,1)S(1)}, u32[]{:S(2)}) copy-start(pred[1024,32]{1,0:T(32,128)(4,1)S(1)} %get-tuple-element.183) | copy-start | bytes 98308
  119.8 10.8 %copy-start.31 = (pred[1024,32]{1,0:T(32,128)(4,1)}, pred[1024,32]{1,0:T(32,128)(4,1)S(1)}, u32[]{:S(2)}) copy-start(pred[1024,32]{1,0:T(32,128)(4,1)S(1)} %get-tuple-element.184) | copy-start | bytes 98308
  120.2 68.9 %copy-start.20 = (f32[1024,128]{1,0:T(8,128)}, f32[1024,128]{1,0:T(8,128)S(1)}, u32[]{:S(2)}) copy-start(f32[1024,128]{1,0:T(8,128)S(1)} %add_convert_fusion.7) | copy-start | bytes 1572868
  135.0 25.0 %copy-start.7 = (bf16[512,768]{0,1:T(8,128)(2,1)}, bf16[512,768]{0,1:T(8,128)(2,1)S(1)}, u32[]{:S(2)}) copy-start(bf16[512,768]{0,1:T(8,128)(2,1)S(1)} %copy.106) | copy-start | bytes 2359300
  159.9 10.6 %copy-start.1 = (bf16[1024,768]{0,1:T(8,128)(2,1)}, bf16[1024,768]{0,1:T(8,128)(2,1)S(1)}, u32[]{:S(2)}) copy-start(bf16[1024,768]{0,1:T(8,128)(2,1)S(1)} %copy.107) | copy-start | bytes 4718596
  170.5 18.6 %copy-start.34 = (bf16[64,64,12]{1,0,2:T(8,128)(2,1)S(1)}, bf16[64,64,12]{1,0,2:T(8,128)(2,1)}, u32[]{:S(2)}) copy-start(bf16[64,64,12]{1,0,2:T(8,128)(2,1)} %copy.109) | copy-start | bytes 294916
  170.5 18.6 %copy-start.38 = (bf16[32,32,12]{1,0,2:T(8,128)(2,1)S(1)}, bf16[32,32,12]{1,0,2:T(8,128)(2,1)}, u32[]{:S(2)}) copy-start(bf16[32,32,12]{1,0,2:T(8,128)(2,1)} %copy.113) | copy-start | bytes 73732
  170.5 18.6 %copy-start.40 = (bf16[128,128]{1,0:T(8,128)(2,1)S(1)}, bf16[128,128]{1,0:T(8,128)(2,1)}, u32[]{:S(2)}) copy-start(bf16[128,128]{1,0:T(8,128)(2,1)} %pad.36.clone) | copy-start | bytes 98308
  220.7 11.3 %copy-start.79 = (f32[768]{0:T(1024)S(1)}, f32[768]{0:T(1024)}, u32[]{:S(2)}) copy-start(f32[768]{0:T(1024)} %param.46) | copy-start | bytes 9220
  234.9 121.5 %copy-start.18 = (f32[512,768]{1,0:T(8,128)}, f32[512,768]{1,0:T(8,128)S(1)}, u32[]{:S(2)}) copy-start(f32[512,768]{1,0:T(8,128)S(1)} %get-tuple-element.172) | copy-start | bytes 4718596
  234.9 47.7 %copy-start.69 = (f32[768]{0:T(1024)S(1)}, f32[768]{0:T(1024)}, u32[]{:S(2)}) copy-start(f32[768]{0:T(1024)} %param.50) | copy-start | bytes 9220
  234.9 47.7 %copy-start.76 = (f32[3072]{0:T(1024)S(1)}, f32[3072]{0:T(1024)}, u32[]{:S(2)}) copy-start(f32[3072]{0:T(1024)} %param.53) | copy-start | bytes 36868
  234.9 47.6 %copy-start.81 = (f32[768]{0:T(1024)S(1)}, f32[768]{0:T(1024)}, u32[]{:S(2)}) copy-start(f32[768]{0:T(1024)} %param.51) | copy-start | bytes 9220
  235.2 101.6 %copy-start.80 = (f32[768]{0:T(1024)S(1)}, f32[768]{0:T(1024)}, u32[]{:S(2)}) copy-start(f32[768]{0:T(1024)} %param.55) | copy-start | bytes 9220
  346.4 10.0 slice-start
  379.6 63.9 %reduce-scatter.9.cloned.1.call-start = ((), (), s32[]{:S(2)}) async-start(), calls=%async_computation.16 | async-start | bytes 2359296 | tf_op jit(solution)/shard_map/reduce_scatter | solution.py:241
  396.8 16.7 %copy-start.8 = (bf16[512,768]{0,1:T(8,128)(2,1)S(1)}, bf16[512,768]{0,1:T(8,128)(2,1)}, u32[]{:S(2)}) copy-start(bf16[512,768]{0,1:T(8,128)(2,1)} %copy-done.7) | copy-start | bytes 2359300
  418.5 107.1 %reduce-scatter.19.cloned.1.call-start = ((), (), s32[]{:S(2)}) async-start(), calls=%async_computation.21 | async-start | bytes 2506752 | tf_op jit(solution)/shard_map/reduce_scatter | solution.py:341
  422.0 154.3 %reduce-scatter.13.cloned.1.call-start = ((), (), s32[]{:S(2)}) async-start(), calls=%async_computation.18 | async-start | bytes 2506752 | tf_op jit(solution)/shard_map/reduce_scatter | solution.py:338
  435.3 206.9 %reduce-scatter.17.cloned.1.call-start = ((), (), s32[]{:S(2)}) async-start(), calls=%async_computation.20 | async-start | bytes 2506752 | tf_op jit(solution)/shard_map/reduce_scatter | solution.py:340
  439.8 268.5 %reduce-scatter.15.cloned.1.call-start = ((), (), s32[]{:S(2)}) async-start(), calls=%async_computation.19 | async-start | bytes 2506752 | tf_op jit(solution)/shard_map/reduce_scatter | solution.py:339
  446.8 375.8 %reduce-scatter.21.cloned.1.call-start = ((), (), s32[]{:S(2)}) async-start(), calls=%async_computation.22 | async-start | bytes 10027008 | tf_op jit(solution)/shard_map/reduce_scatter | solution.py:342
  455.4 482.8 %reduce-scatter.23.cloned.1.call-start = ((), (), s32[]{:S(2)}) async-start(), calls=%async_computation.23 | async-start | bytes 10027008 | tf_op jit(solution)/shard_map/reduce_scatter | solution.py:343
  464.9 526.7 %all-reduce.15.cloned.1.call-start = ((), (), s32[]{:S(2)}) async-start(), calls=%async_computation.24 | async-start | bytes 1769472 | tf_op jit(solution)/shard_map/psum | solution.py:346
  494.9 25.7 %copy-start.23 = (bf16[12,64,512]{2,1,0:T(8,128)(2,1)S(1)}, bf16[12,64,512]{2,1,0:T(8,128)(2,1)}, u32[]{:S(2)}) copy-start(bf16[12,64,512]{2,1,0:T(8,128)(2,1)} %copy-done.22) | copy-start | bytes 2359300
  577.9 362.1 %copy-start.46 = (f32[768]{0:T(1024)S(1)}, f32[768]{0:T(1024)}, u32[]{:S(2)}) copy-start(f32[768]{0:T(1024)} %copy-done.45) | copy-start | bytes 9220
  577.9 362.1 %copy-start.48 = (f32[768]{0:T(1024)S(1)}, f32[768]{0:T(1024)}, u32[]{:S(2)}) copy-start(f32[768]{0:T(1024)} %copy-done.47) | copy-start | bytes 9220
  577.9 362.1 %copy-start.59 = (pred[512]{0:T(512)(128)(4,1)S(1)}, pred[512]{0:T(512)(128)(4,1)}, u32[]{:S(2)}) copy-start(pred[512]{0:T(512)(128)(4,1)} %copy-done.58) | copy-start | bytes 1540
  577.9 362.1 %copy-start.72 = (pred[510]{0:T(512)(128)(4,1)S(1)}, pred[510]{0:T(512)(128)(4,1)}, u32[]{:S(2)}) copy-start(pred[510]{0:T(512)(128)(4,1)} %slice.58) | copy-start | bytes 1534
  (54 other events, 139.3 us)
Sparse Core Ops, SparseCore 0:
  10.3 41.0 all-gather.14
  53.7 37.2 all-gather.8
  93.3 37.2 all-gather.12
  132.0 26.1 all-gather.16
  160.1 27.1 all-gather.10
  189.5 38.3 all-gather.18
  230.2 52.3 all-gather.20
  284.8 51.9 all-gather.22
  379.7 24.6 reduce-scatter.10
  418.6 24.8 reduce-scatter.8
  447.3 62.9 reduce-scatter.18
  514.4 61.9 reduce-scatter.12
  580.1 61.9 reduce-scatter.16
  646.3 61.9 reduce-scatter.14
  712.2 110.3 reduce-scatter.20
  827.1 111.0 reduce-scatter.22
  942.4 38.5 all-reduce.14
where the time goes:
time: 1010 us
  waiting for transfers between devices  617 us (61%)
  matrix products  179 us (18%)
  other arithmetic  96.7 us (10%)
  local copies, waits for them, and re-layouts  53.3 us (5%)
  blocking collectives  44.6 us (4%)
  between operations  15.4 us (2%)
    reduce_scatter x1, waiting for transfers between devices, local(): lax.psum_scatter(g_wdown, 'page', scatter_dimension=0, tiled=True)  114 us
    reduce_scatter x1, waiting for transfers between devices, local(): lax.psum_scatter(g_wup, 'page', scatter_dimension=0, tiled=True)  113 us
    reduce_scatter x1, waiting for transfers between devices, local(): lax.psum_scatter(g_wk, 'page', scatter_dimension=0, tiled=True)  64.5 us
    reduce_scatter x1, waiting for transfers between devices, local(): lax.psum_scatter(g_wv, 'page', scatter_dimension=0, tiled=True)  64.2 us
    reduce_scatter x1, waiting for transfers between devices, local(): lax.psum_scatter(g_wq, 'page', scatter_dimension=0, tiled=True)  49.2 us
    all_gather x1, waiting for transfers between devices, local(): lax.all_gather(w_up, 'page', axis=0, tiled=True)  47.3 us
    psum x1, blocking collectives, local(): lax.psum((g_conv_w, g_conv_b, g_bq, g_bv, g_bo, g_tpos, g_tx, g_ty, g_gai...  44.6 us
    dot_general x6, matrix products, plain_dot(): return jnp.dot(left_side, right_side, preferred_element_type=jnp.float32)  37.9 us
  transfers between devices with their start and end apart: 17, of which 13 were waited for; matrix products, arithmetic and copies ran while one was open for 26% of the time, Pallas kernels for 0%

commit v1 on v0

v1 whole, which is shorter than its diff:
```python
import functools

import jax
import jax.numpy as jnp
import numpy as np
from jax import lax
from jax.experimental import pallas as pl
from jax.experimental.pallas import tpu as pltpu
from jax.sharding import PartitionSpec as P

HEADS = 12
HEAD = 64
GRID = 8
PAGES = 8
POS_BINS = 64
BOX_BINS = 32
PATCH = 64
TEXT = 512
PAIRS = HEADS // 2
LANES = 2 * HEAD
WINDOW = 144
KEYS = WINDOW + PATCH

dilation = 2
norm_eps = 1e-05
mask_fill = -1000000000.0
bf16 = jnp.bfloat16
f32 = jnp.float32


def shifted(values, offset, fill_value):
    padding = jnp.full((abs(offset),) + values.shape[1:], fill_value, values.dtype)
    if offset > 0:
        return jnp.concatenate([values[offset:], padding], axis=0)
    return jnp.concatenate([padding, values[:offset]], axis=0)


def dilated_mix(inputs, page_ids, conv_weight, conv_bias):
    summed = inputs + conv_bias + conv_weight[1] * inputs
    for tap_index, offset in ((0, -dilation), (2, dilation)):
        moved_rows = shifted(inputs, offset, 0.0)
        moved_pages = shifted(page_ids, offset, -1)
        same_page = (moved_pages == page_ids)[:, None]
        summed = summed + conv_weight[tap_index] * jnp.where(same_page, moved_rows, 0.0)
    return summed


def bin_features(pos_bins, bins_x, bins_y):
    return jnp.concatenate(
        [
            jax.nn.one_hot(pos_bins, POS_BINS, dtype=bf16),
            jax.nn.one_hot(bins_x, BOX_BINS, dtype=bf16),
            jax.nn.one_hot(bins_y, BOX_BINS, dtype=bf16),
        ],
        axis=1,
    )


def token_ids(text_pages, text_x, text_y):
    text_index = jnp.arange(TEXT, dtype=jnp.int32)
    text_pos = text_index * POS_BINS // TEXT
    patch_pos = text_index % PATCH * POS_BINS // PATCH
    patch_page = text_index // PATCH
    patch_x = text_index % GRID * BOX_BINS // GRID
    patch_y = text_index // GRID % GRID * BOX_BINS // GRID
    page_ids = jnp.stack([text_pages, patch_page])
    pos_bins = jnp.stack([text_pos, patch_pos])
    bins_x = jnp.stack([text_x, patch_x])
    bins_y = jnp.stack([text_y, patch_y])
    return (page_ids, pos_bins, bins_x, bins_y)


def layer_norm(values, gain_vec, bias_vec):
    centered = values - jnp.mean(values, axis=-1, keepdims=True)
    variance = jnp.mean(centered * centered, axis=-1, keepdims=True)
    return centered * lax.rsqrt(variance + norm_eps) * gain_vec + bias_vec


def exact_gelu(values):
    return jax.nn.gelu(values, approximate=False)


def plain_dot(left_side, right_side):
    return jnp.dot(left_side, right_side, preferred_element_type=f32)


def dot_left_t(left_side, right_side):
    return lax.dot_general(
        left_side, right_side, (((0,), (0,)), ((), ())), preferred_element_type=f32
    )


def dot_right_t(left_side, right_side):
    return lax.dot_general(
        left_side, right_side, (((1,), (1,)), ((), ())), preferred_element_type=f32
    )


def column_sum(values):
    return jnp.sum(values, axis=0, keepdims=True, dtype=f32)


def iota(shape, axis):
    return lax.broadcasted_iota(jnp.int32, shape, axis)


def bias_block(table_rows):
    pos_part = pltpu.roll(
        jnp.broadcast_to(table_rows[0:1], (POS_BINS, LANES)), 65, 1, stride=1, stride_axis=0
    )
    x_part = pltpu.roll(
        jnp.broadcast_to(table_rows[1:2], (BOX_BINS, LANES)), 33, 1, stride=1, stride_axis=0
    )
    y_part = pltpu.roll(
        jnp.broadcast_to(table_rows[2:3], (BOX_BINS, LANES)), 65, 1, stride=1, stride_axis=0
    )
    lane = iota((POS_BINS, LANES), 1)
    pos_part = jnp.where(lane < POS_BINS, pos_part, 0.0)
    lane = iota((BOX_BINS, LANES), 1)
    x_part = jnp.where((lane >= 64) & (lane < 96), x_part, 0.0)
    y_part = jnp.where(lane >= 96, y_part, 0.0)
    return jnp.concatenate([pos_part, x_part, y_part], axis=0).astype(bf16)


def diagonal_sums(grad_block):
    lane = iota((POS_BINS, LANES), 1)
    pos_part = jnp.where(lane < POS_BINS, grad_block[:64], 0.0)
    lane = iota((BOX_BINS, LANES), 1)
    x_part = jnp.where((lane >= 64) & (lane < 96), grad_block[64:96], 0.0)
    y_part = jnp.where(lane >= 96, grad_block[96:], 0.0)
    pos_part = pltpu.roll(pos_part, 0, 1, stride=1, stride_axis=0)
    x_part = pltpu.roll(x_part, 0, 1, stride=1, stride_axis=0)
    y_part = pltpu.roll(y_part, 96, 1, stride=1, stride_axis=0)
    rows = [jnp.sum(part, axis=0, keepdims=True) for part in (pos_part, x_part, y_part)]
    return jnp.concatenate(rows + [jnp.zeros((5, LANES), f32)], axis=0)


def stacked_heads(rows, low_lane):
    zero = jnp.zeros_like(rows)
    return jnp.concatenate(
        [jnp.where(low_lane, rows, zero), jnp.where(low_lane, zero, rows)], axis=0
    )


def page_operands(page, bounds, q_ref, k_ref, feat_ref, lookup):
    own_at = pl.multiple_of(bounds[page], 16)
    key_at = pl.multiple_of(bounds[3 * PAGES + page], 16)
    low_lane = iota((WINDOW, LANES), 1) < HEAD
    queries = stacked_heads(q_ref[pl.ds(own_at, WINDOW), :], low_lane)
    rel = jnp.concatenate(
        [lookup[pl.ds(own_at, WINDOW), :LANES], lookup[pl.ds(own_at, WINDOW), LANES:]], axis=0
    )
    query_side = jnp.concatenate([rel, queries], axis=1)
    patch_rows = pl.ds(TEXT + PATCH * page, PATCH)
    text_rows = pl.ds(key_at, WINDOW)
    key_side = jnp.concatenate(
        [
            jnp.concatenate([feat_ref[text_rows, :], k_ref[text_rows, :]], axis=1),
            jnp.concatenate([feat_ref[patch_rows, :], k_ref[patch_rows, :]], axis=1),
        ],
        axis=0,
    )
    own_row = iota((WINDOW, LANES), 0) + own_at
    own_ok = (own_row >= bounds[PAGES + page]) & (own_row < bounds[2 * PAGES + page])
    return own_at, key_at, low_lane, own_ok, queries, query_side, key_side, text_rows, patch_rows


def attend_kernel(bounds, q_ref, k_ref, v_ref, feat_ref, own_feat_ref, table_ref, context_ref, lookup):
    blocks = jnp.concatenate([bias_block(table_ref[0]), bias_block(table_ref[1])], axis=1)
    lookup[...] = jnp.dot(own_feat_ref[...], blocks, preferred_element_type=f32).astype(bf16)
    for page in range(PAGES):
        own_at, key_at, low_lane, own_ok, queries, query_side, key_side, text_rows, patch_rows = (
            page_operands(page, bounds, q_ref, k_ref, feat_ref, lookup)
        )
        scores = dot_right_t(query_side, key_side)
        column = iota((1, KEYS), 1)
        key_row = column + key_at
        key_ok = (column >= WINDOW) | (
            (key_row >= bounds[4 * PAGES + page]) & (key_row < bounds[5 * PAGES + page])
        )
        scores = jnp.where(key_ok, scores, mask_fill)
        row_max = jnp.max(scores, axis=1, keepdims=True)
        weights = jnp.exp(scores - row_max)
        total = jnp.sum(weights, axis=1, keepdims=True)
        prob = (weights * (1.0 / total)).astype(bf16)
        values = jnp.concatenate([v_ref[text_rows, :], v_ref[patch_rows, :]], axis=0)
        mixed = jnp.dot(prob, values, preferred_element_type=f32)
        picked = jnp.where(low_lane, mixed[:WINDOW], mixed[WINDOW:])
        before = context_ref[pl.ds(own_at, WINDOW), :].astype(f32)
        context_ref[pl.ds(own_at, WINDOW), :] = jnp.where(own_ok, picked, before).astype(bf16)


def attend_back_kernel(
    bounds,
    q_ref,
    k_ref,
    v_ref,
    grad_ref,
    feat_ref,
    own_feat_ref,
    flip_feat_ref,
    table_ref,
    grad_q_ref,
    grad_k_ref,
    grad_v_ref,
    grad_table_ref,
    lookup,
    grad_lookup,
):
    blocks = jnp.concatenate([bias_block(table_ref[0]), bias_block(table_ref[1])], axis=1)
    lookup[...] = jnp.dot(own_feat_ref[...], blocks, preferred_element_type=f32).astype(bf16)
    for page in range(PAGES):
        own_at, key_at, low_lane, own_ok, queries, query_side, key_side, text_rows, patch_rows = (
            page_operands(page, bounds, q_ref, k_ref, feat_ref, lookup)
        )
        scores = dot_right_t(key_side, query_side)
        row = iota((KEYS, 1), 0)
        key_row = row + key_at
        key_in = (key_row >= bounds[4 * PAGES + page]) & (key_row < bounds[5 * PAGES + page])
        scores = jnp.where((row >= WINDOW) | key_in, scores, mask_fill)
        col_max = jnp.max(scores, axis=0, keepdims=True)
        weights = jnp.exp(scores - col_max)
        total = jnp.sum(weights, axis=0, keepdims=True)
        prob = weights * (1.0 / total)
        grad_rows = grad_ref[pl.ds(own_at, WINDOW), :]
        grad_rows = jnp.where(own_ok, grad_rows, jnp.zeros_like(grad_rows))
        grads = stacked_heads(grad_rows, low_lane)
        values = jnp.concatenate([v_ref[text_rows, :], v_ref[patch_rows, :]], axis=0)
        grad_prob = dot_right_t(values, grads)
        inner = jnp.sum(prob * grad_prob, axis=0, keepdims=True)
        grad_scores = (prob * (grad_prob - inner)).astype(bf16)
        grad_v = jnp.dot(prob.astype(bf16), grads, preferred_element_type=f32)
        grad_k = jnp.dot(grad_scores, queries, preferred_element_type=f32)
        back = dot_left_t(grad_scores, key_side)
        grad_q = jnp.where(low_lane, back[:WINDOW, LANES:], back[WINDOW:, LANES:]) * 0.125
        own_rows = pl.ds(own_at, WINDOW)
        before = grad_q_ref[own_rows, :].astype(f32)
        grad_q_ref[own_rows, :] = jnp.where(own_ok, grad_q, before).astype(bf16)
        grad_lookup[own_rows, :LANES] = jnp.where(
            own_ok, back[:WINDOW, :LANES], grad_lookup[own_rows, :LANES]
        )
        grad_lookup[own_rows, LANES:] = jnp.where(
            own_ok, back[WINDOW:, :LANES], grad_lookup[own_rows, LANES:]
        )
        wide_row = iota((WINDOW, LANES), 0) + key_at
        text_ok = (wide_row >= bounds[4 * PAGES + page]) & (wide_row < bounds[5 * PAGES + page])
        for grad, ref in ((grad_k, grad_k_ref), (grad_v, grad_v_ref)):
            before = ref[text_rows, :].astype(f32)
            ref[text_rows, :] = jnp.where(text_ok, grad[:WINDOW], before).astype(bf16)
            ref[patch_rows, :] = grad[WINDOW:].astype(bf16)
    grad_high = grad_lookup[...].astype(bf16)
    grad_rest = (grad_lookup[...] - grad_high.astype(f32)).astype(bf16)
    flip = flip_feat_ref[...]
    grad_block = dot_left_t(flip, grad_high) + dot_left_t(flip, grad_rest)
    grad_table_ref[0] = diagonal_sums(grad_block[:, :LANES])
    grad_table_ref[1] = diagonal_sums(grad_block[:, LANES:])


def column_spec(rows, first=0):
    return pl.BlockSpec((rows, LANES), lambda pair, bounds: (0, pair + first))


def whole_spec(rows):
    return pl.BlockSpec((rows, LANES), lambda pair, bounds: (0, 0))


table_spec = pl.BlockSpec((2, 8, LANES), lambda pair, bounds: (pair, 0, 0))


def attend(bounds, queries, keys_values, features, own_features, tables):
    return pl.pallas_call(
        attend_kernel,
        grid_spec=pltpu.PrefetchScalarGridSpec(
            num_scalar_prefetch=1,
            grid=(PAIRS,),
            in_specs=[
                column_spec(TEXT),
                column_spec(2 * TEXT),
                column_spec(2 * TEXT, PAIRS),
                whole_spec(2 * TEXT),
                whole_spec(TEXT),
                table_spec,
            ],
            out_specs=column_spec(TEXT),
            scratch_shapes=[pltpu.VMEM((TEXT, 2 * LANES), bf16)],
        ),
        out_shape=jax.ShapeDtypeStruct((TEXT, HEADS * HEAD), bf16),
        cost_estimate=pl.CostEstimate(
            flops=4_000_000_000, bytes_accessed=6_000_000, transcendentals=3_000_000
        ),
        name="attend",
    )(bounds, queries, keys_values, keys_values, features, own_features, tables)


def attend_back(bounds, queries, keys_values, grad_context, features, own_features, flip, tables):
    return pl.pallas_call(
        attend_back_kernel,
        grid_spec=pltpu.PrefetchScalarGridSpec(
            num_scalar_prefetch=1,
            grid=(PAIRS,),
            in_specs=[
                column_spec(TEXT),
                column_spec(2 * TEXT),
                column_spec(2 * TEXT, PAIRS),
                column_spec(TEXT),
                whole_spec(2 * TEXT),
                whole_spec(TEXT),
                whole_spec(TEXT),
                table_spec,
            ],
            out_specs=[
                column_spec(TEXT),
                column_spec(2 * TEXT),
                column_spec(2 * TEXT),
                table_spec,
            ],
            scratch_shapes=[
                pltpu.VMEM((TEXT, 2 * LANES), bf16),
                pltpu.VMEM((TEXT, 2 * LANES), f32),
            ],
        ),
        out_shape=[
            jax.ShapeDtypeStruct((TEXT, HEADS * HEAD), bf16),
            jax.ShapeDtypeStruct((2 * TEXT, HEADS * HEAD), bf16),
            jax.ShapeDtypeStruct((2 * TEXT, HEADS * HEAD), bf16),
            jax.ShapeDtypeStruct((HEADS, 8, LANES), f32),
        ],
        cost_estimate=pl.CostEstimate(
            flops=9_000_000_000, bytes_accessed=9_000_000, transcendentals=3_000_000
        ),
        name="attend_back",
    )(
        bounds,
        queries,
        keys_values,
        keys_values,
        grad_context,
        features,
        own_features,
        flip,
        tables,
    )


def page_bounds(segments, is_text):
    pages = jnp.arange(PAGES, dtype=jnp.int32)
    low = jnp.sum(segments[None, :] < pages[:, None], axis=1, dtype=jnp.int32)
    high = jnp.sum(segments[None, :] <= pages[:, None], axis=1, dtype=jnp.int32)
    own_low = jnp.where(is_text, low, pages * PATCH)
    own_high = jnp.where(is_text, high, (pages + 1) * PATCH)

    def aligned(start):
        return jnp.minimum(start // 16 * 16, TEXT - WINDOW)

    return jnp.concatenate([aligned(own_low), own_low, own_high, aligned(low), low, high])


def sum_everywhere(values):
    count = lax.axis_size("page")
    if count & (count - 1):
        values = lax.psum(values, "page")
    else:
        step = 1
        while step < count:
            values = values + lax.ppermute(values, "page", [(i, i ^ step) for i in range(count)])
            step = step * 2
    return values + swap(values)


def swap(values):
    return lax.ppermute(values, "mod", [(0, 1), (1, 0)])


def local(
    states,
    cotangent,
    segments,
    box_x,
    box_y,
    conv_weight,
    conv_bias,
    w_query,
    b_query,
    w_key,
    w_value,
    b_value,
    w_out,
    b_out,
    table_pos,
    table_x,
    table_y,
    gain_one,
    bias_one,
    w_up,
    b_up,
    w_down,
    b_down,
    gain_two,
    bias_two,
):
    is_text = lax.axis_index("mod") == 0
    d_model = states.shape[3]
    own_low = states[0, 0]
    other_low = swap(own_low)
    rows_each = w_query.shape[0]
    d_ff = w_up.shape[1]
    pack_qkv = jnp.concatenate([w_query, w_key, w_value], axis=1)
    full_qkv = lax.all_gather(pack_qkv, "page", axis=0, tiled=True)
    full_query = full_qkv[:, :d_model]
    full_kv = full_qkv[:, d_model:]
    pack_rest = jnp.concatenate([w_out, w_up], axis=1)
    pack_rest, w_down = lax.optimization_barrier((pack_rest, w_down, full_qkv))[:2]
    full_rest = lax.all_gather(pack_rest, "page", axis=0, tiled=True)
    full_out = full_rest[:, :d_model]
    full_up = full_rest[:, d_model:]
    full_down = lax.all_gather(w_down, "page", axis=0, tiled=True)

    page_ids, pos_bins, bins_x, bins_y = token_ids(segments[0], box_x[0], box_y[0])
    bounds = page_bounds(segments[0], is_text)
    own_pages = jnp.where(is_text, page_ids[0], page_ids[1])
    features = bin_features(pos_bins.reshape(-1), bins_x.reshape(-1), bins_y.reshape(-1))
    flipped = bin_features(
        POS_BINS - 1 - pos_bins.reshape(-1),
        BOX_BINS - 1 - bins_x.reshape(-1),
        BOX_BINS - 1 - bins_y.reshape(-1),
    )
    own_feats = jnp.where(is_text, features[:TEXT], features[TEXT:])
    own_flip = jnp.where(is_text, flipped[:TEXT], flipped[TEXT:])
    tables = jnp.stack(
        [
            jnp.pad(table_pos, ((0, 0), (0, LANES - table_pos.shape[1]))),
            jnp.pad(table_x, ((0, 0), (0, LANES - table_x.shape[1]))),
            jnp.pad(table_y, ((0, 0), (0, LANES - table_y.shape[1]))),
        ],
        axis=1,
    )
    tables = jnp.pad(tables, ((0, 0), (0, 5), (0, 0)))

    def mix_fn(inputs_f, weight_f, bias_f):
        return dilated_mix(inputs_f, own_pages, weight_f, bias_f)

    own_states = own_low.astype(f32)
    mixed, mix_pull = jax.vjp(mix_fn, own_states, conv_weight, conv_bias)
    mixed_low = mixed.astype(bf16)
    other_pages = jnp.where(is_text, page_ids[1], page_ids[0])
    other_mixed = dilated_mix(other_low.astype(f32), other_pages, conv_weight, conv_bias)
    other_mixed = other_mixed.astype(bf16)
    mixed_all = jnp.concatenate(
        [jnp.where(is_text, mixed_low, other_mixed), jnp.where(is_text, other_mixed, mixed_low)],
        axis=0,
    )
    queries = ((plain_dot(mixed_low, full_query) + b_query).astype(bf16) * 0.125).astype(bf16)
    kv_bias = jnp.concatenate([jnp.zeros_like(b_value), b_value])
    keys_values = (plain_dot(mixed_all, full_kv) + kv_bias).astype(bf16)
    context = attend(bounds, queries, keys_values, features, own_feats, tables)

    first_sum = mixed + plain_dot(context, full_out) + b_out
    normed, norm_one_pull = jax.vjp(layer_norm, first_sum, gain_one, bias_one)
    normed_low = normed.astype(bf16)
    hidden = plain_dot(normed_low, full_up) + b_up
    active, gelu_pull = jax.vjp(exact_gelu, hidden)
    active_low = active.astype(bf16)
    ffn_out = plain_dot(active_low, full_down) + b_down
    output_row, norm_two_pull = jax.vjp(layer_norm, normed + ffn_out, gain_two, bias_two)
    grad_out = cotangent[0, 0].astype(f32)
    grad_sum_two, grad_gain_two, grad_bias_two = norm_two_pull(grad_out)
    grad_ffn = grad_sum_two.astype(bf16)
    g_wdown = dot_left_t(active_low, grad_ffn).astype(bf16)
    grad_b_down = column_sum(grad_ffn)
    (grad_hidden_f,) = gelu_pull(dot_right_t(grad_ffn, full_down))
    grad_hidden = grad_hidden_f.astype(bf16)
    g_wup = dot_left_t(normed_low, grad_hidden).astype(bf16)
    grad_b_up = column_sum(grad_hidden)
    grad_normed = grad_sum_two + dot_right_t(grad_hidden, full_up)
    grad_first, grad_gain_one, grad_bias_one = norm_one_pull(grad_normed)
    grad_branch = grad_first.astype(bf16)
    g_wout = dot_left_t(context, grad_branch).astype(bf16)
    grad_b_out = column_sum(grad_branch)
    shard_down = lax.psum_scatter(g_wdown, "page", scatter_dimension=0, tiled=True)
    shard_rest = lax.psum_scatter(
        jnp.concatenate([g_wout, g_wup], axis=1), "page", scatter_dimension=0, tiled=True
    )
    grad_context = dot_right_t(grad_branch, full_out).astype(bf16)
    grad_queries, grad_keys, grad_values, grad_tables = attend_back(
        bounds, queries, keys_values, grad_context, features, own_feats, own_flip, tables
    )
    g_wq = dot_left_t(mixed_low, grad_queries).astype(bf16)
    g_wk = dot_left_t(mixed_all, grad_keys).astype(bf16)
    g_wv = dot_left_t(mixed_all, grad_values).astype(bf16)
    shard_qkv = lax.psum_scatter(
        jnp.concatenate([g_wq, g_wk, g_wv], axis=1), "page", scatter_dimension=0, tiled=True
    )
    grad_b_query = column_sum(grad_queries)
    grad_b_value = column_sum(grad_values)
    from_keys = dot_right_t(grad_keys, full_kv[:, :d_model]) + dot_right_t(
        grad_values, full_kv[:, d_model:]
    )
    to_other = jnp.where(is_text, from_keys[TEXT:], from_keys[:TEXT]).astype(bf16)
    from_other = swap(to_other).astype(f32)
    grad_mixed = (
        grad_first
        + dot_right_t(grad_queries, full_query)
        + jnp.where(is_text, from_keys[:TEXT], from_keys[TEXT:])
        + from_other
    )
    grad_in, grad_conv_w, grad_conv_b = mix_pull(grad_mixed)

    table_rows = grad_tables[:, :3].reshape(6, 768)
    packed = jnp.concatenate(
        [
            grad_conv_w,
            grad_conv_b[None],
            grad_b_query,
            grad_b_value,
            grad_b_out,
            grad_gain_one[None],
            grad_bias_one[None],
            grad_b_down,
            grad_gain_two[None],
            grad_bias_two[None],
            grad_b_up.reshape(d_ff // d_model, d_model),
            table_rows,
            jnp.zeros((2, d_model), f32),
        ],
        axis=0,
    )
    packed = sum_everywhere(packed)
    g_tables = packed[16:22].reshape(HEADS, 3, LANES)

    def both(shard):
        return shard.astype(f32) + swap(shard).astype(f32)

    shard_down = both(shard_down)
    shard_rest = both(shard_rest)
    shard_qkv = both(shard_qkv)
    return (
        output_row.astype(bf16)[None, None],
        grad_in.astype(bf16)[None, None],
        packed[0:3],
        packed[3],
        shard_qkv[:, :d_model],
        packed[4],
        shard_qkv[:, d_model : 2 * d_model],
        shard_qkv[:, 2 * d_model :],
        packed[5],
        shard_rest[:, :d_model],
        packed[6],
        g_tables[:, 0, : table_pos.shape[1]],
        g_tables[:, 1, 64 : 64 + table_x.shape[1]],
        g_tables[:, 2, 64 : 64 + table_y.shape[1]],
        packed[7],
        packed[8],
        shard_rest[:, d_model:],
        packed[12:16].reshape(d_ff),
        shard_down,
        packed[9],
        packed[10],
        packed[11],
    )


def solution(mesh):
    rows = P("mod", "page", None, None)
    ids = P("page", None)
    cut = P("page", None)
    return jax.shard_map(
        local,
        mesh=mesh,
        in_specs=(
            rows, rows, ids, ids, ids, P(), P(), cut, P(), cut, cut, P(), cut,
            P(), P(), P(), P(), P(), P(), cut, P(), cut, P(), P(), P(),
        ),
        out_specs=(
            rows, rows, P(), P(), cut, P(), cut, cut, P(), cut, P(), P(), P(),
            P(), P(), P(), cut, P(), cut, P(), P(), P(),
        ),
        check_vma=False,
    )
```

time: 1010 us -> 508 us (0.50)
  waiting for transfers between devices: 617 us -> 297 us
  matrix products: 179 us -> 77.2 us
  other arithmetic: 96.7 us -> 24.5 us
  blocking collectives: 44.6 us -> 0 us
  Pallas kernels: 0 us -> 43.2 us
  local copies, waits for them, and re-layouts: 53.3 us -> 28.2 us
  starting transfers between devices: 1.3 us -> 12.3 us
    reduce_scatter x7 -> x2, waiting for transfers between devices: 294 us -> 84.5 us  [the longest x1 84.5 us: local(): lax.psum_scatter(jnp.concatenate([g_wout, g_wup], axis=1), 'page', scatte...]
    all_gather x8 -> x3, waiting for transfers between devices: 205 us -> 101 us  [the longest x1 50 us: local(): full_qkv = lax.all_gather(pack_qkv, 'page', axis=0, tiled=True)]
    dot_general x15 -> x5, matrix products: 134 us -> 33.1 us  [plain_dot(): return jnp.dot(left_side, right_side, preferred_element_type=f32)]
    reduce_scatter x1, waiting for transfers between devices: 114 us -> 61.2 us  [local(): lax.psum_scatter(g_wdown, 'page', scatter_dimension=0, tiled=True)]
    ppermute x0 -> x10, waiting for transfers between devices: none -> 51 us  [the longest x6 37.5 us: swap(): return lax.ppermute(values, 'mod', [(0, 1), (1, 0)])]
    psum x1 -> x0, blocking collectives: 44.6 us -> none  [local(): lax.psum((g_conv_w, g_conv_b, g_bq, g_bv, g_bo, g_tpos, g_tx, g_ty, g_gai...]
    pallas_call x0 -> x2, Pallas kernels: none -> 43.2 us  [the longest x1 29.7 us: attend_back(): pl.pallas_call(attend_back_kernel, grid_spec=pltpu.PrefetchScalarGridSpec...]
    convert_element_type x18 -> x2, other arithmetic: 38.6 us -> 0.25 us  [the longest x1 0.14 us: local(): jnp.where(is_text, from_keys[TEXT:], from_keys[:TEXT]).astype(bf16)]
  transfers between devices with their start and end apart: 17 -> 16, of which waited for: 13 -> 13; matrix products, arithmetic and copies ran while one was open for 26% -> 15% of each run, Pallas kernels for 0% -> 3%
where the time goes in v1:
time: 508 us; the launch traced here: 499 us
  waiting for transfers between devices  297 us (58%)
  matrix products  77.2 us (15%)
  Pallas kernels  43.2 us (9%)
  local copies, waits for them, and re-layouts  28.2 us (6%)
  other arithmetic  24.5 us (5%)
  between operations  15.7 us (3%)
  starting transfers between devices  12.3 us (2%)
    reduce_scatter x1, waiting for transfers between devices, local(): lax.psum_scatter(jnp.concatenate([g_wout, g_wup], axis=1), 'page', scatte...  84.5 us
    reduce_scatter x1, waiting for transfers between devices, local(): lax.psum_scatter(g_wdown, 'page', scatter_dimension=0, tiled=True)  61.2 us
    all_gather x1, waiting for transfers between devices, local(): full_qkv = lax.all_gather(pack_qkv, 'page', axis=0, tiled=True)  50 us
    ppermute x6, waiting for transfers between devices, swap(): return lax.ppermute(values, 'mod', [(0, 1), (1, 0)])  37.5 us
    dot_general x5, matrix products, plain_dot(): return jnp.dot(left_side, right_side, preferred_element_type=f32)  33.1 us
    all_gather x1, waiting for transfers between devices, local(): full_down = lax.all_gather(w_down, 'page', axis=0, tiled=True)  32.1 us
    pallas_call x1, Pallas kernels, attend_back(): pl.pallas_call(attend_back_kernel, grid_spec=pltpu.PrefetchScalarGridSpec...  29.7 us
    dot_general x6, matrix products, dot_right_t(): lax.dot_general(left_side, right_side, (((1,), (1,)), ((), ())), preferre...  25.1 us
  transfers between devices with their start and end apart: 16, of which 13 were waited for; matrix products, arithmetic and copies ran while one was open for 15% of the time, Pallas kernels for 3%

profile of v1, /device:TPU:0, one launch (start us, length us, event | category | flops | bytes accessed | tf_op | source)
XLA Modules:
  0.0 498.6 jit_solution(13332525614028746968)
XLA Ops:
  7.3 1.7 pad_maximum_fusion.7
  9.1 1.7 pad_maximum_fusion.6
  10.8 50.0 %all-gather.4.cloned.1.call-done = bf16[768,2304]{1,0:T(8,128)(2,1)} async-done(((bf16[48,2304]{1,0:T(8,128)(2,1)}), bf16[768,2304]{1,0:T(8,128)(2,1)}) %all-gather.4.cloned.1.call-update) | async-done | bytes 3538960 | tf_op jit(solution)/shard_map/all_gather | solution.py:408
  60.9 1.5 collective-permute-start
  68.2 12.5 %collective-permute-done = bf16[512,768]{1,0:T(8,128)(2,1)S(1)} collective-permute-done((bf16[512,768]{1,0:T(8,128)(2,1)S(1)}, bf16[512,768]{1,0:T(8,128)(2,1)S(1)}, u32[]{:S(2)}, u32[]{:S(2)}) %collective-permute-start) | collective-permute-done | bytes 786464 | tf_op jit(solution)/shard_map/ppermute | solution.py:371
  81.0 3.0 broadcast_select_fusion.1
  84.7 1.7 fusion.21.q_ref
  86.3 4.1 add_convert_fusion.1.k_ref.v_ref
  90.5 13.6 %attend.1 = bf16[512,768]{1,0:T(8,128)(2,1)} custom-call(s32[48]{0:T(128)} %concatenate.63.bounds, bf16[512,768]{1,0:T(8,128)(2,1)} %fusion.21.q_ref, bf16[1024,1536]{1,0:T(8,128)(2,1)} %add_convert_fusion.1.k_ref.v_ref, bf16[1024,1536]{1,0:T(8,128)(2,1)} %add_convert_fusion.1.k_ref.v_ref, bf16[1024,128]{1,0:T(8,128)(2,1)} %copy-done.18, ...), custom_call_target="tpu_custom_call" | custom-call | flops 4000000000 | bytes 6000000 | tf_op jit(solution)/shard_map/attend/pallas_call | solution.py:271
  104.0 18.5 %all-gather.6.cloned.1.call-done = bf16[768,3840]{1,0:T(8,128)(2,1)} async-done(((bf16[48,3840]{1,0:T(8,128)(2,1)}), bf16[768,3840]{1,0:T(8,128)(2,1)}) %all-gather.6.cloned.1.call-update) | async-done | bytes 5898256 | tf_op jit(solution)/shard_map/all_gather | solution.py:413
  122.5 3.0 fusion.58
  126.5 18.2 %multiply_convert_fusion = (bf16[512,3072]{1,0:T(8,128)(2,1)}, f32[512,3072]{1,0:T(8,128)}, f32[512,3072]{1,0:T(8,128)}) fusion(f32[3072]{0:T(1024)S(1)} %copy-done.57, bf16[768,3840]{1,0:T(8,128)(2,1)S(1)} %copy-done.55, f32[512,768]{1,0:T(8,128)S(1)} %get-tuple-element.188, f32[768]{0:T(1024)S(1)} %copy-done.61, f32[768]{0:T(1024)S(1)} %copy-done.51, ...), kind=kOutput, calls=%fused_computation.4 | convolution fusion | flops 2521694208 | bytes 22044672 | tf_op jit(solution)/shard_map/dot_general | solution.py:84
  144.7 32.1 %all-gather.8.cloned.1.call-done = bf16[3072,768]{1,0:T(8,128)(2,1)} async-done(((bf16[192,768]{1,0:T(8,128)(2,1)}), bf16[3072,768]{1,0:T(8,128)(2,1)}) %all-gather.8.cloned.1.call-update) | async-done | bytes 4718608 | tf_op jit(solution)/shard_map/all_gather | solution.py:416
  176.8 6.0 %fusion.59 = (f32[512]{0:T(512)S(1)}, f32[512,768]{1,0:T(8,128)S(1)}) fusion(f32[768]{0:T(1024)S(1)} %copy-done.60, bf16[512,3072]{1,0:T(8,128)(2,1)} %get-tuple-element.155, bf16[3072,768]{1,0:T(8,128)(2,1)} %all-gather.8.cloned.1.call-done, f32[768]{0:T(1024)S(1)} %copy-done.61, f32[768]{0:T(1024)S(1)} %copy-done.51, f32[512]{0:T(512)S(1)} %fusion.41, ...), kind=kOutput, calls=%fused_computation.210 | convolution fusion | flops 2418671104 | bytes 11025408 | tf_op jit(solution)/shard_map/dot_general | solution.py:84
  184.0 1.3 fusion.16
  185.3 1.6 fusion.50
  187.9 10.0 %convert_reduce_fusion = (f32[3072]{0:T(1024)}, bf16[512,3072]{1,0:T(8,128)(2,1)}) fusion(f32[512,3072]{1,0:T(8,128)} %get-tuple-element.156, f32[512,3072]{1,0:T(8,128)} %get-tuple-element.189, f32[3072]{0:T(1024)S(1)} %copy-done.57, bf16[512,768]{1,0:T(8,128)(2,1)S(1)} %get-tuple-element.148, bf16[3072,768]{1,0:T(8,128)(2,1)S(1)} %copy-done.56), kind=kOutput, calls=%fused_computation.2 | convolution fusion | flops 2442654720 | bytes 21258240 | tf_op jit(solution)/shard_map/dot_general | solution.py:94
  197.9 5.6 %multiply_reduce_fusion = (f32[768]{0:T(1024)}, f32[512]{0:T(512)S(1)}, f32[768]{0:T(1024)}, f32[512,768]{1,0:T(8,128)S(1)}) fusion(f32[512,768]{1,0:T(8,128)S(1)} %get-tuple-element.188, f32[512]{0:T(512)S(1)} %fusion.41, f32[512]{0:T(512)S(1)} %broadcast_multiply_fusion.1, f32[768]{0:T(1024)S(1)} %copy-done.51, bf16[512,3072]{1,0:T(8,128)(2,1)} %get-tuple-element.146, ...), kind=kOutput, calls=%fused_computation.46 | convolution fusion | flops 2419849216 | bytes 12601344 | tf_op jit(solution)/shard_map/dot_general | solution.py:94
  207.1 1.7 convolution_convert_fusion.6.grad_ref
  208.8 29.7 %attend_back.1 = (bf16[512,768]{1,0:T(8,128)(2,1)}, bf16[1024,768]{1,0:T(8,128)(2,1)}, bf16[1024,768]{1,0:T(8,128)(2,1)}, f32[12,8,128]{2,1,0:T(8,128)}) custom-call(s32[48]{0:T(128)} %concatenate.63.bounds, bf16[512,768]{1,0:T(8,128)(2,1)} %fusion.21.q_ref, bf16[1024,1536]{1,0:T(8,128)(2,1)} %add_convert_fusion.1.k_ref.v_ref, ...), custom_call_target="tpu_custom_call" | custom-call | flops 8999999488 | bytes 9000000 | tf_op jit(solution)/shard_map/attend_back/pallas_call | solution.py:296
  238.5 3.0 convolution_convert_fusion.3
  241.5 1.5 convolution_convert_fusion.4
  244.2 4.0 copy.67
  249.3 6.7 %convolution_convert_fusion = bf16[3072,768]{1,0:T(8,128)(2,1)} fusion(bf16[512,3072]{1,0:T(8,128)(2,1)} %get-tuple-element.155, bf16[512,768]{1,0:T(8,128)(2,1)S(1)} %copy-done.22), kind=kOutput, calls=%fused_computation.20 | convolution fusion | flops 2418278400 | bytes 8650752 | tf_op jit(solution)/shard_map/dot_general | solution.py:88
  257.5 1.9 convolution_convert_fusion.2
  259.4 2.1 copy.63
  261.5 5.2 %convolution_convert_fusion.1 = bf16[768,3072]{1,0:T(8,128)(2,1)S(1)} fusion(bf16[512,3072]{1,0:T(8,128)(2,1)} %get-tuple-element.146, f32[512,768]{1,0:T(8,128)S(1)} %copy-done.12, f32[768]{0:T(1024)S(1)} %copy-done.62, f32[768]{0:T(1024)S(1)} %copy-done.52, f32[512]{0:T(512)S(1)} %copy-done.36, f32[512]{0:T(512)S(1)} %broadcast_multiply_fusion.1), kind=kOutput, calls=%fused_computation.21 | convolution fusion | flops 2420244480 | bytes 9447424 | tf_op jit(solution)/shard_map/dot_general | solution.py:88
  266.7 2.9 pad_maximum_fusion
  269.7 2.0 copy-done.17
  271.7 3.0 fusion.24
  274.6 1.4 convolution_add_fusion
  276.3 1.5 collective-permute-start.1
  279.2 17.0 %collective-permute-done.1 = bf16[512,768]{1,0:T(8,128)(2,1)} collective-permute-done((bf16[512,768]{1,0:T(8,128)(2,1)S(1)}, bf16[512,768]{1,0:T(8,128)(2,1)}, u32[]{:S(2)}, u32[]{:S(2)}) %collective-permute-start.1) | collective-permute-done | bytes 786464 | tf_op jit(solution)/shard_map/ppermute | solution.py:371
  296.2 3.5 convert_add_fusion
  301.9 2.4 fusion.48
  306.2 4.0 collective-permute-done.3
  310.2 1.6 collective-permute-start.4
  311.8 3.2 collective-permute-done.4
  315.0 1.3 collective-permute-start.5
  316.3 5.0 %collective-permute-done.5 = f32[24,768]{1,0:T(8,128)S(1)} collective-permute-done((f32[24,768]{1,0:T(8,128)S(1)}, f32[24,768]{1,0:T(8,128)S(1)}, u32[]{:S(2)}, u32[]{:S(2)}) %collective-permute-start.5) | collective-permute-done | bytes 73760 | tf_op jit(solution)/shard_map/ppermute | solution.py:365
  321.3 1.4 collective-permute-start.6
  322.7 3.0 collective-permute-done.6
  325.8 1.4 collective-permute-start.7
  332.6 61.2 %reduce-scatter.8.cloned.1.call-done = bf16[192,768]{1,0:T(8,128)(2,1)} async-done(((bf16[3072,768]{1,0:T(8,128)(2,1)}), bf16[192,768]{1,0:T(8,128)(2,1)}) %reduce-scatter.8.cloned.1.call-update) | async-done | bytes 294928 | tf_op jit(solution)/shard_map/reduce_scatter | solution.py:479
  393.8 1.5 collective-permute-start.9
  395.4 84.5 %reduce-scatter.6.cloned.1.call-done = bf16[48,3840]{1,0:T(8,128)(2,1)} async-done(((bf16[768,3840]{1,0:T(8,128)(2,1)}), bf16[48,3840]{1,0:T(8,128)(2,1)}) %reduce-scatter.6.cloned.1.call-update) | async-done | bytes 368656 | tf_op jit(solution)/shard_map/reduce_scatter | solution.py:480
  479.9 1.4 collective-permute-start.8
  484.7 5.0 %collective-permute-done.8 = bf16[48,3840]{1,0:T(8,128)(2,1)S(1)} collective-permute-done((bf16[48,3840]{1,0:T(8,128)(2,1)}, bf16[48,3840]{1,0:T(8,128)(2,1)S(1)}, u32[]{:S(2)}, u32[]{:S(2)}) %collective-permute-start.8) | collective-permute-done | bytes 368672 | tf_op jit(solution)/shard_map/ppermute | solution.py:371
  (259 shorter events, 32.9 us)
Async XLA Ops:
  7.2 53.7 %copy-start.9 = (bf16[1,1,512,768]{3,2,1,0:T(8,128)(2,1)S(1)}, bf16[1,1,512,768]{3,2,1,0:T(8,128)(2,1)}, u32[]{:S(2)}) copy-start(bf16[1,1,512,768]{3,2,1,0:T(8,128)(2,1)} %param.25) | copy-start | bytes 2359300
  7.2 55.3 %copy-start.53 = (s32[1,512]{1,0:T(1,128)S(1)}, s32[1,512]{1,0:T(1,128)}, u32[]{:S(2)}) copy-start(s32[1,512]{1,0:T(1,128)} %param.29) | copy-start | bytes 6148
  7.2 55.3 %copy-start.54 = (s32[1,512]{1,0:T(1,128)S(1)}, s32[1,512]{1,0:T(1,128)}, u32[]{:S(2)}) copy-start(s32[1,512]{1,0:T(1,128)} %param.28) | copy-start | bytes 6148
  7.2 55.4 %copy-start.40 = (s32[1,512]{1,0:T(1,128)S(1)}, s32[1,512]{1,0:T(1,128)}, u32[]{:S(2)}) copy-start(s32[1,512]{1,0:T(1,128)} %param.27) | copy-start | bytes 6148
  7.2 53.6 %all-gather.4.cloned.1.call-start = ((), (), s32[]{:S(2)}) async-start(), calls=%async_computation.3 | async-start | bytes 3760128 | tf_op jit(solution)/shard_map/all_gather | solution.py:408
  9.0 56.3 %copy-start.37 = (f32[12,63]{1,0:T(8,128)S(1)}, f32[12,63]{1,0:T(8,128)}, u32[]{:S(2)}) copy-start(f32[12,63]{1,0:T(8,128)} %param.41) | copy-start | bytes 9076
  9.0 56.4 %copy-start.38 = (f32[12,63]{1,0:T(8,128)S(1)}, f32[12,63]{1,0:T(8,128)}, u32[]{:S(2)}) copy-start(f32[12,63]{1,0:T(8,128)} %param.40) | copy-start | bytes 9076
  9.0 56.4 %copy-start.39 = (f32[12,127]{1,0:T(8,128)S(1)}, f32[12,127]{1,0:T(8,128)}, u32[]{:S(2)}) copy-start(f32[12,127]{1,0:T(8,128)} %param.39) | copy-start | bytes 18292
  9.1 113.4 %all-gather.6.cloned.1.call-start = ((), (), s32[]{:S(2)}) async-start(), calls=%async_computation.4 | async-start | bytes 6266880 | tf_op jit(solution)/shard_map/all_gather | solution.py:413
  60.9 115.9 %all-gather.8.cloned.1.call-start = ((), (), s32[]{:S(2)}) async-start(), calls=%async_computation.5 | async-start | bytes 5013504 | tf_op jit(solution)/shard_map/all_gather | solution.py:416
  60.9 19.8 %collective-permute-start = (bf16[512,768]{1,0:T(8,128)(2,1)S(1)}, bf16[512,768]{1,0:T(8,128)(2,1)S(1)}, u32[]{:S(2)}, u32[]{:S(2)}) collective-permute-start(bf16[512,768]{1,0:T(8,128)(2,1)S(1)} %bitcast.67), channel_id=1, source_target_pairs={{0,16},{16,0},{1,17},{17,1},{2,18},{18,2},{3,19},{19,3},{4,20},{20... | collective-permute-start | bytes 2359304 | tf_op jit(solution)/shard_map/ppermute | solution.py:371
  63.4 3.8 copy-start.48
  63.4 4.4 copy-start.43
  63.7 4.2 copy-start.18
  64.0 16.9 %copy-start.41 = (pred[512]{0:T(512)(128)(4,1)}, pred[512]{0:T(512)(128)(4,1)S(1)}, u32[]{:S(2)}) copy-start(pred[512]{0:T(512)(128)(4,1)S(1)} %get-tuple-element.177) | copy-start | bytes 1540
  64.0 16.9 %copy-start.44 = (pred[512]{0:T(512)(128)(4,1)}, pred[512]{0:T(512)(128)(4,1)S(1)}, u32[]{:S(2)}) copy-start(pred[512]{0:T(512)(128)(4,1)S(1)} %get-tuple-element.176) | copy-start | bytes 1540
  65.3 260.5 %reduce-scatter.10.cloned.1.call-start = ((), (), s32[]{:S(2)}) async-start(), calls=%async_computation.8 | async-start | bytes 3760128 | tf_op jit(solution)/shard_map/reduce_scatter | solution.py:490
  68.2 12.8 %copy-start = (f32[510,768]{1,0:T(8,128)}, f32[510,768]{1,0:T(8,128)S(1)}, u32[]{:S(2)}) copy-start(f32[510,768]{1,0:T(8,128)S(1)} %get-tuple-element.167) | copy-start | bytes 4700164
  68.2 12.8 %copy-start.2 = (f32[510,768]{1,0:T(8,128)}, f32[510,768]{1,0:T(8,128)S(1)}, u32[]{:S(2)}) copy-start(f32[510,768]{1,0:T(8,128)S(1)} %get-tuple-element.168) | copy-start | bytes 4700164
  68.2 12.8 %copy-start.46 = (f32[768]{0:T(1024)S(1)}, f32[768]{0:T(1024)}, u32[]{:S(2)}) copy-start(f32[768]{0:T(1024)} %param.31) | copy-start | bytes 9220
  81.0 3.1 copy-start.16
  90.5 32.0 %copy-start.59 = (f32[768]{0:T(1024)S(1)}, f32[768]{0:T(1024)}, u32[]{:S(2)}) copy-start(f32[768]{0:T(1024)} %param.38) | copy-start | bytes 9220
  122.5 3.7 copy-start.55
  125.5 78.0 %copy-start.11 = (f32[512,768]{1,0:T(8,128)}, f32[512,768]{1,0:T(8,128)S(1)}, u32[]{:S(2)}) copy-start(f32[512,768]{1,0:T(8,128)S(1)} %get-tuple-element.188) | copy-start | bytes 4718596
  126.5 77.0 %copy-start.35 = (f32[512]{0:T(512)}, f32[512]{0:T(512)S(1)}, u32[]{:S(2)}) copy-start(f32[512]{0:T(512)S(1)} %fusion.41) | copy-start | bytes 6148
  126.5 50.3 %copy-start.60 = (f32[768]{0:T(1024)S(1)}, f32[768]{0:T(1024)}, u32[]{:S(2)}) copy-start(f32[768]{0:T(1024)} %param.47) | copy-start | bytes 9220
  185.3 12.6 %slice-start = ((s8[5898240]{0:T(1024)(128)(4,1)}), s8[4194304]{0:T(1024)(128)(4,1)S(1)}, s32[]{:S(2)}) async-start(s8[5898240]{0:T(1024)(128)(4,1)} %bitcast.80), calls=%async_computation.9 | async-start | bytes 8388608
  187.7 10.1 %copy-start.21 = (bf16[512,768]{1,0:T(8,128)(2,1)}, bf16[512,768]{1,0:T(8,128)(2,1)S(1)}, u32[]{:S(2)}) copy-start(bf16[512,768]{1,0:T(8,128)(2,1)S(1)} %get-tuple-element.148) | copy-start | bytes 2359300
  187.9 10.0 %slice-start.1 = ((s8[5898240]{0:T(1024)(128)(4,1)}), s8[1703936]{0:T(1024)(128)(4,1)S(1)}, s32[]{:S(2)}) async-start(s8[5898240]{0:T(1024)(128)(4,1)} %bitcast.80), calls=%async_computation.10 | async-start | bytes 3407872
  204.2 4.6 copy-start.27
  208.8 29.7 %copy-start.20 = (bf16[512,768]{1,0:T(8,128)(2,1)S(1)}, bf16[512,768]{1,0:T(8,128)(2,1)}, u32[]{:S(2)}) copy-start(bf16[512,768]{1,0:T(8,128)(2,1)} %copy-done.19) | copy-start | bytes 2359300
  238.5 3.0 copy-start.64
  248.2 145.5 %reduce-scatter.8.cloned.1.call-start = ((), (), s32[]{:S(2)}) async-start(), calls=%async_computation.7 | async-start | bytes 5013504 | tf_op jit(solution)/shard_map/reduce_scatter | solution.py:479
  256.1 223.8 %reduce-scatter.6.cloned.1.call-start = ((), (), s32[]{:S(2)}) async-start(), calls=%async_computation.6 | async-start | bytes 6266880 | tf_op jit(solution)/shard_map/reduce_scatter | solution.py:480
  276.3 20.0 %collective-permute-start.1 = (bf16[512,768]{1,0:T(8,128)(2,1)S(1)}, bf16[512,768]{1,0:T(8,128)(2,1)}, u32[]{:S(2)}, u32[]{:S(2)}) collective-permute-start(bf16[512,768]{1,0:T(8,128)(2,1)S(1)} %select_convert_fusion), channel_id=1, source_target_pairs={{0,16},{16,0},{1,17},{17,1},{2,18},{18,2},{3,19},{19,3},{4,20},{20... | collective-permute-start | bytes 2359304 | tf_op jit(solution)/shard_map/ppermute | solution.py:371
  277.9 18.3 %copy-start.5 = (f32[512,768]{1,0:T(8,128)S(1)}, f32[512,768]{1,0:T(8,128)}, u32[]{:S(2)}) copy-start(f32[512,768]{1,0:T(8,128)} %copy-done.4) | copy-start | bytes 4718596
  277.9 18.3 %copy-start.28 = (f32[512]{0:T(512)S(1)}, f32[512]{0:T(512)}, u32[]{:S(2)}) copy-start(f32[512]{0:T(512)} %copy-done.27) | copy-start | bytes 6148
  279.2 20.5 %copy-start.42 = (pred[512]{0:T(512)(128)(4,1)S(1)}, pred[512]{0:T(512)(128)(4,1)}, u32[]{:S(2)}) copy-start(pred[512]{0:T(512)(128)(4,1)} %copy-done.41) | copy-start | bytes 1540
  304.5 1.3 collective-permute-start.2
  305.8 4.4 collective-permute-start.3
  310.2 4.8 collective-permute-start.4
  315.0 6.3 %collective-permute-start.5 = (f32[24,768]{1,0:T(8,128)S(1)}, f32[24,768]{1,0:T(8,128)S(1)}, u32[]{:S(2)}, u32[]{:S(2)}) collective-permute-start(f32[24,768]{1,0:T(8,128)S(1)} %add.314), channel_id=1, source_target_pairs={{0,8},{1,9},{2,10},{3,11},{4,12},{5,13},{6,14},{7,15},{8,0},{9,1},... | collective-permute-start | bytes 221192 | tf_op jit(solution)/shard_map/ppermute | solution.py:365
  321.3 4.4 collective-permute-start.6
  325.8 6.5 %collective-permute-start.7 = (bf16[48,2304]{1,0:T(8,128)(2,1)}, bf16[48,2304]{1,0:T(8,128)(2,1)S(1)}, u32[]{:S(2)}, u32[]{:S(2)}) collective-permute-start(bf16[48,2304]{1,0:T(8,128)(2,1)} %reduce-scatter.10.cloned.1.call-done), channel_id=1, source_target_pairs={{0,16},{16,0},{1,17},{17,1},{2,18},{18,2},{3,19},{19,3},{4,20},{20... | collective-permute-start | bytes 663560 | tf_op jit(solution)/shard_map/ppermute | solution.py:371
  393.8 90.1 %collective-permute-start.9 = (bf16[192,768]{1,0:T(8,128)(2,1)}, bf16[192,768]{1,0:T(8,128)(2,1)S(1)}, u32[]{:S(2)}, u32[]{:S(2)}) collective-permute-start(bf16[192,768]{1,0:T(8,128)(2,1)} %reduce-scatter.8.cloned.1.call-done), channel_id=1, source_target_pairs={{0,16},{16,0},{1,17},{17,1},{2,18},{18,2},{3,19},{19,3},{4,20},{20... | collective-permute-start | bytes 884744 | tf_op jit(solution)/shard_map/ppermute | solution.py:371
  395.4 88.5 %copy-start.26 = (bf16[192,768]{1,0:T(8,128)(2,1)S(1)}, bf16[192,768]{1,0:T(8,128)(2,1)}, u32[]{:S(2)}) copy-start(bf16[192,768]{1,0:T(8,128)(2,1)} %reduce-scatter.8.cloned.1.call-done) | copy-start | bytes 884740
  479.9 9.8 %collective-permute-start.8 = (bf16[48,3840]{1,0:T(8,128)(2,1)}, bf16[48,3840]{1,0:T(8,128)(2,1)S(1)}, u32[]{:S(2)}, u32[]{:S(2)}) collective-permute-start(bf16[48,3840]{1,0:T(8,128)(2,1)} %reduce-scatter.6.cloned.1.call-done), channel_id=1, source_target_pairs={{0,16},{16,0},{1,17},{17,1},{2,18},{18,2},{3,19},{19,3},{4,20},{20... | collective-permute-start | bytes 1105928 | tf_op jit(solution)/shard_map/ppermute | solution.py:371
  481.4 8.3 %copy-start.25 = (bf16[48,3840]{1,0:T(8,128)(2,1)S(1)}, bf16[48,3840]{1,0:T(8,128)(2,1)}, u32[]{:S(2)}) copy-start(bf16[48,3840]{1,0:T(8,128)(2,1)} %reduce-scatter.6.cloned.1.call-done) | copy-start | bytes 1105924
  (35 other events, 54.7 us)
Sparse Core Ops, SparseCore 0:
  10.9 49.8 all-gather.3
  63.7 58.7 all-gather.5
  124.8 51.9 all-gather.7
  248.4 66.7 reduce-scatter.9
  318.8 74.8 reduce-scatter.7
  398.1 81.7 reduce-scatter.5

commit v2 on v1

--- a/solution.py
+++ b/solution.py
@@ -342,6 +342,175 @@
     )
 
 
+def exchange(values, mask):
+    count = lax.axis_size("page")
+    return lax.ppermute(values, "page", [(i, i ^ mask) for i in range(count)])
+
+
+def place_kernel(page, *refs):
+    pieces, full_ref, sems = refs[:4], refs[4], refs[5]
+    rows = pieces[0].shape[1]
+    copies = []
+    for mask in range(16):
+        at = pl.multiple_of((page[0] ^ mask) * rows, 16)
+        copies.append(
+            pltpu.make_async_copy(
+                pieces[mask & 3].at[mask >> 2], full_ref.at[pl.ds(at, rows)], sems.at[mask]
+            )
+        )
+    for copy in copies:
+        copy.start()
+    for copy in copies:
+        copy.wait()
+
+
+def gathered(shard, page):
+    rows, width = shard.shape
+    column = jnp.stack([shard] + [exchange(shard, 4 * step) for step in (1, 2, 3)])
+    across = exchange(column, 2)
+    partner = exchange(column, 1)
+    partner_across = exchange(across, 1)
+    full = pl.pallas_call(
+        place_kernel,
+        grid_spec=pltpu.PrefetchScalarGridSpec(
+            num_scalar_prefetch=1,
+            grid=(),
+            in_specs=[pl.BlockSpec(memory_space=pl.ANY)] * 4,
+            out_specs=pl.BlockSpec(memory_space=pltpu.VMEM),
+            scratch_shapes=[pltpu.SemaphoreType.DMA((16,))],
+        ),
+        out_shape=jax.ShapeDtypeStruct((16 * rows, width), shard.dtype),
+        cost_estimate=pl.CostEstimate(
+            flops=0, bytes_accessed=64 * rows * width, transcendentals=0
+        ),
+        name="place_rows",
+    )(page, column, partner, across, partner_across)
+    return full, column
+
+
+def grad_rows_kernel(page, x_ref, h_ref, keep_ref, send_ref, product):
+    rows = keep_ref.shape[1]
+    product[...] = dot_left_t(x_ref[...], h_ref[...])
+    mine = pl.multiple_of((page[0] & 1) * rows, 16)
+    theirs = pl.multiple_of((1 - (page[0] & 1)) * rows, 16)
+    keep_ref[0] = product[pl.ds(mine, rows), :].astype(bf16)
+    send_ref[0] = product[pl.ds(theirs, rows), :].astype(bf16)
+
+
+def grad_by_rows(inputs, grads, page):
+    tokens, width = inputs.shape
+    columns = grads.shape[1]
+    rows = width // 16
+
+    def slot(block, page):
+        mask = block ^ (page[0] >> 1)
+        return ((mask & 1) * 4 + (mask >> 1), 0, 0)
+
+    half = jax.ShapeDtypeStruct((8, rows, columns), bf16)
+    return pl.pallas_call(
+        grad_rows_kernel,
+        grid_spec=pltpu.PrefetchScalarGridSpec(
+            num_scalar_prefetch=1,
+            grid=(8,),
+            in_specs=[
+                pl.BlockSpec((tokens, 2 * rows), lambda block, page: (0, block)),
+                pl.BlockSpec((tokens, columns), lambda block, page: (0, 0)),
+            ],
+            out_specs=[pl.BlockSpec((1, rows, columns), slot)] * 2,
+            scratch_shapes=[pltpu.VMEM((2 * rows, columns), f32)],
+        ),
+        out_shape=[half, half],
+        cost_estimate=pl.CostEstimate(
+            flops=2 * tokens * width * columns,
+            bytes_accessed=2 * (tokens * (width + columns) + width * columns),
+            transcendentals=0,
+        ),
+        name="grad_rows",
+    )(page, inputs, grads)
+
+
+def grad_columns_kernel(parts, page, *refs):
+    ins, keep_ref, send_ref, product = refs[: 2 * len(parts)], refs[-3], refs[-2], refs[-1]
+    rows, width = keep_ref.shape[1], keep_ref.shape[2]
+    step = pl.program_id(0)
+    first = 0
+    for index, count in enumerate(parts):
+        x_ref, h_ref = ins[2 * index], ins[2 * index + 1]
+
+        @pl.when((step >= first) & (step < first + count))
+        def _():
+            product[...] = dot_left_t(x_ref[...], h_ref[...])
+
+        first = first + count
+    for slot in range(8):
+        mask = (slot & 3) * 4 + (slot >> 2) * 2
+        mine = pl.multiple_of((page[0] ^ mask) * rows, 16)
+        theirs = pl.multiple_of((page[0] ^ (mask + 1)) * rows, 16)
+        keep_ref[slot] = product[pl.ds(mine, rows), :].astype(bf16)
+        send_ref[slot] = product[pl.ds(theirs, rows), :].astype(bf16)
+
+
+def grad_by_columns(pairs, page, tile):
+    width = pairs[0][0].shape[1]
+    rows = width // 16
+    parts = tuple(grads.shape[1] // tile for _, grads in pairs)
+    steps = sum(parts)
+    specs = []
+    operands = []
+    first = 0
+    flops = 0
+    for (inputs, grads), count in zip(pairs, parts):
+        specs.append(pl.BlockSpec(inputs.shape, lambda step, page: (0, 0)))
+
+        def column(step, page, first=first, count=count):
+            return (0, jnp.clip(step - first, 0, count - 1))
+
+        specs.append(pl.BlockSpec((grads.shape[0], tile), column))
+        operands += [inputs, grads]
+        first = first + count
+        flops = flops + 2 * inputs.shape[0] * width * grads.shape[1]
+    half = jax.ShapeDtypeStruct((8, rows, steps * tile), bf16)
+    return pl.pallas_call(
+        functools.partial(grad_columns_kernel, parts),
+        grid_spec=pltpu.PrefetchScalarGridSpec(
+            num_scalar_prefetch=1,
+            grid=(steps,),
+            in_specs=specs,
+            out_specs=[pl.BlockSpec((8, rows, tile), lambda step, page: (0, 0, step))] * 2,
+            scratch_shapes=[pltpu.VMEM((width, tile), f32)],
+        ),
+        out_shape=[half, half],
+        cost_estimate=pl.CostEstimate(
+            flops=flops, bytes_accessed=4 * width * steps * tile, transcendentals=0
+        ),
+        name="grad_columns",
+    )(page, *operands)
+
+
+def scattered(keep, send):
+    partner = exchange(send, 1)
+
+    def pair(at):
+        return keep[at].astype(f32) + partner[at].astype(f32)
+
+    across = exchange(pair(slice(4, 8)).astype(bf16), 2)
+
+    def four(z):
+        return pair(z) + across[z].astype(f32)
+
+    total = four(0)
+    for step in (1, 2, 3):
+        total = total + exchange(four(step).astype(bf16), 4 * step).astype(f32)
+    low = total.astype(bf16)
+    return low.astype(f32) + swap(low).astype(f32)
+
+
+def summed_rows(pairs):
+    grads = jnp.concatenate([dot_left_t(*pair).astype(bf16) for pair in pairs], axis=1)
+    shard = lax.psum_scatter(grads, "page", scatter_dimension=0, tiled=True)
+    return shard.astype(f32) + swap(shard).astype(f32)
+
+
 def page_bounds(segments, is_text):
     pages = jnp.arange(PAGES, dtype=jnp.int32)
     low = jnp.sum(segments[None, :] < pages[:, None], axis=1, dtype=jnp.int32)
@@ -404,16 +573,24 @@
     other_low = swap(own_low)
     rows_each = w_query.shape[0]
     d_ff = w_up.shape[1]
+    page = lax.axis_index("page").astype(jnp.int32)[None]
+    fast = lax.axis_size("page") == 16 and rows_each % 16 == 0 and w_down.shape[0] % 16 == 0
     pack_qkv = jnp.concatenate([w_query, w_key, w_value], axis=1)
-    full_qkv = lax.all_gather(pack_qkv, "page", axis=0, tiled=True)
+    pack_rest = jnp.concatenate([w_out, w_up], axis=1)
+    if fast:
+        full_qkv, column = gathered(pack_qkv, page)
+        pack_rest, column = lax.optimization_barrier((pack_rest, column))
+        full_rest, column = gathered(pack_rest, page)
+        w_down, column = lax.optimization_barrier((w_down, column))
+        full_down, column = gathered(w_down, page)
+    else:
+        full_qkv = lax.all_gather(pack_qkv, "page", axis=0, tiled=True)
+        full_rest = lax.all_gather(pack_rest, "page", axis=0, tiled=True)
+        full_down = lax.all_gather(w_down, "page", axis=0, tiled=True)
     full_query = full_qkv[:, :d_model]
     full_kv = full_qkv[:, d_model:]
-    pack_rest = jnp.concatenate([w_out, w_up], axis=1)
-    pack_rest, w_down = lax.optimization_barrier((pack_rest, w_down, full_qkv))[:2]
-    full_rest = lax.all_gather(pack_rest, "page", axis=0, tiled=True)
     full_out = full_rest[:, :d_model]
     full_up = full_rest[:, d_model:]
-    full_down = lax.all_gather(w_down, "page", axis=0, tiled=True)
 
     page_ids, pos_bins, bins_x, bins_y = token_ids(segments[0], box_x[0], box_y[0])
     bounds = page_bounds(segments[0], is_text)
@@ -465,31 +642,32 @@
     grad_out = cotangent[0, 0].astype(f32)
     grad_sum_two, grad_gain_two, grad_bias_two = norm_two_pull(grad_out)
     grad_ffn = grad_sum_two.astype(bf16)
-    g_wdown = dot_left_t(active_low, grad_ffn).astype(bf16)
+    if fast:
+        shard_down = scattered(*grad_by_rows(active_low, grad_ffn, page))
+    else:
+        shard_down = summed_rows([(active_low, grad_ffn)])
     grad_b_down = column_sum(grad_ffn)
     (grad_hidden_f,) = gelu_pull(dot_right_t(grad_ffn, full_down))
     grad_hidden = grad_hidden_f.astype(bf16)
-    g_wup = dot_left_t(normed_low, grad_hidden).astype(bf16)
     grad_b_up = column_sum(grad_hidden)
     grad_normed = grad_sum_two + dot_right_t(grad_hidden, full_up)
     grad_first, grad_gain_one, grad_bias_one = norm_one_pull(grad_normed)
     grad_branch = grad_first.astype(bf16)
-    g_wout = dot_left_t(context, grad_branch).astype(bf16)
     grad_b_out = column_sum(grad_branch)
-    shard_down = lax.psum_scatter(g_wdown, "page", scatter_dimension=0, tiled=True)
-    shard_rest = lax.psum_scatter(
-        jnp.concatenate([g_wout, g_wup], axis=1), "page", scatter_dimension=0, tiled=True
-    )
+    pairs = [(context, grad_branch), (normed_low, grad_hidden)]
+    if fast:
+        shard_rest = scattered(*grad_by_columns(pairs, page, d_model))
+    else:
+        shard_rest = summed_rows(pairs)
     grad_context = dot_right_t(grad_branch, full_out).astype(bf16)
     grad_queries, grad_keys, grad_values, grad_tables = attend_back(
         bounds, queries, keys_values, grad_context, features, own_feats, own_flip, tables
     )
-    g_wq = dot_left_t(mixed_low, grad_queries).astype(bf16)
-    g_wk = dot_left_t(mixed_all, grad_keys).astype(bf16)
-    g_wv = dot_left_t(mixed_all, grad_values).astype(bf16)
-    shard_qkv = lax.psum_scatter(
-        jnp.concatenate([g_wq, g_wk, g_wv], axis=1), "page", scatter_dimension=0, tiled=True
-    )
+    pairs = [(mixed_low, grad_queries), (mixed_all, grad_keys), (mixed_all, grad_values)]
+    if fast:
+        shard_qkv = scattered(*grad_by_columns(pairs, page, d_model))
+    else:
+        shard_qkv = summed_rows(pairs)
     grad_b_query = column_sum(grad_queries)
     grad_b_value = column_sum(grad_values)
     from_keys = dot_right_t(grad_keys, full_kv[:, :d_model]) + dot_right_t(
@@ -527,12 +705,6 @@
     packed = sum_everywhere(packed)
     g_tables = packed[16:22].reshape(HEADS, 3, LANES)
 
-    def both(shard):
-        return shard.astype(f32) + swap(shard).astype(f32)
-
-    shard_down = both(shard_down)
-    shard_rest = both(shard_rest)
-    shard_qkv = both(shard_qkv)
     return (
         output_row.astype(bf16)[None, None],
         grad_in.astype(bf16)[None, None],

time: 508 us -> 439 us (0.86)
  waiting for transfers between devices: 297 us -> 170 us
  starting transfers between devices: 12.3 us -> 55.5 us
  Pallas kernels: 43.2 us -> 83.8 us
  other arithmetic: 24.5 us -> 45.7 us
  matrix products: 77.2 us -> 57.8 us
  between operations: 15.7 us -> 1.82 us
  local copies, waits for them, and re-layouts: 28.2 us -> 18.6 us
    ppermute x0 -> x33, waiting for transfers between devices: none -> 150 us  [exchange(): return lax.ppermute(values, 'page', [(i, i ^ mask) for i in range(count)])]
    reduce_scatter x3 -> x0, waiting for transfers between devices: 146 us -> none  [the longest x1 84.5 us: local(): lax.psum_scatter(jnp.concatenate([g_wout, g_wup], axis=1), 'page', scatte...]
    all_gather x3 -> x0, waiting for transfers between devices: 101 us -> none  [the longest x1 50 us: local(): full_qkv = lax.all_gather(pack_qkv, 'page', axis=0, tiled=True)]
    ppermute x0 -> x33, starting transfers between devices: none -> 43.3 us  [exchange(): return lax.ppermute(values, 'page', [(i, i ^ mask) for i in range(count)])]
    pallas_call x0 -> x6, Pallas kernels: none -> 41.1 us  [the longest x2 17.6 us: grad_by_columns(): pl.pallas_call(functools.partial(grad_columns_kernel, parts), grid_spec=p...]
    ppermute x6, waiting for transfers between devices: 37.5 us -> 7.62 us  [swap(): return lax.ppermute(values, 'mod', [(0, 1), (1, 0)])]
    dot_general x6 -> x0, matrix products: 19.1 us -> none  [dot_left_t(): lax.dot_general(left_side, right_side, (((0,), (0,)), ((), ())), preferre...]
    convert_element_type x0 -> x10, other arithmetic: none -> 18.3 us  [the longest x3 7.32 us: scattered(): across = exchange(pair(slice(4, 8)).astype(bf16), 2)]
  transfers between devices with their start and end apart: 16 -> 43, of which waited for: 13 -> 20; matrix products, arithmetic and copies ran while one was open for 15% -> 14% of each run, Pallas kernels for 3% -> 9%
where the time goes in v2:
time: 439 us; the launch traced here: 433 us
  waiting for transfers between devices  170 us (39%)
  Pallas kernels  83.8 us (19%)
  matrix products  57.8 us (13%)
  starting transfers between devices  55.5 us (13%)
  other arithmetic  45.7 us (10%)
  local copies, waits for them, and re-layouts  18.6 us (4%)
    ppermute x33, waiting for transfers between devices, exchange(): return lax.ppermute(values, 'page', [(i, i ^ mask) for i in range(count)])  150 us
    ppermute x33, starting transfers between devices, exchange(): return lax.ppermute(values, 'page', [(i, i ^ mask) for i in range(count)])  43.3 us
    dot_general x5, matrix products, plain_dot(): return jnp.dot(left_side, right_side, preferred_element_type=f32)  32.3 us
    pallas_call x1, Pallas kernels, attend_back(): pl.pallas_call(attend_back_kernel, grid_spec=pltpu.PrefetchScalarGridSpec...  29.8 us
    dot_general x6, matrix products, dot_right_t(): lax.dot_general(left_side, right_side, (((1,), (1,)), ((), ())), preferre...  25.5 us
    pallas_call x2, Pallas kernels, grad_by_columns(): pl.pallas_call(functools.partial(grad_columns_kernel, parts), grid_spec=p...  17.6 us
    pallas_call x3, Pallas kernels, gathered(): pl.pallas_call(place_kernel, grid_spec=pltpu.PrefetchScalarGridSpec(num_s...  14.1 us
    ppermute x4, waiting for transfers between devices, sum_everywhere(): lax.ppermute(values, 'page', [(i, i ^ step) for i in range(count)])  12.9 us
  transfers between devices with their start and end apart: 43, of which 20 were waited for; matrix products, arithmetic and copies ran while one was open for 14% of the time, Pallas kernels for 9%

profile of v2, /device:TPU:0, one launch (start us, length us, event | category | flops | bytes accessed | tf_op | source)
XLA Modules:
  0.0 433.4 jit_solution(11095444543251526137)
XLA Ops:
  3.3 5.1 %collective-permute-start.2 = (bf16[48,2304]{1,0:T(8,128)(2,1)S(1)}, bf16[48,2304]{1,0:T(8,128)(2,1)S(1)}, u32[]{:S(2)}, u32[]{:S(2)}) collective-permute-start(bf16[48,2304]{1,0:T(8,128)(2,1)S(1)} %constant_dynamic-update-slice_fusion), channel_id=1, source_target_pairs={{0,12},{1,13},{2,14},{3,15},{4,8},{5,9},{6,10},{7,11},{8,4},{9,5},... | collective-permute-start | bytes 663560 | tf_op jit(solution)/shard_map/ppermute | solution.py:347
  17.3 9.9 %collective-permute-done.1 = bf16[48,2304]{1,0:T(8,128)(2,1)S(1)} collective-permute-done((bf16[48,2304]{1,0:T(8,128)(2,1)S(1)}, bf16[48,2304]{1,0:T(8,128)(2,1)S(1)}, u32[]{:S(2)}, u32[]{:S(2)}) %collective-permute-start.1) | collective-permute-done | bytes 221216 | tf_op jit(solution)/shard_map/ppermute | solution.py:347
  28.3 2.5 collective-permute-start.9
  33.9 7.8 %collective-permute-done.9 = bf16[48,3840]{1,0:T(8,128)(2,1)S(1)} collective-permute-done((bf16[48,3840]{1,0:T(8,128)(2,1)S(1)}, bf16[48,3840]{1,0:T(8,128)(2,1)S(1)}, u32[]{:S(2)}, u32[]{:S(2)}) %collective-permute-start.9) | collective-permute-done | bytes 368672 | tf_op jit(solution)/shard_map/ppermute | solution.py:347
  41.7 18.8 %collective-permute-done.8 = bf16[48,3840]{1,0:T(8,128)(2,1)S(1)} collective-permute-done((bf16[48,3840]{1,0:T(8,128)(2,1)S(1)}, bf16[48,3840]{1,0:T(8,128)(2,1)S(1)}, u32[]{:S(2)}, u32[]{:S(2)}) %collective-permute-start.8) | collective-permute-done | bytes 368672 | tf_op jit(solution)/shard_map/ppermute | solution.py:347
  67.2 6.5 %collective-permute-done.15 = bf16[192,768]{1,0:T(8,128)(2,1)S(1)} collective-permute-done((bf16[192,768]{1,0:T(8,128)(2,1)S(1)}, bf16[192,768]{1,0:T(8,128)(2,1)S(1)}, u32[]{:S(2)}, u32[]{:S(2)}) %collective-permute-start.15) | collective-permute-done | bytes 294944 | tf_op jit(solution)/shard_map/ppermute | solution.py:347
  74.5 9.4 %collective-permute-start.13 = (bf16[192,768]{1,0:T(8,128)(2,1)S(1)}, bf16[192,768]{1,0:T(8,128)(2,1)S(1)}, u32[]{:S(2)}, u32[]{:S(2)}) collective-permute-start(bf16[192,768]{1,0:T(8,128)(2,1)S(1)} %copy-done.26), channel_id=1, source_target_pairs={{0,4},{1,5},{2,6},{3,7},{4,0},{5,1},{6,2},{7,3},{8,12},{9,13},{10,... | collective-permute-start | bytes 884744 | tf_op jit(solution)/shard_map/ppermute | solution.py:347
  86.3 3.1 collective-permute-done.13
  92.3 26.5 %collective-permute-done.4.refs_2_ = bf16[4,48,2304]{2,1,0:T(8,128)(2,1)S(1)} collective-permute-done((bf16[4,48,2304]{2,1,0:T(8,128)(2,1)}, bf16[4,48,2304]{2,1,0:T(8,128)(2,1)S(1)}, u32[]{:S(2)}, u32[]{:S(2)}) %collective-permute-start.4) | collective-permute-done | bytes 884768 | tf_op jit(solution)/shard_map/ppermute | solution.py:347
  118.9 3.2 broadcast_select_fusion.1
  126.1 4.1 place_rows.3
  130.2 11.0 %collective-permute-done.17.refs_2_ = bf16[4,192,768]{2,1,0:T(8,128)(2,1)} collective-permute-done((bf16[4,192,768]{2,1,0:T(8,128)(2,1)}, bf16[4,192,768]{2,1,0:T(8,128)(2,1)}, u32[]{:S(2)}, u32[]{:S(2)}) %collective-permute-start.17) | collective-permute-done | bytes 1179680 | tf_op jit(solution)/shard_map/ppermute | solution.py:347
  141.2 2.9 fusion.21.q_ref
  144.1 5.2 %add_convert_fusion.1.k_ref.v_ref = bf16[1024,1536]{1,0:T(8,128)(2,1)} fusion(f32[1536]{0:T(1024)S(1)} %concatenate.64, bf16[768,2304]{1,0:T(8,128)(2,1)S(1)} %copy-done.3, bf16[512,768]{1,0:T(8,128)(2,1)} %copy-done.13, bf16[512,768]{1,0:T(8,128)(2,1)S(1)} %copy-done.12), kind=kOutput, calls=%fused_computation.17 | convolution fusion | flops 2422210560 | bytes 7086080 | tf_op jit(solution)/shard_map/dot_general | solution.py:84
  149.3 12.9 %attend.1.refs_0_ = bf16[512,768]{1,0:T(8,128)(2,1)} custom-call(s32[48]{0:T(128)} %concatenate.57.bounds, bf16[512,768]{1,0:T(8,128)(2,1)} %fusion.21.q_ref, bf16[1024,1536]{1,0:T(8,128)(2,1)} %add_convert_fusion.1.k_ref.v_ref, bf16[1024,1536]{1,0:T(8,128)(2,1)} %add_convert_fusion.1.k_ref.v_ref, bf16[1024,128]{1,0:T(8,128)(2,1)} %copy-done.18, ...), custom_call_target="tpu_custom_call" | custom-call | flops 4000000000 | bytes 6000000 | tf_op jit(solution)/shard_map/attend/pallas_call | solution.py:271
  162.2 4.7 %place_rows.5 = bf16[3072,768]{1,0:T(8,128)(2,1)} custom-call(s32[1]{0:T(128)} %bitcast.2.page, bf16[4,192,768]{2,1,0:T(8,128)(2,1)} %pad_maximum_fusion.2.refs_0_, bf16[4,192,768]{2,1,0:T(8,128)(2,1)} %collective-permute-done.16.refs_1_, bf16[4,192,768]{2,1,0:T(8,128)(2,1)} %collective-permute-done.17.refs_2_, ...), custom_call_target="tpu_custom_call" | custom-call | bytes 9437184 | tf_op jit(solution)/shard_map/place_rows/pallas_call | solution.py:373
  166.9 5.4 %place_rows.4 = bf16[768,3840]{1,0:T(8,128)(2,1)} custom-call(s32[1]{0:T(128)} %bitcast.2.page, bf16[4,48,3840]{2,1,0:T(8,128)(2,1)} %pad_maximum_fusion.1.refs_0_, bf16[4,48,3840]{2,1,0:T(8,128)(2,1)} %collective-permute-done.10.refs_1_, bf16[4,48,3840]{2,1,0:T(8,128)(2,1)} %collective-permute-done.11.refs_2_, ...), custom_call_target="tpu_custom_call" | custom-call | bytes 11796480 | tf_op jit(solution)/shard_map/place_rows/pallas_call | solution.py:373
  172.3 2.8 fusion.71
  176.3 18.6 %multiply_convert_fusion = (bf16[512,3072]{1,0:T(8,128)(2,1)S(1)}, f32[512,3072]{1,0:T(8,128)}, f32[512,3072]{1,0:T(8,128)}) fusion(f32[3072]{0:T(1024)S(1)} %copy-done.42, bf16[512,768]{1,0:T(8,128)(2,1)S(1)} %fusion.22.refs_2_, bf16[768,3840]{1,0:T(8,128)(2,1)S(1)} %copy-done.8), kind=kOutput, calls=%fused_computation.4 | convolution fusion | flops 2519728128 | bytes 21245952 | tf_op jit(solution)/shard_map/dot_general | solution.py:84
  195.0 2.8 fusion.72
  201.1 9.1 %convert_reduce_fusion = (f32[3072]{0:T(1024)S(1)}, bf16[512,3072]{1,0:T(8,128)(2,1)}) fusion(f32[512,3072]{1,0:T(8,128)} %get-tuple-element.80, f32[512,3072]{1,0:T(8,128)} %get-tuple-element.122, f32[3072]{0:T(1024)S(1)} %copy-done.42, bf16[512,768]{1,0:T(8,128)(2,1)S(1)} %get-tuple-element.72.h_ref, bf16[3072,768]{1,0:T(8,128)(2,1)S(1)} %bitcast.115), kind=kOutput, calls=%fused_computation.2 | convolution fusion | flops 2442654720 | bytes 21258240 | tf_op jit(solution)/shard_map/dot_general | solution.py:94
  210.2 5.0 %multiply_reduce_fusion = (f32[768]{0:T(1024)S(1)}, f32[512]{0:T(512)S(1)}, f32[768]{0:T(1024)S(1)}, f32[512,768]{1,0:T(8,128)S(1)}) fusion(f32[512,768]{1,0:T(8,128)S(1)} %get-tuple-element.121, f32[512]{0:T(512)S(1)} %fusion.59, f32[512]{0:T(512)S(1)} %broadcast_multiply_fusion.1, f32[768]{0:T(1024)S(1)} %copy-done.32, ...), kind=kOutput, calls=%fused_computation.45 | convolution fusion | flops 2419849216 | bytes 12601344 | tf_op jit(solution)/shard_map/dot_general | solution.py:94
  218.8 9.0 %grad_columns.3 = (bf16[8,48,3840]{2,1,0:T(8,128)(2,1)}, bf16[8,48,3840]{2,1,0:T(8,128)(2,1)}) custom-call(s32[1]{0:T(128)} %bitcast.2.page, bf16[512,768]{1,0:T(8,128)(2,1)} %attend.1.refs_0_, bf16[512,768]{1,0:T(8,128)(2,1)} %copy-done.25, bf16[512,768]{1,0:T(8,128)(2,1)} %copy-done.24, bf16[512,3072]{1,0:T(8,128)(2,1)} %get-tuple-element.70.refs_3_), custom_call_target="tpu_custom_call" | custom-call | flops 3019898880 | bytes 11796480 | tf_op jit(solution)/shard_map/grad_columns/pallas_call | solution.py:473
  227.8 29.8 %attend_back.1 = (bf16[512,768]{1,0:T(8,128)(2,1)}, bf16[1024,768]{1,0:T(8,128)(2,1)}, bf16[1024,768]{1,0:T(8,128)(2,1)}, f32[12,8,128]{2,1,0:T(8,128)}) custom-call(s32[48]{0:T(128)} %concatenate.57.bounds, bf16[512,768]{1,0:T(8,128)(2,1)} %fusion.21.q_ref, bf16[1024,1536]{1,0:T(8,128)(2,1)} %add_convert_fusion.1.k_ref.v_ref, ...), custom_call_target="tpu_custom_call" | custom-call | flops 8999999488 | bytes 9000000 | tf_op jit(solution)/shard_map/attend_back/pallas_call | solution.py:296
  257.6 3.3 fusion.23
  260.9 2.7 convolution_add_fusion
  266.5 8.6 %grad_columns.2 = (bf16[8,48,2304]{2,1,0:T(8,128)(2,1)}, bf16[8,48,2304]{2,1,0:T(8,128)(2,1)}) custom-call(s32[1]{0:T(128)} %bitcast.2.page, bf16[512,768]{1,0:T(8,128)(2,1)} %copy-done.9, bf16[512,768]{1,0:T(8,128)(2,1)} %get-tuple-element.36.refs_1_, bf16[1024,768]{1,0:T(8,128)(2,1)} %pad_maximum_fusion.refs_2_.refs_4_, ...), custom_call_target="tpu_custom_call" | custom-call | flops 3019898880 | bytes 7077888 | tf_op jit(solution)/shard_map/grad_columns/pallas_call | solution.py:473
  277.0 9.4 %grad_rows.1 = (bf16[8,192,768]{2,1,0:T(8,128)(2,1)}, bf16[8,192,768]{2,1,0:T(8,128)(2,1)}) custom-call(s32[1]{0:T(128)} %bitcast.2.page, bf16[512,3072]{1,0:T(8,128)(2,1)} %copy-done.47, bf16[512,768]{1,0:T(8,128)(2,1)} %copy-done.23), custom_call_target="tpu_custom_call" | custom-call | flops 2415919104 | bytes 8650752 | tf_op jit(solution)/shard_map/grad_rows/pallas_call | solution.py:410
  286.6 3.7 convert_add_fusion
  291.9 2.6 fusion.61
  297.6 2.9 collective-permute-done.21
  300.6 4.3 %collective-permute-done.22 = f32[24,768]{1,0:T(8,128)S(1)} collective-permute-done((f32[24,768]{1,0:T(8,128)S(1)}, f32[24,768]{1,0:T(8,128)S(1)}, u32[]{:S(2)}, u32[]{:S(2)}) %collective-permute-start.22) | collective-permute-done | bytes 73760 | tf_op jit(solution)/shard_map/ppermute | solution.py:534
  305.7 4.8 %collective-permute-done.23 = f32[24,768]{1,0:T(8,128)S(1)} collective-permute-done((f32[24,768]{1,0:T(8,128)S(1)}, f32[24,768]{1,0:T(8,128)S(1)}, u32[]{:S(2)}, u32[]{:S(2)}) %collective-permute-start.23) | collective-permute-done | bytes 73760 | tf_op jit(solution)/shard_map/ppermute | solution.py:534
  312.0 2.9 collective-permute-done.24
  318.1 3.1 add_convert_fusion.3
  321.5 2.9 add_convert_fusion.2
  326.0 13.0 %collective-permute-done.26 = bf16[4,48,2304]{2,1,0:T(8,128)(2,1)S(1)} collective-permute-done((bf16[4,48,2304]{2,1,0:T(8,128)(2,1)S(1)}, bf16[4,48,2304]{2,1,0:T(8,128)(2,1)S(1)}, u32[]{:S(2)}, u32[]{:S(2)}) %collective-permute-start.26) | collective-permute-done | bytes 884768 | tf_op jit(solution)/shard_map/ppermute | solution.py:347
  340.0 2.4 fusion.47
  344.6 2.2 collective-permute-start.27
  350.6 4.7 %collective-permute-done.28 = bf16[48,2304]{1,0:T(8,128)(2,1)} collective-permute-done((bf16[48,2304]{1,0:T(8,128)(2,1)}, bf16[48,2304]{1,0:T(8,128)(2,1)}, u32[]{:S(2)}, u32[]{:S(2)}) %collective-permute-start.28) | collective-permute-done | bytes 221216 | tf_op jit(solution)/shard_map/ppermute | solution.py:347
  358.3 6.1 %collective-permute-done.38 = bf16[4,192,768]{2,1,0:T(8,128)(2,1)} collective-permute-done((bf16[4,192,768]{2,1,0:T(8,128)(2,1)}, bf16[4,192,768]{2,1,0:T(8,128)(2,1)}, u32[]{:S(2)}, u32[]{:S(2)}) %collective-permute-start.38) | collective-permute-done | bytes 1179680 | tf_op jit(solution)/shard_map/ppermute | solution.py:347
  366.4 2.2 collective-permute-start.41
  368.6 2.2 collective-permute-start.39
  370.8 20.5 %collective-permute-done.32 = bf16[4,48,3840]{2,1,0:T(8,128)(2,1)} collective-permute-done((bf16[4,48,3840]{2,1,0:T(8,128)(2,1)}, bf16[4,48,3840]{2,1,0:T(8,128)(2,1)}, u32[]{:S(2)}, u32[]{:S(2)}) %collective-permute-start.32) | collective-permute-done | bytes 1474592 | tf_op jit(solution)/shard_map/ppermute | solution.py:347
  395.5 2.2 collective-permute-start.33
  400.7 5.9 %collective-permute-done.35 = bf16[48,3840]{1,0:T(8,128)(2,1)S(1)} collective-permute-done((bf16[48,3840]{1,0:T(8,128)(2,1)S(1)}, bf16[48,3840]{1,0:T(8,128)(2,1)S(1)}, u32[]{:S(2)}, u32[]{:S(2)}) %collective-permute-start.35) | collective-permute-done | bytes 368672 | tf_op jit(solution)/shard_map/ppermute | solution.py:347
  406.6 15.6 %collective-permute-done.34 = bf16[48,3840]{1,0:T(8,128)(2,1)S(1)} collective-permute-done((bf16[48,3840]{1,0:T(8,128)(2,1)S(1)}, bf16[48,3840]{1,0:T(8,128)(2,1)S(1)}, u32[]{:S(2)}, u32[]{:S(2)}) %collective-permute-start.34) | collective-permute-done | bytes 368672 | tf_op jit(solution)/shard_map/ppermute | solution.py:347
  426.9 4.7 %collective-permute-done.36 = bf16[48,3840]{1,0:T(8,128)(2,1)S(1)} collective-permute-done((bf16[48,3840]{1,0:T(8,128)(2,1)S(1)}, bf16[48,3840]{1,0:T(8,128)(2,1)S(1)}, u32[]{:S(2)}, u32[]{:S(2)}) %collective-permute-start.36) | collective-permute-done | bytes 368672 | tf_op jit(solution)/shard_map/ppermute | solution.py:540
  (280 shorter events, 82.7 us)
Async XLA Ops:
  3.3 14.0 %collective-permute-start.2 = (bf16[48,2304]{1,0:T(8,128)(2,1)S(1)}, bf16[48,2304]{1,0:T(8,128)(2,1)S(1)}, u32[]{:S(2)}, u32[]{:S(2)}) collective-permute-start(bf16[48,2304]{1,0:T(8,128)(2,1)S(1)} %constant_dynamic-update-slice_fusion), channel_id=1, source_target_pairs={{0,12},{1,13},{2,14},{3,15},{4,8},{5,9},{6,10},{7,11},{8,4},{9,5},... | collective-permute-start | bytes 663560 | tf_op jit(solution)/shard_map/ppermute | solution.py:347
  8.4 18.8 %collective-permute-start.1 = (bf16[48,2304]{1,0:T(8,128)(2,1)S(1)}, bf16[48,2304]{1,0:T(8,128)(2,1)S(1)}, u32[]{:S(2)}, u32[]{:S(2)}) collective-permute-start(bf16[48,2304]{1,0:T(8,128)(2,1)S(1)} %constant_dynamic-update-slice_fusion), channel_id=1, source_target_pairs={{0,8},{1,9},{2,10},{3,11},{4,12},{5,13},{6,14},{7,15},{8,0},{9,1},... | collective-permute-start | bytes 663560 | tf_op jit(solution)/shard_map/ppermute | solution.py:347
  8.5 18.8 %collective-permute-start = (bf16[48,2304]{1,0:T(8,128)(2,1)S(1)}, bf16[48,2304]{1,0:T(8,128)(2,1)S(1)}, u32[]{:S(2)}, u32[]{:S(2)}) collective-permute-start(bf16[48,2304]{1,0:T(8,128)(2,1)S(1)} %constant_dynamic-update-slice_fusion), channel_id=1, source_target_pairs={{0,4},{1,5},{2,6},{3,7},{4,0},{5,1},{6,2},{7,3},{8,12},{9,13},{10,... | collective-permute-start | bytes 663560 | tf_op jit(solution)/shard_map/ppermute | solution.py:347
  9.1 81.5 %collective-permute-start.6 = (bf16[512,768]{1,0:T(8,128)(2,1)}, bf16[512,768]{1,0:T(8,128)(2,1)S(1)}, u32[]{:S(2)}, u32[]{:S(2)}) collective-permute-start(bf16[512,768]{1,0:T(8,128)(2,1)} %bitcast.113), channel_id=1, source_target_pairs={{0,16},{16,0},{1,17},{17,1},{2,18},{18,2},{3,19},{19,3},{4,20},{20... | collective-permute-start | bytes 2359304 | tf_op jit(solution)/shard_map/ppermute | solution.py:540
  28.3 13.4 %collective-permute-start.9 = (bf16[48,3840]{1,0:T(8,128)(2,1)S(1)}, bf16[48,3840]{1,0:T(8,128)(2,1)S(1)}, u32[]{:S(2)}, u32[]{:S(2)}) collective-permute-start(bf16[48,3840]{1,0:T(8,128)(2,1)S(1)} %pad_maximum_fusion.4), channel_id=1, source_target_pairs={{0,12},{1,13},{2,14},{3,15},{4,8},{5,9},{6,10},{7,11},{8,4},{9,5},... | collective-permute-start | bytes 1105928 | tf_op jit(solution)/shard_map/ppermute | solution.py:347
  30.8 29.8 %collective-permute-start.8 = (bf16[48,3840]{1,0:T(8,128)(2,1)S(1)}, bf16[48,3840]{1,0:T(8,128)(2,1)S(1)}, u32[]{:S(2)}, u32[]{:S(2)}) collective-permute-start(bf16[48,3840]{1,0:T(8,128)(2,1)S(1)} %pad_maximum_fusion.4), channel_id=1, source_target_pairs={{0,8},{1,9},{2,10},{3,11},{4,12},{5,13},{6,14},{7,15},{8,0},{9,1},... | collective-permute-start | bytes 1105928 | tf_op jit(solution)/shard_map/ppermute | solution.py:347
  30.8 29.8 %collective-permute-start.7 = (bf16[48,3840]{1,0:T(8,128)(2,1)S(1)}, bf16[48,3840]{1,0:T(8,128)(2,1)S(1)}, u32[]{:S(2)}, u32[]{:S(2)}) collective-permute-start(bf16[48,3840]{1,0:T(8,128)(2,1)S(1)} %pad_maximum_fusion.4), channel_id=1, source_target_pairs={{0,4},{1,5},{2,6},{3,7},{4,0},{5,1},{6,2},{7,3},{8,12},{9,13},{10,... | collective-permute-start | bytes 1105928 | tf_op jit(solution)/shard_map/ppermute | solution.py:347
  33.9 28.0 %copy-start.26 = (bf16[192,768]{1,0:T(8,128)(2,1)S(1)}, bf16[192,768]{1,0:T(8,128)(2,1)}, u32[]{:S(2)}) copy-start(bf16[192,768]{1,0:T(8,128)(2,1)} %param.46) | copy-start | bytes 884740
  33.9 29.6 %copy-start.4 = (bf16[1,1,512,768]{3,2,1,0:T(8,128)(2,1)S(1)}, bf16[1,1,512,768]{3,2,1,0:T(8,128)(2,1)}, u32[]{:S(2)}) copy-start(bf16[1,1,512,768]{3,2,1,0:T(8,128)(2,1)} %param.26) | copy-start | bytes 2359300
  62.0 11.8 %collective-permute-start.15 = (bf16[192,768]{1,0:T(8,128)(2,1)S(1)}, bf16[192,768]{1,0:T(8,128)(2,1)S(1)}, u32[]{:S(2)}, u32[]{:S(2)}) collective-permute-start(bf16[192,768]{1,0:T(8,128)(2,1)S(1)} %copy-done.26), channel_id=1, source_target_pairs={{0,12},{1,13},{2,14},{3,15},{4,8},{5,9},{6,10},{7,11},{8,4},{9,5},... | collective-permute-start | bytes 884744 | tf_op jit(solution)/shard_map/ppermute | solution.py:347
  64.5 57.6 %collective-permute-start.11 = (bf16[4,48,3840]{2,1,0:T(8,128)(2,1)}, bf16[4,48,3840]{2,1,0:T(8,128)(2,1)}, u32[]{:S(2)}, u32[]{:S(2)}) collective-permute-start(bf16[4,48,3840]{2,1,0:T(8,128)(2,1)} %pad_maximum_fusion.1.refs_0_), channel_id=1, source_target_pairs={{0,2},{1,3},{2,0},{3,1},{4,6},{5,7},{6,4},{7,5},{8,10},{9,11},{10,... | collective-permute-start | bytes 4423688 | tf_op jit(solution)/shard_map/ppermute | solution.py:347
  66.0 52.8 %collective-permute-start.4 = (bf16[4,48,2304]{2,1,0:T(8,128)(2,1)}, bf16[4,48,2304]{2,1,0:T(8,128)(2,1)S(1)}, u32[]{:S(2)}, u32[]{:S(2)}) collective-permute-start(bf16[4,48,2304]{2,1,0:T(8,128)(2,1)} %pad_maximum_fusion.3.refs_0_), channel_id=1, source_target_pairs={{0,2},{1,3},{2,0},{3,1},{4,6},{5,7},{6,4},{7,5},{8,10},{9,11},{10,... | collective-permute-start | bytes 2654216 | tf_op jit(solution)/shard_map/ppermute | solution.py:347
  67.2 19.1 %collective-permute-start.14 = (bf16[192,768]{1,0:T(8,128)(2,1)S(1)}, bf16[192,768]{1,0:T(8,128)(2,1)S(1)}, u32[]{:S(2)}, u32[]{:S(2)}) collective-permute-start(bf16[192,768]{1,0:T(8,128)(2,1)S(1)} %copy-done.26), channel_id=1, source_target_pairs={{0,8},{1,9},{2,10},{3,11},{4,12},{5,13},{6,14},{7,15},{8,0},{9,1},... | collective-permute-start | bytes 884744 | tf_op jit(solution)/shard_map/ppermute | solution.py:347
  74.5 14.9 %collective-permute-start.13 = (bf16[192,768]{1,0:T(8,128)(2,1)S(1)}, bf16[192,768]{1,0:T(8,128)(2,1)S(1)}, u32[]{:S(2)}, u32[]{:S(2)}) collective-permute-start(bf16[192,768]{1,0:T(8,128)(2,1)S(1)} %copy-done.26), channel_id=1, source_target_pairs={{0,4},{1,5},{2,6},{3,7},{4,0},{5,1},{6,2},{7,3},{8,12},{9,13},{10,... | collective-permute-start | bytes 884744 | tf_op jit(solution)/shard_map/ppermute | solution.py:347
  86.0 32.8 %copy-start = (f32[510,768]{1,0:T(8,128)}, f32[510,768]{1,0:T(8,128)S(1)}, u32[]{:S(2)}) copy-start(f32[510,768]{1,0:T(8,128)S(1)} %get-tuple-element.101) | copy-start | bytes 4700164
  86.3 37.9 %collective-permute-start.3 = (bf16[4,48,2304]{2,1,0:T(8,128)(2,1)}, bf16[4,48,2304]{2,1,0:T(8,128)(2,1)S(1)}, u32[]{:S(2)}, u32[]{:S(2)}) collective-permute-start(bf16[4,48,2304]{2,1,0:T(8,128)(2,1)} %pad_maximum_fusion.3.refs_0_), channel_id=1, source_target_pairs={{0,1},{1,0},{2,3},{3,2},{4,5},{5,4},{6,7},{7,6},{8,9},{9,8},{10,11... | collective-permute-start | bytes 2654216 | tf_op jit(solution)/shard_map/ppermute | solution.py:347
  89.4 77.5 %collective-permute-start.10 = (bf16[4,48,3840]{2,1,0:T(8,128)(2,1)}, bf16[4,48,3840]{2,1,0:T(8,128)(2,1)}, u32[]{:S(2)}, u32[]{:S(2)}) collective-permute-start(bf16[4,48,3840]{2,1,0:T(8,128)(2,1)} %pad_maximum_fusion.1.refs_0_), channel_id=1, source_target_pairs={{0,1},{1,0},{2,3},{3,2},{4,5},{5,4},{6,7},{7,6},{8,9},{9,8},{10,11... | collective-permute-start | bytes 4423688 | tf_op jit(solution)/shard_map/ppermute | solution.py:347
  90.6 28.3 %copy-start.6 = (bf16[1,1,512,768]{3,2,1,0:T(8,128)(2,1)S(1)}, bf16[1,1,512,768]{3,2,1,0:T(8,128)(2,1)}, u32[]{:S(2)}) copy-start(bf16[1,1,512,768]{3,2,1,0:T(8,128)(2,1)} %param.25) | copy-start | bytes 2359300
  90.6 28.3 %copy-start.38 = (f32[768]{0:T(1024)S(1)}, f32[768]{0:T(1024)}, u32[]{:S(2)}) copy-start(f32[768]{0:T(1024)} %param.31) | copy-start | bytes 9220
  90.6 50.6 %collective-permute-start.17 = (bf16[4,192,768]{2,1,0:T(8,128)(2,1)}, bf16[4,192,768]{2,1,0:T(8,128)(2,1)}, u32[]{:S(2)}, u32[]{:S(2)}) collective-permute-start(bf16[4,192,768]{2,1,0:T(8,128)(2,1)} %pad_maximum_fusion.2.refs_0_), channel_id=1, source_target_pairs={{0,2},{1,3},{2,0},{3,1},{4,6},{5,7},{6,4},{7,5},{8,10},{9,11},{10,... | collective-permute-start | bytes 3538952 | tf_op jit(solution)/shard_map/ppermute | solution.py:347
  118.9 5.6 %collective-permute-start.5 = (bf16[4,48,2304]{2,1,0:T(8,128)(2,1)S(1)}, bf16[4,48,2304]{2,1,0:T(8,128)(2,1)S(1)}, u32[]{:S(2)}, u32[]{:S(2)}) collective-permute-start(bf16[4,48,2304]{2,1,0:T(8,128)(2,1)S(1)} %collective-permute-done.4.refs_2_), channel_id=1, source_target_pairs={{0,1},{1,0},{2,3},{3,2},{4,5},{5,4},{6,7},{7,6},{8,9},{9,8},{10,11... | collective-permute-start | bytes 2654216 | tf_op jit(solution)/shard_map/ppermute | solution.py:347
  122.1 44.8 %collective-permute-start.12 = (bf16[4,48,3840]{2,1,0:T(8,128)(2,1)}, bf16[4,48,3840]{2,1,0:T(8,128)(2,1)}, u32[]{:S(2)}, u32[]{:S(2)}) collective-permute-start(bf16[4,48,3840]{2,1,0:T(8,128)(2,1)} %collective-permute-done.11.refs_2_), channel_id=1, source_target_pairs={{0,1},{1,0},{2,3},{3,2},{4,5},{5,4},{6,7},{7,6},{8,9},{9,8},{10,11... | collective-permute-start | bytes 4423688 | tf_op jit(solution)/shard_map/ppermute | solution.py:347
  124.2 38.0 %collective-permute-start.16 = (bf16[4,192,768]{2,1,0:T(8,128)(2,1)}, bf16[4,192,768]{2,1,0:T(8,128)(2,1)}, u32[]{:S(2)}, u32[]{:S(2)}) collective-permute-start(bf16[4,192,768]{2,1,0:T(8,128)(2,1)} %pad_maximum_fusion.2.refs_0_), channel_id=1, source_target_pairs={{0,1},{1,0},{2,3},{3,2},{4,5},{5,4},{6,7},{7,6},{8,9},{9,8},{10,11... | collective-permute-start | bytes 3538952 | tf_op jit(solution)/shard_map/ppermute | solution.py:347
  141.2 21.1 %collective-permute-start.18 = (bf16[4,192,768]{2,1,0:T(8,128)(2,1)}, bf16[4,192,768]{2,1,0:T(8,128)(2,1)}, u32[]{:S(2)}, u32[]{:S(2)}) collective-permute-start(bf16[4,192,768]{2,1,0:T(8,128)(2,1)} %collective-permute-done.17.refs_2_), channel_id=1, source_target_pairs={{0,1},{1,0},{2,3},{3,2},{4,5},{5,4},{6,7},{7,6},{8,9},{9,8},{10,11... | collective-permute-start | bytes 3538952 | tf_op jit(solution)/shard_map/ppermute | solution.py:347
  264.6 22.0 %collective-permute-start.19 = (bf16[512,768]{1,0:T(8,128)(2,1)}, bf16[512,768]{1,0:T(8,128)(2,1)}, u32[]{:S(2)}, u32[]{:S(2)}) collective-permute-start(bf16[512,768]{1,0:T(8,128)(2,1)} %select_convert_fusion), channel_id=1, source_target_pairs={{0,16},{16,0},{1,17},{17,1},{2,18},{18,2},{3,19},{19,3},{4,20},{20... | collective-permute-start | bytes 2359304 | tf_op jit(solution)/shard_map/ppermute | solution.py:540
  266.1 55.5 %collective-permute-start.31 = (bf16[8,48,3840]{2,1,0:T(8,128)(2,1)}, bf16[8,48,3840]{2,1,0:T(8,128)(2,1)}, u32[]{:S(2)}, u32[]{:S(2)}) collective-permute-start(bf16[8,48,3840]{2,1,0:T(8,128)(2,1)} %get-tuple-element.43), channel_id=1, source_target_pairs={{0,1},{1,0},{2,3},{3,2},{4,5},{5,4},{6,7},{7,6},{8,9},{9,8},{10,11... | collective-permute-start | bytes 8847368 | tf_op jit(solution)/shard_map/ppermute | solution.py:347
  276.6 38.3 %collective-permute-start.25 = (bf16[8,48,2304]{2,1,0:T(8,128)(2,1)}, bf16[8,48,2304]{2,1,0:T(8,128)(2,1)}, u32[]{:S(2)}, u32[]{:S(2)}) collective-permute-start(bf16[8,48,2304]{2,1,0:T(8,128)(2,1)} %get-tuple-element.41), channel_id=1, source_target_pairs={{0,1},{1,0},{2,3},{3,2},{4,5},{5,4},{6,7},{7,6},{8,9},{9,8},{10,11... | collective-permute-start | bytes 5308424 | tf_op jit(solution)/shard_map/ppermute | solution.py:347
  286.4 31.7 %collective-permute-start.37 = (bf16[8,192,768]{2,1,0:T(8,128)(2,1)}, bf16[8,192,768]{2,1,0:T(8,128)(2,1)}, u32[]{:S(2)}, u32[]{:S(2)}) collective-permute-start(bf16[8,192,768]{2,1,0:T(8,128)(2,1)} %get-tuple-element.45), channel_id=1, source_target_pairs={{0,1},{1,0},{2,3},{3,2},{4,5},{5,4},{6,7},{7,6},{8,9},{9,8},{10,11... | collective-permute-start | bytes 7077896 | tf_op jit(solution)/shard_map/ppermute | solution.py:347
  294.6 1.3 collective-permute-start.20
  295.9 4.6 %collective-permute-start.21 = (f32[24,768]{1,0:T(8,128)S(1)}, f32[24,768]{1,0:T(8,128)S(1)}, u32[]{:S(2)}, u32[]{:S(2)}) collective-permute-start(f32[24,768]{1,0:T(8,128)S(1)} %add.444), channel_id=1, source_target_pairs={{0,2},{1,3},{2,0},{3,1},{4,6},{5,7},{6,4},{7,5},{8,10},{9,11},{10,... | collective-permute-start | bytes 221192 | tf_op jit(solution)/shard_map/ppermute | solution.py:534
  300.5 4.4 %collective-permute-start.22 = (f32[24,768]{1,0:T(8,128)S(1)}, f32[24,768]{1,0:T(8,128)S(1)}, u32[]{:S(2)}, u32[]{:S(2)}) collective-permute-start(f32[24,768]{1,0:T(8,128)S(1)} %add.445), channel_id=1, source_target_pairs={{0,4},{1,5},{2,6},{3,7},{4,0},{5,1},{6,2},{7,3},{8,12},{9,13},{10,... | collective-permute-start | bytes 221192 | tf_op jit(solution)/shard_map/ppermute | solution.py:534
  304.9 5.5 %collective-permute-start.23 = (f32[24,768]{1,0:T(8,128)S(1)}, f32[24,768]{1,0:T(8,128)S(1)}, u32[]{:S(2)}, u32[]{:S(2)}) collective-permute-start(f32[24,768]{1,0:T(8,128)S(1)} %add.446), channel_id=1, source_target_pairs={{0,8},{1,9},{2,10},{3,11},{4,12},{5,13},{6,14},{7,15},{8,0},{9,1},... | collective-permute-start | bytes 221192 | tf_op jit(solution)/shard_map/ppermute | solution.py:534
  310.5 4.4 %collective-permute-start.24 = (f32[24,768]{1,0:T(8,128)S(1)}, f32[24,768]{1,0:T(8,128)S(1)}, u32[]{:S(2)}, u32[]{:S(2)}) collective-permute-start(f32[24,768]{1,0:T(8,128)S(1)} %add.447), channel_id=1, source_target_pairs={{0,16},{16,0},{1,17},{17,1},{2,18},{18,2},{3,19},{19,3},{4,20},{20... | collective-permute-start | bytes 221192 | tf_op jit(solution)/shard_map/ppermute | solution.py:540
  316.3 22.7 %collective-permute-start.26 = (bf16[4,48,2304]{2,1,0:T(8,128)(2,1)S(1)}, bf16[4,48,2304]{2,1,0:T(8,128)(2,1)S(1)}, u32[]{:S(2)}, u32[]{:S(2)}) collective-permute-start(bf16[4,48,2304]{2,1,0:T(8,128)(2,1)S(1)} %add_convert_fusion.4), channel_id=1, source_target_pairs={{0,2},{1,3},{2,0},{3,1},{4,6},{5,7},{6,4},{7,5},{8,10},{9,11},{10,... | collective-permute-start | bytes 2654216 | tf_op jit(solution)/shard_map/ppermute | solution.py:347
  321.2 43.2 %collective-permute-start.38 = (bf16[4,192,768]{2,1,0:T(8,128)(2,1)}, bf16[4,192,768]{2,1,0:T(8,128)(2,1)}, u32[]{:S(2)}, u32[]{:S(2)}) collective-permute-start(bf16[4,192,768]{2,1,0:T(8,128)(2,1)} %add_convert_fusion.3), channel_id=1, source_target_pairs={{0,2},{1,3},{2,0},{3,1},{4,6},{5,7},{6,4},{7,5},{8,10},{9,11},{10,... | collective-permute-start | bytes 3538952 | tf_op jit(solution)/shard_map/ppermute | solution.py:347
  324.4 66.9 %collective-permute-start.32 = (bf16[4,48,3840]{2,1,0:T(8,128)(2,1)}, bf16[4,48,3840]{2,1,0:T(8,128)(2,1)}, u32[]{:S(2)}, u32[]{:S(2)}) collective-permute-start(bf16[4,48,3840]{2,1,0:T(8,128)(2,1)} %add_convert_fusion.2), channel_id=1, source_target_pairs={{0,2},{1,3},{2,0},{3,1},{4,6},{5,7},{6,4},{7,5},{8,10},{9,11},{10,... | collective-permute-start | bytes 4423688 | tf_op jit(solution)/shard_map/ppermute | solution.py:347
  342.4 8.2 %collective-permute-start.29 = (bf16[48,2304]{1,0:T(8,128)(2,1)}, bf16[48,2304]{1,0:T(8,128)(2,1)S(1)}, u32[]{:S(2)}, u32[]{:S(2)}) collective-permute-start(bf16[48,2304]{1,0:T(8,128)(2,1)} %get-tuple-element.94), channel_id=1, source_target_pairs={{0,12},{1,13},{2,14},{3,15},{4,8},{5,9},{6,10},{7,11},{8,4},{9,5},... | collective-permute-start | bytes 663560 | tf_op jit(solution)/shard_map/ppermute | solution.py:347
  344.6 10.7 %collective-permute-start.28 = (bf16[48,2304]{1,0:T(8,128)(2,1)}, bf16[48,2304]{1,0:T(8,128)(2,1)}, u32[]{:S(2)}, u32[]{:S(2)}) collective-permute-start(bf16[48,2304]{1,0:T(8,128)(2,1)} %get-tuple-element.95), channel_id=1, source_target_pairs={{0,8},{1,9},{2,10},{3,11},{4,12},{5,13},{6,14},{7,15},{8,0},{9,1},... | collective-permute-start | bytes 663560 | tf_op jit(solution)/shard_map/ppermute | solution.py:347
  344.6 10.7 %collective-permute-start.27 = (bf16[48,2304]{1,0:T(8,128)(2,1)}, bf16[48,2304]{1,0:T(8,128)(2,1)}, u32[]{:S(2)}, u32[]{:S(2)}) collective-permute-start(bf16[48,2304]{1,0:T(8,128)(2,1)} %get-tuple-element.93), channel_id=1, source_target_pairs={{0,4},{1,5},{2,6},{3,7},{4,0},{5,1},{6,2},{7,3},{8,12},{9,13},{10,... | collective-permute-start | bytes 663560 | tf_op jit(solution)/shard_map/ppermute | solution.py:347
  356.7 38.7 %collective-permute-start.30 = (bf16[48,2304]{1,0:T(8,128)(2,1)S(1)}, bf16[48,2304]{1,0:T(8,128)(2,1)S(1)}, u32[]{:S(2)}, u32[]{:S(2)}) collective-permute-start(bf16[48,2304]{1,0:T(8,128)(2,1)S(1)} %fusion.40), channel_id=1, source_target_pairs={{0,16},{16,0},{1,17},{17,1},{2,18},{18,2},{3,19},{19,3},{4,20},{20... | collective-permute-start | bytes 663560 | tf_op jit(solution)/shard_map/ppermute | solution.py:540
  366.4 29.1 %collective-permute-start.41 = (bf16[192,768]{1,0:T(8,128)(2,1)S(1)}, bf16[192,768]{1,0:T(8,128)(2,1)S(1)}, u32[]{:S(2)}, u32[]{:S(2)}) collective-permute-start(bf16[192,768]{1,0:T(8,128)(2,1)S(1)} %get-tuple-element.91), channel_id=1, source_target_pairs={{0,12},{1,13},{2,14},{3,15},{4,8},{5,9},{6,10},{7,11},{8,4},{9,5},... | collective-permute-start | bytes 884744 | tf_op jit(solution)/shard_map/ppermute | solution.py:347
  368.6 29.1 %collective-permute-start.40 = (bf16[192,768]{1,0:T(8,128)(2,1)S(1)}, bf16[192,768]{1,0:T(8,128)(2,1)S(1)}, u32[]{:S(2)}, u32[]{:S(2)}) collective-permute-start(bf16[192,768]{1,0:T(8,128)(2,1)S(1)} %get-tuple-element.92), channel_id=1, source_target_pairs={{0,8},{1,9},{2,10},{3,11},{4,12},{5,13},{6,14},{7,15},{8,0},{9,1},... | collective-permute-start | bytes 884744 | tf_op jit(solution)/shard_map/ppermute | solution.py:347
  368.6 29.1 %collective-permute-start.39 = (bf16[192,768]{1,0:T(8,128)(2,1)S(1)}, bf16[192,768]{1,0:T(8,128)(2,1)S(1)}, u32[]{:S(2)}, u32[]{:S(2)}) collective-permute-start(bf16[192,768]{1,0:T(8,128)(2,1)S(1)} %get-tuple-element.90), channel_id=1, source_target_pairs={{0,4},{1,5},{2,6},{3,7},{4,0},{5,1},{6,2},{7,3},{8,12},{9,13},{10,... | collective-permute-start | bytes 884744 | tf_op jit(solution)/shard_map/ppermute | solution.py:347
  393.2 13.4 %collective-permute-start.35 = (bf16[48,3840]{1,0:T(8,128)(2,1)S(1)}, bf16[48,3840]{1,0:T(8,128)(2,1)S(1)}, u32[]{:S(2)}, u32[]{:S(2)}) collective-permute-start(bf16[48,3840]{1,0:T(8,128)(2,1)S(1)} %get-tuple-element.88), channel_id=1, source_target_pairs={{0,12},{1,13},{2,14},{3,15},{4,8},{5,9},{6,10},{7,11},{8,4},{9,5},... | collective-permute-start | bytes 1105928 | tf_op jit(solution)/shard_map/ppermute | solution.py:347
  395.4 26.8 %collective-permute-start.34 = (bf16[48,3840]{1,0:T(8,128)(2,1)S(1)}, bf16[48,3840]{1,0:T(8,128)(2,1)S(1)}, u32[]{:S(2)}, u32[]{:S(2)}) collective-permute-start(bf16[48,3840]{1,0:T(8,128)(2,1)S(1)} %get-tuple-element.89), channel_id=1, source_target_pairs={{0,8},{1,9},{2,10},{3,11},{4,12},{5,13},{6,14},{7,15},{8,0},{9,1},... | collective-permute-start | bytes 1105928 | tf_op jit(solution)/shard_map/ppermute | solution.py:347
  395.5 26.8 %collective-permute-start.33 = (bf16[48,3840]{1,0:T(8,128)(2,1)S(1)}, bf16[48,3840]{1,0:T(8,128)(2,1)S(1)}, u32[]{:S(2)}, u32[]{:S(2)}) collective-permute-start(bf16[48,3840]{1,0:T(8,128)(2,1)S(1)} %get-tuple-element.87), channel_id=1, source_target_pairs={{0,4},{1,5},{2,6},{3,7},{4,0},{5,1},{6,2},{7,3},{8,12},{9,13},{10,... | collective-permute-start | bytes 1105928 | tf_op jit(solution)/shard_map/ppermute | solution.py:347
  399.2 26.8 %collective-permute-start.42 = (bf16[192,768]{1,0:T(8,128)(2,1)S(1)}, bf16[192,768]{1,0:T(8,128)(2,1)S(1)}, u32[]{:S(2)}, u32[]{:S(2)}) collective-permute-start(bf16[192,768]{1,0:T(8,128)(2,1)S(1)} %fusion.37), channel_id=1, source_target_pairs={{0,16},{16,0},{1,17},{17,1},{2,18},{18,2},{3,19},{19,3},{4,20},{20... | collective-permute-start | bytes 884744 | tf_op jit(solution)/shard_map/ppermute | solution.py:540
  423.6 8.0 %collective-permute-start.36 = (bf16[48,3840]{1,0:T(8,128)(2,1)S(1)}, bf16[48,3840]{1,0:T(8,128)(2,1)S(1)}, u32[]{:S(2)}, u32[]{:S(2)}) collective-permute-start(bf16[48,3840]{1,0:T(8,128)(2,1)S(1)} %fusion.34), channel_id=1, source_target_pairs={{0,16},{16,0},{1,17},{17,1},{2,18},{18,2},{3,19},{19,3},{4,20},{20... | collective-permute-start | bytes 1105928 | tf_op jit(solution)/shard_map/ppermute | solution.py:540
  (45 other events, 307.1 us)

commit v3 on v2

--- a/solution.py
+++ b/solution.py
@@ -260,11 +260,12 @@
     return pl.BlockSpec((rows, LANES), lambda pair, bounds: (0, pair + first))
 
 
+def tables_spec(first=0):
+    return pl.BlockSpec((2, 8, LANES), lambda pair, bounds: (pair + first, 0, 0))
+
+
 def whole_spec(rows):
     return pl.BlockSpec((rows, LANES), lambda pair, bounds: (0, 0))
-
-
-table_spec = pl.BlockSpec((2, 8, LANES), lambda pair, bounds: (pair, 0, 0))
 
 
 def attend(bounds, queries, keys_values, features, own_features, tables):
@@ -279,7 +280,7 @@
                 column_spec(2 * TEXT, PAIRS),
                 whole_spec(2 * TEXT),
                 whole_spec(TEXT),
-                table_spec,
+                tables_spec(),
             ],
             out_specs=column_spec(TEXT),
             scratch_shapes=[pltpu.VMEM((TEXT, 2 * LANES), bf16)],
@@ -292,27 +293,29 @@
     )(bounds, queries, keys_values, keys_values, features, own_features, tables)
 
 
-def attend_back(bounds, queries, keys_values, grad_context, features, own_features, flip, tables):
+def attend_back(
+    bounds, queries, keys_values, grad_context, features, own_features, flip, tables, first, count
+):
     return pl.pallas_call(
         attend_back_kernel,
         grid_spec=pltpu.PrefetchScalarGridSpec(
             num_scalar_prefetch=1,
-            grid=(PAIRS,),
+            grid=(count,),
             in_specs=[
-                column_spec(TEXT),
-                column_spec(2 * TEXT),
-                column_spec(2 * TEXT, PAIRS),
-                column_spec(TEXT),
+                column_spec(TEXT, first),
+                column_spec(2 * TEXT, first),
+                column_spec(2 * TEXT, PAIRS + first),
+                column_spec(TEXT, first),
                 whole_spec(2 * TEXT),
                 whole_spec(TEXT),
                 whole_spec(TEXT),
-                table_spec,
+                tables_spec(first),
             ],
             out_specs=[
                 column_spec(TEXT),
                 column_spec(2 * TEXT),
                 column_spec(2 * TEXT),
-                table_spec,
+                tables_spec(),
             ],
             scratch_shapes=[
                 pltpu.VMEM((TEXT, 2 * LANES), bf16),
@@ -320,13 +323,13 @@
             ],
         ),
         out_shape=[
-            jax.ShapeDtypeStruct((TEXT, HEADS * HEAD), bf16),
-            jax.ShapeDtypeStruct((2 * TEXT, HEADS * HEAD), bf16),
-            jax.ShapeDtypeStruct((2 * TEXT, HEADS * HEAD), bf16),
-            jax.ShapeDtypeStruct((HEADS, 8, LANES), f32),
+            jax.ShapeDtypeStruct((TEXT, count * LANES), bf16),
+            jax.ShapeDtypeStruct((2 * TEXT, count * LANES), bf16),
+            jax.ShapeDtypeStruct((2 * TEXT, count * LANES), bf16),
+            jax.ShapeDtypeStruct((2 * count, 8, LANES), f32),
         ],
         cost_estimate=pl.CostEstimate(
-            flops=9_000_000_000, bytes_accessed=9_000_000, transcendentals=3_000_000
+            flops=4_000_000_000 * count, bytes_accessed=1_500_000 * count, transcendentals=500_000
         ),
         name="attend_back",
     )(
@@ -347,15 +350,24 @@
     return lax.ppermute(values, "page", [(i, i ^ mask) for i in range(count)])
 
 
-def place_kernel(page, *refs):
+def after(value, *earlier):
+    return lax.optimization_barrier((value, *earlier))[0]
+
+
+def slot_mask(slot):
+    return (slot & 3) * 4 + (slot >> 2) * 2
+
+
+def place_kernel(place, *refs):
     pieces, full_ref, sems = refs[:4], refs[4], refs[5]
     rows = pieces[0].shape[1]
     copies = []
-    for mask in range(16):
-        at = pl.multiple_of((page[0] ^ mask) * rows, 16)
+    for index in range(16):
+        mask = (index >> 2) * 4 + (index & 3)
+        at = pl.multiple_of((place[0] ^ mask) * rows, 16)
         copies.append(
             pltpu.make_async_copy(
-                pieces[mask & 3].at[mask >> 2], full_ref.at[pl.ds(at, rows)], sems.at[mask]
+                pieces[index & 3].at[index >> 2], full_ref.at[pl.ds(at, rows)], sems.at[index]
             )
         )
     for copy in copies:
@@ -364,28 +376,54 @@
         copy.wait()
 
 
-def gathered(shard, page):
-    rows, width = shard.shape
-    column = jnp.stack([shard] + [exchange(shard, 4 * step) for step in (1, 2, 3)])
-    across = exchange(column, 2)
-    partner = exchange(column, 1)
-    partner_across = exchange(across, 1)
-    full = pl.pallas_call(
-        place_kernel,
+def place_halves_kernel(place, *refs):
+    pieces, full_ref, sems = refs[:4], refs[4], refs[5]
+    rows, half = pieces[0].shape[1], pieces[0].shape[2]
+    copies = []
+    for index in range(32):
+        kind = index >> 3
+        mask = slot_mask(index & 7) + (kind & 1)
+        at = pl.multiple_of((place[0] ^ mask) * rows, 16)
+        column = pl.multiple_of((place[1] ^ (kind >> 1)) * half, 128)
+        copies.append(
+            pltpu.make_async_copy(
+                pieces[kind].at[index & 7],
+                full_ref.at[pl.ds(at, rows), pl.ds(column, half)],
+                sems.at[index],
+            )
+        )
+    for copy in copies:
+        copy.start()
+    for copy in copies:
+        copy.wait()
+
+
+def place_rows(place, pieces, width, kernel):
+    rows = pieces[0].shape[1]
+    return pl.pallas_call(
+        kernel,
         grid_spec=pltpu.PrefetchScalarGridSpec(
             num_scalar_prefetch=1,
             grid=(),
             in_specs=[pl.BlockSpec(memory_space=pl.ANY)] * 4,
             out_specs=pl.BlockSpec(memory_space=pltpu.VMEM),
-            scratch_shapes=[pltpu.SemaphoreType.DMA((16,))],
-        ),
-        out_shape=jax.ShapeDtypeStruct((16 * rows, width), shard.dtype),
+            scratch_shapes=[pltpu.SemaphoreType.DMA((32,))],
+        ),
+        out_shape=jax.ShapeDtypeStruct((16 * rows, width), bf16),
         cost_estimate=pl.CostEstimate(
             flops=0, bytes_accessed=64 * rows * width, transcendentals=0
         ),
         name="place_rows",
-    )(page, column, partner, across, partner_across)
-    return full, column
+    )(place, *pieces)
+
+
+def column_of(shard):
+    return jnp.stack([shard] + [exchange(shard, 4 * step) for step in (1, 2, 3)])
+
+
+def pieces_of(column):
+    across = exchange(column, 2)
+    return column, exchange(column, 1), across, exchange(across, 1)
 
 
 def grad_rows_kernel(page, x_ref, h_ref, keep_ref, send_ref, product):
@@ -443,7 +481,7 @@
 
         first = first + count
     for slot in range(8):
-        mask = (slot & 3) * 4 + (slot >> 2) * 2
+        mask = slot_mask(slot)
         mine = pl.multiple_of((page[0] ^ mask) * rows, 16)
         theirs = pl.multiple_of((page[0] ^ (mask + 1)) * rows, 16)
         keep_ref[slot] = product[pl.ds(mine, rows), :].astype(bf16)
@@ -487,22 +525,31 @@
     )(page, *operands)
 
 
-def scattered(keep, send):
-    partner = exchange(send, 1)
-
-    def pair(at):
-        return keep[at].astype(f32) + partner[at].astype(f32)
-
-    across = exchange(pair(slice(4, 8)).astype(bf16), 2)
-
-    def four(z):
-        return pair(z) + across[z].astype(f32)
-
-    total = four(0)
-    for step in (1, 2, 3):
-        total = total + exchange(four(step).astype(bf16), 4 * step).astype(f32)
-    low = total.astype(bf16)
-    return low.astype(f32) + swap(low).astype(f32)
+def pair_sum(keep, partner, at):
+    return keep[at].astype(f32) + partner[at].astype(f32)
+
+
+def across_send(keep, partner):
+    return pair_sum(keep, partner, slice(4, 8)).astype(bf16)
+
+
+def column_sends(keep, partner, across):
+    return [
+        (pair_sum(keep, partner, step) + across[step].astype(f32)).astype(bf16)
+        for step in (1, 2, 3)
+    ]
+
+
+def column_total(keep, partner, across, arrived):
+    total = pair_sum(keep, partner, 0) + across[0].astype(f32)
+    for part in arrived:
+        total = total + part.astype(f32)
+    return total.astype(bf16)
+
+
+def half_columns(values, first):
+    half = values.shape[-1] // 2
+    return jnp.where(first, values[..., :half], values[..., half:])
 
 
 def summed_rows(pairs):
@@ -570,27 +617,27 @@
     is_text = lax.axis_index("mod") == 0
     d_model = states.shape[3]
     own_low = states[0, 0]
-    other_low = swap(own_low)
     rows_each = w_query.shape[0]
     d_ff = w_up.shape[1]
-    page = lax.axis_index("page").astype(jnp.int32)[None]
+    half = d_model // 2
     fast = lax.axis_size("page") == 16 and rows_each % 16 == 0 and w_down.shape[0] % 16 == 0
+    place = jnp.stack([lax.axis_index("page"), lax.axis_index("mod")]).astype(jnp.int32)
     pack_qkv = jnp.concatenate([w_query, w_key, w_value], axis=1)
     pack_rest = jnp.concatenate([w_out, w_up], axis=1)
-    if fast:
-        full_qkv, column = gathered(pack_qkv, page)
-        pack_rest, column = lax.optimization_barrier((pack_rest, column))
-        full_rest, column = gathered(pack_rest, page)
-        w_down, column = lax.optimization_barrier((w_down, column))
-        full_down, column = gathered(w_down, page)
+    other_low = swap(own_low)
+    if fast:
+        column_qkv = column_of(half_columns(pack_qkv, is_text))
+        eight = jnp.concatenate([column_qkv, exchange(column_qkv, 2)])
+        far = swap(eight)
+        pieces = [eight, exchange(eight, 1), far, exchange(far, 1)]
+        column_rest = column_of(after(pack_rest, column_qkv))
+        column_down = column_of(after(w_down, column_rest))
+        pieces[0] = after(pieces[0], column_rest)
+        full_qkv = place_rows(place, pieces, pack_qkv.shape[1], place_halves_kernel)
     else:
         full_qkv = lax.all_gather(pack_qkv, "page", axis=0, tiled=True)
-        full_rest = lax.all_gather(pack_rest, "page", axis=0, tiled=True)
-        full_down = lax.all_gather(w_down, "page", axis=0, tiled=True)
     full_query = full_qkv[:, :d_model]
     full_kv = full_qkv[:, d_model:]
-    full_out = full_rest[:, :d_model]
-    full_up = full_rest[:, d_model:]
 
     page_ids, pos_bins, bins_x, bins_y = token_ids(segments[0], box_x[0], box_y[0])
     bounds = page_bounds(segments[0], is_text)
@@ -626,10 +673,26 @@
         [jnp.where(is_text, mixed_low, other_mixed), jnp.where(is_text, other_mixed, mixed_low)],
         axis=0,
     )
+    if fast:
+        full_qkv = after(full_qkv, mixed_all, features, tables, bounds, own_flip)
+        full_query = full_qkv[:, :d_model]
+        full_kv = full_qkv[:, d_model:]
     queries = ((plain_dot(mixed_low, full_query) + b_query).astype(bf16) * 0.125).astype(bf16)
     kv_bias = jnp.concatenate([jnp.zeros_like(b_value), b_value])
     keys_values = (plain_dot(mixed_all, full_kv) + kv_bias).astype(bf16)
     context = attend(bounds, queries, keys_values, features, own_feats, tables)
+    if fast:
+        column_down = after(column_down, context)
+        pieces_rest = list(pieces_of(column_rest))
+        pieces_rest[0] = after(pieces_rest[0], column_down)
+        full_rest = place_rows(place, pieces_rest, pack_rest.shape[1], place_kernel)
+        pieces_down = pieces_of(column_down)
+        full_down = place_rows(place, pieces_down, d_model, place_kernel)
+    else:
+        full_rest = lax.all_gather(pack_rest, "page", axis=0, tiled=True)
+        full_down = lax.all_gather(w_down, "page", axis=0, tiled=True)
+    full_out = full_rest[:, :d_model]
+    full_up = full_rest[:, d_model:]
 
     first_sum = mixed + plain_dot(context, full_out) + b_out
     normed, norm_one_pull = jax.vjp(layer_norm, first_sum, gain_one, bias_one)
@@ -642,48 +705,106 @@
     grad_out = cotangent[0, 0].astype(f32)
     grad_sum_two, grad_gain_two, grad_bias_two = norm_two_pull(grad_out)
     grad_ffn = grad_sum_two.astype(bf16)
-    if fast:
-        shard_down = scattered(*grad_by_rows(active_low, grad_ffn, page))
+    grad_b_down = column_sum(grad_ffn)
+    if fast:
+        keep_down, send_down = grad_by_rows(active_low, grad_ffn, place)
+        partner_down = exchange(send_down, 1)
+        grad_hidden_in = after(grad_ffn, keep_down, send_down)
     else:
         shard_down = summed_rows([(active_low, grad_ffn)])
-    grad_b_down = column_sum(grad_ffn)
-    (grad_hidden_f,) = gelu_pull(dot_right_t(grad_ffn, full_down))
+        grad_hidden_in = grad_ffn
+    (grad_hidden_f,) = gelu_pull(dot_right_t(grad_hidden_in, full_down))
     grad_hidden = grad_hidden_f.astype(bf16)
     grad_b_up = column_sum(grad_hidden)
-    grad_normed = grad_sum_two + dot_right_t(grad_hidden, full_up)
+    grad_up_in = grad_hidden
+    if fast:
+        partner_down = after(partner_down, grad_hidden)
+        across_out = across_send(keep_down, partner_down)
+        across_down = exchange(across_out, 2)
+        grad_up_in = after(grad_hidden, across_out)
+    grad_normed = grad_sum_two + dot_right_t(grad_up_in, full_up)
     grad_first, grad_gain_one, grad_bias_one = norm_one_pull(grad_normed)
     grad_branch = grad_first.astype(bf16)
     grad_b_out = column_sum(grad_branch)
     pairs = [(context, grad_branch), (normed_low, grad_hidden)]
-    if fast:
-        shard_rest = scattered(*grad_by_columns(pairs, page, d_model))
+    grad_context_in = grad_branch
+    if fast:
+        keep_rest, send_rest = grad_by_columns(pairs, place, d_model)
+        partner_rest = exchange(send_rest, 1)
+        grad_context_in = after(grad_branch, keep_rest, send_rest)
     else:
         shard_rest = summed_rows(pairs)
-    grad_context = dot_right_t(grad_branch, full_out).astype(bf16)
-    grad_queries, grad_keys, grad_values, grad_tables = attend_back(
-        bounds, queries, keys_values, grad_context, features, own_feats, own_flip, tables
-    )
-    pairs = [(mixed_low, grad_queries), (mixed_all, grad_keys), (mixed_all, grad_values)]
-    if fast:
-        shard_qkv = scattered(*grad_by_columns(pairs, page, d_model))
+    grad_context = dot_right_t(grad_context_in, full_out).astype(bf16)
+    back = functools.partial(attend_back, bounds, queries, keys_values)
+    rest = (features, own_feats, own_flip, tables)
+    grad_q1, grad_k1, grad_v1, grad_t1 = back(grad_context, *rest, 0, PAIRS // 2)
+    pairs = [(mixed_low, grad_q1), (mixed_all, grad_k1), (mixed_all, grad_v1)]
+    grad_context_in = grad_context
+    if fast:
+        keep_one, send_one = grad_by_columns(pairs, place, half)
+        partner_one = exchange(send_one, 1)
+        partner_rest = after(partner_rest, grad_q1)
+        both_rest = pair_sum(keep_rest, partner_rest, slice(0, 8))
+        plane_out = half_columns(both_rest, ~is_text).astype(bf16)
+        plane_rest = swap(plane_out)
+        across_down = after(across_down, grad_q1)
+        sends_down = column_sends(keep_down, partner_down, across_down)
+        column_in_down = [exchange(x, 4 * i) for i, x in enumerate(sends_down, 1)]
+        grad_context_in = after(grad_context, keep_one, send_one, plane_out, *sends_down)
     else:
-        shard_qkv = summed_rows(pairs)
-    grad_b_query = column_sum(grad_queries)
-    grad_b_value = column_sum(grad_values)
-    from_keys = dot_right_t(grad_keys, full_kv[:, :d_model]) + dot_right_t(
-        grad_values, full_kv[:, d_model:]
+        shard_one = summed_rows(pairs)
+    grad_q2, grad_k2, grad_v2, grad_t2 = back(grad_context_in, *rest, PAIRS // 2, PAIRS // 2)
+    pairs = [(mixed_low, grad_q2), (mixed_all, grad_k2), (mixed_all, grad_v2)]
+    if fast:
+        keep_two, send_two = grad_by_columns(pairs, place, half)
+        partner_two = exchange(send_two, 1)
+        partner_one = after(partner_one, send_two)
+        across_one_out = across_send(keep_one, partner_one)
+        across_one = exchange(across_one_out, 2)
+        plane_rest = after(plane_rest, send_two)
+        both_rest = half_columns(both_rest, is_text) + plane_rest.astype(f32)
+        across_rest_out = both_rest[4:].astype(bf16)
+        across_rest = exchange(across_rest_out, 2)
+        grad_keys_in = [
+            after(x, across_one_out, across_rest_out, send_two) for x in (grad_k1, grad_v1)
+        ]
+    else:
+        shard_two = summed_rows(pairs)
+        grad_keys_in = [grad_k1, grad_v1]
+    grad_b_query = jnp.concatenate([column_sum(grad_q1), column_sum(grad_q2)], axis=1)
+    grad_b_value = jnp.concatenate([column_sum(grad_v1), column_sum(grad_v2)], axis=1)
+    from_keys = (
+        dot_right_t(grad_keys_in[0], full_kv[:, :half])
+        + dot_right_t(grad_k2, full_kv[:, half:d_model])
+        + dot_right_t(grad_keys_in[1], full_kv[:, d_model : d_model + half])
+        + dot_right_t(grad_v2, full_kv[:, d_model + half :])
     )
     to_other = jnp.where(is_text, from_keys[TEXT:], from_keys[:TEXT]).astype(bf16)
-    from_other = swap(to_other).astype(f32)
+    from_other = swap(to_other)
+    from_queries = dot_right_t(grad_q1, full_query[:, :half]) + dot_right_t(
+        grad_q2, full_query[:, half:]
+    )
+    if fast:
+        column_in_down = [after(x, to_other) for x in column_in_down]
+        total_down = column_total(keep_down, partner_down, across_down, column_in_down)
+        shard_down = total_down.astype(f32) + swap(total_down).astype(f32)
+        partner_two = after(partner_two, to_other)
+        across_two_out = across_send(keep_two, partner_two)
+        across_two = exchange(across_two_out, 2)
+        sends_one = column_sends(keep_one, partner_one, across_one)
+        column_in_one = [exchange(x, 4 * i) for i, x in enumerate(sends_one, 1)]
+        sum_rest = both_rest[:4] + across_rest.astype(f32)
+        sends_rest = [sum_rest[step].astype(bf16) for step in (1, 2, 3)]
+        column_in_rest = [exchange(x, 4 * i) for i, x in enumerate(sends_rest, 1)]
     grad_mixed = (
         grad_first
-        + dot_right_t(grad_queries, full_query)
+        + from_queries
         + jnp.where(is_text, from_keys[:TEXT], from_keys[TEXT:])
-        + from_other
+        + from_other.astype(f32)
     )
     grad_in, grad_conv_w, grad_conv_b = mix_pull(grad_mixed)
 
-    table_rows = grad_tables[:, :3].reshape(6, 768)
+    table_rows = jnp.concatenate([grad_t1[:, :3], grad_t2[:, :3]]).reshape(6, 768)
     packed = jnp.concatenate(
         [
             grad_conv_w,
@@ -704,16 +825,39 @@
     )
     packed = sum_everywhere(packed)
     g_tables = packed[16:22].reshape(HEADS, 3, LANES)
-
+    if fast:
+        sends_two = column_sends(keep_two, partner_two, across_two)
+        column_in_two = [exchange(x, 4 * i) for i, x in enumerate(sends_two, 1)]
+        total_one = column_total(keep_one, partner_one, across_one, column_in_one)
+        shard_one = total_one.astype(f32) + swap(total_one).astype(f32)
+        total_rest = sum_rest[0]
+        for part in column_in_rest:
+            total_rest = total_rest + part.astype(f32)
+        low_rest = total_rest.astype(bf16)
+        far_rest = swap(low_rest)
+        shard_rest = jnp.where(
+            is_text,
+            jnp.concatenate([low_rest, far_rest], axis=1),
+            jnp.concatenate([far_rest, low_rest], axis=1),
+        ).astype(f32)
+        total_two = column_total(keep_two, partner_two, across_two, column_in_two)
+        shard_two = total_two.astype(f32) + swap(total_two).astype(f32)
+    shard_q, shard_k, shard_v = [
+        jnp.concatenate(
+            [shard_one[:, i * half : (i + 1) * half], shard_two[:, i * half : (i + 1) * half]],
+            axis=1,
+        )
+        for i in range(3)
+    ]
     return (
         output_row.astype(bf16)[None, None],
         grad_in.astype(bf16)[None, None],
         packed[0:3],
         packed[3],
-        shard_qkv[:, :d_model],
+        shard_q,
         packed[4],
-        shard_qkv[:, d_model : 2 * d_model],
-        shard_qkv[:, 2 * d_model :],
+        shard_k,
+        shard_v,
         packed[5],
         shard_rest[:, :d_model],
         packed[6],

time: 439 us -> 437 us (level)
  waiting for transfers between devices: 170 us -> 105 us
  local copies, waits for them, and re-layouts: 18.6 us -> 40.2 us
  other arithmetic: 45.7 us -> 59.4 us
  Pallas kernels: 83.8 us -> 96.1 us
  matrix products: 57.8 us -> 66.5 us
  starting transfers between devices: 55.5 us -> 62.4 us
    ppermute x33 -> x38, waiting for transfers between devices: 150 us -> 91.8 us  [exchange(): return lax.ppermute(values, 'page', [(i, i ^ mask) for i in range(count)])]
    ppermute x33 -> x38, starting transfers between devices: 43.3 us -> 53.1 us  [exchange(): return lax.ppermute(values, 'page', [(i, i ^ mask) for i in range(count)])]
    unnamed x108 -> x205, local copies, waits for them, and re-layouts: 10 us -> 18.9 us
    reduce_sum x4 -> x6, other arithmetic: 1.98 us -> 8.76 us  [column_sum(): return jnp.sum(values, axis=0, keepdims=True, dtype=f32)]
    pallas_call x2 -> x3, Pallas kernels: 17.6 us -> 24.3 us  [grad_by_columns(): pl.pallas_call(functools.partial(grad_columns_kernel, parts), grid_spec=p...]
    add x3 -> x5, other arithmetic: 1 us -> 6.9 us  [the longest x1 3.54 us: local(): both_rest = half_columns(both_rest, is_text) + plane_rest.astype(f32)]
    convert_element_type x9 -> x12, other arithmetic: 18 us -> 13 us  [the longest x3 4.24 us: column_sends(): (pair_sum(keep, partner, step) + across[step].astype(f32)).astype(bf16)]
    ppermute x4, waiting for transfers between devices: 12.9 us -> 8.44 us  [sum_everywhere(): lax.ppermute(values, 'page', [(i, i ^ step) for i in range(count)])]
  transfers between devices with their start and end apart: 43 -> 51, of which waited for: 20 -> 19; matrix products, arithmetic and copies ran while one was open for 14% -> 29% of each run, Pallas kernels for 9% -> 16%
where the time goes in v3:
time: 437 us; the launch traced here: 432 us
  waiting for transfers between devices  105 us (24%)
  Pallas kernels  96.1 us (22%)
  matrix products  66.5 us (15%)
  starting transfers between devices  62.4 us (14%)
  other arithmetic  59.4 us (14%)
  local copies, waits for them, and re-layouts  40.2 us (9%)
    ppermute x38, waiting for transfers between devices, exchange(): return lax.ppermute(values, 'page', [(i, i ^ mask) for i in range(count)])  91.8 us
    ppermute x38, starting transfers between devices, exchange(): return lax.ppermute(values, 'page', [(i, i ^ mask) for i in range(count)])  53.1 us
    dot_general x5, matrix products, plain_dot(): return jnp.dot(left_side, right_side, preferred_element_type=f32)  36.7 us
    pallas_call x2, Pallas kernels, attend_back(): pl.pallas_call(attend_back_kernel, grid_spec=pltpu.PrefetchScalarGridSpec...  32.6 us
    dot_general x9, matrix products, dot_right_t(): lax.dot_general(left_side, right_side, (((1,), (1,)), ((), ())), preferre...  29.8 us
    pallas_call x3, Pallas kernels, grad_by_columns(): pl.pallas_call(functools.partial(grad_columns_kernel, parts), grid_spec=p...  24.3 us
    unnamed x205, local copies, waits for them, and re-layouts  18.9 us
    pallas_call x3, Pallas kernels, place_rows(): pl.pallas_call(kernel, grid_spec=pltpu.PrefetchScalarGridSpec(num_scalar_...  16.2 us
  transfers between devices with their start and end apart: 51, of which 19 were waited for; matrix products, arithmetic and copies ran while one was open for 29% of the time, Pallas kernels for 16%

profile of v3, /device:TPU:0, one launch (start us, length us, event | category | flops | bytes accessed | tf_op | source)
XLA Modules:
  0.0 431.6 jit_solution(11783601422142643987)
XLA Ops:
  2.4 3.1 collective-permute-start
  5.5 2.6 collective-permute-start.1
  21.8 3.6 collective-permute-start.6
  28.2 7.1 %collective-permute-done.6 = bf16[48,3840]{1,0:T(8,128)(2,1)S(1)} collective-permute-done((bf16[48,3840]{1,0:T(8,128)(2,1)S(1)}, bf16[48,3840]{1,0:T(8,128)(2,1)S(1)}, u32[]{:S(2)}, u32[]{:S(2)}) %collective-permute-start.6) | collective-permute-done | bytes 368672 | tf_op jit(solution)/shard_map/ppermute | solution.py:350
  35.3 19.3 %collective-permute-done.5 = bf16[48,3840]{1,0:T(8,128)(2,1)S(1)} collective-permute-done((bf16[48,3840]{1,0:T(8,128)(2,1)S(1)}, bf16[48,3840]{1,0:T(8,128)(2,1)S(1)}, u32[]{:S(2)}, u32[]{:S(2)}) %collective-permute-start.5) | collective-permute-done | bytes 368672 | tf_op jit(solution)/shard_map/ppermute | solution.py:350
  56.4 2.5 collective-permute-start.13
  60.2 8.1 %collective-permute-done.13 = bf16[192,768]{1,0:T(8,128)(2,1)S(1)} collective-permute-done((bf16[192,768]{1,0:T(8,128)(2,1)S(1)}, bf16[192,768]{1,0:T(8,128)(2,1)S(1)}, u32[]{:S(2)}, u32[]{:S(2)}) %collective-permute-start.13) | collective-permute-done | bytes 294944 | tf_op jit(solution)/shard_map/ppermute | solution.py:350
  68.2 9.9 %collective-permute-start.11 = (bf16[192,768]{1,0:T(8,128)(2,1)S(1)}, bf16[192,768]{1,0:T(8,128)(2,1)S(1)}, u32[]{:S(2)}, u32[]{:S(2)}) collective-permute-start(bf16[192,768]{1,0:T(8,128)(2,1)S(1)} %copy-done.36), channel_id=1, source_target_pairs={{0,4},{1,5},{2,6},{3,7},{4,0},{5,1},{6,2},{7,3},{8,12},{9,13},{10,... | collective-permute-start | bytes 884744 | tf_op jit(solution)/shard_map/ppermute | solution.py:350
  78.4 2.5 collective-permute-done.12
  81.0 3.1 collective-permute-done.11
  86.4 3.4 broadcast_select_fusion.1
  92.8 4.8 %place_rows.3 = bf16[768,2304]{1,0:T(8,128)(2,1)} custom-call(s32[2]{0:T(128)} %pad_add_fusion.1.place.page, bf16[8,48,1152]{2,1,0:T(8,128)(2,1)} %copy-done.29, bf16[8,48,1152]{2,1,0:T(8,128)(2,1)} %copy-done.32, bf16[8,48,1152]{2,1,0:T(8,128)(2,1)} %copy-done.31, bf16[8,48,1152]{2,1,0:T(8,128)(2,1)} %collective-permute-done.9.refs_3_), custom_call_target="tpu_custom_call" | custom-call | bytes 7077888 | tf_op jit(solution)/shard_map/place_rows/pallas_call | solution.py:403
  97.6 3.4 fusion.21.q_ref
  100.9 5.1 %add_convert_fusion.1.k_ref.v_ref = bf16[1024,1536]{1,0:T(8,128)(2,1)} fusion(f32[1536]{0:T(1024)S(1)} %concatenate.103, bf16[768,2304]{1,0:T(8,128)(2,1)S(1)} %copy-done.1, bf16[512,768]{1,0:T(8,128)(2,1)} %copy-done.23, bf16[512,768]{1,0:T(8,128)(2,1)S(1)} %copy-done.22), kind=kOutput, calls=%fused_computation.17 | convolution fusion | flops 2422210560 | bytes 7086080 | tf_op jit(solution)/shard_map/dot_general | solution.py:84
  106.1 13.0 %attend.1.refs_0_ = bf16[512,768]{1,0:T(8,128)(2,1)} custom-call(s32[48]{0:T(128)} %concatenate.89.bounds, bf16[512,768]{1,0:T(8,128)(2,1)} %fusion.21.q_ref, bf16[1024,1536]{1,0:T(8,128)(2,1)} %add_convert_fusion.1.k_ref.v_ref, bf16[1024,1536]{1,0:T(8,128)(2,1)} %add_convert_fusion.1.k_ref.v_ref, bf16[1024,128]{1,0:T(8,128)(2,1)} %copy-done.30, ...), custom_call_target="tpu_custom_call" | custom-call | flops 4000000000 | bytes 6000000 | tf_op jit(solution)/shard_map/attend/pallas_call | solution.py:272
  120.9 6.1 %place_rows.4 = bf16[768,3840]{1,0:T(8,128)(2,1)} custom-call(s32[2]{0:T(128)} %pad_add_fusion.1.place.page, bf16[4,48,3840]{2,1,0:T(8,128)(2,1)} %pad_maximum_fusion.1.refs_0_, bf16[4,48,3840]{2,1,0:T(8,128)(2,1)} %collective-permute-done.14.refs_1_, bf16[4,48,3840]{2,1,0:T(8,128)(2,1)} %collective-permute-done.15.refs_2_, ...), custom_call_target="tpu_custom_call" | custom-call | bytes 11796480 | tf_op jit(solution)/shard_map/place_rows/pallas_call | solution.py:403
  127.0 3.0 fusion.86
  131.2 16.5 %collective-permute-done.18.refs_2_ = bf16[4,192,768]{2,1,0:T(8,128)(2,1)} collective-permute-done((bf16[4,192,768]{2,1,0:T(8,128)(2,1)}, bf16[4,192,768]{2,1,0:T(8,128)(2,1)}, u32[]{:S(2)}, u32[]{:S(2)}) %collective-permute-start.18) | collective-permute-done | bytes 1179680 | tf_op jit(solution)/shard_map/ppermute | solution.py:350
  147.7 18.7 %multiply_convert_fusion = (bf16[512,3072]{1,0:T(8,128)(2,1)}, f32[512,3072]{1,0:T(8,128)}, f32[512,3072]{1,0:T(8,128)}) fusion(f32[3072]{0:T(1024)S(1)} %copy-done.94, bf16[512,768]{1,0:T(8,128)(2,1)S(1)} %fusion.22.refs_2_, bf16[768,3840]{1,0:T(8,128)(2,1)S(1)} %copy-done.19), kind=kOutput, calls=%fused_computation.4 | convolution fusion | flops 2519728128 | bytes 21245952 | tf_op jit(solution)/shard_map/dot_general | solution.py:84
  166.5 5.4 %place_rows.5 = bf16[3072,768]{1,0:T(8,128)(2,1)} custom-call(s32[2]{0:T(128)} %pad_add_fusion.1.place.page, bf16[4,192,768]{2,1,0:T(8,128)(2,1)} %pad_maximum_fusion.2.refs_0_, bf16[4,192,768]{2,1,0:T(8,128)(2,1)} %collective-permute-done.17.refs_1_, bf16[4,192,768]{2,1,0:T(8,128)(2,1)} %collective-permute-done.18.refs_2_, ...), custom_call_target="tpu_custom_call" | custom-call | bytes 9437184 | tf_op jit(solution)/shard_map/place_rows/pallas_call | solution.py:403
  171.9 6.5 %fusion.87 = (f32[512]{0:T(512)S(1)}, f32[512,768]{1,0:T(8,128)S(1)}) fusion(f32[768]{0:T(1024)} %param.47, bf16[512,3072]{1,0:T(8,128)(2,1)} %get-tuple-element.131.x_ref, bf16[3072,768]{1,0:T(8,128)(2,1)} %place_rows.5, f32[768]{0:T(1024)} %param.43, f32[768]{0:T(1024)S(1)} %copy-done.58, f32[512]{0:T(512)S(1)} %fusion.71, f32[512,768]{1,0:T(8,128)} %copy-done.6, ...), kind=kOutput, calls=%fused_computation.274 | convolution fusion | flops 2418671104 | bytes 11025408 | tf_op jit(solution)/shard_map/dot_general | solution.py:84
  185.3 10.0 %grad_rows.1 = (bf16[8,192,768]{2,1,0:T(8,128)(2,1)}, bf16[8,192,768]{2,1,0:T(8,128)(2,1)}) custom-call(s32[2]{0:T(128)} %pad_add_fusion.1.place.page, bf16[512,3072]{1,0:T(8,128)(2,1)} %get-tuple-element.131.x_ref, bf16[512,768]{1,0:T(8,128)(2,1)} %get-tuple-element.67.h_ref), custom_call_target="tpu_custom_call" | custom-call | flops 2415919104 | bytes 8650752 | tf_op jit(solution)/shard_map/grad_rows/pallas_call | solution.py:448
  195.8 11.3 %convert_reduce_fusion = (f32[3072]{0:T(1024)}, bf16[512,3072]{1,0:T(8,128)(2,1)S(1)}) fusion(f32[512,3072]{1,0:T(8,128)} %get-tuple-element.132, f32[512,3072]{1,0:T(8,128)} %get-tuple-element.182, f32[3072]{0:T(1024)} %param.45, bf16[512,768]{1,0:T(8,128)(2,1)} %get-tuple-element.67.h_ref, bf16[3072,768]{1,0:T(8,128)(2,1)} %place_rows.5), kind=kOutput, calls=%fused_computation.2 | convolution fusion | flops 2442654720 | bytes 21258240 | tf_op jit(solution)/shard_map/dot_general | solution.py:94
  211.4 6.1 %multiply_reduce_fusion = (f32[768]{0:T(1024)}, f32[512]{0:T(512)S(1)}, f32[768]{0:T(1024)}, f32[512,768]{1,0:T(8,128)S(1)}) fusion(f32[512,768]{1,0:T(8,128)S(1)} %copy-done.7, f32[512]{0:T(512)S(1)} %fusion.71, f32[512]{0:T(512)S(1)} %broadcast_multiply_fusion.1, f32[768]{0:T(1024)S(1)} %copy-done.58, ...), kind=kOutput, calls=%fused_computation.45 | convolution fusion | flops 2419849216 | bytes 12600320 | tf_op jit(solution)/shard_map/dot_general | solution.py:94
  221.0 9.8 %grad_columns.3 = (bf16[8,48,3840]{2,1,0:T(8,128)(2,1)}, bf16[8,48,3840]{2,1,0:T(8,128)(2,1)}) custom-call(s32[2]{0:T(128)} %pad_add_fusion.1.place.page, bf16[512,768]{1,0:T(8,128)(2,1)} %attend.1.refs_0_, bf16[512,768]{1,0:T(8,128)(2,1)} %get-tuple-element.72.refs_1_, bf16[512,768]{1,0:T(8,128)(2,1)} %copy-done.35, bf16[512,3072]{1,0:T(8,128)(2,1)} %copy-done.97), custom_call_target="tpu_custom_call" | custom-call | flops 3019898880 | bytes 11796480 | tf_op jit(solution)/shard_map/grad_columns/pallas_call | solution.py:511
  236.7 3.2 convolution_convert_fusion.grad_ref
  239.9 16.5 %attend_back.2 = (bf16[512,384]{1,0:T(8,128)(2,1)}, bf16[1024,384]{1,0:T(8,128)(2,1)}, bf16[1024,384]{1,0:T(8,128)(2,1)}, f32[6,8,128]{2,1,0:T(8,128)}) custom-call(s32[48]{0:T(128)} %concatenate.89.bounds, bf16[512,768]{1,0:T(8,128)(2,1)} %fusion.21.q_ref, bf16[1024,1536]{1,0:T(8,128)(2,1)} %add_convert_fusion.1.k_ref.v_ref, ...), custom_call_target="tpu_custom_call" | custom-call | flops 12000000000 | bytes 4500000 | tf_op jit(solution)/shard_map/attend_back/pallas_call | solution.py:299
  256.4 7.2 %grad_columns.4 = (bf16[8,48,1152]{2,1,0:T(8,128)(2,1)}, bf16[8,48,1152]{2,1,0:T(8,128)(2,1)}) custom-call(s32[2]{0:T(128)} %pad_add_fusion.1.place.page, bf16[512,768]{1,0:T(8,128)(2,1)} %copy-done.10, bf16[512,384]{1,0:T(8,128)(2,1)} %get-tuple-element.73.refs_1_, bf16[1024,768]{1,0:T(8,128)(2,1)} %pad_maximum_fusion.refs_2_.refs_4_, ...), custom_call_target="tpu_custom_call" | custom-call | flops 1509949440 | bytes 3538944 | tf_op jit(solution)/shard_map/grad_columns/pallas_call | solution.py:511
  272.5 2.7 fusion.39
  275.2 3.0 fusion.48
  279.9 2.4 convert_add_fusion
  282.4 2.6 copy-done
  286.9 16.1 %attend_back.3 = (bf16[512,384]{1,0:T(8,128)(2,1)}, bf16[1024,384]{1,0:T(8,128)(2,1)}, bf16[1024,384]{1,0:T(8,128)(2,1)}, f32[6,8,128]{2,1,0:T(8,128)}) custom-call(s32[48]{0:T(128)} %concatenate.89.bounds, bf16[512,768]{1,0:T(8,128)(2,1)} %fusion.21.q_ref, bf16[1024,1536]{1,0:T(8,128)(2,1)} %add_convert_fusion.1.k_ref.v_ref, ...), custom_call_target="tpu_custom_call" | custom-call | flops 12000000000 | bytes 4500000 | tf_op jit(solution)/shard_map/attend_back/pallas_call | solution.py:299
  304.7 7.4 %grad_columns.5 = (bf16[8,48,1152]{2,1,0:T(8,128)(2,1)}, bf16[8,48,1152]{2,1,0:T(8,128)(2,1)}) custom-call(s32[2]{0:T(128)} %pad_add_fusion.1.place.page, bf16[512,768]{1,0:T(8,128)(2,1)} %copy-done.10, bf16[512,384]{1,0:T(8,128)(2,1)} %get-tuple-element.81.refs_1_, bf16[1024,768]{1,0:T(8,128)(2,1)} %pad_maximum_fusion.refs_2_.refs_4_, ...), custom_call_target="tpu_custom_call" | custom-call | flops 1509949440 | bytes 3538944 | tf_op jit(solution)/shard_map/grad_columns/pallas_call | solution.py:511
  320.4 2.3 fusion.34
  322.7 7.8 %collective-permute-done.31 = bf16[4,48,1152]{2,1,0:T(8,128)(2,1)S(1)} collective-permute-done((bf16[4,48,1152]{2,1,0:T(8,128)(2,1)}, bf16[4,48,1152]{2,1,0:T(8,128)(2,1)S(1)}, u32[]{:S(2)}, u32[]{:S(2)}) %collective-permute-start.31) | collective-permute-done | bytes 442400 | tf_op jit(solution)/shard_map/ppermute | solution.py:350
  333.8 2.3 collective-permute-start.32
  336.7 2.8 collective-permute-done.34
  339.5 4.5 %collective-permute-start.48 = (bf16[192,768]{1,0:T(8,128)(2,1)S(1)}, bf16[192,768]{1,0:T(8,128)(2,1)S(1)}, u32[]{:S(2)}, u32[]{:S(2)}) collective-permute-start(bf16[192,768]{1,0:T(8,128)(2,1)S(1)} %copy-done.38), channel_id=1, source_target_pairs={{0,8},{1,9},{2,10},{3,11},{4,12},{5,13},{6,14},{7,15},{8,0},{9,1},... | collective-permute-start | bytes 884744 | tf_op jit(solution)/shard_map/ppermute | solution.py:350
  344.0 3.1 collective-permute-done.33
  349.8 3.5 convert_add_fusion.1
  362.5 9.8 %collective-permute-done.37 = bf16[4,48,1152]{2,1,0:T(8,128)(2,1)S(1)} collective-permute-done((bf16[4,48,1152]{2,1,0:T(8,128)(2,1)S(1)}, bf16[4,48,1152]{2,1,0:T(8,128)(2,1)S(1)}, u32[]{:S(2)}, u32[]{:S(2)}) %collective-permute-start.37) | collective-permute-done | bytes 442400 | tf_op jit(solution)/shard_map/ppermute | solution.py:350
  380.7 3.9 collective-permute-done.39
  394.5 2.7 collective-permute-start.44
  401.0 2.4 fusion.73
  405.5 5.9 %collective-permute-done.44 = bf16[48,1920]{1,0:T(8,128)(2,1)} collective-permute-done((bf16[48,1920]{1,0:T(8,128)(2,1)}, bf16[48,1920]{1,0:T(8,128)(2,1)}, u32[]{:S(2)}, u32[]{:S(2)}) %collective-permute-start.44) | collective-permute-done | bytes 184352 | tf_op jit(solution)/shard_map/ppermute | solution.py:350
  414.0 3.6 collective-permute-done.28
  419.0 4.2 collective-permute-done.29
  (419 shorter events, 124.7 us)
Async XLA Ops:
  2.4 17.8 %collective-permute-start = (bf16[48,1152]{1,0:T(8,128)(2,1)S(1)}, bf16[48,1152]{1,0:T(8,128)(2,1)S(1)}, u32[]{:S(2)}, u32[]{:S(2)}) collective-permute-start(bf16[48,1152]{1,0:T(8,128)(2,1)S(1)} %get-tuple-element.138), channel_id=1, source_target_pairs={{0,4},{1,5},{2,6},{3,7},{4,0},{5,1},{6,2},{7,3},{8,12},{9,13},{10,... | collective-permute-start | bytes 331784 | tf_op jit(solution)/shard_map/ppermute | solution.py:350
  5.5 14.7 %collective-permute-start.1 = (bf16[48,1152]{1,0:T(8,128)(2,1)S(1)}, bf16[48,1152]{1,0:T(8,128)(2,1)S(1)}, u32[]{:S(2)}, u32[]{:S(2)}) collective-permute-start(bf16[48,1152]{1,0:T(8,128)(2,1)S(1)} %get-tuple-element.138), channel_id=1, source_target_pairs={{0,8},{1,9},{2,10},{3,11},{4,12},{5,13},{6,14},{7,15},{8,0},{9,1},... | collective-permute-start | bytes 331784 | tf_op jit(solution)/shard_map/ppermute | solution.py:350
  8.0 12.1 %collective-permute-start.2 = (bf16[48,1152]{1,0:T(8,128)(2,1)S(1)}, bf16[48,1152]{1,0:T(8,128)(2,1)S(1)}, u32[]{:S(2)}, u32[]{:S(2)}) collective-permute-start(bf16[48,1152]{1,0:T(8,128)(2,1)S(1)} %get-tuple-element.138), channel_id=1, source_target_pairs={{0,12},{1,13},{2,14},{3,15},{4,8},{5,9},{6,10},{7,11},{8,4},{9,5},... | collective-permute-start | bytes 331784 | tf_op jit(solution)/shard_map/ppermute | solution.py:350
  8.0 77.2 %collective-permute-start.10 = (bf16[512,768]{1,0:T(8,128)(2,1)}, bf16[512,768]{1,0:T(8,128)(2,1)S(1)}, u32[]{:S(2)}, u32[]{:S(2)}) collective-permute-start(bf16[512,768]{1,0:T(8,128)(2,1)} %bitcast.137), channel_id=1, source_target_pairs={{0,16},{16,0},{1,17},{17,1},{2,18},{18,2},{3,19},{19,3},{4,20},{20... | collective-permute-start | bytes 2359304 | tf_op jit(solution)/shard_map/ppermute | solution.py:587
  20.2 38.7 %collective-permute-start.3 = (bf16[4,48,1152]{2,1,0:T(8,128)(2,1)S(1)}, bf16[4,48,1152]{2,1,0:T(8,128)(2,1)S(1)}, u32[]{:S(2)}, u32[]{:S(2)}) collective-permute-start(bf16[4,48,1152]{2,1,0:T(8,128)(2,1)S(1)} %pad_maximum_fusion.3), channel_id=1, source_target_pairs={{0,2},{1,3},{2,0},{3,1},{4,6},{5,7},{6,4},{7,5},{8,10},{9,11},{10,... | collective-permute-start | bytes 1327112 | tf_op jit(solution)/shard_map/ppermute | solution.py:350
  21.8 13.4 %collective-permute-start.6 = (bf16[48,3840]{1,0:T(8,128)(2,1)S(1)}, bf16[48,3840]{1,0:T(8,128)(2,1)S(1)}, u32[]{:S(2)}, u32[]{:S(2)}) collective-permute-start(bf16[48,3840]{1,0:T(8,128)(2,1)S(1)} %pad_maximum_fusion.4), channel_id=1, source_target_pairs={{0,12},{1,13},{2,14},{3,15},{4,8},{5,9},{6,10},{7,11},{8,4},{9,5},... | collective-permute-start | bytes 1105928 | tf_op jit(solution)/shard_map/ppermute | solution.py:350
  25.4 29.1 %collective-permute-start.5 = (bf16[48,3840]{1,0:T(8,128)(2,1)S(1)}, bf16[48,3840]{1,0:T(8,128)(2,1)S(1)}, u32[]{:S(2)}, u32[]{:S(2)}) collective-permute-start(bf16[48,3840]{1,0:T(8,128)(2,1)S(1)} %pad_maximum_fusion.4), channel_id=1, source_target_pairs={{0,8},{1,9},{2,10},{3,11},{4,12},{5,13},{6,14},{7,15},{8,0},{9,1},... | collective-permute-start | bytes 1105928 | tf_op jit(solution)/shard_map/ppermute | solution.py:350
  25.4 29.1 %collective-permute-start.4 = (bf16[48,3840]{1,0:T(8,128)(2,1)S(1)}, bf16[48,3840]{1,0:T(8,128)(2,1)S(1)}, u32[]{:S(2)}, u32[]{:S(2)}) collective-permute-start(bf16[48,3840]{1,0:T(8,128)(2,1)S(1)} %pad_maximum_fusion.4), channel_id=1, source_target_pairs={{0,4},{1,5},{2,6},{3,7},{4,0},{5,1},{6,2},{7,3},{8,12},{9,13},{10,... | collective-permute-start | bytes 1105928 | tf_op jit(solution)/shard_map/ppermute | solution.py:350
  55.9 33.8 %collective-permute-start.15 = (bf16[4,48,3840]{2,1,0:T(8,128)(2,1)}, bf16[4,48,3840]{2,1,0:T(8,128)(2,1)}, u32[]{:S(2)}, u32[]{:S(2)}) collective-permute-start(bf16[4,48,3840]{2,1,0:T(8,128)(2,1)} %pad_maximum_fusion.1.refs_0_), channel_id=1, source_target_pairs={{0,2},{1,3},{2,0},{3,1},{4,6},{5,7},{6,4},{7,5},{8,10},{9,11},{10,... | collective-permute-start | bytes 4423688 | tf_op jit(solution)/shard_map/ppermute | solution.py:350
  56.4 11.8 %collective-permute-start.13 = (bf16[192,768]{1,0:T(8,128)(2,1)S(1)}, bf16[192,768]{1,0:T(8,128)(2,1)S(1)}, u32[]{:S(2)}, u32[]{:S(2)}) collective-permute-start(bf16[192,768]{1,0:T(8,128)(2,1)S(1)} %copy-done.36), channel_id=1, source_target_pairs={{0,12},{1,13},{2,14},{3,15},{4,8},{5,9},{6,10},{7,11},{8,4},{9,5},... | collective-permute-start | bytes 884744 | tf_op jit(solution)/shard_map/ppermute | solution.py:350
  59.0 26.5 %collective-permute-start.8 = (bf16[8,48,1152]{2,1,0:T(8,128)(2,1)S(1)}, bf16[8,48,1152]{2,1,0:T(8,128)(2,1)S(1)}, u32[]{:S(2)}, u32[]{:S(2)}) collective-permute-start(bf16[8,48,1152]{2,1,0:T(8,128)(2,1)S(1)} %constant_dynamic-update-slice_fusion.refs_0_), channel_id=1, source_target_pairs={{0,16},{16,0},{1,17},{17,1},{2,18},{18,2},{3,19},{19,3},{4,20},{20... | collective-permute-start | bytes 2654216 | tf_op jit(solution)/shard_map/ppermute | solution.py:587
  60.2 20.8 %collective-permute-start.12 = (bf16[192,768]{1,0:T(8,128)(2,1)S(1)}, bf16[192,768]{1,0:T(8,128)(2,1)S(1)}, u32[]{:S(2)}, u32[]{:S(2)}) collective-permute-start(bf16[192,768]{1,0:T(8,128)(2,1)S(1)} %copy-done.36), channel_id=1, source_target_pairs={{0,8},{1,9},{2,10},{3,11},{4,12},{5,13},{6,14},{7,15},{8,0},{9,1},... | collective-permute-start | bytes 884744 | tf_op jit(solution)/shard_map/ppermute | solution.py:350
  68.2 15.8 %collective-permute-start.11 = (bf16[192,768]{1,0:T(8,128)(2,1)S(1)}, bf16[192,768]{1,0:T(8,128)(2,1)S(1)}, u32[]{:S(2)}, u32[]{:S(2)}) collective-permute-start(bf16[192,768]{1,0:T(8,128)(2,1)S(1)} %copy-done.36), channel_id=1, source_target_pairs={{0,4},{1,5},{2,6},{3,7},{4,0},{5,1},{6,2},{7,3},{8,12},{9,13},{10,... | collective-permute-start | bytes 884744 | tf_op jit(solution)/shard_map/ppermute | solution.py:350
  81.0 39.9 %collective-permute-start.14 = (bf16[4,48,3840]{2,1,0:T(8,128)(2,1)}, bf16[4,48,3840]{2,1,0:T(8,128)(2,1)}, u32[]{:S(2)}, u32[]{:S(2)}) collective-permute-start(bf16[4,48,3840]{2,1,0:T(8,128)(2,1)} %pad_maximum_fusion.1.refs_0_), channel_id=1, source_target_pairs={{0,1},{1,0},{2,3},{3,2},{4,5},{5,4},{6,7},{7,6},{8,9},{9,8},{10,11... | collective-permute-start | bytes 4423688 | tf_op jit(solution)/shard_map/ppermute | solution.py:350
  84.0 7.8 %collective-permute-start.7 = (bf16[8,48,1152]{2,1,0:T(8,128)(2,1)S(1)}, bf16[8,48,1152]{2,1,0:T(8,128)(2,1)S(1)}, u32[]{:S(2)}, u32[]{:S(2)}) collective-permute-start(bf16[8,48,1152]{2,1,0:T(8,128)(2,1)S(1)} %constant_dynamic-update-slice_fusion.refs_0_), channel_id=1, source_target_pairs={{0,1},{1,0},{2,3},{3,2},{4,5},{5,4},{6,7},{7,6},{8,9},{9,8},{10,11... | collective-permute-start | bytes 2654216 | tf_op jit(solution)/shard_map/ppermute | solution.py:350
  85.5 6.4 %collective-permute-start.9 = (bf16[8,48,1152]{2,1,0:T(8,128)(2,1)S(1)}, bf16[8,48,1152]{2,1,0:T(8,128)(2,1)}, u32[]{:S(2)}, u32[]{:S(2)}) collective-permute-start(bf16[8,48,1152]{2,1,0:T(8,128)(2,1)S(1)} %collective-permute-done.8.refs_2_), channel_id=1, source_target_pairs={{0,1},{1,0},{2,3},{3,2},{4,5},{5,4},{6,7},{7,6},{8,9},{9,8},{10,11... | collective-permute-start | bytes 2654216 | tf_op jit(solution)/shard_map/ppermute | solution.py:350
  89.8 31.1 %collective-permute-start.16 = (bf16[4,48,3840]{2,1,0:T(8,128)(2,1)}, bf16[4,48,3840]{2,1,0:T(8,128)(2,1)}, u32[]{:S(2)}, u32[]{:S(2)}) collective-permute-start(bf16[4,48,3840]{2,1,0:T(8,128)(2,1)} %collective-permute-done.15.refs_2_), channel_id=1, source_target_pairs={{0,1},{1,0},{2,3},{3,2},{4,5},{5,4},{6,7},{7,6},{8,9},{9,8},{10,11... | collective-permute-start | bytes 4423688 | tf_op jit(solution)/shard_map/ppermute | solution.py:350
  119.0 47.5 %collective-permute-start.17 = (bf16[4,192,768]{2,1,0:T(8,128)(2,1)}, bf16[4,192,768]{2,1,0:T(8,128)(2,1)}, u32[]{:S(2)}, u32[]{:S(2)}) collective-permute-start(bf16[4,192,768]{2,1,0:T(8,128)(2,1)} %pad_maximum_fusion.2.refs_0_), channel_id=1, source_target_pairs={{0,1},{1,0},{2,3},{3,2},{4,5},{5,4},{6,7},{7,6},{8,9},{9,8},{10,11... | collective-permute-start | bytes 3538952 | tf_op jit(solution)/shard_map/ppermute | solution.py:350
  119.3 28.4 %collective-permute-start.18 = (bf16[4,192,768]{2,1,0:T(8,128)(2,1)}, bf16[4,192,768]{2,1,0:T(8,128)(2,1)}, u32[]{:S(2)}, u32[]{:S(2)}) collective-permute-start(bf16[4,192,768]{2,1,0:T(8,128)(2,1)} %pad_maximum_fusion.2.refs_0_), channel_id=1, source_target_pairs={{0,2},{1,3},{2,0},{3,1},{4,6},{5,7},{6,4},{7,5},{8,10},{9,11},{10,... | collective-permute-start | bytes 3538952 | tf_op jit(solution)/shard_map/ppermute | solution.py:350
  147.7 18.8 %collective-permute-start.19 = (bf16[4,192,768]{2,1,0:T(8,128)(2,1)}, bf16[4,192,768]{2,1,0:T(8,128)(2,1)}, u32[]{:S(2)}, u32[]{:S(2)}) collective-permute-start(bf16[4,192,768]{2,1,0:T(8,128)(2,1)} %collective-permute-done.18.refs_2_), channel_id=1, source_target_pairs={{0,1},{1,0},{2,3},{3,2},{4,5},{5,4},{6,7},{7,6},{8,9},{9,8},{10,11... | collective-permute-start | bytes 3538952 | tf_op jit(solution)/shard_map/ppermute | solution.py:350
  195.3 11.8 %collective-permute-start.20 = (bf16[8,192,768]{2,1,0:T(8,128)(2,1)}, bf16[8,192,768]{2,1,0:T(8,128)(2,1)S(1)}, u32[]{:S(2)}, u32[]{:S(2)}) collective-permute-start(bf16[8,192,768]{2,1,0:T(8,128)(2,1)} %get-tuple-element.66), channel_id=1, source_target_pairs={{0,1},{1,0},{2,3},{3,2},{4,5},{5,4},{6,7},{7,6},{8,9},{9,8},{10,11... | collective-permute-start | bytes 7077896 | tf_op jit(solution)/shard_map/ppermute | solution.py:350
  230.7 49.2 %collective-permute-start.21 = (bf16[8,48,3840]{2,1,0:T(8,128)(2,1)}, bf16[8,48,3840]{2,1,0:T(8,128)(2,1)}, u32[]{:S(2)}, u32[]{:S(2)}) collective-permute-start(bf16[8,48,3840]{2,1,0:T(8,128)(2,1)} %get-tuple-element.71), channel_id=1, source_target_pairs={{0,1},{1,0},{2,3},{3,2},{4,5},{5,4},{6,7},{7,6},{8,9},{9,8},{10,11... | collective-permute-start | bytes 8847368 | tf_op jit(solution)/shard_map/ppermute | solution.py:350
  235.2 40.1 %collective-permute-start.22 = (bf16[4,192,768]{2,1,0:T(8,128)(2,1)}, bf16[4,192,768]{2,1,0:T(8,128)(2,1)}, u32[]{:S(2)}, u32[]{:S(2)}) collective-permute-start(bf16[4,192,768]{2,1,0:T(8,128)(2,1)} %add_convert_fusion.2), channel_id=1, source_target_pairs={{0,2},{1,3},{2,0},{3,1},{4,6},{5,7},{6,4},{7,5},{8,10},{9,11},{10,... | collective-permute-start | bytes 3538952 | tf_op jit(solution)/shard_map/ppermute | solution.py:350
  263.6 49.8 %collective-permute-start.23 = (bf16[8,48,1152]{2,1,0:T(8,128)(2,1)}, bf16[8,48,1152]{2,1,0:T(8,128)(2,1)}, u32[]{:S(2)}, u32[]{:S(2)}) collective-permute-start(bf16[8,48,1152]{2,1,0:T(8,128)(2,1)} %get-tuple-element.77), channel_id=1, source_target_pairs={{0,1},{1,0},{2,3},{3,2},{4,5},{5,4},{6,7},{7,6},{8,9},{9,8},{10,11... | collective-permute-start | bytes 2654216 | tf_op jit(solution)/shard_map/ppermute | solution.py:350
  278.2 82.7 %collective-permute-start.49 = (bf16[192,768]{1,0:T(8,128)(2,1)}, bf16[192,768]{1,0:T(8,128)(2,1)}, u32[]{:S(2)}, u32[]{:S(2)}) collective-permute-start(bf16[192,768]{1,0:T(8,128)(2,1)} %get-tuple-element.141), channel_id=1, source_target_pairs={{0,12},{1,13},{2,14},{3,15},{4,8},{5,9},{6,10},{7,11},{8,4},{9,5},... | collective-permute-start | bytes 884744 | tf_op jit(solution)/shard_map/ppermute | solution.py:350
  286.4 61.8 %collective-permute-start.24 = (bf16[8,48,1920]{2,1,0:T(8,128)(2,1)}, bf16[8,48,1920]{2,1,0:T(8,128)(2,1)}, u32[]{:S(2)}, u32[]{:S(2)}) collective-permute-start(bf16[8,48,1920]{2,1,0:T(8,128)(2,1)} %select_convert_fusion), channel_id=1, source_target_pairs={{0,16},{16,0},{1,17},{17,1},{2,18},{18,2},{3,19},{19,3},{4,20},{20... | collective-permute-start | bytes 4423688 | tf_op jit(solution)/shard_map/ppermute | solution.py:587
  318.5 12.0 %collective-permute-start.31 = (bf16[4,48,1152]{2,1,0:T(8,128)(2,1)}, bf16[4,48,1152]{2,1,0:T(8,128)(2,1)S(1)}, u32[]{:S(2)}, u32[]{:S(2)}) collective-permute-start(bf16[4,48,1152]{2,1,0:T(8,128)(2,1)} %add_convert_fusion.10), channel_id=1, source_target_pairs={{0,2},{1,3},{2,0},{3,1},{4,6},{5,7},{6,4},{7,5},{8,10},{9,11},{10,... | collective-permute-start | bytes 1327112 | tf_op jit(solution)/shard_map/ppermute | solution.py:350
  331.7 7.9 %collective-permute-start.34 = (bf16[48,1152]{1,0:T(8,128)(2,1)S(1)}, bf16[48,1152]{1,0:T(8,128)(2,1)S(1)}, u32[]{:S(2)}, u32[]{:S(2)}) collective-permute-start(bf16[48,1152]{1,0:T(8,128)(2,1)S(1)} %get-tuple-element.145), channel_id=1, source_target_pairs={{0,12},{1,13},{2,14},{3,15},{4,8},{5,9},{6,10},{7,11},{8,4},{9,5},... | collective-permute-start | bytes 331784 | tf_op jit(solution)/shard_map/ppermute | solution.py:350
  333.8 13.3 %collective-permute-start.33 = (bf16[48,1152]{1,0:T(8,128)(2,1)S(1)}, bf16[48,1152]{1,0:T(8,128)(2,1)S(1)}, u32[]{:S(2)}, u32[]{:S(2)}) collective-permute-start(bf16[48,1152]{1,0:T(8,128)(2,1)S(1)} %get-tuple-element.146), channel_id=1, source_target_pairs={{0,8},{1,9},{2,10},{3,11},{4,12},{5,13},{6,14},{7,15},{8,0},{9,1},... | collective-permute-start | bytes 331784 | tf_op jit(solution)/shard_map/ppermute | solution.py:350
  333.8 13.3 %collective-permute-start.32 = (bf16[48,1152]{1,0:T(8,128)(2,1)S(1)}, bf16[48,1152]{1,0:T(8,128)(2,1)S(1)}, u32[]{:S(2)}, u32[]{:S(2)}) collective-permute-start(bf16[48,1152]{1,0:T(8,128)(2,1)S(1)} %get-tuple-element.144), channel_id=1, source_target_pairs={{0,4},{1,5},{2,6},{3,7},{4,0},{5,1},{6,2},{7,3},{8,12},{9,13},{10,... | collective-permute-start | bytes 331784 | tf_op jit(solution)/shard_map/ppermute | solution.py:350
  339.5 23.0 %collective-permute-start.48 = (bf16[192,768]{1,0:T(8,128)(2,1)S(1)}, bf16[192,768]{1,0:T(8,128)(2,1)S(1)}, u32[]{:S(2)}, u32[]{:S(2)}) collective-permute-start(bf16[192,768]{1,0:T(8,128)(2,1)S(1)} %copy-done.38), channel_id=1, source_target_pairs={{0,8},{1,9},{2,10},{3,11},{4,12},{5,13},{6,14},{7,15},{8,0},{9,1},... | collective-permute-start | bytes 884744 | tf_op jit(solution)/shard_map/ppermute | solution.py:350
  347.1 15.4 %collective-permute-start.47 = (bf16[192,768]{1,0:T(8,128)(2,1)S(1)}, bf16[192,768]{1,0:T(8,128)(2,1)S(1)}, u32[]{:S(2)}, u32[]{:S(2)}) collective-permute-start(bf16[192,768]{1,0:T(8,128)(2,1)S(1)} %copy-done.37), channel_id=1, source_target_pairs={{0,4},{1,5},{2,6},{3,7},{4,0},{5,1},{6,2},{7,3},{8,12},{9,13},{10,... | collective-permute-start | bytes 884744 | tf_op jit(solution)/shard_map/ppermute | solution.py:350
  347.1 11.0 %collective-permute-start.36 = (bf16[8,48,1152]{2,1,0:T(8,128)(2,1)S(1)}, bf16[8,48,1152]{2,1,0:T(8,128)(2,1)S(1)}, u32[]{:S(2)}, u32[]{:S(2)}) collective-permute-start(bf16[8,48,1152]{2,1,0:T(8,128)(2,1)S(1)} %copy-done.93), channel_id=1, source_target_pairs={{0,1},{1,0},{2,3},{3,2},{4,5},{5,4},{6,7},{7,6},{8,9},{9,8},{10,11... | collective-permute-start | bytes 2654216 | tf_op jit(solution)/shard_map/ppermute | solution.py:350
  348.2 11.5 %collective-permute-start.35 = (bf16[48,1152]{1,0:T(8,128)(2,1)S(1)}, bf16[48,1152]{1,0:T(8,128)(2,1)S(1)}, u32[]{:S(2)}, u32[]{:S(2)}) collective-permute-start(bf16[48,1152]{1,0:T(8,128)(2,1)S(1)} %fusion.54), channel_id=1, source_target_pairs={{0,16},{16,0},{1,17},{17,1},{2,18},{18,2},{3,19},{19,3},{4,20},{20... | collective-permute-start | bytes 331784 | tf_op jit(solution)/shard_map/ppermute | solution.py:587
  359.2 13.1 %collective-permute-start.37 = (bf16[4,48,1152]{2,1,0:T(8,128)(2,1)S(1)}, bf16[4,48,1152]{2,1,0:T(8,128)(2,1)S(1)}, u32[]{:S(2)}, u32[]{:S(2)}) collective-permute-start(bf16[4,48,1152]{2,1,0:T(8,128)(2,1)S(1)} %add_convert_fusion.9), channel_id=1, source_target_pairs={{0,2},{1,3},{2,0},{3,1},{4,6},{5,7},{6,4},{7,5},{8,10},{9,11},{10,... | collective-permute-start | bytes 1327112 | tf_op jit(solution)/shard_map/ppermute | solution.py:350
  360.4 37.3 %collective-permute-start.25 = (bf16[512,768]{1,0:T(8,128)(2,1)S(1)}, bf16[512,768]{1,0:T(8,128)(2,1)S(1)}, u32[]{:S(2)}, u32[]{:S(2)}) collective-permute-start(bf16[512,768]{1,0:T(8,128)(2,1)S(1)} %select_convert_fusion.1), channel_id=1, source_target_pairs={{0,16},{16,0},{1,17},{17,1},{2,18},{18,2},{3,19},{19,3},{4,20},{20... | collective-permute-start | bytes 2359304 | tf_op jit(solution)/shard_map/ppermute | solution.py:587
  360.9 29.4 %collective-permute-start.42 = (bf16[4,48,1920]{2,1,0:T(8,128)(2,1)S(1)}, bf16[4,48,1920]{2,1,0:T(8,128)(2,1)S(1)}, u32[]{:S(2)}, u32[]{:S(2)}) collective-permute-start(bf16[4,48,1920]{2,1,0:T(8,128)(2,1)S(1)} %slice.594), channel_id=1, source_target_pairs={{0,2},{1,3},{2,0},{3,1},{4,6},{5,7},{6,4},{7,5},{8,10},{9,11},{10,... | collective-permute-start | bytes 2211848 | tf_op jit(solution)/shard_map/ppermute | solution.py:350
  372.4 7.8 %collective-permute-start.40 = (bf16[48,1152]{1,0:T(8,128)(2,1)S(1)}, bf16[48,1152]{1,0:T(8,128)(2,1)S(1)}, u32[]{:S(2)}, u32[]{:S(2)}) collective-permute-start(bf16[48,1152]{1,0:T(8,128)(2,1)S(1)} %get-tuple-element.148), channel_id=1, source_target_pairs={{0,12},{1,13},{2,14},{3,15},{4,8},{5,9},{6,10},{7,11},{8,4},{9,5},... | collective-permute-start | bytes 331784 | tf_op jit(solution)/shard_map/ppermute | solution.py:350
  374.5 10.1 %collective-permute-start.39 = (bf16[48,1152]{1,0:T(8,128)(2,1)S(1)}, bf16[48,1152]{1,0:T(8,128)(2,1)S(1)}, u32[]{:S(2)}, u32[]{:S(2)}) collective-permute-start(bf16[48,1152]{1,0:T(8,128)(2,1)S(1)} %get-tuple-element.149), channel_id=1, source_target_pairs={{0,8},{1,9},{2,10},{3,11},{4,12},{5,13},{6,14},{7,15},{8,0},{9,1},... | collective-permute-start | bytes 331784 | tf_op jit(solution)/shard_map/ppermute | solution.py:350
  375.9 8.7 %collective-permute-start.38 = (bf16[48,1152]{1,0:T(8,128)(2,1)S(1)}, bf16[48,1152]{1,0:T(8,128)(2,1)S(1)}, u32[]{:S(2)}, u32[]{:S(2)}) collective-permute-start(bf16[48,1152]{1,0:T(8,128)(2,1)S(1)} %get-tuple-element.147), channel_id=1, source_target_pairs={{0,4},{1,5},{2,6},{3,7},{4,0},{5,1},{6,2},{7,3},{8,12},{9,13},{10,... | collective-permute-start | bytes 331784 | tf_op jit(solution)/shard_map/ppermute | solution.py:350
  380.2 6.8 %collective-permute-start.50 = (bf16[192,768]{1,0:T(8,128)(2,1)S(1)}, bf16[192,768]{1,0:T(8,128)(2,1)S(1)}, u32[]{:S(2)}, u32[]{:S(2)}) collective-permute-start(bf16[192,768]{1,0:T(8,128)(2,1)S(1)} %fusion.30), channel_id=1, source_target_pairs={{0,16},{16,0},{1,17},{17,1},{2,18},{18,2},{3,19},{19,3},{4,20},{20... | collective-permute-start | bytes 884744 | tf_op jit(solution)/shard_map/ppermute | solution.py:587
  384.7 4.8 %collective-permute-start.41 = (bf16[48,1152]{1,0:T(8,128)(2,1)S(1)}, bf16[48,1152]{1,0:T(8,128)(2,1)S(1)}, u32[]{:S(2)}, u32[]{:S(2)}) collective-permute-start(bf16[48,1152]{1,0:T(8,128)(2,1)S(1)} %fusion.51), channel_id=1, source_target_pairs={{0,16},{16,0},{1,17},{17,1},{2,18},{18,2},{3,19},{19,3},{4,20},{20... | collective-permute-start | bytes 331784 | tf_op jit(solution)/shard_map/ppermute | solution.py:587
  392.5 13.0 %collective-permute-start.45 = (bf16[48,1920]{1,0:T(8,128)(2,1)}, bf16[48,1920]{1,0:T(8,128)(2,1)}, u32[]{:S(2)}, u32[]{:S(2)}) collective-permute-start(bf16[48,1920]{1,0:T(8,128)(2,1)} %get-tuple-element.159), channel_id=1, source_target_pairs={{0,12},{1,13},{2,14},{3,15},{4,8},{5,9},{6,10},{7,11},{8,4},{9,5},... | collective-permute-start | bytes 552968 | tf_op jit(solution)/shard_map/ppermute | solution.py:350
  394.5 16.9 %collective-permute-start.44 = (bf16[48,1920]{1,0:T(8,128)(2,1)}, bf16[48,1920]{1,0:T(8,128)(2,1)}, u32[]{:S(2)}, u32[]{:S(2)}) collective-permute-start(bf16[48,1920]{1,0:T(8,128)(2,1)} %get-tuple-element.160), channel_id=1, source_target_pairs={{0,8},{1,9},{2,10},{3,11},{4,12},{5,13},{6,14},{7,15},{8,0},{9,1},... | collective-permute-start | bytes 552968 | tf_op jit(solution)/shard_map/ppermute | solution.py:350
  397.1 14.2 %collective-permute-start.43 = (bf16[48,1920]{1,0:T(8,128)(2,1)}, bf16[48,1920]{1,0:T(8,128)(2,1)}, u32[]{:S(2)}, u32[]{:S(2)}) collective-permute-start(bf16[48,1920]{1,0:T(8,128)(2,1)} %get-tuple-element.158), channel_id=1, source_target_pairs={{0,4},{1,5},{2,6},{3,7},{4,0},{5,1},{6,2},{7,3},{8,12},{9,13},{10,... | collective-permute-start | bytes 552968 | tf_op jit(solution)/shard_map/ppermute | solution.py:350
  405.0 8.2 %collective-permute-start.27 = (f32[24,768]{1,0:T(8,128)S(1)}, f32[24,768]{1,0:T(8,128)S(1)}, u32[]{:S(2)}, u32[]{:S(2)}) collective-permute-start(f32[24,768]{1,0:T(8,128)S(1)} %add.484), channel_id=1, source_target_pairs={{0,2},{1,3},{2,0},{3,1},{4,6},{5,7},{6,4},{7,5},{8,10},{9,11},{10,... | collective-permute-start | bytes 221192 | tf_op jit(solution)/shard_map/ppermute | solution.py:581
  412.6 12.2 %collective-permute-start.46 = (bf16[48,1920]{1,0:T(8,128)(2,1)S(1)}, bf16[48,1920]{1,0:T(8,128)(2,1)S(1)}, u32[]{:S(2)}, u32[]{:S(2)}) collective-permute-start(bf16[48,1920]{1,0:T(8,128)(2,1)S(1)} %fusion.44), channel_id=1, source_target_pairs={{0,16},{16,0},{1,17},{17,1},{2,18},{18,2},{3,19},{19,3},{4,20},{20... | collective-permute-start | bytes 552968 | tf_op jit(solution)/shard_map/ppermute | solution.py:587
  417.6 5.5 %collective-permute-start.29 = (f32[24,768]{1,0:T(8,128)S(1)}, f32[24,768]{1,0:T(8,128)S(1)}, u32[]{:S(2)}, u32[]{:S(2)}) collective-permute-start(f32[24,768]{1,0:T(8,128)S(1)} %add.486), channel_id=1, source_target_pairs={{0,8},{1,9},{2,10},{3,11},{4,12},{5,13},{6,14},{7,15},{8,0},{9,1},... | collective-permute-start | bytes 221192 | tf_op jit(solution)/shard_map/ppermute | solution.py:581
  (101 other events, 1011.1 us)

commit v4 on v3

--- a/solution.py
+++ b/solution.py
@@ -22,6 +22,7 @@
 KEYS = WINDOW + PATCH
 
 dilation = 2
+small_cost = pl.CostEstimate(flops=1000, bytes_accessed=1000, transcendentals=0)
 norm_eps = 1e-05
 mask_fill = -1000000000.0
 bf16 = jnp.bfloat16
@@ -286,9 +287,7 @@
             scratch_shapes=[pltpu.VMEM((TEXT, 2 * LANES), bf16)],
         ),
         out_shape=jax.ShapeDtypeStruct((TEXT, HEADS * HEAD), bf16),
-        cost_estimate=pl.CostEstimate(
-            flops=4_000_000_000, bytes_accessed=6_000_000, transcendentals=3_000_000
-        ),
+        cost_estimate=small_cost,
         name="attend",
     )(bounds, queries, keys_values, keys_values, features, own_features, tables)
 
@@ -328,9 +327,7 @@
             jax.ShapeDtypeStruct((2 * TEXT, count * LANES), bf16),
             jax.ShapeDtypeStruct((2 * count, 8, LANES), f32),
         ],
-        cost_estimate=pl.CostEstimate(
-            flops=4_000_000_000 * count, bytes_accessed=1_500_000 * count, transcendentals=500_000
-        ),
+        cost_estimate=small_cost,
         name="attend_back",
     )(
         bounds,
@@ -410,20 +407,17 @@
             scratch_shapes=[pltpu.SemaphoreType.DMA((32,))],
         ),
         out_shape=jax.ShapeDtypeStruct((16 * rows, width), bf16),
-        cost_estimate=pl.CostEstimate(
-            flops=0, bytes_accessed=64 * rows * width, transcendentals=0
-        ),
+        cost_estimate=small_cost,
         name="place_rows",
     )(place, *pieces)
 
 
+def column_parts(shard):
+    return [shard] + [exchange(shard, 4 * step) for step in (1, 2, 3)]
+
+
 def column_of(shard):
-    return jnp.stack([shard] + [exchange(shard, 4 * step) for step in (1, 2, 3)])
-
-
-def pieces_of(column):
-    across = exchange(column, 2)
-    return column, exchange(column, 1), across, exchange(across, 1)
+    return jnp.stack(column_parts(shard))
 
 
 def grad_rows_kernel(page, x_ref, h_ref, keep_ref, send_ref, product):
@@ -458,11 +452,7 @@
             scratch_shapes=[pltpu.VMEM((2 * rows, columns), f32)],
         ),
         out_shape=[half, half],
-        cost_estimate=pl.CostEstimate(
-            flops=2 * tokens * width * columns,
-            bytes_accessed=2 * (tokens * (width + columns) + width * columns),
-            transcendentals=0,
-        ),
+        cost_estimate=small_cost,
         name="grad_rows",
     )(page, inputs, grads)
 
@@ -518,30 +508,81 @@
             scratch_shapes=[pltpu.VMEM((width, tile), f32)],
         ),
         out_shape=[half, half],
-        cost_estimate=pl.CostEstimate(
-            flops=flops, bytes_accessed=4 * width * steps * tile, transcendentals=0
-        ),
+        cost_estimate=small_cost,
         name="grad_columns",
     )(page, *operands)
 
 
-def pair_sum(keep, partner, at):
-    return keep[at].astype(f32) + partner[at].astype(f32)
-
-
-def across_send(keep, partner):
-    return pair_sum(keep, partner, slice(4, 8)).astype(bf16)
-
-
-def column_sends(keep, partner, across):
-    return [
-        (pair_sum(keep, partner, step) + across[step].astype(f32)).astype(bf16)
-        for step in (1, 2, 3)
-    ]
-
-
-def column_total(keep, partner, across, arrived):
-    total = pair_sum(keep, partner, 0) + across[0].astype(f32)
+def first_half_kernel(place, keep_near, part_near, keep_far, part_far, held_ref, out_ref):
+    held_ref[...] = keep_near[...].astype(f32) + part_near[...].astype(f32)
+    out_ref[...] = (keep_far[...].astype(f32) + part_far[...].astype(f32)).astype(bf16)
+
+
+def halve_call(place, keep, partner, specs, half_shape, steps):
+    near, far, out = specs
+    return pl.pallas_call(
+        first_half_kernel,
+        grid_spec=pltpu.PrefetchScalarGridSpec(
+            num_scalar_prefetch=1,
+            grid=(steps,),
+            in_specs=[near, near, far, far],
+            out_specs=[out, out],
+        ),
+        out_shape=[
+            jax.ShapeDtypeStruct(half_shape, f32),
+            jax.ShapeDtypeStruct(half_shape, bf16),
+        ],
+        cost_estimate=small_cost,
+        name="halve",
+    )(place, keep, partner, keep, partner)
+
+
+def halve_across(place, keep, partner):
+    _, rows, width = keep.shape
+    near = pl.BlockSpec((1, rows, width), lambda step, place: (step, 0, 0))
+    far = pl.BlockSpec((1, rows, width), lambda step, place: (step + 4, 0, 0))
+    return halve_call(place, keep, partner, (near, far, near), (4, rows, width), 4)
+
+
+def halve_plane(place, keep, partner):
+    _, rows, width = keep.shape
+    block = (2, rows, width // 2)
+    near = pl.BlockSpec(block, lambda step, place: (step, 0, place[1]))
+    far = pl.BlockSpec(block, lambda step, place: (step, 0, 1 - place[1]))
+    out = pl.BlockSpec(block, lambda step, place: (step, 0, 0))
+    return halve_call(place, keep, partner, (near, far, out), (8, rows, width // 2), 4)
+
+
+def column_kernel(held_ref, across_ref, own_ref, *sends):
+    own_ref[...] = held_ref[0] + across_ref[0].astype(f32)
+    for step, send in enumerate(sends, 1):
+        send[...] = (held_ref[step] + across_ref[step].astype(f32)).astype(bf16)
+
+
+def column_sends(held, across):
+    _, rows, width = held.shape
+    tile = 384
+    out = pl.BlockSpec((rows, tile), lambda step: (0, step))
+    block = pl.BlockSpec((4, rows, tile), lambda step: (0, 0, step))
+    own, *sends = pl.pallas_call(
+        column_kernel,
+        grid=(width // tile,),
+        in_specs=[block, block],
+        out_specs=[out] * 4,
+        out_shape=[jax.ShapeDtypeStruct((rows, width), f32)]
+        + [jax.ShapeDtypeStruct((rows, width), bf16)] * 3,
+        cost_estimate=small_cost,
+        name="column_sends",
+    )(held, across)
+    return own, sends
+
+
+def column_arrivals(sends):
+    return [exchange(send, 4 * step) for step, send in enumerate(sends, 1)]
+
+
+def column_total(own, arrived):
+    total = own
     for part in arrived:
         total = total + part.astype(f32)
     return total.astype(bf16)
@@ -619,7 +660,6 @@
     own_low = states[0, 0]
     rows_each = w_query.shape[0]
     d_ff = w_up.shape[1]
-    half = d_model // 2
     fast = lax.axis_size("page") == 16 and rows_each % 16 == 0 and w_down.shape[0] % 16 == 0
     place = jnp.stack([lax.axis_index("page"), lax.axis_index("mod")]).astype(jnp.int32)
     pack_qkv = jnp.concatenate([w_query, w_key, w_value], axis=1)
@@ -627,17 +667,16 @@
     other_low = swap(own_low)
     if fast:
         column_qkv = column_of(half_columns(pack_qkv, is_text))
+        parts_rest = column_parts(after(pack_rest, column_qkv))
         eight = jnp.concatenate([column_qkv, exchange(column_qkv, 2)])
         far = swap(eight)
         pieces = [eight, exchange(eight, 1), far, exchange(far, 1)]
-        column_rest = column_of(after(pack_rest, column_qkv))
-        column_down = column_of(after(w_down, column_rest))
+        column_rest = jnp.stack([after(part, eight, far) for part in parts_rest])
+        parts_down = column_parts(after(w_down, column_rest))
         pieces[0] = after(pieces[0], column_rest)
         full_qkv = place_rows(place, pieces, pack_qkv.shape[1], place_halves_kernel)
     else:
         full_qkv = lax.all_gather(pack_qkv, "page", axis=0, tiled=True)
-    full_query = full_qkv[:, :d_model]
-    full_kv = full_qkv[:, d_model:]
 
     page_ids, pos_bins, bins_x, bins_y = token_ids(segments[0], box_x[0], box_y[0])
     bounds = page_bounds(segments[0], is_text)
@@ -675,22 +714,20 @@
     )
     if fast:
         full_qkv = after(full_qkv, mixed_all, features, tables, bounds, own_flip)
-        full_query = full_qkv[:, :d_model]
-        full_kv = full_qkv[:, d_model:]
+    full_query = full_qkv[:, :d_model]
+    full_kv = full_qkv[:, d_model:]
     queries = ((plain_dot(mixed_low, full_query) + b_query).astype(bf16) * 0.125).astype(bf16)
     kv_bias = jnp.concatenate([jnp.zeros_like(b_value), b_value])
     keys_values = (plain_dot(mixed_all, full_kv) + kv_bias).astype(bf16)
     context = attend(bounds, queries, keys_values, features, own_feats, tables)
     if fast:
-        column_down = after(column_down, context)
-        pieces_rest = list(pieces_of(column_rest))
-        pieces_rest[0] = after(pieces_rest[0], column_down)
+        across_rest = exchange(column_rest, 2)
+        column_down = jnp.stack([after(part, context) for part in parts_down])
+        across_rest = after(across_rest, column_down)
+        pieces_rest = [column_rest, exchange(column_rest, 1), across_rest, exchange(across_rest, 1)]
         full_rest = place_rows(place, pieces_rest, pack_rest.shape[1], place_kernel)
-        pieces_down = pieces_of(column_down)
-        full_down = place_rows(place, pieces_down, d_model, place_kernel)
     else:
         full_rest = lax.all_gather(pack_rest, "page", axis=0, tiled=True)
-        full_down = lax.all_gather(w_down, "page", axis=0, tiled=True)
     full_out = full_rest[:, :d_model]
     full_up = full_rest[:, d_model:]
 
@@ -700,28 +737,35 @@
     hidden = plain_dot(normed_low, full_up) + b_up
     active, gelu_pull = jax.vjp(exact_gelu, hidden)
     active_low = active.astype(bf16)
+    if fast:
+        across_down = after(exchange(column_down, 2), normed_low)
+        pieces_down = [column_down, exchange(column_down, 1), across_down, exchange(across_down, 1)]
+        pieces_down[0] = after(pieces_down[0], active_low)
+        full_down = place_rows(place, pieces_down, d_model, place_kernel)
+    else:
+        full_down = lax.all_gather(w_down, "page", axis=0, tiled=True)
     ffn_out = plain_dot(active_low, full_down) + b_down
     output_row, norm_two_pull = jax.vjp(layer_norm, normed + ffn_out, gain_two, bias_two)
     grad_out = cotangent[0, 0].astype(f32)
     grad_sum_two, grad_gain_two, grad_bias_two = norm_two_pull(grad_out)
     grad_ffn = grad_sum_two.astype(bf16)
     grad_b_down = column_sum(grad_ffn)
+    grad_hidden_in = grad_ffn
     if fast:
         keep_down, send_down = grad_by_rows(active_low, grad_ffn, place)
         partner_down = exchange(send_down, 1)
         grad_hidden_in = after(grad_ffn, keep_down, send_down)
     else:
         shard_down = summed_rows([(active_low, grad_ffn)])
-        grad_hidden_in = grad_ffn
     (grad_hidden_f,) = gelu_pull(dot_right_t(grad_hidden_in, full_down))
     grad_hidden = grad_hidden_f.astype(bf16)
     grad_b_up = column_sum(grad_hidden)
     grad_up_in = grad_hidden
     if fast:
         partner_down = after(partner_down, grad_hidden)
-        across_out = across_send(keep_down, partner_down)
-        across_down = exchange(across_out, 2)
-        grad_up_in = after(grad_hidden, across_out)
+        held_down, across_out_down = halve_across(place, keep_down, partner_down)
+        across_down = exchange(across_out_down, 2)
+        grad_up_in = after(grad_hidden, across_out_down)
     grad_normed = grad_sum_two + dot_right_t(grad_up_in, full_up)
     grad_first, grad_gain_one, grad_bias_one = norm_one_pull(grad_normed)
     grad_branch = grad_first.astype(bf16)
@@ -731,71 +775,60 @@
     if fast:
         keep_rest, send_rest = grad_by_columns(pairs, place, d_model)
         partner_rest = exchange(send_rest, 1)
-        grad_context_in = after(grad_branch, keep_rest, send_rest)
+        across_down = after(across_down, send_rest)
+        grad_context_in = after(grad_branch, keep_rest, across_down)
     else:
         shard_rest = summed_rows(pairs)
     grad_context = dot_right_t(grad_context_in, full_out).astype(bf16)
-    back = functools.partial(attend_back, bounds, queries, keys_values)
-    rest = (features, own_feats, own_flip, tables)
-    grad_q1, grad_k1, grad_v1, grad_t1 = back(grad_context, *rest, 0, PAIRS // 2)
-    pairs = [(mixed_low, grad_q1), (mixed_all, grad_k1), (mixed_all, grad_v1)]
-    grad_context_in = grad_context
-    if fast:
-        keep_one, send_one = grad_by_columns(pairs, place, half)
-        partner_one = exchange(send_one, 1)
-        partner_rest = after(partner_rest, grad_q1)
-        both_rest = pair_sum(keep_rest, partner_rest, slice(0, 8))
-        plane_out = half_columns(both_rest, ~is_text).astype(bf16)
+    attend_in = grad_context
+    if fast:
+        partner_rest = after(partner_rest, grad_context)
+        held_rest, plane_out = halve_plane(place, keep_rest, partner_rest)
         plane_rest = swap(plane_out)
-        across_down = after(across_down, grad_q1)
-        sends_down = column_sends(keep_down, partner_down, across_down)
-        column_in_down = [exchange(x, 4 * i) for i, x in enumerate(sends_down, 1)]
-        grad_context_in = after(grad_context, keep_one, send_one, plane_out, *sends_down)
+        own_down, sends_down = column_sends(held_down, across_down)
+        arrived_down = column_arrivals(sends_down)
+        attend_in = after(grad_context, plane_out, *sends_down)
+    grad_queries, grad_keys, grad_values, grad_tables = attend_back(
+        bounds, queries, keys_values, attend_in, features, own_feats, own_flip, tables, 0, PAIRS
+    )
+    grad_keys_in, grad_queries_in = grad_keys, grad_queries
+    if fast:
+        plane_rest = after(plane_rest, grad_queries)
+        held_rest, across_out_rest = halve_across(place, held_rest, plane_rest)
+        across_rest = exchange(across_out_rest, 2)
+        arrived_down = [after(part, grad_queries) for part in arrived_down]
+        total_down = column_total(own_down, arrived_down)
+        far_down = swap(total_down)
+        grad_queries_in = after(grad_queries, across_out_rest, total_down)
+    pairs = [(mixed_low, grad_queries_in), (mixed_all, grad_keys), (mixed_all, grad_values)]
+    if fast:
+        keep_qkv, send_qkv = grad_by_columns(pairs, place, d_model)
+        partner_qkv = exchange(send_qkv, 1)
+        across_rest = after(across_rest, send_qkv)
+        own_rest, sends_rest = column_sends(held_rest, across_rest)
+        arrived_rest = column_arrivals(sends_rest)
+        far_down = after(far_down, send_qkv)
+        partner_qkv = after(partner_qkv, far_down, *sends_rest)
+        held_qkv, across_out_qkv = halve_across(place, keep_qkv, partner_qkv)
+        across_qkv = exchange(across_out_qkv, 2)
+        grad_keys_in = after(grad_keys, across_out_qkv)
     else:
-        shard_one = summed_rows(pairs)
-    grad_q2, grad_k2, grad_v2, grad_t2 = back(grad_context_in, *rest, PAIRS // 2, PAIRS // 2)
-    pairs = [(mixed_low, grad_q2), (mixed_all, grad_k2), (mixed_all, grad_v2)]
-    if fast:
-        keep_two, send_two = grad_by_columns(pairs, place, half)
-        partner_two = exchange(send_two, 1)
-        partner_one = after(partner_one, send_two)
-        across_one_out = across_send(keep_one, partner_one)
-        across_one = exchange(across_one_out, 2)
-        plane_rest = after(plane_rest, send_two)
-        both_rest = half_columns(both_rest, is_text) + plane_rest.astype(f32)
-        across_rest_out = both_rest[4:].astype(bf16)
-        across_rest = exchange(across_rest_out, 2)
-        grad_keys_in = [
-            after(x, across_one_out, across_rest_out, send_two) for x in (grad_k1, grad_v1)
-        ]
-    else:
-        shard_two = summed_rows(pairs)
-        grad_keys_in = [grad_k1, grad_v1]
-    grad_b_query = jnp.concatenate([column_sum(grad_q1), column_sum(grad_q2)], axis=1)
-    grad_b_value = jnp.concatenate([column_sum(grad_v1), column_sum(grad_v2)], axis=1)
-    from_keys = (
-        dot_right_t(grad_keys_in[0], full_kv[:, :half])
-        + dot_right_t(grad_k2, full_kv[:, half:d_model])
-        + dot_right_t(grad_keys_in[1], full_kv[:, d_model : d_model + half])
-        + dot_right_t(grad_v2, full_kv[:, d_model + half :])
+        shard_qkv = summed_rows(pairs)
+    grad_b_query = column_sum(grad_queries)
+    grad_b_value = column_sum(grad_values)
+    from_keys = dot_right_t(grad_keys_in, full_kv[:, :d_model]) + dot_right_t(
+        grad_values, full_kv[:, d_model:]
     )
     to_other = jnp.where(is_text, from_keys[TEXT:], from_keys[:TEXT]).astype(bf16)
     from_other = swap(to_other)
-    from_queries = dot_right_t(grad_q1, full_query[:, :half]) + dot_right_t(
-        grad_q2, full_query[:, half:]
-    )
-    if fast:
-        column_in_down = [after(x, to_other) for x in column_in_down]
-        total_down = column_total(keep_down, partner_down, across_down, column_in_down)
-        shard_down = total_down.astype(f32) + swap(total_down).astype(f32)
-        partner_two = after(partner_two, to_other)
-        across_two_out = across_send(keep_two, partner_two)
-        across_two = exchange(across_two_out, 2)
-        sends_one = column_sends(keep_one, partner_one, across_one)
-        column_in_one = [exchange(x, 4 * i) for i, x in enumerate(sends_one, 1)]
-        sum_rest = both_rest[:4] + across_rest.astype(f32)
-        sends_rest = [sum_rest[step].astype(bf16) for step in (1, 2, 3)]
-        column_in_rest = [exchange(x, 4 * i) for i, x in enumerate(sends_rest, 1)]
+    if fast:
+        grad_queries = after(grad_queries, to_other)
+    from_queries = dot_right_t(grad_queries, full_query)
+    if fast:
+        across_qkv = after(across_qkv, from_queries)
+        own_qkv, sends_qkv = column_sends(held_qkv, across_qkv)
+        arrived_qkv = column_arrivals(sends_qkv)
+        from_other = after(from_other, *sends_qkv)
     grad_mixed = (
         grad_first
         + from_queries
@@ -804,7 +837,7 @@
     )
     grad_in, grad_conv_w, grad_conv_b = mix_pull(grad_mixed)
 
-    table_rows = jnp.concatenate([grad_t1[:, :3], grad_t2[:, :3]]).reshape(6, 768)
+    table_rows = grad_tables[:, :3].reshape(6, 768)
     packed = jnp.concatenate(
         [
             grad_conv_w,
@@ -823,41 +856,32 @@
         ],
         axis=0,
     )
+    if fast:
+        arrived_rest = [after(part, packed) for part in arrived_rest]
+        total_rest = column_total(own_rest, arrived_rest)
+        far_rest = swap(total_rest)
+        arrived_qkv = [after(part, total_rest) for part in arrived_qkv]
+        total_qkv = column_total(own_qkv, arrived_qkv)
+        far_qkv = swap(total_qkv)
     packed = sum_everywhere(packed)
     g_tables = packed[16:22].reshape(HEADS, 3, LANES)
     if fast:
-        sends_two = column_sends(keep_two, partner_two, across_two)
-        column_in_two = [exchange(x, 4 * i) for i, x in enumerate(sends_two, 1)]
-        total_one = column_total(keep_one, partner_one, across_one, column_in_one)
-        shard_one = total_one.astype(f32) + swap(total_one).astype(f32)
-        total_rest = sum_rest[0]
-        for part in column_in_rest:
-            total_rest = total_rest + part.astype(f32)
-        low_rest = total_rest.astype(bf16)
-        far_rest = swap(low_rest)
+        shard_down = total_down.astype(f32) + far_down.astype(f32)
+        shard_qkv = total_qkv.astype(f32) + far_qkv.astype(f32)
         shard_rest = jnp.where(
             is_text,
-            jnp.concatenate([low_rest, far_rest], axis=1),
-            jnp.concatenate([far_rest, low_rest], axis=1),
+            jnp.concatenate([total_rest, far_rest], axis=1),
+            jnp.concatenate([far_rest, total_rest], axis=1),
         ).astype(f32)
-        total_two = column_total(keep_two, partner_two, across_two, column_in_two)
-        shard_two = total_two.astype(f32) + swap(total_two).astype(f32)
-    shard_q, shard_k, shard_v = [
-        jnp.concatenate(
-            [shard_one[:, i * half : (i + 1) * half], shard_two[:, i * half : (i + 1) * half]],
-            axis=1,
-        )
-        for i in range(3)
-    ]
     return (
         output_row.astype(bf16)[None, None],
         grad_in.astype(bf16)[None, None],
         packed[0:3],
         packed[3],
-        shard_q,
+        shard_qkv[:, :d_model],
         packed[4],
-        shard_k,
-        shard_v,
+        shard_qkv[:, d_model : 2 * d_model],
+        shard_qkv[:, 2 * d_model :],
         packed[5],
         shard_rest[:, :d_model],
         packed[6],

time: 437 us -> 415 us (0.950)
  Pallas kernels: 96.1 us -> 121 us
  other arithmetic: 59.4 us -> 42.6 us
  starting transfers between devices: 62.4 us -> 46.6 us
  local copies, waits for them, and re-layouts: 40.2 us -> 27.4 us
    pallas_call x0 -> x7, Pallas kernels: none -> 32.8 us  [the longest x4 21.2 us: halve_call(): pl.pallas_call(first_half_kernel, grid_spec=pltpu.PrefetchScalarGridSpec(...]
    ppermute x38 -> x33, starting transfers between devices: 53.1 us -> 31.7 us  [exchange(): return lax.ppermute(values, 'page', [(i, i ^ mask) for i in range(count)])]
    convert_element_type x9 -> x1, other arithmetic: 10.5 us -> 0.09 us  [local(): shard_rest = jnp.where(is_text, jnp.concatenate([total_rest, far_rest], a...]
    unnamed x205 -> x123, local copies, waits for them, and re-layouts: 18.9 us -> 11 us
    reduce_sum x6 -> x4, other arithmetic: 8.76 us -> 2.57 us  [column_sum(): return jnp.sum(values, axis=0, keepdims=True, dtype=f32)]
    ppermute x4, starting transfers between devices: 1.24 us -> 6.73 us  [sum_everywhere(): lax.ppermute(values, 'page', [(i, i ^ step) for i in range(count)])]
    pallas_call x3 -> x2, Pallas kernels: 24.3 us -> 19.3 us  [grad_by_columns(): pl.pallas_call(functools.partial(grad_columns_kernel, parts), grid_spec=p...]
    add x5 -> x2, other arithmetic: 6.9 us -> 1.88 us  [the longest x1 1.83 us: local(): shard_down = total_down.astype(f32) + far_down.astype(f32)]
  transfers between devices with their start and end apart: 51 -> 45, of which waited for: 19 -> 15; matrix products, arithmetic and copies ran while one was open for 29% -> 27% of each run, Pallas kernels for 16% -> 16%
where the time goes in v4:
time: 415 us; the launch traced here: 410 us
  Pallas kernels  121 us (29%)
  waiting for transfers between devices  102 us (25%)
  matrix products  68.1 us (16%)
  starting transfers between devices  46.6 us (11%)
  other arithmetic  42.6 us (10%)
  local copies, waits for them, and re-layouts  27.4 us (7%)
    ppermute x33, waiting for transfers between devices, exchange(): return lax.ppermute(values, 'page', [(i, i ^ mask) for i in range(count)])  88.9 us
    dot_general x5, matrix products, plain_dot(): return jnp.dot(left_side, right_side, preferred_element_type=f32)  37 us
    ppermute x33, starting transfers between devices, exchange(): return lax.ppermute(values, 'page', [(i, i ^ mask) for i in range(count)])  31.7 us
    dot_general x6, matrix products, dot_right_t(): lax.dot_general(left_side, right_side, (((1,), (1,)), ((), ())), preferre...  31.1 us
    pallas_call x1, Pallas kernels, attend_back(): pl.pallas_call(attend_back_kernel, grid_spec=pltpu.PrefetchScalarGridSpec...  29.3 us
    pallas_call x4, Pallas kernels, halve_call(): pl.pallas_call(first_half_kernel, grid_spec=pltpu.PrefetchScalarGridSpec(...  21.2 us
    pallas_call x2, Pallas kernels, grad_by_columns(): pl.pallas_call(functools.partial(grad_columns_kernel, parts), grid_spec=p...  19.3 us
    pallas_call x3, Pallas kernels, place_rows(): pl.pallas_call(kernel, grid_spec=pltpu.PrefetchScalarGridSpec(num_scalar_...  16.3 us
  transfers between devices with their start and end apart: 45, of which 15 were waited for; matrix products, arithmetic and copies ran while one was open for 27% of the time, Pallas kernels for 16%

profile of v4, /device:TPU:0, one launch (start us, length us, event | category | flops | bytes accessed | tf_op | source)
XLA Modules:
  0.0 409.5 jit_solution(12573691882075173908)
XLA Ops:
  2.4 3.0 collective-permute-start
  5.4 2.6 collective-permute-start.1
  24.7 7.4 %collective-permute-done.3 = bf16[4,48,1152]{2,1,0:T(8,128)(2,1)S(1)} collective-permute-done((bf16[4,48,1152]{2,1,0:T(8,128)(2,1)S(1)}, bf16[4,48,1152]{2,1,0:T(8,128)(2,1)S(1)}, u32[]{:S(2)}, u32[]{:S(2)}) %collective-permute-start.3) | collective-permute-done | bytes 442400 | tf_op jit(solution)/shard_map/ppermute | solution.py:347
  34.1 3.6 collective-permute-start.7
  38.9 3.5 broadcast_select_fusion.1
  42.4 5.4 %collective-permute-done.7 = bf16[48,3840]{1,0:T(8,128)(2,1)S(1)} collective-permute-done((bf16[48,3840]{1,0:T(8,128)(2,1)}, bf16[48,3840]{1,0:T(8,128)(2,1)S(1)}, u32[]{:S(2)}, u32[]{:S(2)}) %collective-permute-start.7) | collective-permute-done | bytes 368672 | tf_op jit(solution)/shard_map/ppermute | solution.py:347
  47.8 4.8 %collective-permute-done.4.refs_2_ = bf16[8,48,1152]{2,1,0:T(8,128)(2,1)S(1)} collective-permute-done((bf16[8,48,1152]{2,1,0:T(8,128)(2,1)}, bf16[8,48,1152]{2,1,0:T(8,128)(2,1)S(1)}, u32[]{:S(2)}, u32[]{:S(2)}) %collective-permute-start.4) | collective-permute-done | bytes 884768 | tf_op jit(solution)/shard_map/ppermute | solution.py:628
  52.5 13.6 %collective-permute-done.6 = bf16[48,3840]{1,0:T(8,128)(2,1)S(1)} collective-permute-done((bf16[48,3840]{1,0:T(8,128)(2,1)}, bf16[48,3840]{1,0:T(8,128)(2,1)S(1)}, u32[]{:S(2)}, u32[]{:S(2)}) %collective-permute-start.6) | collective-permute-done | bytes 368672 | tf_op jit(solution)/shard_map/ppermute | solution.py:347
  66.1 2.3 pad_maximum_fusion.1.refs_0_
  71.4 2.5 collective-permute-start.15
  75.8 4.8 %place_rows.3 = bf16[768,2304]{1,0:T(8,128)(2,1)} custom-call(s32[2]{0:T(128)} %pad_add_fusion.1.place.page, bf16[8,48,1152]{2,1,0:T(8,128)(2,1)} %constant_dynamic-update-slice_fusion.refs_0_, bf16[8,48,1152]{2,1,0:T(8,128)(2,1)} %collective-permute-done.8.refs_1_, bf16[8,48,1152]{2,1,0:T(8,128)(2,1)} %copy-done.20, ...), custom_call_target="tpu_custom_call" | custom-call | flops 1000 | bytes 1000 | tf_op jit(solution)/shard_map/place_rows/pallas_call | solution.py:400
  80.7 6.3 %add_convert_fusion.1.k_ref.v_ref = bf16[1024,1536]{1,0:T(8,128)(2,1)} fusion(f32[1536]{0:T(1024)S(1)} %concatenate.85, bf16[768,2304]{1,0:T(8,128)(2,1)} %place_rows.3, bf16[512,768]{1,0:T(8,128)(2,1)} %copy-done.14, bf16[512,768]{1,0:T(8,128)(2,1)S(1)} %copy-done.13), kind=kOutput, calls=%fused_computation.17 | convolution fusion | flops 2422210560 | bytes 7084032 | tf_op jit(solution)/shard_map/dot_general | solution.py:85
  86.9 2.9 fusion.21.q_ref
  89.9 12.9 %attend.1.refs_0_ = bf16[512,768]{1,0:T(8,128)(2,1)} custom-call(s32[48]{0:T(128)} %concatenate.71.bounds, bf16[512,768]{1,0:T(8,128)(2,1)} %fusion.21.q_ref, bf16[1024,1536]{1,0:T(8,128)(2,1)} %add_convert_fusion.1.k_ref.v_ref, bf16[1024,1536]{1,0:T(8,128)(2,1)} %add_convert_fusion.1.k_ref.v_ref, bf16[1024,128]{1,0:T(8,128)(2,1)} %copy-done.11, ...), custom_call_target="tpu_custom_call" | custom-call | flops 1000 | bytes 1000 | tf_op jit(solution)/shard_map/attend/pallas_call | solution.py:273
  102.8 2.3 pad_maximum_fusion.2.refs_0_
  106.2 2.8 collective-permute-done.16.refs_3_
  109.0 6.1 %place_rows.4 = bf16[768,3840]{1,0:T(8,128)(2,1)} custom-call(s32[2]{0:T(128)} %pad_add_fusion.1.place.page, bf16[4,48,3840]{2,1,0:T(8,128)(2,1)} %pad_maximum_fusion.1.refs_0_, bf16[4,48,3840]{2,1,0:T(8,128)(2,1)} %copy-done.18, bf16[4,48,3840]{2,1,0:T(8,128)(2,1)} %collective-permute-done.12.refs_2_, bf16[4,48,3840]{2,1,0:T(8,128)(2,1)} %collective-permute-done.16.refs_3_), custom_call_target="tpu_custom_call" | custom-call | flops 1000 | bytes 1000 | tf_op jit(solution)/shard_map/place_rows/pallas_call | solution.py:400
  115.1 3.0 fusion.57
  119.1 15.3 %collective-permute-done.18.refs_2_ = bf16[4,192,768]{2,1,0:T(8,128)(2,1)} collective-permute-done((bf16[4,192,768]{2,1,0:T(8,128)(2,1)}, bf16[4,192,768]{2,1,0:T(8,128)(2,1)}, u32[]{:S(2)}, u32[]{:S(2)}) %collective-permute-start.18) | collective-permute-done | bytes 1179680 | tf_op jit(solution)/shard_map/ppermute | solution.py:347
  134.4 18.7 %multiply_convert_fusion = (bf16[512,3072]{1,0:T(8,128)(2,1)}, f32[512,3072]{1,0:T(8,128)}, f32[512,3072]{1,0:T(8,128)}) fusion(f32[3072]{0:T(1024)S(1)} %copy-done.53, bf16[512,768]{1,0:T(8,128)(2,1)S(1)} %fusion.22.refs_2_, bf16[768,3840]{1,0:T(8,128)(2,1)S(1)} %copy-done.10), kind=kOutput, calls=%fused_computation.4 | convolution fusion | flops 2519728128 | bytes 21245952 | tf_op jit(solution)/shard_map/dot_general | solution.py:85
  153.2 5.4 %place_rows.5 = bf16[3072,768]{1,0:T(8,128)(2,1)} custom-call(s32[2]{0:T(128)} %pad_add_fusion.1.place.page, bf16[4,192,768]{2,1,0:T(8,128)(2,1)} %pad_maximum_fusion.2.refs_0_, bf16[4,192,768]{2,1,0:T(8,128)(2,1)} %collective-permute-done.17.refs_1_, bf16[4,192,768]{2,1,0:T(8,128)(2,1)} %collective-permute-done.18.refs_2_, ...), custom_call_target="tpu_custom_call" | custom-call | flops 1000 | bytes 1000 | tf_op jit(solution)/shard_map/place_rows/pallas_call | solution.py:400
  158.7 6.0 %fusion.58 = (f32[512]{0:T(512)S(1)}, f32[512,768]{1,0:T(8,128)S(1)}) fusion(f32[768]{0:T(1024)S(1)} %copy-done.56, bf16[512,3072]{1,0:T(8,128)(2,1)} %get-tuple-element.196.x_ref, bf16[3072,768]{1,0:T(8,128)(2,1)} %place_rows.5, f32[768]{0:T(1024)S(1)} %copy-done.40, f32[768]{0:T(1024)S(1)} %copy-done.30, f32[512]{0:T(512)S(1)} %fusion.44, ...), kind=kOutput, calls=%fused_computation.215 | convolution fusion | flops 2418671104 | bytes 11025408 | tf_op jit(solution)/shard_map/dot_general | solution.py:85
  170.4 10.0 %grad_rows.1 = (bf16[8,192,768]{2,1,0:T(8,128)(2,1)}, bf16[8,192,768]{2,1,0:T(8,128)(2,1)}) custom-call(s32[2]{0:T(128)} %pad_add_fusion.1.place.page, bf16[512,3072]{1,0:T(8,128)(2,1)} %get-tuple-element.196.x_ref, bf16[512,768]{1,0:T(8,128)(2,1)} %get-tuple-element.109.h_ref), custom_call_target="tpu_custom_call" | custom-call | flops 1000 | bytes 1000 | tf_op jit(solution)/shard_map/grad_rows/pallas_call | solution.py:442
  180.9 12.3 %convert_reduce_fusion = (f32[3072]{0:T(1024)S(1)}, bf16[512,3072]{1,0:T(8,128)(2,1)}) fusion(f32[512,3072]{1,0:T(8,128)} %get-tuple-element.197, f32[512,3072]{1,0:T(8,128)} %get-tuple-element.231, f32[3072]{0:T(1024)S(1)} %copy-done.53, bf16[512,768]{1,0:T(8,128)(2,1)} %get-tuple-element.109.h_ref, bf16[3072,768]{1,0:T(8,128)(2,1)} %place_rows.5), kind=kOutput, calls=%fused_computation.2 | convolution fusion | flops 2442654720 | bytes 21258240 | tf_op jit(solution)/shard_map/dot_general | solution.py:95
  193.2 5.5 %halve.4 = (f32[4,192,768]{2,1,0:T(8,128)}, bf16[4,192,768]{2,1,0:T(8,128)(2,1)}) custom-call(s32[2]{0:T(128)} %pad_add_fusion.1.place.page, bf16[8,192,768]{2,1,0:T(8,128)(2,1)} %get-tuple-element.107.keep_near.keep_far, bf16[8,192,768]{2,1,0:T(8,128)(2,1)} %collective-permute-done.20.part_near.part_far, ...), custom_call_target="tpu_custom_call" | custom-call | flops 1000 | bytes 1000 | tf_op jit(solution)/shard_map/halve/pallas_call | solution.py:523
  198.7 6.8 %multiply_reduce_fusion = (f32[768]{0:T(1024)S(1)}, f32[512]{0:T(512)S(1)}, f32[768]{0:T(1024)S(1)}, f32[512,768]{1,0:T(8,128)S(1)}) fusion(f32[512,768]{1,0:T(8,128)S(1)} %get-tuple-element.230, f32[512]{0:T(512)S(1)} %fusion.44, f32[512]{0:T(512)S(1)} %broadcast_multiply_fusion.1, f32[768]{0:T(1024)S(1)} %copy-done.30, ...), kind=kOutput, calls=%fused_computation.42 | convolution fusion | flops 2419849216 | bytes 12600320 | tf_op jit(solution)/shard_map/dot_general | solution.py:95
  208.5 9.8 %grad_columns.2 = (bf16[8,48,3840]{2,1,0:T(8,128)(2,1)}, bf16[8,48,3840]{2,1,0:T(8,128)(2,1)}) custom-call(s32[2]{0:T(128)} %pad_add_fusion.1.place.page, bf16[512,768]{1,0:T(8,128)(2,1)} %attend.1.refs_0_, bf16[512,768]{1,0:T(8,128)(2,1)} %get-tuple-element.116.refs_1_, bf16[512,768]{1,0:T(8,128)(2,1)} %copy-done.15, ...), custom_call_target="tpu_custom_call" | custom-call | flops 1000 | bytes 1000 | tf_op jit(solution)/shard_map/grad_columns/pallas_call | solution.py:501
  218.7 28.3 %collective-permute-done.21.across_ref = bf16[4,192,768]{2,1,0:T(8,128)(2,1)} collective-permute-done((bf16[4,192,768]{2,1,0:T(8,128)(2,1)}, bf16[4,192,768]{2,1,0:T(8,128)(2,1)}, u32[]{:S(2)}, u32[]{:S(2)}) %collective-permute-start.21) | collective-permute-done | bytes 1179680 | tf_op jit(solution)/shard_map/ppermute | solution.py:347
  247.0 3.0 convolution_convert_fusion.grad_ref
  250.0 5.8 %halve.5 = (f32[8,48,1920]{2,1,0:T(8,128)}, bf16[8,48,1920]{2,1,0:T(8,128)(2,1)}) custom-call(s32[2]{0:T(128)} %pad_add_fusion.1.place.page, bf16[8,48,3840]{2,1,0:T(8,128)(2,1)} %get-tuple-element.113.keep_near.keep_far, bf16[8,48,3840]{2,1,0:T(8,128)(2,1)} %collective-permute-done.22.part_near.part_far, ...), custom_call_target="tpu_custom_call" | custom-call | flops 1000 | bytes 1000 | tf_op jit(solution)/shard_map/halve/pallas_call | solution.py:523
  257.1 2.9 column_sends.3
  260.0 2.4 collective-permute-start.26
  264.4 29.3 %attend_back.1 = (bf16[512,768]{1,0:T(8,128)(2,1)}, bf16[1024,768]{1,0:T(8,128)(2,1)}, bf16[1024,768]{1,0:T(8,128)(2,1)}, f32[12,8,128]{2,1,0:T(8,128)}) custom-call(s32[48]{0:T(128)} %concatenate.71.bounds, bf16[512,768]{1,0:T(8,128)(2,1)} %fusion.21.q_ref, bf16[1024,1536]{1,0:T(8,128)(2,1)} %add_convert_fusion.1.k_ref.v_ref, ...), custom_call_target="tpu_custom_call" | custom-call | flops 1000 | bytes 1000 | tf_op jit(solution)/shard_map/attend_back/pallas_call | solution.py:298
  297.1 4.9 %halve.6 = (f32[4,48,1920]{2,1,0:T(8,128)}, bf16[4,48,1920]{2,1,0:T(8,128)(2,1)}) custom-call(s32[2]{0:T(128)} %pad_add_fusion.1.place.page, f32[8,48,1920]{2,1,0:T(8,128)} %get-tuple-element.126.keep_near.keep_far, bf16[8,48,1920]{2,1,0:T(8,128)(2,1)} %copy-done.9, f32[8,48,1920]{2,1,0:T(8,128)} %get-tuple-element.126.keep_near.keep_far, ...), custom_call_target="tpu_custom_call" | custom-call | flops 1000 | bytes 1000 | tf_op jit(solution)/shard_map/halve/pallas_call | solution.py:523
  301.9 9.4 %grad_columns.3 = (bf16[8,48,2304]{2,1,0:T(8,128)(2,1)}, bf16[8,48,2304]{2,1,0:T(8,128)(2,1)}) custom-call(s32[2]{0:T(128)} %pad_add_fusion.1.place.page, bf16[512,768]{1,0:T(8,128)(2,1)} %copy-done.7, bf16[512,768]{1,0:T(8,128)(2,1)} %get-tuple-element.146.refs_1_, bf16[1024,768]{1,0:T(8,128)(2,1)} %pad_maximum_fusion.refs_2_.refs_4_, ...), custom_call_target="tpu_custom_call" | custom-call | flops 1000 | bytes 1000 | tf_op jit(solution)/shard_map/grad_columns/pallas_call | solution.py:501
  317.8 3.5 collective-permute-done.28
  321.3 9.3 %collective-permute-done.29.across_ref = bf16[4,48,1920]{2,1,0:T(8,128)(2,1)} collective-permute-done((bf16[4,48,1920]{2,1,0:T(8,128)(2,1)}, bf16[4,48,1920]{2,1,0:T(8,128)(2,1)}, u32[]{:S(2)}, u32[]{:S(2)}) %collective-permute-start.29) | collective-permute-done | bytes 737312 | tf_op jit(solution)/shard_map/ppermute | solution.py:347
  330.6 4.0 column_sends.4
  335.9 5.0 %halve.7 = (f32[4,48,2304]{2,1,0:T(8,128)}, bf16[4,48,2304]{2,1,0:T(8,128)(2,1)}) custom-call(s32[2]{0:T(128)} %pad_add_fusion.1.place.page, bf16[8,48,2304]{2,1,0:T(8,128)(2,1)} %get-tuple-element.135.keep_near.keep_far, bf16[8,48,2304]{2,1,0:T(8,128)(2,1)} %copy-done.4, bf16[8,48,2304]{2,1,0:T(8,128)(2,1)} %get-tuple-element.135.keep_near.keep_far, ...), custom_call_target="tpu_custom_call" | custom-call | flops 1000 | bytes 1000 | tf_op jit(solution)/shard_map/halve/pallas_call | solution.py:523
  341.3 3.2 fusion.24
  344.5 2.7 convolution_add_fusion
  354.4 2.5 collective-permute-start.40
  358.8 3.2 fusion.28
  363.2 4.7 %column_sends.5 = (f32[48,2304]{1,0:T(8,128)}, bf16[48,2304]{1,0:T(8,128)(2,1)}, bf16[48,2304]{1,0:T(8,128)(2,1)}, bf16[48,2304]{1,0:T(8,128)(2,1)}) custom-call(f32[4,48,2304]{2,1,0:T(8,128)} %get-tuple-element.147.held_ref, bf16[4,48,2304]{2,1,0:T(8,128)(2,1)} %copy-done.21), custom_call_target="tpu_custom_call" | custom-call | flops 1000 | bytes 1000 | tf_op jit(solution)/shard_map/column_sends/pallas_call | solution.py:567
  367.9 2.4 collective-permute-start.42
  370.4 4.5 %fusion.46 = (f32[768]{0:T(1024)S(1)}, f32[768]{0:T(1024)S(1)}, f32[768]{0:T(1024)S(1)}, f32[768]{0:T(1024)S(1)}, f32[512,768]{1,0:T(8,128)S(1)}) fusion(bf16[1,1,512,768]{3,2,1,0:T(8,128)(2,1)} %param.25, f32[510,768]{1,0:T(8,128)S(1)} %get-tuple-element.209, pred[512]{0:T(512)(128)(4,1)} %get-tuple-element.236, f32[510,768]{1,0:T(8,128)} %get-tuple-element.210, ...), kind=kLoop, calls=%fused_computation.205 | loop fusion | flops 6288384 | bytes 12585985 | tf_op jit(solution)/shard_map/transpose(jvp())/reduce_sum | solution.py:40
  376.6 6.5 %collective-permute-done.39 = bf16[48,1920]{1,0:T(8,128)(2,1)} collective-permute-done((bf16[48,1920]{1,0:T(8,128)(2,1)}, bf16[48,1920]{1,0:T(8,128)(2,1)}, u32[]{:S(2)}, u32[]{:S(2)}) %collective-permute-start.39) | collective-permute-done | bytes 184352 | tf_op jit(solution)/shard_map/ppermute | solution.py:347
  394.5 3.3 collective-permute-start.35
  (302 shorter events, 87.0 us)
Async XLA Ops:
  2.4 18.7 %collective-permute-start = (bf16[48,1152]{1,0:T(8,128)(2,1)S(1)}, bf16[48,1152]{1,0:T(8,128)(2,1)S(1)}, u32[]{:S(2)}, u32[]{:S(2)}) collective-permute-start(bf16[48,1152]{1,0:T(8,128)(2,1)S(1)} %get-tuple-element.203), channel_id=1, source_target_pairs={{0,4},{1,5},{2,6},{3,7},{4,0},{5,1},{6,2},{7,3},{8,12},{9,13},{10,... | collective-permute-start | bytes 331784 | tf_op jit(solution)/shard_map/ppermute | solution.py:347
  5.4 15.7 %collective-permute-start.1 = (bf16[48,1152]{1,0:T(8,128)(2,1)S(1)}, bf16[48,1152]{1,0:T(8,128)(2,1)S(1)}, u32[]{:S(2)}, u32[]{:S(2)}) collective-permute-start(bf16[48,1152]{1,0:T(8,128)(2,1)S(1)} %get-tuple-element.203), channel_id=1, source_target_pairs={{0,8},{1,9},{2,10},{3,11},{4,12},{5,13},{6,14},{7,15},{8,0},{9,1},... | collective-permute-start | bytes 331784 | tf_op jit(solution)/shard_map/ppermute | solution.py:347
  8.0 13.1 %collective-permute-start.2 = (bf16[48,1152]{1,0:T(8,128)(2,1)S(1)}, bf16[48,1152]{1,0:T(8,128)(2,1)S(1)}, u32[]{:S(2)}, u32[]{:S(2)}) collective-permute-start(bf16[48,1152]{1,0:T(8,128)(2,1)S(1)} %get-tuple-element.203), channel_id=1, source_target_pairs={{0,12},{1,13},{2,14},{3,15},{4,8},{5,9},{6,10},{7,11},{8,4},{9,5},... | collective-permute-start | bytes 331784 | tf_op jit(solution)/shard_map/ppermute | solution.py:347
  8.0 30.5 %collective-permute-start.10 = (bf16[512,768]{1,0:T(8,128)(2,1)}, bf16[512,768]{1,0:T(8,128)(2,1)S(1)}, u32[]{:S(2)}, u32[]{:S(2)}) collective-permute-start(bf16[512,768]{1,0:T(8,128)(2,1)} %bitcast.76), channel_id=1, source_target_pairs={{0,16},{16,0},{1,17},{17,1},{2,18},{18,2},{3,19},{19,3},{4,20},{20... | collective-permute-start | bytes 2359304 | tf_op jit(solution)/shard_map/ppermute | solution.py:628
  21.2 10.9 %collective-permute-start.3 = (bf16[4,48,1152]{2,1,0:T(8,128)(2,1)S(1)}, bf16[4,48,1152]{2,1,0:T(8,128)(2,1)S(1)}, u32[]{:S(2)}, u32[]{:S(2)}) collective-permute-start(bf16[4,48,1152]{2,1,0:T(8,128)(2,1)S(1)} %pad_maximum_fusion.3), channel_id=1, source_target_pairs={{0,2},{1,3},{2,0},{3,1},{4,6},{5,7},{6,4},{7,5},{8,10},{9,11},{10,... | collective-permute-start | bytes 1327112 | tf_op jit(solution)/shard_map/ppermute | solution.py:347
  32.9 19.6 %collective-permute-start.4 = (bf16[8,48,1152]{2,1,0:T(8,128)(2,1)}, bf16[8,48,1152]{2,1,0:T(8,128)(2,1)S(1)}, u32[]{:S(2)}, u32[]{:S(2)}) collective-permute-start(bf16[8,48,1152]{2,1,0:T(8,128)(2,1)} %constant_dynamic-update-slice_fusion.refs_0_), channel_id=1, source_target_pairs={{0,16},{16,0},{1,17},{17,1},{2,18},{18,2},{3,19},{19,3},{4,20},{20... | collective-permute-start | bytes 2654216 | tf_op jit(solution)/shard_map/ppermute | solution.py:628
  34.1 13.7 %collective-permute-start.7 = (bf16[48,3840]{1,0:T(8,128)(2,1)}, bf16[48,3840]{1,0:T(8,128)(2,1)S(1)}, u32[]{:S(2)}, u32[]{:S(2)}) collective-permute-start(bf16[48,3840]{1,0:T(8,128)(2,1)} %pad_maximum_fusion.4), channel_id=1, source_target_pairs={{0,12},{1,13},{2,14},{3,15},{4,8},{5,9},{6,10},{7,11},{8,4},{9,5},... | collective-permute-start | bytes 1105928 | tf_op jit(solution)/shard_map/ppermute | solution.py:347
  37.7 28.4 %collective-permute-start.6 = (bf16[48,3840]{1,0:T(8,128)(2,1)}, bf16[48,3840]{1,0:T(8,128)(2,1)S(1)}, u32[]{:S(2)}, u32[]{:S(2)}) collective-permute-start(bf16[48,3840]{1,0:T(8,128)(2,1)} %pad_maximum_fusion.4), channel_id=1, source_target_pairs={{0,8},{1,9},{2,10},{3,11},{4,12},{5,13},{6,14},{7,15},{8,0},{9,1},... | collective-permute-start | bytes 1105928 | tf_op jit(solution)/shard_map/ppermute | solution.py:347
  37.7 28.4 %collective-permute-start.5 = (bf16[48,3840]{1,0:T(8,128)(2,1)}, bf16[48,3840]{1,0:T(8,128)(2,1)S(1)}, u32[]{:S(2)}, u32[]{:S(2)}) collective-permute-start(bf16[48,3840]{1,0:T(8,128)(2,1)} %pad_maximum_fusion.4), channel_id=1, source_target_pairs={{0,4},{1,5},{2,6},{3,7},{4,0},{5,1},{6,2},{7,3},{8,12},{9,13},{10,... | collective-permute-start | bytes 1105928 | tf_op jit(solution)/shard_map/ppermute | solution.py:347
  38.5 35.4 %collective-permute-start.8 = (bf16[8,48,1152]{2,1,0:T(8,128)(2,1)}, bf16[8,48,1152]{2,1,0:T(8,128)(2,1)}, u32[]{:S(2)}, u32[]{:S(2)}) collective-permute-start(bf16[8,48,1152]{2,1,0:T(8,128)(2,1)} %constant_dynamic-update-slice_fusion.refs_0_), channel_id=1, source_target_pairs={{0,1},{1,0},{2,3},{3,2},{4,5},{5,4},{6,7},{7,6},{8,9},{9,8},{10,11... | collective-permute-start | bytes 2654216 | tf_op jit(solution)/shard_map/ppermute | solution.py:347
  42.4 44.6 %copy-start.7 = (bf16[512,768]{1,0:T(8,128)(2,1)}, bf16[512,768]{1,0:T(8,128)(2,1)S(1)}, u32[]{:S(2)}) copy-start(bf16[512,768]{1,0:T(8,128)(2,1)S(1)} %get-tuple-element.200.refs_0_) | copy-start | bytes 2359300
  66.1 9.7 %collective-permute-start.9 = (bf16[8,48,1152]{2,1,0:T(8,128)(2,1)S(1)}, bf16[8,48,1152]{2,1,0:T(8,128)(2,1)}, u32[]{:S(2)}, u32[]{:S(2)}) collective-permute-start(bf16[8,48,1152]{2,1,0:T(8,128)(2,1)S(1)} %collective-permute-done.4.refs_2_), channel_id=1, source_target_pairs={{0,1},{1,0},{2,3},{3,2},{4,5},{5,4},{6,7},{7,6},{8,9},{9,8},{10,11... | collective-permute-start | bytes 2654216 | tf_op jit(solution)/shard_map/ppermute | solution.py:347
  68.4 36.7 %collective-permute-start.12 = (bf16[4,48,3840]{2,1,0:T(8,128)(2,1)}, bf16[4,48,3840]{2,1,0:T(8,128)(2,1)}, u32[]{:S(2)}, u32[]{:S(2)}) collective-permute-start(bf16[4,48,3840]{2,1,0:T(8,128)(2,1)} %pad_maximum_fusion.1.refs_0_), channel_id=1, source_target_pairs={{0,2},{1,3},{2,0},{3,1},{4,6},{5,7},{6,4},{7,5},{8,10},{9,11},{10,... | collective-permute-start | bytes 4423688 | tf_op jit(solution)/shard_map/ppermute | solution.py:347
  71.4 31.3 %collective-permute-start.15 = (bf16[192,768]{1,0:T(8,128)(2,1)S(1)}, bf16[192,768]{1,0:T(8,128)(2,1)}, u32[]{:S(2)}, u32[]{:S(2)}) collective-permute-start(bf16[192,768]{1,0:T(8,128)(2,1)S(1)} %copy-done.24), channel_id=1, source_target_pairs={{0,12},{1,13},{2,14},{3,15},{4,8},{5,9},{6,10},{7,11},{8,4},{9,5},... | collective-permute-start | bytes 884744 | tf_op jit(solution)/shard_map/ppermute | solution.py:347
  73.9 28.9 %collective-permute-start.14 = (bf16[192,768]{1,0:T(8,128)(2,1)S(1)}, bf16[192,768]{1,0:T(8,128)(2,1)}, u32[]{:S(2)}, u32[]{:S(2)}) collective-permute-start(bf16[192,768]{1,0:T(8,128)(2,1)S(1)} %copy-done.24), channel_id=1, source_target_pairs={{0,8},{1,9},{2,10},{3,11},{4,12},{5,13},{6,14},{7,15},{8,0},{9,1},... | collective-permute-start | bytes 884744 | tf_op jit(solution)/shard_map/ppermute | solution.py:347
  73.9 28.9 %collective-permute-start.13 = (bf16[192,768]{1,0:T(8,128)(2,1)S(1)}, bf16[192,768]{1,0:T(8,128)(2,1)}, u32[]{:S(2)}, u32[]{:S(2)}) collective-permute-start(bf16[192,768]{1,0:T(8,128)(2,1)S(1)} %copy-done.24), channel_id=1, source_target_pairs={{0,4},{1,5},{2,6},{3,7},{4,0},{5,1},{6,2},{7,3},{8,12},{9,13},{10,... | collective-permute-start | bytes 884744 | tf_op jit(solution)/shard_map/ppermute | solution.py:347
  89.9 16.3 %collective-permute-start.11 = (bf16[4,48,3840]{2,1,0:T(8,128)(2,1)}, bf16[4,48,3840]{2,1,0:T(8,128)(2,1)S(1)}, u32[]{:S(2)}, u32[]{:S(2)}) collective-permute-start(bf16[4,48,3840]{2,1,0:T(8,128)(2,1)} %pad_maximum_fusion.1.refs_0_), channel_id=1, source_target_pairs={{0,1},{1,0},{2,3},{3,2},{4,5},{5,4},{6,7},{7,6},{8,9},{9,8},{10,11... | collective-permute-start | bytes 4423688 | tf_op jit(solution)/shard_map/ppermute | solution.py:347
  105.1 3.8 collective-permute-start.16
  105.7 47.4 %collective-permute-start.17 = (bf16[4,192,768]{2,1,0:T(8,128)(2,1)}, bf16[4,192,768]{2,1,0:T(8,128)(2,1)}, u32[]{:S(2)}, u32[]{:S(2)}) collective-permute-start(bf16[4,192,768]{2,1,0:T(8,128)(2,1)} %pad_maximum_fusion.2.refs_0_), channel_id=1, source_target_pairs={{0,1},{1,0},{2,3},{3,2},{4,5},{5,4},{6,7},{7,6},{8,9},{9,8},{10,11... | collective-permute-start | bytes 3538952 | tf_op jit(solution)/shard_map/ppermute | solution.py:347
  105.8 28.6 %collective-permute-start.18 = (bf16[4,192,768]{2,1,0:T(8,128)(2,1)}, bf16[4,192,768]{2,1,0:T(8,128)(2,1)}, u32[]{:S(2)}, u32[]{:S(2)}) collective-permute-start(bf16[4,192,768]{2,1,0:T(8,128)(2,1)} %pad_maximum_fusion.2.refs_0_), channel_id=1, source_target_pairs={{0,2},{1,3},{2,0},{3,1},{4,6},{5,7},{6,4},{7,5},{8,10},{9,11},{10,... | collective-permute-start | bytes 3538952 | tf_op jit(solution)/shard_map/ppermute | solution.py:347
  119.1 34.0 %copy-start.15 = (bf16[512,768]{1,0:T(8,128)(2,1)}, bf16[512,768]{1,0:T(8,128)(2,1)S(1)}, u32[]{:S(2)}) copy-start(bf16[512,768]{1,0:T(8,128)(2,1)S(1)} %fusion.22.refs_2_) | copy-start | bytes 2359300
  134.4 18.8 %collective-permute-start.19 = (bf16[4,192,768]{2,1,0:T(8,128)(2,1)}, bf16[4,192,768]{2,1,0:T(8,128)(2,1)}, u32[]{:S(2)}, u32[]{:S(2)}) collective-permute-start(bf16[4,192,768]{2,1,0:T(8,128)(2,1)} %collective-permute-done.18.refs_2_), channel_id=1, source_target_pairs={{0,1},{1,0},{2,3},{3,2},{4,5},{5,4},{6,7},{7,6},{8,9},{9,8},{10,11... | collective-permute-start | bytes 3538952 | tf_op jit(solution)/shard_map/ppermute | solution.py:347
  180.4 12.7 %collective-permute-start.20 = (bf16[8,192,768]{2,1,0:T(8,128)(2,1)}, bf16[8,192,768]{2,1,0:T(8,128)(2,1)}, u32[]{:S(2)}, u32[]{:S(2)}) collective-permute-start(bf16[8,192,768]{2,1,0:T(8,128)(2,1)} %get-tuple-element.108), channel_id=1, source_target_pairs={{0,1},{1,0},{2,3},{3,2},{4,5},{5,4},{6,7},{7,6},{8,9},{9,8},{10,11... | collective-permute-start | bytes 7077896 | tf_op jit(solution)/shard_map/ppermute | solution.py:347
  208.5 38.5 %copy-start.16 = (bf16[512,768]{1,0:T(8,128)(2,1)S(1)}, bf16[512,768]{1,0:T(8,128)(2,1)}, u32[]{:S(2)}) copy-start(bf16[512,768]{1,0:T(8,128)(2,1)} %get-tuple-element.116.refs_1_) | copy-start | bytes 2359300
  218.3 31.7 %collective-permute-start.22 = (bf16[8,48,3840]{2,1,0:T(8,128)(2,1)}, bf16[8,48,3840]{2,1,0:T(8,128)(2,1)}, u32[]{:S(2)}, u32[]{:S(2)}) collective-permute-start(bf16[8,48,3840]{2,1,0:T(8,128)(2,1)} %get-tuple-element.114), channel_id=1, source_target_pairs={{0,1},{1,0},{2,3},{3,2},{4,5},{5,4},{6,7},{7,6},{8,9},{9,8},{10,11... | collective-permute-start | bytes 8847368 | tf_op jit(solution)/shard_map/ppermute | solution.py:347
  218.3 28.7 %collective-permute-start.21 = (bf16[4,192,768]{2,1,0:T(8,128)(2,1)}, bf16[4,192,768]{2,1,0:T(8,128)(2,1)}, u32[]{:S(2)}, u32[]{:S(2)}) collective-permute-start(bf16[4,192,768]{2,1,0:T(8,128)(2,1)} %get-tuple-element.111), channel_id=1, source_target_pairs={{0,2},{1,3},{2,0},{3,1},{4,6},{5,7},{6,4},{7,5},{8,10},{9,11},{10,... | collective-permute-start | bytes 3538952 | tf_op jit(solution)/shard_map/ppermute | solution.py:347
  255.8 40.1 %collective-permute-start.23 = (bf16[8,48,1920]{2,1,0:T(8,128)(2,1)}, bf16[8,48,1920]{2,1,0:T(8,128)(2,1)S(1)}, u32[]{:S(2)}, u32[]{:S(2)}) collective-permute-start(bf16[8,48,1920]{2,1,0:T(8,128)(2,1)} %get-tuple-element.118), channel_id=1, source_target_pairs={{0,16},{16,0},{1,17},{17,1},{2,18},{18,2},{3,19},{19,3},{4,20},{20... | collective-permute-start | bytes 4423688 | tf_op jit(solution)/shard_map/ppermute | solution.py:628
  260.0 33.7 %collective-permute-start.26 = (bf16[192,768]{1,0:T(8,128)(2,1)}, bf16[192,768]{1,0:T(8,128)(2,1)S(1)}, u32[]{:S(2)}, u32[]{:S(2)}) collective-permute-start(bf16[192,768]{1,0:T(8,128)(2,1)} %get-tuple-element.122), channel_id=1, source_target_pairs={{0,12},{1,13},{2,14},{3,15},{4,8},{5,9},{6,10},{7,11},{8,4},{9,5},... | collective-permute-start | bytes 884744 | tf_op jit(solution)/shard_map/ppermute | solution.py:347
  262.5 31.3 %collective-permute-start.25 = (bf16[192,768]{1,0:T(8,128)(2,1)}, bf16[192,768]{1,0:T(8,128)(2,1)}, u32[]{:S(2)}, u32[]{:S(2)}) collective-permute-start(bf16[192,768]{1,0:T(8,128)(2,1)} %get-tuple-element.121), channel_id=1, source_target_pairs={{0,8},{1,9},{2,10},{3,11},{4,12},{5,13},{6,14},{7,15},{8,0},{9,1},... | collective-permute-start | bytes 884744 | tf_op jit(solution)/shard_map/ppermute | solution.py:347
  262.5 31.3 %collective-permute-start.24 = (bf16[192,768]{1,0:T(8,128)(2,1)}, bf16[192,768]{1,0:T(8,128)(2,1)}, u32[]{:S(2)}, u32[]{:S(2)}) collective-permute-start(bf16[192,768]{1,0:T(8,128)(2,1)} %get-tuple-element.120), channel_id=1, source_target_pairs={{0,4},{1,5},{2,6},{3,7},{4,0},{5,1},{6,2},{7,3},{8,12},{9,13},{10,... | collective-permute-start | bytes 884744 | tf_op jit(solution)/shard_map/ppermute | solution.py:347
  311.4 23.3 %collective-permute-start.27 = (bf16[8,48,2304]{2,1,0:T(8,128)(2,1)}, bf16[8,48,2304]{2,1,0:T(8,128)(2,1)S(1)}, u32[]{:S(2)}, u32[]{:S(2)}) collective-permute-start(bf16[8,48,2304]{2,1,0:T(8,128)(2,1)} %get-tuple-element.136), channel_id=1, source_target_pairs={{0,1},{1,0},{2,3},{3,2},{4,5},{5,4},{6,7},{7,6},{8,9},{9,8},{10,11... | collective-permute-start | bytes 5308424 | tf_op jit(solution)/shard_map/ppermute | solution.py:347
  311.4 19.2 %collective-permute-start.29 = (bf16[4,48,1920]{2,1,0:T(8,128)(2,1)}, bf16[4,48,1920]{2,1,0:T(8,128)(2,1)}, u32[]{:S(2)}, u32[]{:S(2)}) collective-permute-start(bf16[4,48,1920]{2,1,0:T(8,128)(2,1)} %get-tuple-element.128), channel_id=1, source_target_pairs={{0,2},{1,3},{2,0},{3,1},{4,6},{5,7},{6,4},{7,5},{8,10},{9,11},{10,... | collective-permute-start | bytes 2211848 | tf_op jit(solution)/shard_map/ppermute | solution.py:347
  311.9 9.4 %collective-permute-start.28 = (bf16[192,768]{1,0:T(8,128)(2,1)}, bf16[192,768]{1,0:T(8,128)(2,1)}, u32[]{:S(2)}, u32[]{:S(2)}) collective-permute-start(bf16[192,768]{1,0:T(8,128)(2,1)} %add_convert_fusion.8), channel_id=1, source_target_pairs={{0,16},{16,0},{1,17},{17,1},{2,18},{18,2},{3,19},{19,3},{4,20},{20... | collective-permute-start | bytes 884744 | tf_op jit(solution)/shard_map/ppermute | solution.py:628
  340.9 21.4 %collective-permute-start.31 = (bf16[4,48,2304]{2,1,0:T(8,128)(2,1)}, bf16[4,48,2304]{2,1,0:T(8,128)(2,1)S(1)}, u32[]{:S(2)}, u32[]{:S(2)}) collective-permute-start(bf16[4,48,2304]{2,1,0:T(8,128)(2,1)} %get-tuple-element.144), channel_id=1, source_target_pairs={{0,2},{1,3},{2,0},{3,1},{4,6},{5,7},{6,4},{7,5},{8,10},{9,11},{10,... | collective-permute-start | bytes 2654216 | tf_op jit(solution)/shard_map/ppermute | solution.py:347
  348.3 22.1 %collective-permute-start.30 = (bf16[512,768]{1,0:T(8,128)(2,1)}, bf16[512,768]{1,0:T(8,128)(2,1)}, u32[]{:S(2)}, u32[]{:S(2)}) collective-permute-start(bf16[512,768]{1,0:T(8,128)(2,1)} %select_convert_fusion), channel_id=1, source_target_pairs={{0,16},{16,0},{1,17},{17,1},{2,18},{18,2},{3,19},{19,3},{4,20},{20... | collective-permute-start | bytes 2359304 | tf_op jit(solution)/shard_map/ppermute | solution.py:628
  354.4 22.1 %collective-permute-start.40 = (bf16[48,1920]{1,0:T(8,128)(2,1)}, bf16[48,1920]{1,0:T(8,128)(2,1)}, u32[]{:S(2)}, u32[]{:S(2)}) collective-permute-start(bf16[48,1920]{1,0:T(8,128)(2,1)} %get-tuple-element.142), channel_id=1, source_target_pairs={{0,12},{1,13},{2,14},{3,15},{4,8},{5,9},{6,10},{7,11},{8,4},{9,5},... | collective-permute-start | bytes 552968 | tf_op jit(solution)/shard_map/ppermute | solution.py:347
  356.9 26.2 %collective-permute-start.39 = (bf16[48,1920]{1,0:T(8,128)(2,1)}, bf16[48,1920]{1,0:T(8,128)(2,1)}, u32[]{:S(2)}, u32[]{:S(2)}) collective-permute-start(bf16[48,1920]{1,0:T(8,128)(2,1)} %get-tuple-element.141), channel_id=1, source_target_pairs={{0,8},{1,9},{2,10},{3,11},{4,12},{5,13},{6,14},{7,15},{8,0},{9,1},... | collective-permute-start | bytes 552968 | tf_op jit(solution)/shard_map/ppermute | solution.py:347
  356.9 26.2 %collective-permute-start.38 = (bf16[48,1920]{1,0:T(8,128)(2,1)}, bf16[48,1920]{1,0:T(8,128)(2,1)}, u32[]{:S(2)}, u32[]{:S(2)}) collective-permute-start(bf16[48,1920]{1,0:T(8,128)(2,1)} %get-tuple-element.140), channel_id=1, source_target_pairs={{0,4},{1,5},{2,6},{3,7},{4,0},{5,1},{6,2},{7,3},{8,12},{9,13},{10,... | collective-permute-start | bytes 552968 | tf_op jit(solution)/shard_map/ppermute | solution.py:347
  367.9 31.5 %collective-permute-start.42 = (bf16[48,2304]{1,0:T(8,128)(2,1)}, bf16[48,2304]{1,0:T(8,128)(2,1)}, u32[]{:S(2)}, u32[]{:S(2)}) collective-permute-start(bf16[48,2304]{1,0:T(8,128)(2,1)} %get-tuple-element.151), channel_id=1, source_target_pairs={{0,12},{1,13},{2,14},{3,15},{4,8},{5,9},{6,10},{7,11},{8,4},{9,5},... | collective-permute-start | bytes 663560 | tf_op jit(solution)/shard_map/ppermute | solution.py:347
  370.4 29.1 %collective-permute-start.41 = (bf16[48,2304]{1,0:T(8,128)(2,1)}, bf16[48,2304]{1,0:T(8,128)(2,1)}, u32[]{:S(2)}, u32[]{:S(2)}) collective-permute-start(bf16[48,2304]{1,0:T(8,128)(2,1)} %get-tuple-element.150), channel_id=1, source_target_pairs={{0,8},{1,9},{2,10},{3,11},{4,12},{5,13},{6,14},{7,15},{8,0},{9,1},... | collective-permute-start | bytes 663560 | tf_op jit(solution)/shard_map/ppermute | solution.py:347
  376.5 9.0 %collective-permute-start.32 = (f32[24,768]{1,0:T(8,128)S(1)}, f32[24,768]{1,0:T(8,128)S(1)}, u32[]{:S(2)}, u32[]{:S(2)}) collective-permute-start(f32[24,768]{1,0:T(8,128)S(1)} %concatenate.86), channel_id=1, source_target_pairs={{0,1},{1,0},{2,3},{3,2},{4,5},{5,4},{6,7},{7,6},{8,9},{9,8},{10,11... | collective-permute-start | bytes 221192 | tf_op jit(solution)/shard_map/ppermute | solution.py:622
  383.1 16.3 %collective-permute-start.37 = (bf16[48,2304]{1,0:T(8,128)(2,1)}, bf16[48,2304]{1,0:T(8,128)(2,1)S(1)}, u32[]{:S(2)}, u32[]{:S(2)}) collective-permute-start(bf16[48,2304]{1,0:T(8,128)(2,1)} %get-tuple-element.149), channel_id=1, source_target_pairs={{0,4},{1,5},{2,6},{3,7},{4,0},{5,1},{6,2},{7,3},{8,12},{9,13},{10,... | collective-permute-start | bytes 663560 | tf_op jit(solution)/shard_map/ppermute | solution.py:347
  384.3 13.5 %collective-permute-start.44 = (bf16[48,1920]{1,0:T(8,128)(2,1)S(1)}, bf16[48,1920]{1,0:T(8,128)(2,1)S(1)}, u32[]{:S(2)}, u32[]{:S(2)}) collective-permute-start(bf16[48,1920]{1,0:T(8,128)(2,1)S(1)} %add_convert_fusion.12), channel_id=1, source_target_pairs={{0,16},{16,0},{1,17},{17,1},{2,18},{18,2},{3,19},{19,3},{4,20},{20... | collective-permute-start | bytes 552968 | tf_op jit(solution)/shard_map/ppermute | solution.py:628
  385.6 4.4 %collective-permute-start.33 = (f32[24,768]{1,0:T(8,128)S(1)}, f32[24,768]{1,0:T(8,128)S(1)}, u32[]{:S(2)}, u32[]{:S(2)}) collective-permute-start(f32[24,768]{1,0:T(8,128)S(1)} %add.333), channel_id=1, source_target_pairs={{0,2},{1,3},{2,0},{3,1},{4,6},{5,7},{6,4},{7,5},{8,10},{9,11},{10,... | collective-permute-start | bytes 221192 | tf_op jit(solution)/shard_map/ppermute | solution.py:622
  390.0 4.5 %collective-permute-start.34 = (f32[24,768]{1,0:T(8,128)S(1)}, f32[24,768]{1,0:T(8,128)S(1)}, u32[]{:S(2)}, u32[]{:S(2)}) collective-permute-start(f32[24,768]{1,0:T(8,128)S(1)} %add.334), channel_id=1, source_target_pairs={{0,4},{1,5},{2,6},{3,7},{4,0},{5,1},{6,2},{7,3},{8,12},{9,13},{10,... | collective-permute-start | bytes 221192 | tf_op jit(solution)/shard_map/ppermute | solution.py:622
  394.5 5.6 %collective-permute-start.35 = (f32[24,768]{1,0:T(8,128)S(1)}, f32[24,768]{1,0:T(8,128)S(1)}, u32[]{:S(2)}, u32[]{:S(2)}) collective-permute-start(f32[24,768]{1,0:T(8,128)S(1)} %add.335), channel_id=1, source_target_pairs={{0,8},{1,9},{2,10},{3,11},{4,12},{5,13},{6,14},{7,15},{8,0},{9,1},... | collective-permute-start | bytes 221192 | tf_op jit(solution)/shard_map/ppermute | solution.py:622
  400.1 4.5 %collective-permute-start.36 = (f32[24,768]{1,0:T(8,128)S(1)}, f32[24,768]{1,0:T(8,128)S(1)}, u32[]{:S(2)}, u32[]{:S(2)}) collective-permute-start(f32[24,768]{1,0:T(8,128)S(1)} %add.336), channel_id=1, source_target_pairs={{0,16},{16,0},{1,17},{17,1},{2,18},{18,2},{3,19},{19,3},{4,20},{20... | collective-permute-start | bytes 221192 | tf_op jit(solution)/shard_map/ppermute | solution.py:628
  402.2 6.2 %collective-permute-start.43 = (bf16[48,2304]{1,0:T(8,128)(2,1)S(1)}, bf16[48,2304]{1,0:T(8,128)(2,1)S(1)}, u32[]{:S(2)}, u32[]{:S(2)}) collective-permute-start(bf16[48,2304]{1,0:T(8,128)(2,1)S(1)} %add_convert_fusion.11), channel_id=1, source_target_pairs={{0,16},{16,0},{1,17},{17,1},{2,18},{18,2},{3,19},{19,3},{4,20},{20... | collective-permute-start | bytes 663560 | tf_op jit(solution)/shard_map/ppermute | solution.py:628
  (54 other events, 353.5 us)

commit v5 on v4

--- a/solution.py
+++ b/solution.py
@@ -25,6 +25,16 @@
 small_cost = pl.CostEstimate(flops=1000, bytes_accessed=1000, transcendentals=0)
 norm_eps = 1e-05
 mask_fill = -1000000000.0
+erfc_poly = (
+    0.2367515965428487,
+    0.24062179898991767,
+    0.18865103029313968,
+    0.2877518531132804,
+    -0.1648672439458568,
+    0.4765735350541787,
+    -0.34041833366480423,
+    0.07493571514857543,
+)
 bf16 = jnp.bfloat16
 f32 = jnp.float32
 
@@ -69,16 +79,6 @@
     bins_x = jnp.stack([text_x, patch_x])
     bins_y = jnp.stack([text_y, patch_y])
     return (page_ids, pos_bins, bins_x, bins_y)
-
-
-def layer_norm(values, gain_vec, bias_vec):
-    centered = values - jnp.mean(values, axis=-1, keepdims=True)
-    variance = jnp.mean(centered * centered, axis=-1, keepdims=True)
-    return centered * lax.rsqrt(variance + norm_eps) * gain_vec + bias_vec
-
-
-def exact_gelu(values):
-    return jax.nn.gelu(values, approximate=False)
 
 
 def plain_dot(left_side, right_side):
@@ -355,24 +355,6 @@
     return (slot & 3) * 4 + (slot >> 2) * 2
 
 
-def place_kernel(place, *refs):
-    pieces, full_ref, sems = refs[:4], refs[4], refs[5]
-    rows = pieces[0].shape[1]
-    copies = []
-    for index in range(16):
-        mask = (index >> 2) * 4 + (index & 3)
-        at = pl.multiple_of((place[0] ^ mask) * rows, 16)
-        copies.append(
-            pltpu.make_async_copy(
-                pieces[index & 3].at[index >> 2], full_ref.at[pl.ds(at, rows)], sems.at[index]
-            )
-        )
-    for copy in copies:
-        copy.start()
-    for copy in copies:
-        copy.wait()
-
-
 def place_halves_kernel(place, *refs):
     pieces, full_ref, sems = refs[:4], refs[4], refs[5]
     rows, half = pieces[0].shape[1], pieces[0].shape[2]
@@ -420,83 +402,382 @@
     return jnp.stack(column_parts(shard))
 
 
-def grad_rows_kernel(page, x_ref, h_ref, keep_ref, send_ref, product):
+def start_rows(place, pieces, full, sems, first=0):
+    if len(pieces) == 1:
+        copies = [pltpu.make_async_copy(pieces[0], full, sems.at[first])]
+    else:
+        rows = pieces[0].shape[1]
+        copies = []
+        for index in range(16):
+            mask = (index >> 2) * 4 + (index & 3)
+            at = pl.multiple_of((place[0] ^ mask) * rows, 16)
+            copies.append(
+                pltpu.make_async_copy(
+                    pieces[index & 3].at[index >> 2],
+                    full.at[pl.ds(at, rows)],
+                    sems.at[first + index],
+                )
+            )
+    for copy in copies:
+        copy.start()
+    return copies
+
+
+def gelu_parts(values):
+    size = jnp.abs(values)
+    t = 1.0 / (1.0 + (0.42 * 0.7071067811865476) * size)
+    poly = jnp.full_like(t, erfc_poly[-1])
+    for coefficient in erfc_poly[-2::-1]:
+        poly = poly * t + coefficient
+    bell = jnp.exp(-0.5 * values * values)
+    tail = (0.5 * t) * (poly * bell)
+    cdf = jnp.where(values >= 0.0, 1.0 - tail, tail)
+    return values * cdf, cdf + (values * 0.3989422804014327) * bell
+
+
+def normalized(values):
+    centered = values - jnp.mean(values, axis=1, keepdims=True)
+    variance = jnp.mean(centered * centered, axis=1, keepdims=True)
+    scale = lax.rsqrt(variance + norm_eps)
+    return centered * scale, scale
+
+
+def norm_back(grads, unit, scale, gain):
+    scaled = grads * gain
+    mean = jnp.mean(scaled, axis=1, keepdims=True)
+    inner = jnp.mean(scaled * unit, axis=1, keepdims=True)
+    return scale * (scaled - mean - unit * inner)
+
+
+def up_kernel(place, context_ref, mixed_ref, vec_ref, bias_ref, *refs):
+    *pieces, unit_ref, scale_ref, low_ref, low_t_ref, active_ref, active_t_ref, slope_ref = refs[:-4]
+    weight, hidden, low, sems = refs[-4:]
+    step = pl.program_id(0)
+    tiles = pl.num_programs(0) - 1
+    width = context_ref.shape[1]
+    tile = active_ref.shape[1]
+
+    @pl.when(step == 0)
+    def _():
+        for copy in start_rows(place, pieces, weight, sems):
+            copy.wait()
+        branch = jnp.dot(context_ref[...], weight[:, :width], preferred_element_type=f32)
+        unit, scale = normalized(mixed_ref[...] + branch + vec_ref[0:1])
+        unit_ref[...] = unit
+        scale_ref[...] = jnp.broadcast_to(scale, scale_ref.shape)
+        normed = (unit * vec_ref[1:2] + vec_ref[2:3]).astype(bf16)
+        low[...] = normed
+        low_ref[...] = normed
+        low_t_ref[...] = normed.T
+
+    def product():
+        at = pl.multiple_of(width + step * tile, 128)
+        return jnp.dot(low[...], weight[:, pl.ds(at, tile)], preferred_element_type=f32)
+
+    def activate():
+        active, slope = gelu_parts(hidden[(step + 1) % 2] + bias_ref[...])
+        active = active.astype(bf16)
+        active_ref[...] = active
+        active_t_ref[...] = active.T
+        slope_ref[...] = slope
+
+    @pl.when(step == 0)
+    def _():
+        hidden[step % 2] = product()
+
+    @pl.when((step > 0) & (step < tiles))
+    def _():
+        hidden[step % 2] = product()
+        activate()
+
+    @pl.when(step == tiles)
+    def _():
+        activate()
+
+
+def any_specs(count):
+    return [pl.BlockSpec(memory_space=pl.ANY)] * count
+
+
+def up_forward(place, context, mixed, vectors, bias_up, pieces):
+    tokens, width = mixed.shape
+    hidden_width = bias_up.shape[1]
+    tile = 512
+    whole = lambda step, place: (0, 0)
+    last = lambda step, place: (0, jnp.maximum(step - 1, 0))
+    last_t = lambda step, place: (jnp.maximum(step - 1, 0), 0)
+    return pl.pallas_call(
+        up_kernel,
+        grid_spec=pltpu.PrefetchScalarGridSpec(
+            num_scalar_prefetch=1,
+            grid=(hidden_width // tile + 1,),
+            in_specs=[
+                pl.BlockSpec((tokens, width), whole),
+                pl.BlockSpec((tokens, width), whole),
+                pl.BlockSpec(vectors.shape, whole),
+                pl.BlockSpec((1, tile), last),
+            ]
+            + any_specs(len(pieces)),
+            out_specs=[
+                pl.BlockSpec((tokens, width), whole),
+                pl.BlockSpec((tokens, 128), whole),
+                pl.BlockSpec((tokens, width), whole),
+                pl.BlockSpec((width, tokens), whole),
+                pl.BlockSpec((tokens, tile), last),
+                pl.BlockSpec((tile, tokens), last_t),
+                pl.BlockSpec((tokens, tile), last),
+            ],
+            scratch_shapes=[
+                pltpu.VMEM((width, width + hidden_width), bf16),
+                pltpu.VMEM((2, tokens, tile), f32),
+                pltpu.VMEM((tokens, width), bf16),
+                pltpu.SemaphoreType.DMA((16,)),
+            ],
+        ),
+        out_shape=[
+            jax.ShapeDtypeStruct((tokens, width), f32),
+            jax.ShapeDtypeStruct((tokens, 128), f32),
+            jax.ShapeDtypeStruct((tokens, width), bf16),
+            jax.ShapeDtypeStruct((width, tokens), bf16),
+            jax.ShapeDtypeStruct((tokens, hidden_width), bf16),
+            jax.ShapeDtypeStruct((hidden_width, tokens), bf16),
+            jax.ShapeDtypeStruct((tokens, hidden_width), f32),
+        ],
+        cost_estimate=small_cost,
+        name="up_forward",
+    )(place, context, mixed, vectors, bias_up, *pieces)
+
+
+def down_kernel(place, active_ref, unit_ref, vec_ref, grad_ref, *refs):
+    *pieces, out_ref, sum_ref, low_ref, small_ref = refs[:-2]
+    weight, sems = refs[-2:]
+    for copy in start_rows(place, pieces, weight, sems):
+        copy.wait()
+    tokens, width = unit_ref.shape
+    half = tokens // 2
+    smalls = [jnp.zeros((1, width), f32)] * 3
+    for part in range(2):
+        rows = pl.ds(part * half, half)
+        ffn = jnp.dot(active_ref[rows, :], weight[...], preferred_element_type=f32)
+        normed = unit_ref[rows, :] * vec_ref[1:2] + vec_ref[2:3]
+        unit, scale = normalized(normed + ffn + vec_ref[3:4])
+        out_ref[rows, :] = (unit * vec_ref[4:5] + vec_ref[5:6]).astype(bf16)
+        grads = grad_ref[rows, :].astype(f32)
+        total = norm_back(grads, unit, scale, vec_ref[4:5])
+        low = total.astype(bf16)
+        sum_ref[rows, :] = total
+        low_ref[rows, :] = low
+        for index, term in enumerate((grads * unit, grads, low.astype(f32))):
+            smalls[index] = smalls[index] + jnp.sum(term, axis=0, keepdims=True)
+    small_ref[...] = jnp.concatenate(smalls + [jnp.zeros((5, width), f32)], axis=0)
+
+
+def down_forward(place, active, unit, vectors, grads, pieces):
+    tokens, width = unit.shape
+    hidden_width = active.shape[1]
+    vmem = pl.BlockSpec(memory_space=pltpu.VMEM)
+    return pl.pallas_call(
+        down_kernel,
+        grid_spec=pltpu.PrefetchScalarGridSpec(
+            num_scalar_prefetch=1,
+            grid=(),
+            in_specs=[vmem] * 4 + any_specs(len(pieces)),
+            out_specs=[vmem] * 4,
+            scratch_shapes=[
+                pltpu.VMEM((hidden_width, width), bf16),
+                pltpu.SemaphoreType.DMA((16,)),
+            ],
+        ),
+        out_shape=[
+            jax.ShapeDtypeStruct((tokens, width), bf16),
+            jax.ShapeDtypeStruct((tokens, width), f32),
+            jax.ShapeDtypeStruct((tokens, width), bf16),
+            jax.ShapeDtypeStruct((8, width), f32),
+        ],
+        cost_estimate=small_cost,
+        name="down_forward",
+    )(place, active, unit, vectors, grads, *pieces)
+
+
+def ffn_back_kernel(count, place, low_ref, slope_ref, sum_ref, unit_ref, scale_ref, vec_ref, *refs):
+    rest, down = refs[:count], refs[count : 2 * count]
+    hidden_ref, bias_ref, first_ref, branch_ref, context_ref, small_ref = refs[2 * count : -4]
+    weight, weight_down, total, sems = refs[-4:]
+    step = pl.program_id(0)
+    tokens, width = unit_ref.shape
+    tile = slope_ref.shape[1]
+    half = tokens // 2
+
+    @pl.when(step == 0)
+    def _():
+        copies = start_rows(place, down, weight_down, sems)
+        copies += start_rows(place, rest, weight, sems, 16)
+        total[...] = sum_ref[...]
+        for copy in copies:
+            copy.wait()
+
+    rows_down = weight_down[pl.ds(pl.multiple_of(step * tile, 128), tile), :]
+    columns = weight[:, pl.ds(pl.multiple_of(width + step * tile, 128), tile)]
+    bias = jnp.zeros((1, tile), f32)
+    for part in range(2):
+        rows = pl.ds(part * half, half)
+        grads = (dot_right_t(low_ref[rows, :], rows_down) * slope_ref[rows, :]).astype(bf16)
+        hidden_ref[rows, :] = grads
+        bias = bias + jnp.sum(grads.astype(f32), axis=0, keepdims=True)
+        total[rows, :] += dot_right_t(grads, columns)
+    bias_ref[...] = bias
+
+    @pl.when(step == pl.num_programs(0) - 1)
+    def _():
+        grads = total[...]
+        unit = unit_ref[...]
+        first = norm_back(grads, unit, scale_ref[:, 0:1], vec_ref[1:2])
+        branch = first.astype(bf16)
+        first_ref[...] = first
+        branch_ref[...] = branch
+        context_ref[...] = dot_right_t(branch, weight[:, :width]).astype(bf16)
+        smalls = [
+            jnp.sum(term, axis=0, keepdims=True)
+            for term in (grads * unit, grads, branch.astype(f32))
+        ]
+        small_ref[...] = jnp.concatenate(smalls + [jnp.zeros((5, width), f32)], axis=0)
+
+
+def ffn_back(place, low, slope, total, unit, scale, vectors, pieces_rest, pieces_down):
+    tokens, width = unit.shape
+    hidden_width = slope.shape[1]
+    tile = 512
+    count = len(pieces_rest)
+    whole = lambda step, place: (0, 0)
+    column = lambda step, place: (0, step)
+    return pl.pallas_call(
+        functools.partial(ffn_back_kernel, count),
+        grid_spec=pltpu.PrefetchScalarGridSpec(
+            num_scalar_prefetch=1,
+            grid=(hidden_width // tile,),
+            in_specs=[
+                pl.BlockSpec((tokens, width), whole),
+                pl.BlockSpec((tokens, tile), column),
+                pl.BlockSpec((tokens, width), whole),
+                pl.BlockSpec((tokens, width), whole),
+                pl.BlockSpec((tokens, 128), whole),
+                pl.BlockSpec(vectors.shape, whole),
+            ]
+            + any_specs(2 * count),
+            out_specs=[
+                pl.BlockSpec((tokens, tile), column),
+                pl.BlockSpec((1, tile), column),
+                pl.BlockSpec((tokens, width), whole),
+                pl.BlockSpec((tokens, width), whole),
+                pl.BlockSpec((tokens, width), whole),
+                pl.BlockSpec((8, width), whole),
+            ],
+            scratch_shapes=[
+                pltpu.VMEM((width, width + hidden_width), bf16),
+                pltpu.VMEM((hidden_width, width), bf16),
+                pltpu.VMEM((tokens, width), f32),
+                pltpu.SemaphoreType.DMA((32,)),
+            ],
+        ),
+        out_shape=[
+            jax.ShapeDtypeStruct((tokens, hidden_width), bf16),
+            jax.ShapeDtypeStruct((1, hidden_width), f32),
+            jax.ShapeDtypeStruct((tokens, width), f32),
+            jax.ShapeDtypeStruct((tokens, width), bf16),
+            jax.ShapeDtypeStruct((tokens, width), bf16),
+            jax.ShapeDtypeStruct((8, width), f32),
+        ],
+        cost_estimate=small_cost,
+        name="ffn_back",
+    )(place, low, slope, total, unit, scale, vectors, *pieces_rest, *pieces_down)
+
+
+def grad_rows_kernel(place, mine_ref, theirs_ref, h_ref, keep_ref, send_ref):
     rows = keep_ref.shape[1]
-    product[...] = dot_left_t(x_ref[...], h_ref[...])
-    mine = pl.multiple_of((page[0] & 1) * rows, 16)
-    theirs = pl.multiple_of((1 - (page[0] & 1)) * rows, 16)
-    keep_ref[0] = product[pl.ds(mine, rows), :].astype(bf16)
-    send_ref[0] = product[pl.ds(theirs, rows), :].astype(bf16)
-
-
-def grad_by_rows(inputs, grads, page):
-    tokens, width = inputs.shape
+    both = jnp.concatenate([mine_ref[0], theirs_ref[0]], axis=0)
+    product = jnp.dot(both, h_ref[...], preferred_element_type=f32)
+    keep_ref[0] = product[:rows].astype(bf16)
+    send_ref[0] = product[rows:].astype(bf16)
+
+
+def grad_by_rows(inputs_t, grads, place):
+    width, tokens = inputs_t.shape
     columns = grads.shape[1]
     rows = width // 16
-
-    def slot(block, page):
-        mask = block ^ (page[0] >> 1)
-        return ((mask & 1) * 4 + (mask >> 1), 0, 0)
-
+    inputs_t = inputs_t.reshape(16, rows, tokens)
     half = jax.ShapeDtypeStruct((8, rows, columns), bf16)
+    out = pl.BlockSpec((1, rows, columns), lambda slot, place: (slot, 0, 0))
     return pl.pallas_call(
         grad_rows_kernel,
         grid_spec=pltpu.PrefetchScalarGridSpec(
             num_scalar_prefetch=1,
             grid=(8,),
             in_specs=[
-                pl.BlockSpec((tokens, 2 * rows), lambda block, page: (0, block)),
-                pl.BlockSpec((tokens, columns), lambda block, page: (0, 0)),
+                pl.BlockSpec((1, rows, tokens), lambda slot, place: (place[0] ^ slot_mask(slot), 0, 0)),
+                pl.BlockSpec(
+                    (1, rows, tokens), lambda slot, place: (place[0] ^ (slot_mask(slot) + 1), 0, 0)
+                ),
+                pl.BlockSpec((tokens, columns), lambda slot, place: (0, 0)),
             ],
-            out_specs=[pl.BlockSpec((1, rows, columns), slot)] * 2,
-            scratch_shapes=[pltpu.VMEM((2 * rows, columns), f32)],
+            out_specs=[out, out],
         ),
         out_shape=[half, half],
         cost_estimate=small_cost,
         name="grad_rows",
-    )(page, inputs, grads)
-
-
-def grad_columns_kernel(parts, page, *refs):
-    ins, keep_ref, send_ref, product = refs[: 2 * len(parts)], refs[-3], refs[-2], refs[-1]
-    rows, width = keep_ref.shape[1], keep_ref.shape[2]
+    )(place, inputs_t, inputs_t, grads)
+
+
+def grad_columns_kernel(parts, place, *refs):
+    count = len(parts)
+    ins, keep_ref, send_ref, scratch = (
+        refs[: 2 * count],
+        refs[2 * count],
+        refs[2 * count + 1],
+        refs[2 * count + 2 :],
+    )
+    rows, tile = keep_ref.shape[1], keep_ref.shape[2]
     step = pl.program_id(0)
     first = 0
-    for index, count in enumerate(parts):
-        x_ref, h_ref = ins[2 * index], ins[2 * index + 1]
-
-        @pl.when((step >= first) & (step < first + count))
+    for index, steps in enumerate(parts):
+        x_ref, h_ref, ordered = ins[2 * index], ins[2 * index + 1], scratch[index]
+
+        @pl.when(step == first)
         def _():
-            product[...] = dot_left_t(x_ref[...], h_ref[...])
-
-        first = first + count
-    for slot in range(8):
-        mask = slot_mask(slot)
-        mine = pl.multiple_of((page[0] ^ mask) * rows, 16)
-        theirs = pl.multiple_of((page[0] ^ (mask + 1)) * rows, 16)
-        keep_ref[slot] = product[pl.ds(mine, rows), :].astype(bf16)
-        send_ref[slot] = product[pl.ds(theirs, rows), :].astype(bf16)
-
-
-def grad_by_columns(pairs, page, tile):
-    width = pairs[0][0].shape[1]
+            for slot in range(16):
+                mask = slot_mask(slot & 7) + (slot >> 3)
+                at = pl.multiple_of((place[0] ^ mask) * rows, 16)
+                ordered[pl.ds(slot * rows, rows), :] = x_ref[pl.ds(at, rows), :]
+
+        @pl.when((step >= first) & (step < first + steps))
+        def _():
+            product = jnp.dot(ordered[...], h_ref[...], preferred_element_type=f32).astype(bf16)
+            keep_ref[...] = product[: 8 * rows].reshape(8, rows, tile)
+            send_ref[...] = product[8 * rows :].reshape(8, rows, tile)
+
+        first = first + steps
+
+
+def grad_by_columns(pairs, place, tile):
+    width = pairs[0][0].shape[0]
     rows = width // 16
-    parts = tuple(grads.shape[1] // tile for _, grads in pairs)
+    parts = tuple(sum(grad.shape[1] for grad in grads) // tile for _, _, *grads in pairs)
     steps = sum(parts)
     specs = []
     operands = []
+    scratch = []
     first = 0
-    flops = 0
-    for (inputs, grads), count in zip(pairs, parts):
-        specs.append(pl.BlockSpec(inputs.shape, lambda step, page: (0, 0)))
-
-        def column(step, page, first=first, count=count):
+    for (inputs_t, own, *grads), count in zip(pairs, parts):
+        tokens = grads[0].shape[0]
+        block = (lambda step, place: (0, place[1])) if own else (lambda step, place: (0, 0))
+        specs.append(pl.BlockSpec((width, tokens), block))
+
+        def column(step, place, first=first, count=count):
             return (0, jnp.clip(step - first, 0, count - 1))
 
-        specs.append(pl.BlockSpec((grads.shape[0], tile), column))
-        operands += [inputs, grads]
+        specs.append(pl.BlockSpec((tokens, tile), column))
+        operands += [inputs_t, *grads]
+        scratch.append(pltpu.VMEM((width, tokens), bf16))
         first = first + count
-        flops = flops + 2 * inputs.shape[0] * width * grads.shape[1]
     half = jax.ShapeDtypeStruct((8, rows, steps * tile), bf16)
     return pl.pallas_call(
         functools.partial(grad_columns_kernel, parts),
@@ -504,13 +785,13 @@
             num_scalar_prefetch=1,
             grid=(steps,),
             in_specs=specs,
-            out_specs=[pl.BlockSpec((8, rows, tile), lambda step, page: (0, 0, step))] * 2,
-            scratch_shapes=[pltpu.VMEM((width, tile), f32)],
+            out_specs=[pl.BlockSpec((8, rows, tile), lambda step, place: (0, 0, step))] * 2,
+            scratch_shapes=scratch,
         ),
         out_shape=[half, half],
         cost_estimate=small_cost,
         name="grad_columns",
-    )(page, *operands)
+    )(place, *operands)
 
 
 def first_half_kernel(place, keep_near, part_near, keep_far, part_far, held_ref, out_ref):
@@ -594,7 +875,7 @@
 
 
 def summed_rows(pairs):
-    grads = jnp.concatenate([dot_left_t(*pair).astype(bf16) for pair in pairs], axis=1)
+    grads = jnp.concatenate([plain_dot(*pair).astype(bf16) for pair in pairs], axis=1)
     shard = lax.psum_scatter(grads, "page", scatter_dimension=0, tiled=True)
     return shard.astype(f32) + swap(shard).astype(f32)
 
@@ -712,8 +993,9 @@
         [jnp.where(is_text, mixed_low, other_mixed), jnp.where(is_text, other_mixed, mixed_low)],
         axis=0,
     )
+    mixed_t = mixed_all.T
     if fast:
-        full_qkv = after(full_qkv, mixed_all, features, tables, bounds, own_flip)
+        full_qkv = after(full_qkv, mixed_all, mixed_t, features, tables, bounds, own_flip)
     full_query = full_qkv[:, :d_model]
     full_kv = full_qkv[:, d_model:]
     queries = ((plain_dot(mixed_low, full_query) + b_query).astype(bf16) * 0.125).astype(bf16)
@@ -725,69 +1007,52 @@
         column_down = jnp.stack([after(part, context) for part in parts_down])
         across_rest = after(across_rest, column_down)
         pieces_rest = [column_rest, exchange(column_rest, 1), across_rest, exchange(across_rest, 1)]
-        full_rest = place_rows(place, pieces_rest, pack_rest.shape[1], place_kernel)
     else:
-        full_rest = lax.all_gather(pack_rest, "page", axis=0, tiled=True)
-    full_out = full_rest[:, :d_model]
-    full_up = full_rest[:, d_model:]
-
-    first_sum = mixed + plain_dot(context, full_out) + b_out
-    normed, norm_one_pull = jax.vjp(layer_norm, first_sum, gain_one, bias_one)
-    normed_low = normed.astype(bf16)
-    hidden = plain_dot(normed_low, full_up) + b_up
-    active, gelu_pull = jax.vjp(exact_gelu, hidden)
-    active_low = active.astype(bf16)
+        pieces_rest = [lax.all_gather(pack_rest, "page", axis=0, tiled=True)]
+    vectors = jnp.stack(
+        [b_out, gain_one, bias_one, b_down, gain_two, bias_two, jnp.zeros_like(b_out), b_out]
+    )
+    unit, scale, normed_low, normed_t, active, active_t, slope = up_forward(
+        place, context, mixed, vectors, b_up[None], pieces_rest
+    )
     if fast:
-        across_down = after(exchange(column_down, 2), normed_low)
+        across_down = exchange(column_down, 2)
         pieces_down = [column_down, exchange(column_down, 1), across_down, exchange(across_down, 1)]
-        pieces_down[0] = after(pieces_down[0], active_low)
-        full_down = place_rows(place, pieces_down, d_model, place_kernel)
+        pieces_down[0] = after(pieces_down[0], active)
     else:
-        full_down = lax.all_gather(w_down, "page", axis=0, tiled=True)
-    ffn_out = plain_dot(active_low, full_down) + b_down
-    output_row, norm_two_pull = jax.vjp(layer_norm, normed + ffn_out, gain_two, bias_two)
-    grad_out = cotangent[0, 0].astype(f32)
-    grad_sum_two, grad_gain_two, grad_bias_two = norm_two_pull(grad_out)
-    grad_ffn = grad_sum_two.astype(bf16)
-    grad_b_down = column_sum(grad_ffn)
-    grad_hidden_in = grad_ffn
+        pieces_down = [lax.all_gather(w_down, "page", axis=0, tiled=True)]
+    output_row, grad_sum_two, grad_ffn, small_two = down_forward(
+        place, active, unit, vectors, cotangent[0, 0], pieces_down
+    )
+    grad_ffn_in = grad_ffn
     if fast:
-        keep_down, send_down = grad_by_rows(active_low, grad_ffn, place)
+        keep_down, send_down = grad_by_rows(active_t, grad_ffn, place)
         partner_down = exchange(send_down, 1)
-        grad_hidden_in = after(grad_ffn, keep_down, send_down)
-    else:
-        shard_down = summed_rows([(active_low, grad_ffn)])
-    (grad_hidden_f,) = gelu_pull(dot_right_t(grad_hidden_in, full_down))
-    grad_hidden = grad_hidden_f.astype(bf16)
-    grad_b_up = column_sum(grad_hidden)
-    grad_up_in = grad_hidden
-    if fast:
-        partner_down = after(partner_down, grad_hidden)
+        context_t = after(context, send_down).T
+        partner_down = after(partner_down, context_t)
         held_down, across_out_down = halve_across(place, keep_down, partner_down)
         across_down = exchange(across_out_down, 2)
-        grad_up_in = after(grad_hidden, across_out_down)
-    grad_normed = grad_sum_two + dot_right_t(grad_up_in, full_up)
-    grad_first, grad_gain_one, grad_bias_one = norm_one_pull(grad_normed)
-    grad_branch = grad_first.astype(bf16)
-    grad_b_out = column_sum(grad_branch)
-    pairs = [(context, grad_branch), (normed_low, grad_hidden)]
-    grad_context_in = grad_branch
+        grad_ffn_in = after(grad_ffn, across_out_down)
+    else:
+        shard_down = summed_rows([(active_t, grad_ffn)])
+        context_t = context.T
+    grad_hidden, grad_b_up, grad_first, grad_branch, grad_context, small_one = ffn_back(
+        place, grad_ffn_in, slope, grad_sum_two, unit, scale, vectors, pieces_rest, pieces_down
+    )
+    attend_in = grad_context
     if fast:
+        pairs = [(context_t, False, grad_branch), (normed_t, False, grad_hidden)]
         keep_rest, send_rest = grad_by_columns(pairs, place, d_model)
         partner_rest = exchange(send_rest, 1)
         across_down = after(across_down, send_rest)
-        grad_context_in = after(grad_branch, keep_rest, across_down)
-    else:
-        shard_rest = summed_rows(pairs)
-    grad_context = dot_right_t(grad_context_in, full_out).astype(bf16)
-    attend_in = grad_context
-    if fast:
-        partner_rest = after(partner_rest, grad_context)
+        own_down, sends_down = column_sends(held_down, across_down)
+        arrived_down = column_arrivals(sends_down)
+        partner_rest = after(partner_rest, *sends_down)
         held_rest, plane_out = halve_plane(place, keep_rest, partner_rest)
         plane_rest = swap(plane_out)
-        own_down, sends_down = column_sends(held_down, across_down)
-        arrived_down = column_arrivals(sends_down)
-        attend_in = after(grad_context, plane_out, *sends_down)
+        attend_in = after(grad_context, plane_out)
+    else:
+        shard_rest = summed_rows([(context_t, grad_branch), (normed_t, grad_hidden)])
     grad_queries, grad_keys, grad_values, grad_tables = attend_back(
         bounds, queries, keys_values, attend_in, features, own_feats, own_flip, tables, 0, PAIRS
     )
@@ -800,7 +1065,7 @@
         total_down = column_total(own_down, arrived_down)
         far_down = swap(total_down)
         grad_queries_in = after(grad_queries, across_out_rest, total_down)
-    pairs = [(mixed_low, grad_queries_in), (mixed_all, grad_keys), (mixed_all, grad_values)]
+    pairs = [(mixed_t, True, grad_queries_in), (mixed_t, False, grad_keys), (mixed_t, False, grad_values)]
     if fast:
         keep_qkv, send_qkv = grad_by_columns(pairs, place, d_model)
         partner_qkv = exchange(send_qkv, 1)
@@ -813,7 +1078,9 @@
         across_qkv = exchange(across_out_qkv, 2)
         grad_keys_in = after(grad_keys, across_out_qkv)
     else:
-        shard_qkv = summed_rows(pairs)
+        shard_qkv = summed_rows(
+            [(mixed_low.T, grad_queries), (mixed_t, grad_keys), (mixed_t, grad_values)]
+        )
     grad_b_query = column_sum(grad_queries)
     grad_b_value = column_sum(grad_values)
     from_keys = dot_right_t(grad_keys_in, full_kv[:, :d_model]) + dot_right_t(
@@ -844,12 +1111,10 @@
             grad_conv_b[None],
             grad_b_query,
             grad_b_value,
-            grad_b_out,
-            grad_gain_one[None],
-            grad_bias_one[None],
-            grad_b_down,
-            grad_gain_two[None],
-            grad_bias_two[None],
+            small_one[2:3],
+            small_one[0:2],
+            small_two[2:3],
+            small_two[0:2],
             grad_b_up.reshape(d_ff // d_model, d_model),
             table_rows,
             jnp.zeros((2, d_model), f32),
@@ -874,7 +1139,7 @@
             jnp.concatenate([far_rest, total_rest], axis=1),
         ).astype(f32)
     return (
-        output_row.astype(bf16)[None, None],
+        output_row[None, None],
         grad_in.astype(bf16)[None, None],
         packed[0:3],
         packed[3],

time: 415 us -> 407 us (0.981)
  matrix products: 68.1 us -> 17.8 us
  Pallas kernels: 121 us -> 157 us
  local copies, waits for them, and re-layouts: 27.4 us -> 39.3 us
  other arithmetic: 42.6 us -> 37.3 us
    pallas_call x0 -> x3, Pallas kernels: none -> 48.9 us  [the longest x1 19.4 us: up_forward(): pl.pallas_call(up_kernel, grid_spec=pltpu.PrefetchScalarGridSpec(num_scal...]
    dot_general x5 -> x2, matrix products: 37 us -> 9.66 us  [plain_dot(): return jnp.dot(left_side, right_side, preferred_element_type=f32)]
    dot_general x6 -> x3, matrix products: 31.1 us -> 8.19 us  [dot_right_t(): lax.dot_general(left_side, right_side, (((1,), (1,)), ((), ())), preferre...]
    pallas_call x3 -> x1, Pallas kernels: 16.3 us -> 4.85 us  [place_rows(): pl.pallas_call(kernel, grid_spec=pltpu.PrefetchScalarGridSpec(num_scalar_...]
    ppermute x33, waiting for transfers between devices: 88.9 us -> 82 us  [exchange(): return lax.ppermute(values, 'page', [(i, i ^ mask) for i in range(count)])]
    slice x0 -> x4, local copies, waits for them, and re-layouts: none -> 5.3 us  [the longest x1 1.33 us: local(): small_two[0:2]]
    ppermute x33, starting transfers between devices: 31.7 us -> 36.7 us  [exchange(): return lax.ppermute(values, 'page', [(i, i ^ mask) for i in range(count)])]
    reduce_sum x6 -> x0, other arithmetic: 4.9 us -> none  [the longest x2 2.25 us: layer_norm(): centered = values - jnp.mean(values, axis=-1, keepdims=True)]
  transfers between devices with their start and end apart: 45 -> 45, of which waited for: 15 -> 12; matrix products, arithmetic and copies ran while one was open for 27% -> 22% of each run, Pallas kernels for 16% -> 20%
where the time goes in v5:
time: 407 us; the launch traced here: 401 us
  Pallas kernels  157 us (39%)
  waiting for transfers between devices  99.3 us (24%)
  starting transfers between devices  48.5 us (12%)
  local copies, waits for them, and re-layouts  39.3 us (10%)
  other arithmetic  37.3 us (9%)
  matrix products  17.8 us (4%)
    ppermute x33, waiting for transfers between devices, exchange(): return lax.ppermute(values, 'page', [(i, i ^ mask) for i in range(count)])  82 us
    ppermute x33, starting transfers between devices, exchange(): return lax.ppermute(values, 'page', [(i, i ^ mask) for i in range(count)])  36.7 us
    pallas_call x1, Pallas kernels, attend_back(): pl.pallas_call(attend_back_kernel, grid_spec=pltpu.PrefetchScalarGridSpec...  29.4 us
    pallas_call x4, Pallas kernels, halve_call(): pl.pallas_call(first_half_kernel, grid_spec=pltpu.PrefetchScalarGridSpec(...  21.1 us
    pallas_call x1, Pallas kernels, up_forward(): pl.pallas_call(up_kernel, grid_spec=pltpu.PrefetchScalarGridSpec(num_scal...  19.4 us
    pallas_call x1, Pallas kernels, ffn_back(): pl.pallas_call(functools.partial(ffn_back_kernel, count), grid_spec=pltpu...  18.8 us
    pallas_call x2, Pallas kernels, grad_by_columns(): pl.pallas_call(functools.partial(grad_columns_kernel, parts), grid_spec=p...  18.6 us
    unnamed x101, local copies, waits for them, and re-layouts  13.9 us
  transfers between devices with their start and end apart: 45, of which 12 were waited for; matrix products, arithmetic and copies ran while one was open for 22% of the time, Pallas kernels for 20%

profile of v5, /device:TPU:0, one launch (start us, length us, event | category | flops | bytes accessed | tf_op | source)
XLA Modules:
  0.0 400.9 jit_solution(4817365141696341024)
XLA Ops:
  2.4 5.0 %collective-permute-start.2 = (bf16[48,1152]{1,0:T(8,128)(2,1)}, bf16[48,1152]{1,0:T(8,128)(2,1)}, u32[]{:S(2)}, u32[]{:S(2)}) collective-permute-start(bf16[48,1152]{1,0:T(8,128)(2,1)} %get-tuple-element.279), channel_id=1, source_target_pairs={{0,12},{1,13},{2,14},{3,15},{4,8},{5,9},{6,10},{7,11},{8,4},{9,5},... | collective-permute-start | bytes 331784 | tf_op jit(solution)/shard_map/ppermute | solution.py:347
  9.5 1.8 collective-permute-start.10
  17.4 1.7 fusion.26
  28.6 4.7 %collective-permute-done.3 = bf16[4,48,1152]{2,1,0:T(8,128)(2,1)S(1)} collective-permute-done((bf16[4,48,1152]{2,1,0:T(8,128)(2,1)S(1)}, bf16[4,48,1152]{2,1,0:T(8,128)(2,1)S(1)}, u32[]{:S(2)}, u32[]{:S(2)}) %collective-permute-start.3) | collective-permute-done | bytes 442400 | tf_op jit(solution)/shard_map/ppermute | solution.py:347
  36.0 3.6 collective-permute-start.7
  41.0 2.6 broadcast_select_fusion.1
  43.7 10.1 %collective-permute-done.4.refs_2_ = bf16[8,48,1152]{2,1,0:T(8,128)(2,1)} collective-permute-done((bf16[8,48,1152]{2,1,0:T(8,128)(2,1)}, bf16[8,48,1152]{2,1,0:T(8,128)(2,1)}, u32[]{:S(2)}, u32[]{:S(2)}) %collective-permute-start.4) | collective-permute-done | bytes 884768 | tf_op jit(solution)/shard_map/ppermute | solution.py:909
  55.3 13.6 %collective-permute-done.6 = bf16[48,3840]{1,0:T(8,128)(2,1)S(1)} collective-permute-done((bf16[48,3840]{1,0:T(8,128)(2,1)S(1)}, bf16[48,3840]{1,0:T(8,128)(2,1)S(1)}, u32[]{:S(2)}, u32[]{:S(2)}) %collective-permute-start.6) | collective-permute-done | bytes 368672 | tf_op jit(solution)/shard_map/ppermute | solution.py:347
  70.3 2.4 collective-permute-start.15
  72.7 2.0 collective-permute-start.13
  76.2 4.8 %place_rows.1 = bf16[768,2304]{1,0:T(8,128)(2,1)} custom-call(s32[2]{0:T(128)} %pad_add_fusion.1.place, bf16[8,48,1152]{2,1,0:T(8,128)(2,1)} %constant_dynamic-update-slice_fusion.refs_0_, bf16[8,48,1152]{2,1,0:T(8,128)(2,1)} %collective-permute-done.8.refs_1_, bf16[8,48,1152]{2,1,0:T(8,128)(2,1)} %collective-permute-done.4.refs_2_, ...), custom_call_target="tpu_custom_call" | custom-call | flops 1000 | bytes 1000 | tf_op jit(solution)/shard_map/place_rows/pallas_call | solution.py:382
  81.1 6.7 %add_convert_fusion.k_ref.v_ref = bf16[1024,1536]{1,0:T(8,128)(2,1)} fusion(f32[1536]{0:T(1024)S(1)} %concatenate.85, bf16[768,2304]{1,0:T(8,128)(2,1)} %place_rows.1, bf16[512,768]{0,1:T(8,128)(2,1)} %copy-done.11, bf16[512,768]{0,1:T(8,128)(2,1)} %copy-done.10), kind=kOutput, calls=%fused_computation | convolution fusion | flops 2422210560 | bytes 7084032 | tf_op jit(solution)/shard_map/dot_general | solution.py:85
  87.8 3.0 fusion.3.q_ref
  90.7 12.9 %attend.1.context_ref = bf16[512,768]{1,0:T(8,128)(2,1)} custom-call(s32[48]{0:T(128)} %concatenate.67.bounds, bf16[512,768]{1,0:T(8,128)(2,1)} %fusion.3.q_ref, bf16[1024,1536]{1,0:T(8,128)(2,1)} %add_convert_fusion.k_ref.v_ref, bf16[1024,1536]{1,0:T(8,128)(2,1)} %add_convert_fusion.k_ref.v_ref, bf16[1024,128]{1,0:T(8,128)(2,1)} %copy-done.9, ...), custom_call_target="tpu_custom_call" | custom-call | flops 1000 | bytes 1000 | tf_op jit(solution)/shard_map/attend/pallas_call | solution.py:273
  103.8 2.3 pad_maximum_fusion.2.refs_0_.refs_4_
  108.8 23.9 %collective-permute-done.18.refs_2_.refs_6_ = bf16[4,192,768]{2,1,0:T(8,128)(2,1)} collective-permute-done((bf16[4,192,768]{2,1,0:T(8,128)(2,1)}, bf16[4,192,768]{2,1,0:T(8,128)(2,1)}, u32[]{:S(2)}, u32[]{:S(2)}) %collective-permute-start.18) | collective-permute-done | bytes 1179680 | tf_op jit(solution)/shard_map/ppermute | solution.py:347
  135.1 19.4 %up_forward.1 = (f32[512,768]{1,0:T(8,128)}, f32[512,128]{1,0:T(8,128)}, bf16[512,768]{1,0:T(8,128)(2,1)}, bf16[768,512]{1,0:T(8,128)(2,1)}, bf16[512,3072]{1,0:...) custom-call(s32[2]{0:T(128)} %pad_add_fusion.1.place, bf16[512,768]{1,0:T(8,128)(2,1)} %attend.1.context_ref, ...), custom_call_target="tpu_custom_call" | custom-call | flops 1000 | bytes 1000 | tf_op jit(solution)/shard_map/up_forward/pallas_call | solution.py:509
  154.6 10.7 %down_forward.1 = (bf16[512,768]{1,0:T(8,128)(2,1)}, f32[512,768]{1,0:T(8,128)}, bf16[512,768]{1,0:T(8,128)(2,1)}, f32[8,768]{1,0:T(8,128)}) custom-call(s32[2]{0:T(128)} %pad_add_fusion.1.place, bf16[512,3072]{1,0:T(8,128)(2,1)} %get-tuple-element.119.active_ref, f32[512,768]{1,0:T(8,128)} %get-tuple-element.120.unit_ref, f32[8,768]{1,0:T(8,128)} %stack.127.vec_ref, ...), custom_call_target="tpu_custom_call" | custom-call | flops 1000 | bytes 1000 | tf_op jit(solution)/shard_map/down_forward/pallas_call | solution.py:579
  165.3 9.1 %grad_rows.1 = (bf16[8,192,768]{2,1,0:T(8,128)(2,1)}, bf16[8,192,768]{2,1,0:T(8,128)(2,1)}) custom-call(s32[2]{0:T(128)} %pad_add_fusion.1.place, bf16[16,192,512]{2,1,0:T(8,128)(2,1)} %bitcast.55, bf16[16,192,512]{2,1,0:T(8,128)(2,1)} %bitcast.56, bf16[512,768]{1,0:T(8,128)(2,1)} %get-tuple-element.130.h_ref.low_ref), custom_call_target="tpu_custom_call" | custom-call | flops 1000 | bytes 1000 | tf_op jit(solution)/shard_map/grad_rows/pallas_call | solution.py:710
  176.1 3.3 collective-permute-done.20.part_near.part_far
  179.4 5.2 %halve.4 = (f32[4,192,768]{2,1,0:T(8,128)}, bf16[4,192,768]{2,1,0:T(8,128)(2,1)}) custom-call(s32[2]{0:T(128)} %pad_add_fusion.1.place, bf16[8,192,768]{2,1,0:T(8,128)(2,1)} %get-tuple-element.125.keep_near.keep_far, bf16[8,192,768]{2,1,0:T(8,128)(2,1)} %collective-permute-done.20.part_near.part_far, ...), custom_call_target="tpu_custom_call" | custom-call | flops 1000 | bytes 1000 | tf_op jit(solution)/shard_map/halve/pallas_call | solution.py:804
  184.6 18.8 %ffn_back.1 = (bf16[512,3072]{1,0:T(8,128)(2,1)}, f32[1,3072]{1,0:T(1,128)}, f32[512,768]{1,0:T(8,128)}, bf16[512,768]{1,0:T(8,128)(2,1)}, bf16[512,768]{1,0:T(8,128)(2,1)}, /*index=5*/f32[8,768]{1,0:T(8,128)}) custom-call(s32[2]{0:T(128)} %pad_add_fusion.1.place, bf16[512,768]{1,0:T(8,128)(2,1)} %get-tuple-element.130.h_ref.low_ref, ...), custom_call_target="tpu_custom_call" | custom-call | flops 1000 | bytes 1000 | tf_op jit(solution)/shard_map/ffn_back/pallas_call | solution.py:653
  203.4 9.4 %grad_columns.2 = (bf16[8,48,3840]{2,1,0:T(8,128)(2,1)}, bf16[8,48,3840]{2,1,0:T(8,128)(2,1)}) custom-call(s32[2]{0:T(128)} %pad_add_fusion.1.place, bf16[768,512]{1,0:T(8,128)(2,1)} %bitcast.58, bf16[512,768]{1,0:T(8,128)(2,1)} %get-tuple-element.136.refs_1_, bf16[768,512]{1,0:T(8,128)(2,1)} %get-tuple-element.137.refs_2_, ...), custom_call_target="tpu_custom_call" | custom-call | flops 1000 | bytes 1000 | tf_op jit(solution)/shard_map/grad_columns/pallas_call | solution.py:782
  213.2 1.7 collective-permute-start.22
  215.0 26.5 %collective-permute-done.22.across_ref = bf16[4,192,768]{2,1,0:T(8,128)(2,1)S(1)} collective-permute-done((bf16[4,192,768]{2,1,0:T(8,128)(2,1)}, bf16[4,192,768]{2,1,0:T(8,128)(2,1)S(1)}, u32[]{:S(2)}, u32[]{:S(2)}) %collective-permute-start.22) | collective-permute-done | bytes 1179680 | tf_op jit(solution)/shard_map/ppermute | solution.py:347
  242.6 2.9 column_sends.3
  245.5 5.8 %halve.5 = (f32[8,48,1920]{2,1,0:T(8,128)}, bf16[8,48,1920]{2,1,0:T(8,128)(2,1)}) custom-call(s32[2]{0:T(128)} %pad_add_fusion.1.place, bf16[8,48,3840]{2,1,0:T(8,128)(2,1)} %get-tuple-element.139.keep_near.keep_far, bf16[8,48,3840]{2,1,0:T(8,128)(2,1)} %collective-permute-done.21.part_near.part_far, ...), custom_call_target="tpu_custom_call" | custom-call | flops 1000 | bytes 1000 | tf_op jit(solution)/shard_map/halve/pallas_call | solution.py:804
  251.3 1.7 collective-permute-start.23
  254.8 2.7 collective-permute-start.24
  257.4 29.4 %attend_back.1 = (bf16[512,768]{1,0:T(8,128)(2,1)}, bf16[1024,768]{1,0:T(8,128)(2,1)}, bf16[1024,768]{1,0:T(8,128)(2,1)}, f32[12,8,128]{2,1,0:T(8,128)}) custom-call(s32[48]{0:T(128)} %concatenate.67.bounds, bf16[512,768]{1,0:T(8,128)(2,1)} %fusion.3.q_ref, bf16[1024,1536]{1,0:T(8,128)(2,1)} %add_convert_fusion.k_ref.v_ref, ...), custom_call_target="tpu_custom_call" | custom-call | flops 1000 | bytes 1000 | tf_op jit(solution)/shard_map/attend_back/pallas_call | solution.py:298
  290.1 4.9 %halve.6 = (f32[4,48,1920]{2,1,0:T(8,128)}, bf16[4,48,1920]{2,1,0:T(8,128)(2,1)}) custom-call(s32[2]{0:T(128)} %pad_add_fusion.1.place, f32[8,48,1920]{2,1,0:T(8,128)} %get-tuple-element.151.keep_near.keep_far, bf16[8,48,1920]{2,1,0:T(8,128)(2,1)} %copy-done.8, f32[8,48,1920]{2,1,0:T(8,128)} %get-tuple-element.151.keep_near.keep_far, ...), custom_call_target="tpu_custom_call" | custom-call | flops 1000 | bytes 1000 | tf_op jit(solution)/shard_map/halve/pallas_call | solution.py:804
  295.0 9.2 %grad_columns.3 = (bf16[8,48,2304]{2,1,0:T(8,128)(2,1)}, bf16[8,48,2304]{2,1,0:T(8,128)(2,1)}) custom-call(s32[2]{0:T(128)} %pad_add_fusion.1.place, bf16[768,1024]{1,0:T(8,128)(2,1)} %fusion.23.refs_0_.refs_2_.refs_4_, bf16[512,768]{1,0:T(8,128)(2,1)} %get-tuple-element.171.refs_1_, bf16[768,1024]{1,0:T(8,128)(2,1)} %fusion.23.refs_0_.refs_2_.refs_4_, ...), custom_call_target="tpu_custom_call" | custom-call | flops 1000 | bytes 1000 | tf_op jit(solution)/shard_map/grad_columns/pallas_call | solution.py:782
  315.1 8.3 %collective-permute-done.29.across_ref = bf16[4,48,1920]{2,1,0:T(8,128)(2,1)} collective-permute-done((bf16[4,48,1920]{2,1,0:T(8,128)(2,1)}, bf16[4,48,1920]{2,1,0:T(8,128)(2,1)}, u32[]{:S(2)}, u32[]{:S(2)}) %collective-permute-start.29) | collective-permute-done | bytes 737312 | tf_op jit(solution)/shard_map/ppermute | solution.py:347
  323.4 4.0 %column_sends.4 = (f32[48,1920]{1,0:T(8,128)}, bf16[48,1920]{1,0:T(8,128)(2,1)}, bf16[48,1920]{1,0:T(8,128)(2,1)}, bf16[48,1920]{1,0:T(8,128)(2,1)}) custom-call(f32[4,48,1920]{2,1,0:T(8,128)} %get-tuple-element.163.held_ref, bf16[4,48,1920]{2,1,0:T(8,128)(2,1)} %collective-permute-done.29.across_ref), custom_call_target="tpu_custom_call" | custom-call | flops 1000 | bytes 1000 | tf_op jit(solution)/shard_map/column_sends/pallas_call | solution.py:848
  327.4 5.2 %halve.7 = (f32[4,48,2304]{2,1,0:T(8,128)}, bf16[4,48,2304]{2,1,0:T(8,128)(2,1)}) custom-call(s32[2]{0:T(128)} %pad_add_fusion.1.place, bf16[8,48,2304]{2,1,0:T(8,128)(2,1)} %get-tuple-element.160.keep_near.keep_far, bf16[8,48,2304]{2,1,0:T(8,128)(2,1)} %collective-permute-done.27.part_near.part_far, ...), custom_call_target="tpu_custom_call" | custom-call | flops 1000 | bytes 1000 | tf_op jit(solution)/shard_map/halve/pallas_call | solution.py:804
  334.2 3.2 fusion.5
  337.4 2.7 convolution_add_fusion
  344.7 1.8 convert_add_fusion.1
  346.6 1.8 collective-permute-start.39
  348.3 2.6 collective-permute-start.40
  350.9 2.3 fusion.7
  354.9 4.7 %column_sends.5 = (f32[48,2304]{1,0:T(8,128)}, bf16[48,2304]{1,0:T(8,128)(2,1)}, bf16[48,2304]{1,0:T(8,128)(2,1)}, bf16[48,2304]{1,0:T(8,128)(2,1)}) custom-call(f32[4,48,2304]{2,1,0:T(8,128)} %get-tuple-element.172.held_ref, bf16[4,48,2304]{2,1,0:T(8,128)(2,1)} %collective-permute-done.31.across_ref), custom_call_target="tpu_custom_call" | custom-call | flops 1000 | bytes 1000 | tf_op jit(solution)/shard_map/column_sends/pallas_call | solution.py:848
  361.4 5.4 %fusion.24 = (f32[768]{0:T(1024)S(1)}, f32[768]{0:T(1024)S(1)}, f32[768]{0:T(1024)S(1)}, f32[768]{0:T(1024)S(1)}, f32[512,768]{0,1:T(8,128)S(1)}) fusion(bf16[1,1,512,768]{2,3,1,0:T(8,128)(2,1)} %copy-done.4, f32[510,768]{0,1:T(8,128)S(1)} %get-tuple-element.284, pred[512]{0:T(512)(128)(4,1)} %copy-done.29, f32[510,768]{0,1:T(8,128)} %get-tuple-element.285, ...), kind=kLoop, calls=%fused_computation.147 | loop fusion | flops 5895168 | bytes 12583937 | tf_op jit(solution)/shard_map/transpose(jvp())/reduce_sum | solution.py:50
  366.9 2.3 concatenate.86
  369.2 2.7 collective-permute-start.42
  377.4 2.4 collective-permute-done.33
  382.7 2.3 copy.70
  388.6 2.5 collective-permute-done.35
  (270 shorter events, 82.6 us)
Async XLA Ops:
  2.4 18.8 %collective-permute-start.2 = (bf16[48,1152]{1,0:T(8,128)(2,1)}, bf16[48,1152]{1,0:T(8,128)(2,1)}, u32[]{:S(2)}, u32[]{:S(2)}) collective-permute-start(bf16[48,1152]{1,0:T(8,128)(2,1)} %get-tuple-element.279), channel_id=1, source_target_pairs={{0,12},{1,13},{2,14},{3,15},{4,8},{5,9},{6,10},{7,11},{8,4},{9,5},... | collective-permute-start | bytes 331784 | tf_op jit(solution)/shard_map/ppermute | solution.py:347
  7.4 13.8 %collective-permute-start.1 = (bf16[48,1152]{1,0:T(8,128)(2,1)}, bf16[48,1152]{1,0:T(8,128)(2,1)}, u32[]{:S(2)}, u32[]{:S(2)}) collective-permute-start(bf16[48,1152]{1,0:T(8,128)(2,1)} %get-tuple-element.279), channel_id=1, source_target_pairs={{0,8},{1,9},{2,10},{3,11},{4,12},{5,13},{6,14},{7,15},{8,0},{9,1},... | collective-permute-start | bytes 331784 | tf_op jit(solution)/shard_map/ppermute | solution.py:347
  7.4 13.8 %collective-permute-start = (bf16[48,1152]{1,0:T(8,128)(2,1)}, bf16[48,1152]{1,0:T(8,128)(2,1)}, u32[]{:S(2)}, u32[]{:S(2)}) collective-permute-start(bf16[48,1152]{1,0:T(8,128)(2,1)} %get-tuple-element.279), channel_id=1, source_target_pairs={{0,4},{1,5},{2,6},{3,7},{4,0},{5,1},{6,2},{7,3},{8,12},{9,13},{10,... | collective-permute-start | bytes 331784 | tf_op jit(solution)/shard_map/ppermute | solution.py:347
  9.4 31.5 %copy-start.4 = (bf16[1,1,512,768]{2,3,1,0:T(8,128)(2,1)}, bf16[1,1,512,768]{2,3,1,0:T(8,128)(2,1)S(1)}, u32[]{:S(2)}) copy-start(bf16[1,1,512,768]{2,3,1,0:T(8,128)(2,1)S(1)} %copy.63) | copy-start | bytes 2359300
  9.5 31.0 %collective-permute-start.10 = (bf16[512,768]{0,1:T(8,128)(2,1)S(1)}, bf16[512,768]{0,1:T(8,128)(2,1)S(1)}, u32[]{:S(2)}, u32[]{:S(2)}) collective-permute-start(bf16[512,768]{0,1:T(8,128)(2,1)S(1)} %bitcast.57), channel_id=1, source_target_pairs={{0,16},{16,0},{1,17},{17,1},{2,18},{18,2},{3,19},{19,3},{4,20},{20... | collective-permute-start | bytes 2359304 | tf_op jit(solution)/shard_map/ppermute | solution.py:909
  19.3 287.0 %copy-start.29 = (pred[512]{0:T(512)(128)(4,1)}, pred[512]{0:T(512)(128)(4,1)S(1)}, u32[]{:S(2)}) copy-start(pred[512]{0:T(512)(128)(4,1)S(1)} %get-tuple-element.299) | copy-start | bytes 1540
  22.3 10.9 %collective-permute-start.3 = (bf16[4,48,1152]{2,1,0:T(8,128)(2,1)S(1)}, bf16[4,48,1152]{2,1,0:T(8,128)(2,1)S(1)}, u32[]{:S(2)}, u32[]{:S(2)}) collective-permute-start(bf16[4,48,1152]{2,1,0:T(8,128)(2,1)S(1)} %pad_maximum_fusion.3), channel_id=1, source_target_pairs={{0,2},{1,3},{2,0},{3,1},{4,6},{5,7},{6,4},{7,5},{8,10},{9,11},{10,... | collective-permute-start | bytes 1327112 | tf_op jit(solution)/shard_map/ppermute | solution.py:347
  34.1 19.7 %collective-permute-start.4 = (bf16[8,48,1152]{2,1,0:T(8,128)(2,1)}, bf16[8,48,1152]{2,1,0:T(8,128)(2,1)}, u32[]{:S(2)}, u32[]{:S(2)}) collective-permute-start(bf16[8,48,1152]{2,1,0:T(8,128)(2,1)} %constant_dynamic-update-slice_fusion.refs_0_), channel_id=1, source_target_pairs={{0,16},{16,0},{1,17},{17,1},{2,18},{18,2},{3,19},{19,3},{4,20},{20... | collective-permute-start | bytes 2654216 | tf_op jit(solution)/shard_map/ppermute | solution.py:909
  36.0 19.3 %collective-permute-start.7 = (bf16[48,3840]{1,0:T(8,128)(2,1)S(1)}, bf16[48,3840]{1,0:T(8,128)(2,1)S(1)}, u32[]{:S(2)}, u32[]{:S(2)}) collective-permute-start(bf16[48,3840]{1,0:T(8,128)(2,1)S(1)} %pad_maximum_fusion.4), channel_id=1, source_target_pairs={{0,12},{1,13},{2,14},{3,15},{4,8},{5,9},{6,10},{7,11},{8,4},{9,5},... | collective-permute-start | bytes 1105928 | tf_op jit(solution)/shard_map/ppermute | solution.py:347
  39.6 29.3 %collective-permute-start.6 = (bf16[48,3840]{1,0:T(8,128)(2,1)S(1)}, bf16[48,3840]{1,0:T(8,128)(2,1)S(1)}, u32[]{:S(2)}, u32[]{:S(2)}) collective-permute-start(bf16[48,3840]{1,0:T(8,128)(2,1)S(1)} %pad_maximum_fusion.4), channel_id=1, source_target_pairs={{0,8},{1,9},{2,10},{3,11},{4,12},{5,13},{6,14},{7,15},{8,0},{9,1},... | collective-permute-start | bytes 1105928 | tf_op jit(solution)/shard_map/ppermute | solution.py:347
  39.6 29.3 %collective-permute-start.5 = (bf16[48,3840]{1,0:T(8,128)(2,1)S(1)}, bf16[48,3840]{1,0:T(8,128)(2,1)S(1)}, u32[]{:S(2)}, u32[]{:S(2)}) collective-permute-start(bf16[48,3840]{1,0:T(8,128)(2,1)S(1)} %pad_maximum_fusion.4), channel_id=1, source_target_pairs={{0,4},{1,5},{2,6},{3,7},{4,0},{5,1},{6,2},{7,3},{8,12},{9,13},{10,... | collective-permute-start | bytes 1105928 | tf_op jit(solution)/shard_map/ppermute | solution.py:347
  40.5 34.2 %collective-permute-start.8 = (bf16[8,48,1152]{2,1,0:T(8,128)(2,1)}, bf16[8,48,1152]{2,1,0:T(8,128)(2,1)}, u32[]{:S(2)}, u32[]{:S(2)}) collective-permute-start(bf16[8,48,1152]{2,1,0:T(8,128)(2,1)} %constant_dynamic-update-slice_fusion.refs_0_), channel_id=1, source_target_pairs={{0,1},{1,0},{2,3},{3,2},{4,5},{5,4},{6,7},{7,6},{8,9},{9,8},{10,11... | collective-permute-start | bytes 2654216 | tf_op jit(solution)/shard_map/ppermute | solution.py:347
  53.8 22.4 %collective-permute-start.9 = (bf16[8,48,1152]{2,1,0:T(8,128)(2,1)}, bf16[8,48,1152]{2,1,0:T(8,128)(2,1)}, u32[]{:S(2)}, u32[]{:S(2)}) collective-permute-start(bf16[8,48,1152]{2,1,0:T(8,128)(2,1)} %collective-permute-done.4.refs_2_), channel_id=1, source_target_pairs={{0,1},{1,0},{2,3},{3,2},{4,5},{5,4},{6,7},{7,6},{8,9},{9,8},{10,11... | collective-permute-start | bytes 2654216 | tf_op jit(solution)/shard_map/ppermute | solution.py:347
  70.3 33.5 %collective-permute-start.15 = (bf16[192,768]{1,0:T(8,128)(2,1)}, bf16[192,768]{1,0:T(8,128)(2,1)S(1)}, u32[]{:S(2)}, u32[]{:S(2)}) collective-permute-start(bf16[192,768]{1,0:T(8,128)(2,1)} %param.46), channel_id=1, source_target_pairs={{0,12},{1,13},{2,14},{3,15},{4,8},{5,9},{6,10},{7,11},{8,4},{9,5},... | collective-permute-start | bytes 884744 | tf_op jit(solution)/shard_map/ppermute | solution.py:347
  72.7 31.1 %collective-permute-start.14 = (bf16[192,768]{1,0:T(8,128)(2,1)}, bf16[192,768]{1,0:T(8,128)(2,1)}, u32[]{:S(2)}, u32[]{:S(2)}) collective-permute-start(bf16[192,768]{1,0:T(8,128)(2,1)} %param.46), channel_id=1, source_target_pairs={{0,8},{1,9},{2,10},{3,11},{4,12},{5,13},{6,14},{7,15},{8,0},{9,1},... | collective-permute-start | bytes 884744 | tf_op jit(solution)/shard_map/ppermute | solution.py:347
  72.7 31.1 %collective-permute-start.13 = (bf16[192,768]{1,0:T(8,128)(2,1)}, bf16[192,768]{1,0:T(8,128)(2,1)}, u32[]{:S(2)}, u32[]{:S(2)}) collective-permute-start(bf16[192,768]{1,0:T(8,128)(2,1)} %param.46), channel_id=1, source_target_pairs={{0,4},{1,5},{2,6},{3,7},{4,0},{5,1},{6,2},{7,3},{8,12},{9,13},{10,... | collective-permute-start | bytes 884744 | tf_op jit(solution)/shard_map/ppermute | solution.py:347
  74.7 33.6 %collective-permute-start.12 = (bf16[4,48,3840]{2,1,0:T(8,128)(2,1)}, bf16[4,48,3840]{2,1,0:T(8,128)(2,1)}, u32[]{:S(2)}, u32[]{:S(2)}) collective-permute-start(bf16[4,48,3840]{2,1,0:T(8,128)(2,1)} %pad_maximum_fusion.1.refs_0_), channel_id=1, source_target_pairs={{0,2},{1,3},{2,0},{3,1},{4,6},{5,7},{6,4},{7,5},{8,10},{9,11},{10,... | collective-permute-start | bytes 4423688 | tf_op jit(solution)/shard_map/ppermute | solution.py:347
  103.7 29.1 %copy-start.37 = (f32[768]{0:T(1024)S(1)}, f32[768]{0:T(1024)}, u32[]{:S(2)}) copy-start(f32[768]{0:T(1024)} %param.49) | copy-start | bytes 9220
  106.1 26.6 %collective-permute-start.18 = (bf16[4,192,768]{2,1,0:T(8,128)(2,1)}, bf16[4,192,768]{2,1,0:T(8,128)(2,1)}, u32[]{:S(2)}, u32[]{:S(2)}) collective-permute-start(bf16[4,192,768]{2,1,0:T(8,128)(2,1)} %pad_maximum_fusion.2.refs_0_.refs_4_), channel_id=1, source_target_pairs={{0,2},{1,3},{2,0},{3,1},{4,6},{5,7},{6,4},{7,5},{8,10},{9,11},{10,... | collective-permute-start | bytes 3538952 | tf_op jit(solution)/shard_map/ppermute | solution.py:347
  106.6 28.5 %collective-permute-start.11 = (bf16[4,48,3840]{2,1,0:T(8,128)(2,1)}, bf16[4,48,3840]{2,1,0:T(8,128)(2,1)}, u32[]{:S(2)}, u32[]{:S(2)}) collective-permute-start(bf16[4,48,3840]{2,1,0:T(8,128)(2,1)} %pad_maximum_fusion.1.refs_0_), channel_id=1, source_target_pairs={{0,1},{1,0},{2,3},{3,2},{4,5},{5,4},{6,7},{7,6},{8,9},{9,8},{10,11... | collective-permute-start | bytes 4423688 | tf_op jit(solution)/shard_map/ppermute | solution.py:347
  108.3 26.8 %collective-permute-start.16 = (bf16[4,48,3840]{2,1,0:T(8,128)(2,1)}, bf16[4,48,3840]{2,1,0:T(8,128)(2,1)}, u32[]{:S(2)}, u32[]{:S(2)}) collective-permute-start(bf16[4,48,3840]{2,1,0:T(8,128)(2,1)} %collective-permute-done.12.refs_2_), channel_id=1, source_target_pairs={{0,1},{1,0},{2,3},{3,2},{4,5},{5,4},{6,7},{7,6},{8,9},{9,8},{10,11... | collective-permute-start | bytes 4423688 | tf_op jit(solution)/shard_map/ppermute | solution.py:347
  108.3 46.3 %collective-permute-start.17 = (bf16[4,192,768]{2,1,0:T(8,128)(2,1)}, bf16[4,192,768]{2,1,0:T(8,128)(2,1)}, u32[]{:S(2)}, u32[]{:S(2)}) collective-permute-start(bf16[4,192,768]{2,1,0:T(8,128)(2,1)} %pad_maximum_fusion.2.refs_0_.refs_4_), channel_id=1, source_target_pairs={{0,1},{1,0},{2,3},{3,2},{4,5},{5,4},{6,7},{7,6},{8,9},{9,8},{10,11... | collective-permute-start | bytes 3538952 | tf_op jit(solution)/shard_map/ppermute | solution.py:347
  132.7 21.9 %collective-permute-start.19 = (bf16[4,192,768]{2,1,0:T(8,128)(2,1)}, bf16[4,192,768]{2,1,0:T(8,128)(2,1)}, u32[]{:S(2)}, u32[]{:S(2)}) collective-permute-start(bf16[4,192,768]{2,1,0:T(8,128)(2,1)} %collective-permute-done.18.refs_2_.refs_6_), channel_id=1, source_target_pairs={{0,1},{1,0},{2,3},{3,2},{4,5},{5,4},{6,7},{7,6},{8,9},{9,8},{10,11... | collective-permute-start | bytes 3538952 | tf_op jit(solution)/shard_map/ppermute | solution.py:347
  174.4 5.0 %collective-permute-start.20 = (bf16[8,192,768]{2,1,0:T(8,128)(2,1)}, bf16[8,192,768]{2,1,0:T(8,128)(2,1)}, u32[]{:S(2)}, u32[]{:S(2)}) collective-permute-start(bf16[8,192,768]{2,1,0:T(8,128)(2,1)} %get-tuple-element.126), channel_id=1, source_target_pairs={{0,1},{1,0},{2,3},{3,2},{4,5},{5,4},{6,7},{7,6},{8,9},{9,8},{10,11... | collective-permute-start | bytes 7077896 | tf_op jit(solution)/shard_map/ppermute | solution.py:347
  212.9 32.6 %collective-permute-start.21 = (bf16[8,48,3840]{2,1,0:T(8,128)(2,1)}, bf16[8,48,3840]{2,1,0:T(8,128)(2,1)}, u32[]{:S(2)}, u32[]{:S(2)}) collective-permute-start(bf16[8,48,3840]{2,1,0:T(8,128)(2,1)} %get-tuple-element.140), channel_id=1, source_target_pairs={{0,1},{1,0},{2,3},{3,2},{4,5},{5,4},{6,7},{7,6},{8,9},{9,8},{10,11... | collective-permute-start | bytes 8847368 | tf_op jit(solution)/shard_map/ppermute | solution.py:347
  213.2 28.2 %collective-permute-start.22 = (bf16[4,192,768]{2,1,0:T(8,128)(2,1)}, bf16[4,192,768]{2,1,0:T(8,128)(2,1)S(1)}, u32[]{:S(2)}, u32[]{:S(2)}) collective-permute-start(bf16[4,192,768]{2,1,0:T(8,128)(2,1)} %get-tuple-element.129), channel_id=1, source_target_pairs={{0,2},{1,3},{2,0},{3,1},{4,6},{5,7},{6,4},{7,5},{8,10},{9,11},{10,... | collective-permute-start | bytes 3538952 | tf_op jit(solution)/shard_map/ppermute | solution.py:347
  251.3 37.6 %collective-permute-start.23 = (bf16[8,48,1920]{2,1,0:T(8,128)(2,1)}, bf16[8,48,1920]{2,1,0:T(8,128)(2,1)S(1)}, u32[]{:S(2)}, u32[]{:S(2)}) collective-permute-start(bf16[8,48,1920]{2,1,0:T(8,128)(2,1)} %get-tuple-element.147), channel_id=1, source_target_pairs={{0,16},{16,0},{1,17},{17,1},{2,18},{18,2},{3,19},{19,3},{4,20},{20... | collective-permute-start | bytes 4423688 | tf_op jit(solution)/shard_map/ppermute | solution.py:909
  253.0 33.8 %collective-permute-start.26 = (bf16[192,768]{1,0:T(8,128)(2,1)}, bf16[192,768]{1,0:T(8,128)(2,1)S(1)}, u32[]{:S(2)}, u32[]{:S(2)}) collective-permute-start(bf16[192,768]{1,0:T(8,128)(2,1)} %get-tuple-element.145), channel_id=1, source_target_pairs={{0,12},{1,13},{2,14},{3,15},{4,8},{5,9},{6,10},{7,11},{8,4},{9,5},... | collective-permute-start | bytes 884744 | tf_op jit(solution)/shard_map/ppermute | solution.py:347
  254.3 32.5 %collective-permute-start.25 = (bf16[192,768]{1,0:T(8,128)(2,1)}, bf16[192,768]{1,0:T(8,128)(2,1)}, u32[]{:S(2)}, u32[]{:S(2)}) collective-permute-start(bf16[192,768]{1,0:T(8,128)(2,1)} %get-tuple-element.144), channel_id=1, source_target_pairs={{0,8},{1,9},{2,10},{3,11},{4,12},{5,13},{6,14},{7,15},{8,0},{9,1},... | collective-permute-start | bytes 884744 | tf_op jit(solution)/shard_map/ppermute | solution.py:347
  254.8 32.0 %collective-permute-start.24 = (bf16[192,768]{1,0:T(8,128)(2,1)}, bf16[192,768]{1,0:T(8,128)(2,1)}, u32[]{:S(2)}, u32[]{:S(2)}) collective-permute-start(bf16[192,768]{1,0:T(8,128)(2,1)} %get-tuple-element.143), channel_id=1, source_target_pairs={{0,4},{1,5},{2,6},{3,7},{4,0},{5,1},{6,2},{7,3},{8,12},{9,13},{10,... | collective-permute-start | bytes 884744 | tf_op jit(solution)/shard_map/ppermute | solution.py:347
  304.2 23.3 %collective-permute-start.27 = (bf16[8,48,2304]{2,1,0:T(8,128)(2,1)}, bf16[8,48,2304]{2,1,0:T(8,128)(2,1)}, u32[]{:S(2)}, u32[]{:S(2)}) collective-permute-start(bf16[8,48,2304]{2,1,0:T(8,128)(2,1)} %get-tuple-element.161), channel_id=1, source_target_pairs={{0,1},{1,0},{2,3},{3,2},{4,5},{5,4},{6,7},{7,6},{8,9},{9,8},{10,11... | collective-permute-start | bytes 5308424 | tf_op jit(solution)/shard_map/ppermute | solution.py:347
  304.2 19.2 %collective-permute-start.29 = (bf16[4,48,1920]{2,1,0:T(8,128)(2,1)}, bf16[4,48,1920]{2,1,0:T(8,128)(2,1)}, u32[]{:S(2)}, u32[]{:S(2)}) collective-permute-start(bf16[4,48,1920]{2,1,0:T(8,128)(2,1)} %get-tuple-element.153), channel_id=1, source_target_pairs={{0,2},{1,3},{2,0},{3,1},{4,6},{5,7},{6,4},{7,5},{8,10},{9,11},{10,... | collective-permute-start | bytes 2211848 | tf_op jit(solution)/shard_map/ppermute | solution.py:347
  305.7 9.4 %collective-permute-start.28 = (bf16[192,768]{1,0:T(8,128)(2,1)S(1)}, bf16[192,768]{1,0:T(8,128)(2,1)}, u32[]{:S(2)}, u32[]{:S(2)}) collective-permute-start(bf16[192,768]{1,0:T(8,128)(2,1)S(1)} %add_convert_fusion.4), channel_id=1, source_target_pairs={{0,16},{16,0},{1,17},{17,1},{2,18},{18,2},{3,19},{19,3},{4,20},{20... | collective-permute-start | bytes 884744 | tf_op jit(solution)/shard_map/ppermute | solution.py:909
  332.6 22.2 %collective-permute-start.31 = (bf16[4,48,2304]{2,1,0:T(8,128)(2,1)}, bf16[4,48,2304]{2,1,0:T(8,128)(2,1)}, u32[]{:S(2)}, u32[]{:S(2)}) collective-permute-start(bf16[4,48,2304]{2,1,0:T(8,128)(2,1)} %get-tuple-element.169), channel_id=1, source_target_pairs={{0,2},{1,3},{2,0},{3,1},{4,6},{5,7},{6,4},{7,5},{8,10},{9,11},{10,... | collective-permute-start | bytes 2654216 | tf_op jit(solution)/shard_map/ppermute | solution.py:347
  341.3 19.1 %collective-permute-start.30 = (bf16[512,768]{0,1:T(8,128)(2,1)}, bf16[512,768]{0,1:T(8,128)(2,1)}, u32[]{:S(2)}, u32[]{:S(2)}) collective-permute-start(bf16[512,768]{0,1:T(8,128)(2,1)} %select_convert_fusion), channel_id=1, source_target_pairs={{0,16},{16,0},{1,17},{17,1},{2,18},{18,2},{3,19},{19,3},{4,20},{20... | collective-permute-start | bytes 2359304 | tf_op jit(solution)/shard_map/ppermute | solution.py:909
  346.6 25.4 %collective-permute-start.38 = (bf16[48,1920]{1,0:T(8,128)(2,1)}, bf16[48,1920]{1,0:T(8,128)(2,1)S(1)}, u32[]{:S(2)}, u32[]{:S(2)}) collective-permute-start(bf16[48,1920]{1,0:T(8,128)(2,1)} %get-tuple-element.165), channel_id=1, source_target_pairs={{0,4},{1,5},{2,6},{3,7},{4,0},{5,1},{6,2},{7,3},{8,12},{9,13},{10,... | collective-permute-start | bytes 552968 | tf_op jit(solution)/shard_map/ppermute | solution.py:347
  346.6 25.3 %collective-permute-start.39 = (bf16[48,1920]{1,0:T(8,128)(2,1)}, bf16[48,1920]{1,0:T(8,128)(2,1)S(1)}, u32[]{:S(2)}, u32[]{:S(2)}) collective-permute-start(bf16[48,1920]{1,0:T(8,128)(2,1)} %get-tuple-element.166), channel_id=1, source_target_pairs={{0,8},{1,9},{2,10},{3,11},{4,12},{5,13},{6,14},{7,15},{8,0},{9,1},... | collective-permute-start | bytes 552968 | tf_op jit(solution)/shard_map/ppermute | solution.py:347
  348.3 20.9 %collective-permute-start.40 = (bf16[48,1920]{1,0:T(8,128)(2,1)}, bf16[48,1920]{1,0:T(8,128)(2,1)}, u32[]{:S(2)}, u32[]{:S(2)}) collective-permute-start(bf16[48,1920]{1,0:T(8,128)(2,1)} %get-tuple-element.167), channel_id=1, source_target_pairs={{0,12},{1,13},{2,14},{3,15},{4,8},{5,9},{6,10},{7,11},{8,4},{9,5},... | collective-permute-start | bytes 552968 | tf_op jit(solution)/shard_map/ppermute | solution.py:347
  359.6 29.0 %collective-permute-start.37 = (bf16[48,2304]{1,0:T(8,128)(2,1)}, bf16[48,2304]{1,0:T(8,128)(2,1)}, u32[]{:S(2)}, u32[]{:S(2)}) collective-permute-start(bf16[48,2304]{1,0:T(8,128)(2,1)} %get-tuple-element.174), channel_id=1, source_target_pairs={{0,4},{1,5},{2,6},{3,7},{4,0},{5,1},{6,2},{7,3},{8,12},{9,13},{10,... | collective-permute-start | bytes 663560 | tf_op jit(solution)/shard_map/ppermute | solution.py:347
  360.5 28.2 %collective-permute-start.41 = (bf16[48,2304]{1,0:T(8,128)(2,1)}, bf16[48,2304]{1,0:T(8,128)(2,1)}, u32[]{:S(2)}, u32[]{:S(2)}) collective-permute-start(bf16[48,2304]{1,0:T(8,128)(2,1)} %get-tuple-element.175), channel_id=1, source_target_pairs={{0,8},{1,9},{2,10},{3,11},{4,12},{5,13},{6,14},{7,15},{8,0},{9,1},... | collective-permute-start | bytes 663560 | tf_op jit(solution)/shard_map/ppermute | solution.py:347
  369.2 19.4 %collective-permute-start.42 = (bf16[48,2304]{1,0:T(8,128)(2,1)}, bf16[48,2304]{1,0:T(8,128)(2,1)}, u32[]{:S(2)}, u32[]{:S(2)}) collective-permute-start(bf16[48,2304]{1,0:T(8,128)(2,1)} %get-tuple-element.176), channel_id=1, source_target_pairs={{0,12},{1,13},{2,14},{3,15},{4,8},{5,9},{6,10},{7,11},{8,4},{9,5},... | collective-permute-start | bytes 663560 | tf_op jit(solution)/shard_map/ppermute | solution.py:347
  371.9 3.4 collective-permute-start.32
  373.8 12.1 %collective-permute-start.44 = (bf16[48,1920]{1,0:T(8,128)(2,1)S(1)}, bf16[48,1920]{1,0:T(8,128)(2,1)}, u32[]{:S(2)}, u32[]{:S(2)}) collective-permute-start(bf16[48,1920]{1,0:T(8,128)(2,1)S(1)} %add_convert_fusion.8), channel_id=1, source_target_pairs={{0,16},{16,0},{1,17},{17,1},{2,18},{18,2},{3,19},{19,3},{4,20},{20... | collective-permute-start | bytes 552968 | tf_op jit(solution)/shard_map/ppermute | solution.py:909
  375.3 4.4 %collective-permute-start.33 = (f32[24,768]{1,0:T(8,128)S(1)}, f32[24,768]{1,0:T(8,128)S(1)}, u32[]{:S(2)}, u32[]{:S(2)}) collective-permute-start(f32[24,768]{1,0:T(8,128)S(1)} %add.249), channel_id=1, source_target_pairs={{0,2},{1,3},{2,0},{3,1},{4,6},{5,7},{6,4},{7,5},{8,10},{9,11},{10,... | collective-permute-start | bytes 221192 | tf_op jit(solution)/shard_map/ppermute | solution.py:903
  379.8 5.2 %collective-permute-start.34 = (f32[24,768]{1,0:T(8,128)S(1)}, f32[24,768]{1,0:T(8,128)S(1)}, u32[]{:S(2)}, u32[]{:S(2)}) collective-permute-start(f32[24,768]{1,0:T(8,128)S(1)} %add.250), channel_id=1, source_target_pairs={{0,4},{1,5},{2,6},{3,7},{4,0},{5,1},{6,2},{7,3},{8,12},{9,13},{10,... | collective-permute-start | bytes 221192 | tf_op jit(solution)/shard_map/ppermute | solution.py:903
  385.0 6.1 %collective-permute-start.35 = (f32[24,768]{1,0:T(8,128)S(1)}, f32[24,768]{1,0:T(8,128)S(1)}, u32[]{:S(2)}, u32[]{:S(2)}) collective-permute-start(f32[24,768]{1,0:T(8,128)S(1)} %add.251), channel_id=1, source_target_pairs={{0,8},{1,9},{2,10},{3,11},{4,12},{5,13},{6,14},{7,15},{8,0},{9,1},... | collective-permute-start | bytes 221192 | tf_op jit(solution)/shard_map/ppermute | solution.py:903
  391.1 4.9 %collective-permute-start.36 = (f32[24,768]{1,0:T(8,128)S(1)}, f32[24,768]{1,0:T(8,128)S(1)}, u32[]{:S(2)}, u32[]{:S(2)}) collective-permute-start(f32[24,768]{1,0:T(8,128)S(1)} %add.252), channel_id=1, source_target_pairs={{0,16},{16,0},{1,17},{17,1},{2,18},{18,2},{3,19},{19,3},{4,20},{20... | collective-permute-start | bytes 221192 | tf_op jit(solution)/shard_map/ppermute | solution.py:909
  393.0 6.8 %collective-permute-start.43 = (bf16[48,2304]{1,0:T(8,128)(2,1)S(1)}, bf16[48,2304]{1,0:T(8,128)(2,1)S(1)}, u32[]{:S(2)}, u32[]{:S(2)}) collective-permute-start(bf16[48,2304]{1,0:T(8,128)(2,1)S(1)} %add_convert_fusion.7), channel_id=1, source_target_pairs={{0,16},{16,0},{1,17},{17,1},{2,18},{18,2},{3,19},{19,3},{4,20},{20... | collective-permute-start | bytes 663560 | tf_op jit(solution)/shard_map/ppermute | solution.py:909
  (42 other events, 381.0 us)

commit v6 on v5

--- a/solution.py
+++ b/solution.py
@@ -355,40 +355,22 @@
     return (slot & 3) * 4 + (slot >> 2) * 2
 
 
-def place_halves_kernel(place, *refs):
-    pieces, full_ref, sems = refs[:4], refs[4], refs[5]
-    rows, half = pieces[0].shape[1], pieces[0].shape[2]
-    copies = []
-    for index in range(32):
-        kind = index >> 3
-        mask = slot_mask(index & 7) + (kind & 1)
-        at = pl.multiple_of((place[0] ^ mask) * rows, 16)
-        column = pl.multiple_of((place[1] ^ (kind >> 1)) * half, 128)
-        copies.append(
-            pltpu.make_async_copy(
-                pieces[kind].at[index & 7],
-                full_ref.at[pl.ds(at, rows), pl.ds(column, half)],
-                sems.at[index],
-            )
-        )
-    for copy in copies:
-        copy.start()
-    for copy in copies:
+def place_kernel(groups, place, *refs):
+    for copy in start_rows(place, groups, refs[:-2], refs[-2], refs[-1]):
         copy.wait()
 
 
-def place_rows(place, pieces, width, kernel):
-    rows = pieces[0].shape[1]
+def place_rows(place, groups, pieces, shape):
     return pl.pallas_call(
-        kernel,
+        functools.partial(place_kernel, groups),
         grid_spec=pltpu.PrefetchScalarGridSpec(
             num_scalar_prefetch=1,
             grid=(),
-            in_specs=[pl.BlockSpec(memory_space=pl.ANY)] * 4,
+            in_specs=any_specs(len(pieces)),
             out_specs=pl.BlockSpec(memory_space=pltpu.VMEM),
             scratch_shapes=[pltpu.SemaphoreType.DMA((32,))],
         ),
-        out_shape=jax.ShapeDtypeStruct((16 * rows, width), bf16),
+        out_shape=jax.ShapeDtypeStruct(shape, bf16),
         cost_estimate=small_cost,
         name="place_rows",
     )(place, *pieces)
@@ -398,24 +380,46 @@
     return [shard] + [exchange(shard, 4 * step) for step in (1, 2, 3)]
 
 
+def half_pieces(column):
+    eight = jnp.concatenate([column, exchange(column, 2)])
+    far = swap(eight)
+    return [eight, exchange(eight, 1), far, exchange(far, 1)]
+
+
+def row_pieces(column, across):
+    return [column, exchange(column, 1), across, exchange(across, 1)]
+
+
 def column_of(shard):
     return jnp.stack(column_parts(shard))
 
 
-def start_rows(place, pieces, full, sems, first=0):
-    if len(pieces) == 1:
-        copies = [pltpu.make_async_copy(pieces[0], full, sems.at[first])]
-    else:
-        rows = pieces[0].shape[1]
-        copies = []
-        for index in range(16):
-            mask = (index >> 2) * 4 + (index & 3)
-            at = pl.multiple_of((place[0] ^ mask) * rows, 16)
+def start_rows(place, groups, refs, full, sems, first=0):
+    copies = []
+    for kind, column in groups:
+        if kind == "full":
+            piece, *refs = refs
+            width = piece.shape[1]
+            target = full.at[:, pl.ds(column, width)]
+            copies.append(pltpu.make_async_copy(piece, target, sems.at[first + len(copies)]))
+            continue
+        pieces, refs = refs[:4], refs[4:]
+        _, rows, width = pieces[0].shape
+        for index in range(32 if kind == "halves" else 16):
+            at = column
+            if kind == "halves":
+                source, slot = index >> 3, index & 7
+                mask = slot_mask(slot) + (source & 1)
+                at = pl.multiple_of(column + (place[1] ^ (source >> 1)) * width, 128)
+            else:
+                source, slot = index & 3, index >> 2
+                mask = slot * 4 + source
+            row = pl.multiple_of((place[0] ^ mask) * rows, 16)
             copies.append(
                 pltpu.make_async_copy(
-                    pieces[index & 3].at[index >> 2],
-                    full.at[pl.ds(at, rows)],
-                    sems.at[first + index],
+                    pieces[source].at[slot],
+                    full.at[pl.ds(row, rows), pl.ds(at, width)],
+                    sems.at[first + len(copies)],
                 )
             )
     for copy in copies:
@@ -449,7 +453,7 @@
     return scale * (scaled - mean - unit * inner)
 
 
-def up_kernel(place, context_ref, mixed_ref, vec_ref, bias_ref, *refs):
+def up_kernel(groups, place, context_ref, mixed_ref, vec_ref, bias_ref, *refs):
     *pieces, unit_ref, scale_ref, low_ref, low_t_ref, active_ref, active_t_ref, slope_ref = refs[:-4]
     weight, hidden, low, sems = refs[-4:]
     step = pl.program_id(0)
@@ -459,7 +463,7 @@
 
     @pl.when(step == 0)
     def _():
-        for copy in start_rows(place, pieces, weight, sems):
+        for copy in start_rows(place, groups, pieces, weight, sems):
             copy.wait()
         branch = jnp.dot(context_ref[...], weight[:, :width], preferred_element_type=f32)
         unit, scale = normalized(mixed_ref[...] + branch + vec_ref[0:1])
@@ -499,7 +503,7 @@
     return [pl.BlockSpec(memory_space=pl.ANY)] * count
 
 
-def up_forward(place, context, mixed, vectors, bias_up, pieces):
+def up_forward(place, context, mixed, vectors, bias_up, groups, pieces):
     tokens, width = mixed.shape
     hidden_width = bias_up.shape[1]
     tile = 512
@@ -507,7 +511,7 @@
     last = lambda step, place: (0, jnp.maximum(step - 1, 0))
     last_t = lambda step, place: (jnp.maximum(step - 1, 0), 0)
     return pl.pallas_call(
-        up_kernel,
+        functools.partial(up_kernel, groups),
         grid_spec=pltpu.PrefetchScalarGridSpec(
             num_scalar_prefetch=1,
             grid=(hidden_width // tile + 1,),
@@ -531,7 +535,7 @@
                 pltpu.VMEM((width, width + hidden_width), bf16),
                 pltpu.VMEM((2, tokens, tile), f32),
                 pltpu.VMEM((tokens, width), bf16),
-                pltpu.SemaphoreType.DMA((16,)),
+                pltpu.SemaphoreType.DMA((48,)),
             ],
         ),
         out_shape=[
@@ -548,10 +552,10 @@
     )(place, context, mixed, vectors, bias_up, *pieces)
 
 
-def down_kernel(place, active_ref, unit_ref, vec_ref, grad_ref, *refs):
+def down_kernel(groups, place, active_ref, unit_ref, vec_ref, grad_ref, *refs):
     *pieces, out_ref, sum_ref, low_ref, small_ref = refs[:-2]
     weight, sems = refs[-2:]
-    for copy in start_rows(place, pieces, weight, sems):
+    for copy in start_rows(place, groups, pieces, weight, sems):
         copy.wait()
     tokens, width = unit_ref.shape
     half = tokens // 2
@@ -572,12 +576,12 @@
     small_ref[...] = jnp.concatenate(smalls + [jnp.zeros((5, width), f32)], axis=0)
 
 
-def down_forward(place, active, unit, vectors, grads, pieces):
+def down_forward(place, active, unit, vectors, grads, groups, pieces):
     tokens, width = unit.shape
     hidden_width = active.shape[1]
     vmem = pl.BlockSpec(memory_space=pltpu.VMEM)
     return pl.pallas_call(
-        down_kernel,
+        functools.partial(down_kernel, groups),
         grid_spec=pltpu.PrefetchScalarGridSpec(
             num_scalar_prefetch=1,
             grid=(),
@@ -599,9 +603,9 @@
     )(place, active, unit, vectors, grads, *pieces)
 
 
-def ffn_back_kernel(count, place, low_ref, slope_ref, sum_ref, unit_ref, scale_ref, vec_ref, *refs):
-    rest, down = refs[:count], refs[count : 2 * count]
-    hidden_ref, bias_ref, first_ref, branch_ref, context_ref, small_ref = refs[2 * count : -4]
+def ffn_back_kernel(groups, groups_down, count, place, low_ref, slope_ref, sum_ref, unit_ref, scale_ref, vec_ref, *refs):
+    rest, down = refs[: count[0]], refs[count[0] : sum(count)]
+    hidden_ref, bias_ref, first_ref, branch_ref, context_ref, small_ref = refs[sum(count) : -4]
     weight, weight_down, total, sems = refs[-4:]
     step = pl.program_id(0)
     tokens, width = unit_ref.shape
@@ -610,8 +614,8 @@
 
     @pl.when(step == 0)
     def _():
-        copies = start_rows(place, down, weight_down, sems)
-        copies += start_rows(place, rest, weight, sems, 16)
+        copies = start_rows(place, groups_down, down, weight_down, sems)
+        copies += start_rows(place, groups, rest, weight, sems, 16)
         total[...] = sum_ref[...]
         for copy in copies:
             copy.wait()
@@ -643,15 +647,17 @@
         small_ref[...] = jnp.concatenate(smalls + [jnp.zeros((5, width), f32)], axis=0)
 
 
-def ffn_back(place, low, slope, total, unit, scale, vectors, pieces_rest, pieces_down):
+def ffn_back(
+    place, low, slope, total, unit, scale, vectors, groups, pieces_rest, groups_down, pieces_down
+):
     tokens, width = unit.shape
     hidden_width = slope.shape[1]
     tile = 512
-    count = len(pieces_rest)
+    count = (len(pieces_rest), len(pieces_down))
     whole = lambda step, place: (0, 0)
     column = lambda step, place: (0, step)
     return pl.pallas_call(
-        functools.partial(ffn_back_kernel, count),
+        functools.partial(ffn_back_kernel, groups, groups_down, count),
         grid_spec=pltpu.PrefetchScalarGridSpec(
             num_scalar_prefetch=1,
             grid=(hidden_width // tile,),
@@ -663,7 +669,7 @@
                 pl.BlockSpec((tokens, 128), whole),
                 pl.BlockSpec(vectors.shape, whole),
             ]
-            + any_specs(2 * count),
+            + any_specs(sum(count)),
             out_specs=[
                 pl.BlockSpec((tokens, tile), column),
                 pl.BlockSpec((1, tile), column),
@@ -676,7 +682,7 @@
                 pltpu.VMEM((width, width + hidden_width), bf16),
                 pltpu.VMEM((hidden_width, width), bf16),
                 pltpu.VMEM((tokens, width), f32),
-                pltpu.SemaphoreType.DMA((32,)),
+                pltpu.SemaphoreType.DMA((64,)),
             ],
         ),
         out_shape=[
@@ -692,12 +698,14 @@
     )(place, low, slope, total, unit, scale, vectors, *pieces_rest, *pieces_down)
 
 
-def grad_rows_kernel(place, mine_ref, theirs_ref, h_ref, keep_ref, send_ref):
+def grad_rows_kernel(place, *refs):
+    *inputs, h_ref, keep_ref, send_ref = refs
     rows = keep_ref.shape[1]
-    both = jnp.concatenate([mine_ref[0], theirs_ref[0]], axis=0)
-    product = jnp.dot(both, h_ref[...], preferred_element_type=f32)
-    keep_ref[0] = product[:rows].astype(bf16)
-    send_ref[0] = product[rows:].astype(bf16)
+    both = jnp.concatenate([ref[0] for ref in inputs], axis=0)
+    product = jnp.dot(both, h_ref[...], preferred_element_type=f32).astype(bf16)
+    for index in range(2):
+        keep_ref[index] = product[index * rows : (index + 1) * rows]
+        send_ref[index] = product[(index + 2) * rows : (index + 3) * rows]
 
 
 def grad_by_rows(inputs_t, grads, place):
@@ -706,25 +714,31 @@
     rows = width // 16
     inputs_t = inputs_t.reshape(16, rows, tokens)
     half = jax.ShapeDtypeStruct((8, rows, columns), bf16)
-    out = pl.BlockSpec((1, rows, columns), lambda slot, place: (slot, 0, 0))
+    out = pl.BlockSpec((2, rows, columns), lambda step, place: (step, 0, 0))
+
+    def input_spec(index):
+        return pl.BlockSpec(
+            (1, rows, tokens),
+            lambda step, place: (
+                place[0] ^ (slot_mask(2 * step + (index & 1)) + (index >> 1)),
+                0,
+                0,
+            ),
+        )
+
     return pl.pallas_call(
         grad_rows_kernel,
         grid_spec=pltpu.PrefetchScalarGridSpec(
             num_scalar_prefetch=1,
-            grid=(8,),
-            in_specs=[
-                pl.BlockSpec((1, rows, tokens), lambda slot, place: (place[0] ^ slot_mask(slot), 0, 0)),
-                pl.BlockSpec(
-                    (1, rows, tokens), lambda slot, place: (place[0] ^ (slot_mask(slot) + 1), 0, 0)
-                ),
-                pl.BlockSpec((tokens, columns), lambda slot, place: (0, 0)),
-            ],
+            grid=(4,),
+            in_specs=[input_spec(index) for index in range(4)]
+            + [pl.BlockSpec((tokens, columns), lambda step, place: (0, 0))],
             out_specs=[out, out],
         ),
         out_shape=[half, half],
         cost_estimate=small_cost,
         name="grad_rows",
-    )(place, inputs_t, inputs_t, grads)
+    )(place, *[inputs_t] * 4, grads)
 
 
 def grad_columns_kernel(parts, place, *refs):
@@ -791,6 +805,40 @@
         out_shape=[half, half],
         cost_estimate=small_cost,
         name="grad_columns",
+    )(place, *operands)
+
+
+def key_back_kernel(place, gk_ref, gv_ref, wk_ref, wv_ref, out_ref):
+    total = dot_right_t(gk_ref[...], wk_ref[...]) + dot_right_t(gv_ref[...], wv_ref[...])
+    out_ref[...] = total.astype(out_ref.dtype)
+
+
+def own_back_kernel(place, first_ref, gq_ref, gk_ref, gv_ref, wq_ref, wk_ref, wv_ref, out_ref):
+    total = dot_right_t(gk_ref[...], wk_ref[...]) + dot_right_t(gv_ref[...], wv_ref[...])
+    out_ref[...] = first_ref[...] + total + dot_right_t(gq_ref[...], wq_ref[...])
+
+
+def input_back(place, weights, grad_keys, grad_values, others):
+    width = weights.shape[0]
+    tokens = grad_keys.shape[0] // 2
+    whole = pl.BlockSpec((tokens, width), lambda step, place: (0, 0))
+    row = lambda step, place: ((place[1] if others else 1 - place[1]), 0)
+    if others:
+        kernel, leading, first, dtype = own_back_kernel, [whole, whole], 0, f32
+    else:
+        kernel, leading, first, dtype = key_back_kernel, [], 1, bf16
+    operands = list(others) + [grad_keys, grad_values] + [weights] * (3 - first)
+    specs = [pl.BlockSpec((tokens, width), row)] * 2
+    for block in range(first, 3):
+        specs.append(pl.BlockSpec((width, width), lambda step, place, block=block: (0, block)))
+    return pl.pallas_call(
+        kernel,
+        grid_spec=pltpu.PrefetchScalarGridSpec(
+            num_scalar_prefetch=1, grid=(1,), in_specs=leading + specs, out_specs=whole
+        ),
+        out_shape=jax.ShapeDtypeStruct((tokens, width), dtype),
+        cost_estimate=small_cost,
+        name="input_back",
     )(place, *operands)
 
 
@@ -947,17 +995,19 @@
     pack_rest = jnp.concatenate([w_out, w_up], axis=1)
     other_low = swap(own_low)
     if fast:
+        split = (pack_rest.shape[1] // 2 + 127) // 256 * 256
         column_qkv = column_of(half_columns(pack_qkv, is_text))
-        parts_rest = column_parts(after(pack_rest, column_qkv))
-        eight = jnp.concatenate([column_qkv, exchange(column_qkv, 2)])
-        far = swap(eight)
-        pieces = [eight, exchange(eight, 1), far, exchange(far, 1)]
-        column_rest = jnp.stack([after(part, eight, far) for part in parts_rest])
-        parts_down = column_parts(after(w_down, column_rest))
-        pieces[0] = after(pieces[0], column_rest)
-        full_qkv = place_rows(place, pieces, pack_qkv.shape[1], place_halves_kernel)
+        parts_near = column_parts(after(half_columns(pack_rest[:, :split], is_text), column_qkv))
+        pieces_qkv = half_pieces(column_qkv)
+        column_near = jnp.stack([after(part, pieces_qkv[0]) for part in parts_near])
+        parts_far = column_parts(after(pack_rest[:, split:], column_near))
+        pieces_near = half_pieces(column_near)
+        pieces_qkv[2] = after(pieces_qkv[2], pieces_near[0])
+        pieces_qkv[3] = exchange(pieces_qkv[2], 1)
+        groups_qkv = (("halves", 0),)
     else:
-        full_qkv = lax.all_gather(pack_qkv, "page", axis=0, tiled=True)
+        groups_qkv = (("full", 0),)
+        pieces_qkv = [lax.all_gather(pack_qkv, "page", axis=0, tiled=True)]
 
     page_ids, pos_bins, bins_x, bins_y = token_ids(segments[0], box_x[0], box_y[0])
     bounds = page_bounds(segments[0], is_text)
@@ -995,34 +1045,45 @@
     )
     mixed_t = mixed_all.T
     if fast:
-        full_qkv = after(full_qkv, mixed_all, mixed_t, features, tables, bounds, own_flip)
+        pieces_qkv[0] = after(pieces_qkv[0], mixed_all, mixed_t, features, tables, bounds, own_flip)
+    full_qkv = place_rows(place, groups_qkv, pieces_qkv, (d_model, pack_qkv.shape[1]))
     full_query = full_qkv[:, :d_model]
     full_kv = full_qkv[:, d_model:]
     queries = ((plain_dot(mixed_low, full_query) + b_query).astype(bf16) * 0.125).astype(bf16)
     kv_bias = jnp.concatenate([jnp.zeros_like(b_value), b_value])
     keys_values = (plain_dot(mixed_all, full_kv) + kv_bias).astype(bf16)
-    context = attend(bounds, queries, keys_values, features, own_feats, tables)
-    if fast:
-        across_rest = exchange(column_rest, 2)
+    attend_in = queries
+    if fast:
+        column_far = jnp.stack([after(part, keys_values, queries) for part in parts_far])
+        parts_down = column_parts(after(w_down, column_far))
+        across_far = exchange(column_far, 2)
+        attend_in = after(queries, column_far)
+    context = attend(bounds, attend_in, keys_values, features, own_feats, tables)
+    if fast:
         column_down = jnp.stack([after(part, context) for part in parts_down])
-        across_rest = after(across_rest, column_down)
-        pieces_rest = [column_rest, exchange(column_rest, 1), across_rest, exchange(across_rest, 1)]
+        pieces_near[2] = after(pieces_near[2], column_down)
+        pieces_near[3] = exchange(pieces_near[2], 1)
+        across_far = after(across_far, column_down)
+        pieces_rest = pieces_near + row_pieces(column_far, across_far)
+        groups_rest = (("halves", 0), ("rows", split))
     else:
         pieces_rest = [lax.all_gather(pack_rest, "page", axis=0, tiled=True)]
+        groups_rest = (("full", 0),)
     vectors = jnp.stack(
         [b_out, gain_one, bias_one, b_down, gain_two, bias_two, jnp.zeros_like(b_out), b_out]
     )
     unit, scale, normed_low, normed_t, active, active_t, slope = up_forward(
-        place, context, mixed, vectors, b_up[None], pieces_rest
-    )
-    if fast:
-        across_down = exchange(column_down, 2)
-        pieces_down = [column_down, exchange(column_down, 1), across_down, exchange(across_down, 1)]
-        pieces_down[0] = after(pieces_down[0], active)
+        place, context, mixed, vectors, b_up[None], groups_rest, pieces_rest
+    )
+    if fast:
+        across_down = after(exchange(column_down, 2), active)
+        pieces_down = row_pieces(column_down, across_down)
+        groups_down = (("rows", 0),)
     else:
+        groups_down = (("full", 0),)
         pieces_down = [lax.all_gather(w_down, "page", axis=0, tiled=True)]
     output_row, grad_sum_two, grad_ffn, small_two = down_forward(
-        place, active, unit, vectors, cotangent[0, 0], pieces_down
+        place, active, unit, vectors, cotangent[0, 0], groups_down, pieces_down
     )
     grad_ffn_in = grad_ffn
     if fast:
@@ -1030,27 +1091,41 @@
         partner_down = exchange(send_down, 1)
         context_t = after(context, send_down).T
         partner_down = after(partner_down, context_t)
-        held_down, across_out_down = halve_across(place, keep_down, partner_down)
-        across_down = exchange(across_out_down, 2)
-        grad_ffn_in = after(grad_ffn, across_out_down)
+        held_down, plane_out = halve_plane(place, keep_down, partner_down)
+        plane_down = swap(plane_out)
+        grad_ffn_in = after(grad_ffn, plane_out)
     else:
         shard_down = summed_rows([(active_t, grad_ffn)])
         context_t = context.T
     grad_hidden, grad_b_up, grad_first, grad_branch, grad_context, small_one = ffn_back(
-        place, grad_ffn_in, slope, grad_sum_two, unit, scale, vectors, pieces_rest, pieces_down
+        place,
+        grad_ffn_in,
+        slope,
+        grad_sum_two,
+        unit,
+        scale,
+        vectors,
+        groups_rest,
+        pieces_rest,
+        groups_down,
+        pieces_down,
     )
     attend_in = grad_context
     if fast:
-        pairs = [(context_t, False, grad_branch), (normed_t, False, grad_hidden)]
+        plane_down = after(plane_down, grad_branch)
+        held_down, across_out = halve_across(place, held_down, plane_down)
+        across_down = exchange(across_out, 2)
+        branch_in = after(grad_branch, across_out)
+        pairs = [(context_t, False, branch_in), (normed_t, False, grad_hidden)]
         keep_rest, send_rest = grad_by_columns(pairs, place, d_model)
-        partner_rest = exchange(send_rest, 1)
-        across_down = after(across_down, send_rest)
+        across_down = after(across_down, keep_rest)
+        partner_rest = exchange(after(send_rest, across_down), 1)
         own_down, sends_down = column_sends(held_down, across_down)
         arrived_down = column_arrivals(sends_down)
         partner_rest = after(partner_rest, *sends_down)
-        held_rest, plane_out = halve_plane(place, keep_rest, partner_rest)
-        plane_rest = swap(plane_out)
-        attend_in = after(grad_context, plane_out)
+        held_rest, across_out = halve_across(place, keep_rest, partner_rest)
+        across_rest = exchange(across_out, 2)
+        attend_in = after(grad_context, across_out)
     else:
         shard_rest = summed_rows([(context_t, grad_branch), (normed_t, grad_hidden)])
     grad_queries, grad_keys, grad_values, grad_tables = attend_back(
@@ -1058,50 +1133,36 @@
     )
     grad_keys_in, grad_queries_in = grad_keys, grad_queries
     if fast:
-        plane_rest = after(plane_rest, grad_queries)
-        held_rest, across_out_rest = halve_across(place, held_rest, plane_rest)
-        across_rest = exchange(across_out_rest, 2)
         arrived_down = [after(part, grad_queries) for part in arrived_down]
         total_down = column_total(own_down, arrived_down)
         far_down = swap(total_down)
-        grad_queries_in = after(grad_queries, across_out_rest, total_down)
+        across_rest = after(across_rest, total_down)
+        own_rest, sends_rest = column_sends(held_rest, across_rest)
+        arrived_rest = column_arrivals(sends_rest)
+        grad_queries_in = after(grad_queries, *sends_rest)
     pairs = [(mixed_t, True, grad_queries_in), (mixed_t, False, grad_keys), (mixed_t, False, grad_values)]
     if fast:
         keep_qkv, send_qkv = grad_by_columns(pairs, place, d_model)
         partner_qkv = exchange(send_qkv, 1)
-        across_rest = after(across_rest, send_qkv)
-        own_rest, sends_rest = column_sends(held_rest, across_rest)
-        arrived_rest = column_arrivals(sends_rest)
-        far_down = after(far_down, send_qkv)
-        partner_qkv = after(partner_qkv, far_down, *sends_rest)
-        held_qkv, across_out_qkv = halve_across(place, keep_qkv, partner_qkv)
-        across_qkv = exchange(across_out_qkv, 2)
-        grad_keys_in = after(grad_keys, across_out_qkv)
+        grad_keys_in = after(grad_keys, send_qkv)
     else:
         shard_qkv = summed_rows(
             [(mixed_low.T, grad_queries), (mixed_t, grad_keys), (mixed_t, grad_values)]
         )
     grad_b_query = column_sum(grad_queries)
     grad_b_value = column_sum(grad_values)
-    from_keys = dot_right_t(grad_keys_in, full_kv[:, :d_model]) + dot_right_t(
-        grad_values, full_kv[:, d_model:]
-    )
-    to_other = jnp.where(is_text, from_keys[TEXT:], from_keys[:TEXT]).astype(bf16)
+    to_other = input_back(place, full_qkv, grad_keys_in, grad_values, ())
     from_other = swap(to_other)
-    if fast:
-        grad_queries = after(grad_queries, to_other)
-    from_queries = dot_right_t(grad_queries, full_query)
-    if fast:
-        across_qkv = after(across_qkv, from_queries)
-        own_qkv, sends_qkv = column_sends(held_qkv, across_qkv)
-        arrived_qkv = column_arrivals(sends_qkv)
-        from_other = after(from_other, *sends_qkv)
-    grad_mixed = (
-        grad_first
-        + from_queries
-        + jnp.where(is_text, from_keys[:TEXT], from_keys[TEXT:])
-        + from_other.astype(f32)
-    )
+    grad_values_in = grad_values
+    if fast:
+        partner_qkv = after(partner_qkv, to_other)
+        held_qkv, across_out = halve_across(place, keep_qkv, partner_qkv)
+        across_qkv = exchange(across_out, 2)
+        grad_values_in = after(grad_values, across_out)
+    own_part = input_back(place, full_qkv, grad_keys, grad_values_in, (grad_first, grad_queries))
+    if fast:
+        from_other = after(from_other, own_part)
+    grad_mixed = own_part + from_other.astype(f32)
     grad_in, grad_conv_w, grad_conv_b = mix_pull(grad_mixed)
 
     table_rows = grad_tables[:, :3].reshape(6, 768)
@@ -1125,19 +1186,24 @@
         arrived_rest = [after(part, packed) for part in arrived_rest]
         total_rest = column_total(own_rest, arrived_rest)
         far_rest = swap(total_rest)
-        arrived_qkv = [after(part, total_rest) for part in arrived_qkv]
+        across_qkv = after(across_qkv, total_rest)
+        own_qkv, sends_qkv = column_sends(held_qkv, across_qkv)
+        arrived_qkv = column_arrivals(sends_qkv)
+        packed = after(packed, *sends_qkv)
+    packed = sum_everywhere(packed)
+    if fast:
+        arrived_qkv = [after(part, packed) for part in arrived_qkv]
         total_qkv = column_total(own_qkv, arrived_qkv)
         far_qkv = swap(total_qkv)
-    packed = sum_everywhere(packed)
     g_tables = packed[16:22].reshape(HEADS, 3, LANES)
     if fast:
-        shard_down = total_down.astype(f32) + far_down.astype(f32)
+        shard_down = jnp.where(
+            is_text,
+            jnp.concatenate([total_down, far_down], axis=1),
+            jnp.concatenate([far_down, total_down], axis=1),
+        ).astype(f32)
         shard_qkv = total_qkv.astype(f32) + far_qkv.astype(f32)
-        shard_rest = jnp.where(
-            is_text,
-            jnp.concatenate([total_rest, far_rest], axis=1),
-            jnp.concatenate([far_rest, total_rest], axis=1),
-        ).astype(f32)
+        shard_rest = total_rest.astype(f32) + far_rest.astype(f32)
     return (
         output_row[None, None],
         grad_in.astype(bf16)[None, None],

time: 407 us -> 395 us (0.971)
  waiting for transfers between devices: 99.3 us -> 83.5 us
  Pallas kernels: 157 us -> 170 us
  matrix products: 17.8 us -> 9.48 us
  starting transfers between devices: 48.5 us -> 54.9 us
  other arithmetic: 37.3 us -> 31.9 us
    ppermute x33 -> x39, waiting for transfers between devices: 82 us -> 56.7 us  [exchange(): return lax.ppermute(values, 'page', [(i, i ^ mask) for i in range(count)])]
    pallas_call x4 -> x6, Pallas kernels: 53.8 us -> 66.9 us  [the longest x1 20 us: up_forward(): pl.pallas_call(functools.partial(up_kernel, groups), grid_spec=pltpu.Pref...]
    ppermute x8 -> x9, waiting for transfers between devices: 12.4 us -> 22.8 us  [swap(): return lax.ppermute(values, 'mod', [(0, 1), (1, 0)])]
    dot_general x3 -> x0, matrix products: 8.19 us -> none  [dot_right_t(): lax.dot_general(left_side, right_side, (((1,), (1,)), ((), ())), preferre...]
    ppermute x33 -> x39, starting transfers between devices: 36.7 us -> 40.3 us  [exchange(): return lax.ppermute(values, 'page', [(i, i ^ mask) for i in range(count)])]
    unnamed x101 -> x119, local copies, waits for them, and re-layouts: 13.9 us -> 11.1 us
    ppermute x8 -> x9, starting transfers between devices: 8.9 us -> 9.07 us  [swap(): return lax.ppermute(values, 'mod', [(0, 1), (1, 0)])]
  transfers between devices with their start and end apart: 45 -> 52, of which waited for: 12 -> 21; matrix products, arithmetic and copies ran while one was open for 22% -> 18% of each run, Pallas kernels for 20% -> 31%
where the time goes in v6:
time: 395 us; the launch traced here: 389 us
  Pallas kernels  170 us (43%)
  waiting for transfers between devices  83.5 us (21%)
  starting transfers between devices  54.9 us (14%)
  local copies, waits for them, and re-layouts  37.4 us (9%)
  other arithmetic  31.9 us (8%)
  matrix products  9.48 us (2%)
    ppermute x39, waiting for transfers between devices, exchange(): return lax.ppermute(values, 'page', [(i, i ^ mask) for i in range(count)])  56.7 us
    ppermute x39, starting transfers between devices, exchange(): return lax.ppermute(values, 'page', [(i, i ^ mask) for i in range(count)])  40.3 us
    pallas_call x1, Pallas kernels, attend_back(): pl.pallas_call(attend_back_kernel, grid_spec=pltpu.PrefetchScalarGridSpec...  29.7 us
    ppermute x9, waiting for transfers between devices, swap(): return lax.ppermute(values, 'mod', [(0, 1), (1, 0)])  22.8 us
    pallas_call x4, Pallas kernels, halve_call(): pl.pallas_call(first_half_kernel, grid_spec=pltpu.PrefetchScalarGridSpec(...  20.7 us
    pallas_call x1, Pallas kernels, up_forward(): pl.pallas_call(functools.partial(up_kernel, groups), grid_spec=pltpu.Pref...  20 us
    pallas_call x1, Pallas kernels, ffn_back(): pl.pallas_call(functools.partial(ffn_back_kernel, groups, groups_down, co...  19 us
    pallas_call x2, Pallas kernels, grad_by_columns(): pl.pallas_call(functools.partial(grad_columns_kernel, parts), grid_spec=p...  18.2 us
  transfers between devices with their start and end apart: 52, of which 21 were waited for; matrix products, arithmetic and copies ran while one was open for 18% of the time, Pallas kernels for 31%

profile of v6, /device:TPU:0, one launch (start us, length us, event | category | flops | bytes accessed | tf_op | source)
XLA Modules:
  0.0 388.9 jit_solution(1449709061698587349)
XLA Ops:
  0.7 1.7 constant_dynamic-update-slice_fusion.4
  2.4 5.1 %collective-permute-start.2 = (bf16[48,1152]{1,0:T(8,128)(2,1)S(1)}, bf16[48,1152]{1,0:T(8,128)(2,1)S(1)}, u32[]{:S(2)}, u32[]{:S(2)}) collective-permute-start(bf16[48,1152]{1,0:T(8,128)(2,1)S(1)} %get-tuple-element.231), channel_id=1, source_target_pairs={{0,12},{1,13},{2,14},{3,15},{4,8},{5,9},{6,10},{7,11},{8,4},{9,5},... | collective-permute-start | bytes 331784 | tf_op jit(solution)/shard_map/ppermute | solution.py:347
  14.0 2.4 bitcast_convert_fusion
  26.3 3.7 collective-permute-start.9
  34.3 6.6 %collective-permute-done.3 = bf16[4,48,1152]{2,1,0:T(8,128)(2,1)S(1)} collective-permute-done((bf16[4,48,1152]{2,1,0:T(8,128)(2,1)S(1)}, bf16[4,48,1152]{2,1,0:T(8,128)(2,1)S(1)}, u32[]{:S(2)}, u32[]{:S(2)}) %collective-permute-start.3) | collective-permute-done | bytes 442400 | tf_op jit(solution)/shard_map/ppermute | solution.py:347
  41.7 3.5 collective-permute-start.14
  53.3 12.3 %collective-permute-done.6.refs_2_ = bf16[8,48,1152]{2,1,0:T(8,128)(2,1)S(1)} collective-permute-done((bf16[8,48,1152]{2,1,0:T(8,128)(2,1)}, bf16[8,48,1152]{2,1,0:T(8,128)(2,1)S(1)}, u32[]{:S(2)}, u32[]{:S(2)}) %collective-permute-start.6) | collective-permute-done | bytes 884768 | tf_op jit(solution)/shard_map/ppermute | solution.py:957
  65.7 2.1 broadcast_select_fusion.1
  70.2 5.0 %place_rows.1.wk_ref.wv_ref.wq_ref = bf16[768,2304]{1,0:T(8,128)(2,1)} custom-call(s32[2]{0:T(128)} %pad_add_fusion.1.place, bf16[8,48,1152]{2,1,0:T(8,128)(2,1)} %constant_dynamic-update-slice_fusion.refs_0_, bf16[8,48,1152]{2,1,0:T(8,128)(2,1)} %collective-permute-done.5.refs_1_, bf16[8,48,1152]{2,1,0:T(8,128)(2,1)} %copy-done.14, ...), custom_call_target="tpu_custom_call" | custom-call | flops 1000 | bytes 1000 | tf_op jit(solution)/shard_map/place_rows/pallas_call | solution.py:364
  75.3 6.5 %add_convert_fusion.k_ref.v_ref = bf16[1024,1536]{1,0:T(8,128)(2,1)} fusion(f32[1536]{0:T(1024)S(1)} %copy-done.34, bf16[768,2304]{1,0:T(8,128)(2,1)} %place_rows.1.wk_ref.wv_ref.wq_ref, bf16[512,768]{1,0:T(8,128)(2,1)S(1)} %broadcast_select_fusion, bf16[512,768]{1,0:T(8,128)(2,1)S(1)} %get-tuple-element.227), kind=kOutput, calls=%fused_computation | convolution fusion | flops 2422210560 | bytes 7084032 | tf_op jit(solution)/shard_map/dot_general | solution.py:85
  81.8 2.9 fusion.3.q_ref
  86.2 1.8 collective-permute-start.19
  88.9 1.7 collective-permute-start.17
  92.3 12.9 %attend.1.context_ref = bf16[512,768]{1,0:T(8,128)(2,1)} custom-call(s32[48]{0:T(128)} %concatenate.71.bounds, bf16[512,768]{1,0:T(8,128)(2,1)} %fusion.3.q_ref, bf16[1024,1536]{1,0:T(8,128)(2,1)} %add_convert_fusion.k_ref.v_ref, bf16[1024,1536]{1,0:T(8,128)(2,1)} %add_convert_fusion.k_ref.v_ref, bf16[1024,128]{1,0:T(8,128)(2,1)} %copy-done.12, ...), custom_call_target="tpu_custom_call" | custom-call | flops 1000 | bytes 1000 | tf_op jit(solution)/shard_map/attend/pallas_call | solution.py:273
  105.3 10.1 %collective-permute-done.18 = bf16[192,768]{1,0:T(8,128)(2,1)S(1)} collective-permute-done((bf16[192,768]{1,0:T(8,128)(2,1)S(1)}, bf16[192,768]{1,0:T(8,128)(2,1)S(1)}, u32[]{:S(2)}, u32[]{:S(2)}) %collective-permute-start.18) | collective-permute-done | bytes 294944 | tf_op jit(solution)/shard_map/ppermute | solution.py:347
  123.9 20.0 %up_forward.1 = (f32[512,768]{1,0:T(8,128)}, f32[512,128]{1,0:T(8,128)}, bf16[512,768]{1,0:T(8,128)(2,1)}, bf16[768,512]{1,0:T(8,128)(2,1)}, bf16[512,3072]{1,0:...) custom-call(s32[2]{0:T(128)} %pad_add_fusion.1.place, bf16[512,768]{1,0:T(8,128)(2,1)} %attend.1.context_ref, ...), custom_call_target="tpu_custom_call" | custom-call | flops 1000 | bytes 1000 | tf_op jit(solution)/shard_map/up_forward/pallas_call | solution.py:513
  145.5 3.2 collective-permute-done.26.refs_3_.refs_11_
  148.7 10.6 %down_forward.1 = (bf16[512,768]{1,0:T(8,128)(2,1)}, f32[512,768]{1,0:T(8,128)}, bf16[512,768]{1,0:T(8,128)(2,1)}, f32[8,768]{1,0:T(8,128)}) custom-call(s32[2]{0:T(128)} %pad_add_fusion.1.place, bf16[512,3072]{1,0:T(8,128)(2,1)} %get-tuple-element.135.active_ref, f32[512,768]{1,0:T(8,128)} %get-tuple-element.136.unit_ref, f32[8,768]{1,0:T(8,128)} %stack.147.vec_ref, ...), custom_call_target="tpu_custom_call" | custom-call | flops 1000 | bytes 1000 | tf_op jit(solution)/shard_map/down_forward/pallas_call | solution.py:583
  159.3 7.2 %grad_rows.1 = (bf16[8,192,768]{2,1,0:T(8,128)(2,1)}, bf16[8,192,768]{2,1,0:T(8,128)(2,1)}) custom-call(s32[2]{0:T(128)} %pad_add_fusion.1.place, bf16[16,192,512]{2,1,0:T(8,128)(2,1)} %bitcast.60, bf16[16,192,512]{2,1,0:T(8,128)(2,1)} %bitcast.61, bf16[16,192,512]{2,1,0:T(8,128)(2,1)} %bitcast.62, bf16[16,192,512]{2,1,0:T(8,128)(2,1)} %bitcast.63, ...), custom_call_target="tpu_custom_call" | custom-call | flops 1000 | bytes 1000 | tf_op jit(solution)/shard_map/grad_rows/pallas_call | solution.py:729
  167.9 3.6 collective-permute-done.27.part_near.part_far
  171.4 5.2 %halve.4 = (f32[8,192,384]{2,1,0:T(8,128)}, bf16[8,192,384]{2,1,0:T(8,128)(2,1)}) custom-call(s32[2]{0:T(128)} %pad_add_fusion.1.place, bf16[8,192,768]{2,1,0:T(8,128)(2,1)} %get-tuple-element.141.keep_near.keep_far, bf16[8,192,768]{2,1,0:T(8,128)(2,1)} %collective-permute-done.27.part_near.part_far, ...), custom_call_target="tpu_custom_call" | custom-call | flops 1000 | bytes 1000 | tf_op jit(solution)/shard_map/halve/pallas_call | solution.py:852
  177.2 19.0 %ffn_back.1 = (bf16[512,3072]{1,0:T(8,128)(2,1)}, f32[1,3072]{1,0:T(1,128)}, f32[512,768]{1,0:T(8,128)}, bf16[512,768]{1,0:T(8,128)(2,1)}, bf16[512,768]{1,0:T(8,128)(2,1)}, /*index=5*/f32[8,768]{1,0:T(8,128)}) custom-call(s32[2]{0:T(128)} %pad_add_fusion.1.place, bf16[512,768]{1,0:T(8,128)(2,1)} %get-tuple-element.146.refs_4_.low_ref, ...), custom_call_target="tpu_custom_call" | custom-call | flops 1000 | bytes 1000 | tf_op jit(solution)/shard_map/ffn_back/pallas_call | solution.py:659
  196.3 8.6 %collective-permute-done.28.part_near.part_far = bf16[8,192,384]{2,1,0:T(8,128)(2,1)S(1)} collective-permute-done((bf16[8,192,384]{2,1,0:T(8,128)(2,1)}, bf16[8,192,384]{2,1,0:T(8,128)(2,1)S(1)}, u32[]{:S(2)}, u32[]{:S(2)}) %collective-permute-start.28) | collective-permute-done | bytes 1179680 | tf_op jit(solution)/shard_map/ppermute | solution.py:957
  205.9 4.6 %halve.5 = (f32[4,192,384]{2,1,0:T(8,128)}, bf16[4,192,384]{2,1,0:T(8,128)(2,1)}) custom-call(s32[2]{0:T(128)} %pad_add_fusion.1.place, f32[8,192,384]{2,1,0:T(8,128)} %get-tuple-element.153.keep_near.keep_far, bf16[8,192,384]{2,1,0:T(8,128)(2,1)} %copy-done.11, f32[8,192,384]{2,1,0:T(8,128)} %get-tuple-element.153.keep_near.keep_far, ...), custom_call_target="tpu_custom_call" | custom-call | flops 1000 | bytes 1000 | tf_op jit(solution)/shard_map/halve/pallas_call | solution.py:852
  211.1 9.2 %grad_columns.2 = (bf16[8,48,3840]{2,1,0:T(8,128)(2,1)}, bf16[8,48,3840]{2,1,0:T(8,128)(2,1)}) custom-call(s32[2]{0:T(128)} %pad_add_fusion.1.place, bf16[768,512]{1,0:T(8,128)(2,1)} %bitcast.65, bf16[512,768]{1,0:T(8,128)(2,1)} %get-tuple-element.156.refs_1_, bf16[768,512]{1,0:T(8,128)(2,1)} %get-tuple-element.157.refs_2_, ...), custom_call_target="tpu_custom_call" | custom-call | flops 1000 | bytes 1000 | tf_op jit(solution)/shard_map/grad_columns/pallas_call | solution.py:796
  220.3 5.1 %collective-permute-done.29.across_ref = bf16[4,192,384]{2,1,0:T(8,128)(2,1)S(1)} collective-permute-done((bf16[4,192,384]{2,1,0:T(8,128)(2,1)}, bf16[4,192,384]{2,1,0:T(8,128)(2,1)S(1)}, u32[]{:S(2)}, u32[]{:S(2)}) %collective-permute-start.29) | collective-permute-done | bytes 589856 | tf_op jit(solution)/shard_map/ppermute | solution.py:347
  226.2 2.3 column_sends.3
  228.5 2.6 collective-permute-done.30.part_near.part_far
  231.1 5.9 %halve.6 = (f32[4,48,3840]{2,1,0:T(8,128)}, bf16[4,48,3840]{2,1,0:T(8,128)(2,1)}) custom-call(s32[2]{0:T(128)} %pad_add_fusion.1.place, bf16[8,48,3840]{2,1,0:T(8,128)(2,1)} %get-tuple-element.159.keep_near.keep_far, bf16[8,48,3840]{2,1,0:T(8,128)(2,1)} %collective-permute-done.30.part_near.part_far, ...), custom_call_target="tpu_custom_call" | custom-call | flops 1000 | bytes 1000 | tf_op jit(solution)/shard_map/halve/pallas_call | solution.py:852
  237.5 2.8 collective-permute-start.34
  243.5 29.7 %attend_back.1 = (bf16[512,768]{1,0:T(8,128)(2,1)}, bf16[1024,768]{1,0:T(8,128)(2,1)}, bf16[1024,768]{1,0:T(8,128)(2,1)}, f32[12,8,128]{2,1,0:T(8,128)}) custom-call(s32[48]{0:T(128)} %concatenate.71.bounds, bf16[512,768]{1,0:T(8,128)(2,1)} %fusion.3.q_ref, bf16[1024,1536]{1,0:T(8,128)(2,1)} %add_convert_fusion.k_ref.v_ref, ...), custom_call_target="tpu_custom_call" | custom-call | flops 1000 | bytes 1000 | tf_op jit(solution)/shard_map/attend_back/pallas_call | solution.py:298
  274.9 6.9 %column_sends.4 = (f32[48,3840]{1,0:T(8,128)}, bf16[48,3840]{1,0:T(8,128)(2,1)}, bf16[48,3840]{1,0:T(8,128)(2,1)}, bf16[48,3840]{1,0:T(8,128)(2,1)}) custom-call(f32[4,48,3840]{2,1,0:T(8,128)} %get-tuple-element.173.held_ref, bf16[4,48,3840]{2,1,0:T(8,128)(2,1)} %collective-permute-done.31.across_ref), custom_call_target="tpu_custom_call" | custom-call | flops 1000 | bytes 1000 | tf_op jit(solution)/shard_map/column_sends/pallas_call | solution.py:896
  281.8 9.0 %grad_columns.3 = (bf16[8,48,2304]{2,1,0:T(8,128)(2,1)}, bf16[8,48,2304]{2,1,0:T(8,128)(2,1)}) custom-call(s32[2]{0:T(128)} %pad_add_fusion.1.place, bf16[768,1024]{1,0:T(8,128)(2,1)} %copy.56.refs_0_.refs_2_.refs_4_, bf16[512,768]{1,0:T(8,128)(2,1)} %get-tuple-element.182.refs_1_.gq_ref, bf16[768,1024]{1,0:T(8,128)(2,1)} %copy.56.refs_0_.refs_2_.refs_4_, ...), custom_call_target="tpu_custom_call" | custom-call | flops 1000 | bytes 1000 | tf_op jit(solution)/shard_map/grad_columns/pallas_call | solution.py:796
  291.0 5.2 %input_back.2 = bf16[512,768]{1,0:T(8,128)(2,1)} custom-call(s32[2]{0:T(128)} %pad_add_fusion.1.place, bf16[1024,768]{1,0:T(8,128)(2,1)} %get-tuple-element.185.refs_3_.gk_ref, bf16[1024,768]{1,0:T(8,128)(2,1)} %get-tuple-element.188.refs_5_.gv_ref, bf16[768,2304]{1,0:T(8,128)(2,1)} %place_rows.1.wk_ref.wv_ref.wq_ref, ...), custom_call_target="tpu_custom_call" | custom-call | flops 1000 | bytes 1000 | tf_op jit(solution)/shard_map/input_back/pallas_call | solution.py:834
  307.2 2.8 collective-permute-start.39
  311.1 4.9 %halve.7 = (f32[4,48,2304]{2,1,0:T(8,128)}, bf16[4,48,2304]{2,1,0:T(8,128)(2,1)}) custom-call(s32[2]{0:T(128)} %pad_add_fusion.1.place, bf16[8,48,2304]{2,1,0:T(8,128)(2,1)} %get-tuple-element.183.keep_near.keep_far, bf16[8,48,2304]{2,1,0:T(8,128)(2,1)} %collective-permute-done.35.part_near.part_far, ...), custom_call_target="tpu_custom_call" | custom-call | flops 1000 | bytes 1000 | tf_op jit(solution)/shard_map/halve/pallas_call | solution.py:852
  316.1 7.0 %input_back.3 = f32[512,768]{1,0:T(8,128)} custom-call(s32[2]{0:T(128)} %pad_add_fusion.1.place, f32[512,768]{1,0:T(8,128)} %get-tuple-element.150.first_ref, bf16[512,768]{1,0:T(8,128)(2,1)} %get-tuple-element.182.refs_1_.gq_ref, bf16[1024,768]{1,0:T(8,128)(2,1)} %get-tuple-element.185.refs_3_.gk_ref, bf16[1024,768]{1,0:T(8,128)(2,1)} %get-tuple-element.188.refs_5_.gv_ref, ...), custom_call_target="tpu_custom_call" | custom-call | flops 1000 | bytes 1000 | tf_op jit(solution)/shard_map/input_back/pallas_call | solution.py:834
  324.6 3.1 fusion.20
  327.8 2.3 concatenate.91
  330.1 4.2 %collective-permute-done.40 = bf16[48,3840]{1,0:T(8,128)(2,1)} collective-permute-done((bf16[48,3840]{1,0:T(8,128)(2,1)}, bf16[48,3840]{1,0:T(8,128)(2,1)}, u32[]{:S(2)}, u32[]{:S(2)}) %collective-permute-start.40) | collective-permute-done | bytes 368672 | tf_op jit(solution)/shard_map/ppermute | solution.py:347
  338.1 5.8 %collective-permute-done.37.across_ref = bf16[4,48,2304]{2,1,0:T(8,128)(2,1)} collective-permute-done((bf16[4,48,2304]{2,1,0:T(8,128)(2,1)}, bf16[4,48,2304]{2,1,0:T(8,128)(2,1)}, u32[]{:S(2)}, u32[]{:S(2)}) %collective-permute-start.37) | collective-permute-done | bytes 884768 | tf_op jit(solution)/shard_map/ppermute | solution.py:347
  343.9 4.7 %column_sends.5 = (f32[48,2304]{1,0:T(8,128)}, bf16[48,2304]{1,0:T(8,128)(2,1)}, bf16[48,2304]{1,0:T(8,128)(2,1)}, bf16[48,2304]{1,0:T(8,128)(2,1)}) custom-call(f32[4,48,2304]{2,1,0:T(8,128)} %get-tuple-element.194.held_ref, bf16[4,48,2304]{2,1,0:T(8,128)(2,1)} %collective-permute-done.37.across_ref), custom_call_target="tpu_custom_call" | custom-call | flops 1000 | bytes 1000 | tf_op jit(solution)/shard_map/column_sends/pallas_call | solution.py:896
  351.5 2.0 fusion.6
  356.3 2.5 collective-permute-done.43
  358.8 2.4 collective-permute-start.44
  364.5 2.4 collective-permute-start.48
  372.4 9.1 %collective-permute-done.47 = bf16[48,2304]{1,0:T(8,128)(2,1)S(1)} collective-permute-done((bf16[48,2304]{1,0:T(8,128)(2,1)}, bf16[48,2304]{1,0:T(8,128)(2,1)S(1)}, u32[]{:S(2)}, u32[]{:S(2)}) %collective-permute-start.47) | collective-permute-done | bytes 221216 | tf_op jit(solution)/shard_map/ppermute | solution.py:347
  381.6 1.9 collective-permute-start.49
  (301 shorter events, 92.2 us)
Async XLA Ops:
  2.4 23.9 %collective-permute-start.2 = (bf16[48,1152]{1,0:T(8,128)(2,1)S(1)}, bf16[48,1152]{1,0:T(8,128)(2,1)S(1)}, u32[]{:S(2)}, u32[]{:S(2)}) collective-permute-start(bf16[48,1152]{1,0:T(8,128)(2,1)S(1)} %get-tuple-element.231), channel_id=1, source_target_pairs={{0,12},{1,13},{2,14},{3,15},{4,8},{5,9},{6,10},{7,11},{8,4},{9,5},... | collective-permute-start | bytes 331784 | tf_op jit(solution)/shard_map/ppermute | solution.py:347
  7.5 18.8 %collective-permute-start.1 = (bf16[48,1152]{1,0:T(8,128)(2,1)S(1)}, bf16[48,1152]{1,0:T(8,128)(2,1)S(1)}, u32[]{:S(2)}, u32[]{:S(2)}) collective-permute-start(bf16[48,1152]{1,0:T(8,128)(2,1)S(1)} %get-tuple-element.231), channel_id=1, source_target_pairs={{0,8},{1,9},{2,10},{3,11},{4,12},{5,13},{6,14},{7,15},{8,0},{9,1},... | collective-permute-start | bytes 331784 | tf_op jit(solution)/shard_map/ppermute | solution.py:347
  7.5 18.8 %collective-permute-start = (bf16[48,1152]{1,0:T(8,128)(2,1)S(1)}, bf16[48,1152]{1,0:T(8,128)(2,1)S(1)}, u32[]{:S(2)}, u32[]{:S(2)}) collective-permute-start(bf16[48,1152]{1,0:T(8,128)(2,1)S(1)} %get-tuple-element.231), channel_id=1, source_target_pairs={{0,4},{1,5},{2,6},{3,7},{4,0},{5,1},{6,2},{7,3},{8,12},{9,13},{10,... | collective-permute-start | bytes 331784 | tf_op jit(solution)/shard_map/ppermute | solution.py:347
  8.1 41.8 %collective-permute-start.4 = (bf16[512,768]{1,0:T(8,128)(2,1)}, bf16[512,768]{1,0:T(8,128)(2,1)S(1)}, u32[]{:S(2)}, u32[]{:S(2)}) collective-permute-start(bf16[512,768]{1,0:T(8,128)(2,1)} %bitcast.64), channel_id=1, source_target_pairs={{0,16},{16,0},{1,17},{17,1},{2,18},{18,2},{3,19},{19,3},{4,20},{20... | collective-permute-start | bytes 2359304 | tf_op jit(solution)/shard_map/ppermute | solution.py:957
  26.3 15.3 %collective-permute-start.9 = (bf16[48,896]{1,0:T(8,128)(2,1)S(1)}, bf16[48,896]{1,0:T(8,128)(2,1)S(1)}, u32[]{:S(2)}, u32[]{:S(2)}) collective-permute-start(bf16[48,896]{1,0:T(8,128)(2,1)S(1)} %fusion.8), channel_id=1, source_target_pairs={{0,12},{1,13},{2,14},{3,15},{4,8},{5,9},{6,10},{7,11},{8,4},{9,5},... | collective-permute-start | bytes 258056 | tf_op jit(solution)/shard_map/ppermute | solution.py:347
  30.0 11.7 %collective-permute-start.8 = (bf16[48,896]{1,0:T(8,128)(2,1)S(1)}, bf16[48,896]{1,0:T(8,128)(2,1)S(1)}, u32[]{:S(2)}, u32[]{:S(2)}) collective-permute-start(bf16[48,896]{1,0:T(8,128)(2,1)S(1)} %fusion.8), channel_id=1, source_target_pairs={{0,8},{1,9},{2,10},{3,11},{4,12},{5,13},{6,14},{7,15},{8,0},{9,1},... | collective-permute-start | bytes 258056 | tf_op jit(solution)/shard_map/ppermute | solution.py:347
  30.0 11.7 %collective-permute-start.7 = (bf16[48,896]{1,0:T(8,128)(2,1)S(1)}, bf16[48,896]{1,0:T(8,128)(2,1)S(1)}, u32[]{:S(2)}, u32[]{:S(2)}) collective-permute-start(bf16[48,896]{1,0:T(8,128)(2,1)S(1)} %fusion.8), channel_id=1, source_target_pairs={{0,4},{1,5},{2,6},{3,7},{4,0},{5,1},{6,2},{7,3},{8,12},{9,13},{10,... | collective-permute-start | bytes 258056 | tf_op jit(solution)/shard_map/ppermute | solution.py:347
  30.8 10.1 %collective-permute-start.3 = (bf16[4,48,1152]{2,1,0:T(8,128)(2,1)S(1)}, bf16[4,48,1152]{2,1,0:T(8,128)(2,1)S(1)}, u32[]{:S(2)}, u32[]{:S(2)}) collective-permute-start(bf16[4,48,1152]{2,1,0:T(8,128)(2,1)S(1)} %pad_maximum_fusion.3), channel_id=1, source_target_pairs={{0,2},{1,3},{2,0},{3,1},{4,6},{5,7},{6,4},{7,5},{8,10},{9,11},{10,... | collective-permute-start | bytes 1327112 | tf_op jit(solution)/shard_map/ppermute | solution.py:347
  41.7 43.0 %collective-permute-start.14 = (bf16[48,2048]{1,0:T(8,128)(2,1)}, bf16[48,2048]{1,0:T(8,128)(2,1)}, u32[]{:S(2)}, u32[]{:S(2)}) collective-permute-start(bf16[48,2048]{1,0:T(8,128)(2,1)} %slice.168), channel_id=1, source_target_pairs={{0,12},{1,13},{2,14},{3,15},{4,8},{5,9},{6,10},{7,11},{8,4},{9,5},... | collective-permute-start | bytes 589832 | tf_op jit(solution)/shard_map/ppermute | solution.py:347
  45.3 39.5 %collective-permute-start.13 = (bf16[48,2048]{1,0:T(8,128)(2,1)}, bf16[48,2048]{1,0:T(8,128)(2,1)}, u32[]{:S(2)}, u32[]{:S(2)}) collective-permute-start(bf16[48,2048]{1,0:T(8,128)(2,1)} %slice.168), channel_id=1, source_target_pairs={{0,8},{1,9},{2,10},{3,11},{4,12},{5,13},{6,14},{7,15},{8,0},{9,1},... | collective-permute-start | bytes 589832 | tf_op jit(solution)/shard_map/ppermute | solution.py:347
  45.3 7.2 %collective-permute-start.10 = (bf16[4,48,896]{2,1,0:T(8,128)(2,1)S(1)}, bf16[4,48,896]{2,1,0:T(8,128)(2,1)S(1)}, u32[]{:S(2)}, u32[]{:S(2)}) collective-permute-start(bf16[4,48,896]{2,1,0:T(8,128)(2,1)S(1)} %pad_maximum_fusion.4), channel_id=1, source_target_pairs={{0,2},{1,3},{2,0},{3,1},{4,6},{5,7},{6,4},{7,5},{8,10},{9,11},{10,... | collective-permute-start | bytes 1032200 | tf_op jit(solution)/shard_map/ppermute | solution.py:347
  47.4 18.2 %collective-permute-start.6 = (bf16[8,48,1152]{2,1,0:T(8,128)(2,1)}, bf16[8,48,1152]{2,1,0:T(8,128)(2,1)S(1)}, u32[]{:S(2)}, u32[]{:S(2)}) collective-permute-start(bf16[8,48,1152]{2,1,0:T(8,128)(2,1)} %constant_dynamic-update-slice_fusion.refs_0_), channel_id=1, source_target_pairs={{0,16},{16,0},{1,17},{17,1},{2,18},{18,2},{3,19},{19,3},{4,20},{20... | collective-permute-start | bytes 2654216 | tf_op jit(solution)/shard_map/ppermute | solution.py:957
  49.9 34.9 %collective-permute-start.12 = (bf16[48,2048]{1,0:T(8,128)(2,1)}, bf16[48,2048]{1,0:T(8,128)(2,1)}, u32[]{:S(2)}, u32[]{:S(2)}) collective-permute-start(bf16[48,2048]{1,0:T(8,128)(2,1)} %slice.168), channel_id=1, source_target_pairs={{0,4},{1,5},{2,6},{3,7},{4,0},{5,1},{6,2},{7,3},{8,12},{9,13},{10,... | collective-permute-start | bytes 589832 | tf_op jit(solution)/shard_map/ppermute | solution.py:347
  52.5 17.7 %collective-permute-start.5 = (bf16[8,48,1152]{2,1,0:T(8,128)(2,1)}, bf16[8,48,1152]{2,1,0:T(8,128)(2,1)}, u32[]{:S(2)}, u32[]{:S(2)}) collective-permute-start(bf16[8,48,1152]{2,1,0:T(8,128)(2,1)} %constant_dynamic-update-slice_fusion.refs_0_), channel_id=1, source_target_pairs={{0,1},{1,0},{2,3},{3,2},{4,5},{5,4},{6,7},{7,6},{8,9},{9,8},{10,11... | collective-permute-start | bytes 2654216 | tf_op jit(solution)/shard_map/ppermute | solution.py:347
  65.6 4.7 %collective-permute-start.11 = (bf16[8,48,1152]{2,1,0:T(8,128)(2,1)S(1)}, bf16[8,48,1152]{2,1,0:T(8,128)(2,1)}, u32[]{:S(2)}, u32[]{:S(2)}) collective-permute-start(bf16[8,48,1152]{2,1,0:T(8,128)(2,1)S(1)} %collective-permute-done.6.refs_2_), channel_id=1, source_target_pairs={{0,1},{1,0},{2,3},{3,2},{4,5},{5,4},{6,7},{7,6},{8,9},{9,8},{10,11... | collective-permute-start | bytes 2654216 | tf_op jit(solution)/shard_map/ppermute | solution.py:347
  86.2 19.2 %collective-permute-start.19 = (bf16[192,768]{1,0:T(8,128)(2,1)S(1)}, bf16[192,768]{1,0:T(8,128)(2,1)S(1)}, u32[]{:S(2)}, u32[]{:S(2)}) collective-permute-start(bf16[192,768]{1,0:T(8,128)(2,1)S(1)} %copy-done.18), channel_id=1, source_target_pairs={{0,12},{1,13},{2,14},{3,15},{4,8},{5,9},{6,10},{7,11},{8,4},{9,5},... | collective-permute-start | bytes 884744 | tf_op jit(solution)/shard_map/ppermute | solution.py:347
  87.9 27.5 %collective-permute-start.18 = (bf16[192,768]{1,0:T(8,128)(2,1)S(1)}, bf16[192,768]{1,0:T(8,128)(2,1)S(1)}, u32[]{:S(2)}, u32[]{:S(2)}) collective-permute-start(bf16[192,768]{1,0:T(8,128)(2,1)S(1)} %copy-done.18), channel_id=1, source_target_pairs={{0,8},{1,9},{2,10},{3,11},{4,12},{5,13},{6,14},{7,15},{8,0},{9,1},... | collective-permute-start | bytes 884744 | tf_op jit(solution)/shard_map/ppermute | solution.py:347
  88.9 26.5 %collective-permute-start.17 = (bf16[192,768]{1,0:T(8,128)(2,1)S(1)}, bf16[192,768]{1,0:T(8,128)(2,1)}, u32[]{:S(2)}, u32[]{:S(2)}) collective-permute-start(bf16[192,768]{1,0:T(8,128)(2,1)S(1)} %copy-done.18), channel_id=1, source_target_pairs={{0,4},{1,5},{2,6},{3,7},{4,0},{5,1},{6,2},{7,3},{8,12},{9,13},{10,... | collective-permute-start | bytes 884744 | tf_op jit(solution)/shard_map/ppermute | solution.py:347
  90.6 27.5 %collective-permute-start.22 = (bf16[4,48,2048]{2,1,0:T(8,128)(2,1)S(1)}, bf16[4,48,2048]{2,1,0:T(8,128)(2,1)}, u32[]{:S(2)}, u32[]{:S(2)}) collective-permute-start(bf16[4,48,2048]{2,1,0:T(8,128)(2,1)S(1)} %pad_maximum_fusion.2.refs_4_), channel_id=1, source_target_pairs={{0,2},{1,3},{2,0},{3,1},{4,6},{5,7},{6,4},{7,5},{8,10},{9,11},{10,... | collective-permute-start | bytes 2359304 | tf_op jit(solution)/shard_map/ppermute | solution.py:347
  91.1 27.6 %collective-permute-start.16 = (bf16[8,48,896]{2,1,0:T(8,128)(2,1)}, bf16[8,48,896]{2,1,0:T(8,128)(2,1)}, u32[]{:S(2)}, u32[]{:S(2)}) collective-permute-start(bf16[8,48,896]{2,1,0:T(8,128)(2,1)} %constant_dynamic-update-slice_fusion.5.refs_0_), channel_id=1, source_target_pairs={{0,16},{16,0},{1,17},{17,1},{2,18},{18,2},{3,19},{19,3},{4,20},{20... | collective-permute-start | bytes 2064392 | tf_op jit(solution)/shard_map/ppermute | solution.py:957
  117.6 27.9 %collective-permute-start.25 = (bf16[4,192,768]{2,1,0:T(8,128)(2,1)S(1)}, bf16[4,192,768]{2,1,0:T(8,128)(2,1)}, u32[]{:S(2)}, u32[]{:S(2)}) collective-permute-start(bf16[4,192,768]{2,1,0:T(8,128)(2,1)S(1)} %pad_maximum_fusion.1.refs_0_.refs_8_), channel_id=1, source_target_pairs={{0,2},{1,3},{2,0},{3,1},{4,6},{5,7},{6,4},{7,5},{8,10},{9,11},{10,... | collective-permute-start | bytes 3538952 | tf_op jit(solution)/shard_map/ppermute | solution.py:347
  118.1 4.9 %collective-permute-start.21 = (bf16[4,48,2048]{2,1,0:T(8,128)(2,1)S(1)}, bf16[4,48,2048]{2,1,0:T(8,128)(2,1)}, u32[]{:S(2)}, u32[]{:S(2)}) collective-permute-start(bf16[4,48,2048]{2,1,0:T(8,128)(2,1)S(1)} %pad_maximum_fusion.2.refs_4_), channel_id=1, source_target_pairs={{0,1},{1,0},{2,3},{3,2},{4,5},{5,4},{6,7},{7,6},{8,9},{9,8},{10,11... | collective-permute-start | bytes 2359304 | tf_op jit(solution)/shard_map/ppermute | solution.py:347
  118.2 5.7 %collective-permute-start.23 = (bf16[4,48,2048]{2,1,0:T(8,128)(2,1)}, bf16[4,48,2048]{2,1,0:T(8,128)(2,1)}, u32[]{:S(2)}, u32[]{:S(2)}) collective-permute-start(bf16[4,48,2048]{2,1,0:T(8,128)(2,1)} %collective-permute-done.22.refs_6_), channel_id=1, source_target_pairs={{0,1},{1,0},{2,3},{3,2},{4,5},{5,4},{6,7},{7,6},{8,9},{9,8},{10,11... | collective-permute-start | bytes 2359304 | tf_op jit(solution)/shard_map/ppermute | solution.py:347
  118.7 5.1 %collective-permute-start.20 = (bf16[8,48,896]{2,1,0:T(8,128)(2,1)}, bf16[8,48,896]{2,1,0:T(8,128)(2,1)}, u32[]{:S(2)}, u32[]{:S(2)}) collective-permute-start(bf16[8,48,896]{2,1,0:T(8,128)(2,1)} %collective-permute-done.16.refs_2_), channel_id=1, source_target_pairs={{0,1},{1,0},{2,3},{3,2},{4,5},{5,4},{6,7},{7,6},{8,9},{9,8},{10,11... | collective-permute-start | bytes 2064392 | tf_op jit(solution)/shard_map/ppermute | solution.py:347
  122.9 22.6 %collective-permute-start.24 = (bf16[4,192,768]{2,1,0:T(8,128)(2,1)S(1)}, bf16[4,192,768]{2,1,0:T(8,128)(2,1)}, u32[]{:S(2)}, u32[]{:S(2)}) collective-permute-start(bf16[4,192,768]{2,1,0:T(8,128)(2,1)S(1)} %pad_maximum_fusion.1.refs_0_.refs_8_), channel_id=1, source_target_pairs={{0,1},{1,0},{2,3},{3,2},{4,5},{5,4},{6,7},{7,6},{8,9},{9,8},{10,11... | collective-permute-start | bytes 3538952 | tf_op jit(solution)/shard_map/ppermute | solution.py:347
  166.6 4.9 %collective-permute-start.27 = (bf16[8,192,768]{2,1,0:T(8,128)(2,1)}, bf16[8,192,768]{2,1,0:T(8,128)(2,1)}, u32[]{:S(2)}, u32[]{:S(2)}) collective-permute-start(bf16[8,192,768]{2,1,0:T(8,128)(2,1)} %get-tuple-element.142), channel_id=1, source_target_pairs={{0,1},{1,0},{2,3},{3,2},{4,5},{5,4},{6,7},{7,6},{8,9},{9,8},{10,11... | collective-permute-start | bytes 7077896 | tf_op jit(solution)/shard_map/ppermute | solution.py:347
  176.7 28.2 %collective-permute-start.28 = (bf16[8,192,384]{2,1,0:T(8,128)(2,1)}, bf16[8,192,384]{2,1,0:T(8,128)(2,1)S(1)}, u32[]{:S(2)}, u32[]{:S(2)}) collective-permute-start(bf16[8,192,384]{2,1,0:T(8,128)(2,1)} %get-tuple-element.145), channel_id=1, source_target_pairs={{0,16},{16,0},{1,17},{17,1},{2,18},{18,2},{3,19},{19,3},{4,20},{20... | collective-permute-start | bytes 3538952 | tf_op jit(solution)/shard_map/ppermute | solution.py:957
  210.6 14.8 %collective-permute-start.29 = (bf16[4,192,384]{2,1,0:T(8,128)(2,1)}, bf16[4,192,384]{2,1,0:T(8,128)(2,1)S(1)}, u32[]{:S(2)}, u32[]{:S(2)}) collective-permute-start(bf16[4,192,384]{2,1,0:T(8,128)(2,1)} %get-tuple-element.155), channel_id=1, source_target_pairs={{0,2},{1,3},{2,0},{3,1},{4,6},{5,7},{6,4},{7,5},{8,10},{9,11},{10,... | collective-permute-start | bytes 1769480 | tf_op jit(solution)/shard_map/ppermute | solution.py:347
  225.3 5.7 %collective-permute-start.30 = (bf16[8,48,3840]{2,1,0:T(8,128)(2,1)}, bf16[8,48,3840]{2,1,0:T(8,128)(2,1)}, u32[]{:S(2)}, u32[]{:S(2)}) collective-permute-start(bf16[8,48,3840]{2,1,0:T(8,128)(2,1)} %get-tuple-element.162), channel_id=1, source_target_pairs={{0,1},{1,0},{2,3},{3,2},{4,5},{5,4},{6,7},{7,6},{8,9},{9,8},{10,11... | collective-permute-start | bytes 8847368 | tf_op jit(solution)/shard_map/ppermute | solution.py:347
  237.0 37.9 %collective-permute-start.31 = (bf16[4,48,3840]{2,1,0:T(8,128)(2,1)}, bf16[4,48,3840]{2,1,0:T(8,128)(2,1)}, u32[]{:S(2)}, u32[]{:S(2)}) collective-permute-start(bf16[4,48,3840]{2,1,0:T(8,128)(2,1)} %get-tuple-element.168), channel_id=1, source_target_pairs={{0,2},{1,3},{2,0},{3,1},{4,6},{5,7},{6,4},{7,5},{8,10},{9,11},{10,... | collective-permute-start | bytes 4423688 | tf_op jit(solution)/shard_map/ppermute | solution.py:347
  237.5 35.7 %collective-permute-start.34 = (bf16[192,384]{1,0:T(8,128)(2,1)}, bf16[192,384]{1,0:T(8,128)(2,1)S(1)}, u32[]{:S(2)}, u32[]{:S(2)}) collective-permute-start(bf16[192,384]{1,0:T(8,128)(2,1)} %get-tuple-element.166), channel_id=1, source_target_pairs={{0,12},{1,13},{2,14},{3,15},{4,8},{5,9},{6,10},{7,11},{8,4},{9,5},... | collective-permute-start | bytes 442376 | tf_op jit(solution)/shard_map/ppermute | solution.py:347
  240.3 32.9 %collective-permute-start.33 = (bf16[192,384]{1,0:T(8,128)(2,1)}, bf16[192,384]{1,0:T(8,128)(2,1)S(1)}, u32[]{:S(2)}, u32[]{:S(2)}) collective-permute-start(bf16[192,384]{1,0:T(8,128)(2,1)} %get-tuple-element.165), channel_id=1, source_target_pairs={{0,8},{1,9},{2,10},{3,11},{4,12},{5,13},{6,14},{7,15},{8,0},{9,1},... | collective-permute-start | bytes 442376 | tf_op jit(solution)/shard_map/ppermute | solution.py:347
  240.3 33.0 %collective-permute-start.32 = (bf16[192,384]{1,0:T(8,128)(2,1)}, bf16[192,384]{1,0:T(8,128)(2,1)}, u32[]{:S(2)}, u32[]{:S(2)}) collective-permute-start(bf16[192,384]{1,0:T(8,128)(2,1)} %get-tuple-element.164), channel_id=1, source_target_pairs={{0,4},{1,5},{2,6},{3,7},{4,0},{5,1},{6,2},{7,3},{8,12},{9,13},{10,... | collective-permute-start | bytes 442376 | tf_op jit(solution)/shard_map/ppermute | solution.py:347
  290.9 19.2 %collective-permute-start.35 = (bf16[8,48,2304]{2,1,0:T(8,128)(2,1)}, bf16[8,48,2304]{2,1,0:T(8,128)(2,1)}, u32[]{:S(2)}, u32[]{:S(2)}) collective-permute-start(bf16[8,48,2304]{2,1,0:T(8,128)(2,1)} %get-tuple-element.184), channel_id=1, source_target_pairs={{0,1},{1,0},{2,3},{3,2},{4,5},{5,4},{6,7},{7,6},{8,9},{9,8},{10,11... | collective-permute-start | bytes 5308424 | tf_op jit(solution)/shard_map/ppermute | solution.py:347
  296.2 26.9 %collective-permute-start.36 = (bf16[512,768]{1,0:T(8,128)(2,1)}, bf16[512,768]{1,0:T(8,128)(2,1)}, u32[]{:S(2)}, u32[]{:S(2)}) collective-permute-start(bf16[512,768]{1,0:T(8,128)(2,1)} %input_back.2), channel_id=1, source_target_pairs={{0,16},{16,0},{1,17},{17,1},{2,18},{18,2},{3,19},{19,3},{4,20},{20... | collective-permute-start | bytes 2359304 | tf_op jit(solution)/shard_map/ppermute | solution.py:957
  303.3 48.2 %collective-permute-start.51 = (bf16[192,384]{1,0:T(8,128)(2,1)}, bf16[192,384]{1,0:T(8,128)(2,1)}, u32[]{:S(2)}, u32[]{:S(2)}) collective-permute-start(bf16[192,384]{1,0:T(8,128)(2,1)} %add_convert_fusion.8), channel_id=1, source_target_pairs={{0,16},{16,0},{1,17},{17,1},{2,18},{18,2},{3,19},{19,3},{4,20},{20... | collective-permute-start | bytes 442376 | tf_op jit(solution)/shard_map/ppermute | solution.py:957
  306.7 29.0 %collective-permute-start.38 = (bf16[48,3840]{1,0:T(8,128)(2,1)}, bf16[48,3840]{1,0:T(8,128)(2,1)S(1)}, u32[]{:S(2)}, u32[]{:S(2)}) collective-permute-start(bf16[48,3840]{1,0:T(8,128)(2,1)} %get-tuple-element.179), channel_id=1, source_target_pairs={{0,4},{1,5},{2,6},{3,7},{4,0},{5,1},{6,2},{7,3},{8,12},{9,13},{10,... | collective-permute-start | bytes 1105928 | tf_op jit(solution)/shard_map/ppermute | solution.py:347
  307.2 28.5 %collective-permute-start.39 = (bf16[48,3840]{1,0:T(8,128)(2,1)}, bf16[48,3840]{1,0:T(8,128)(2,1)}, u32[]{:S(2)}, u32[]{:S(2)}) collective-permute-start(bf16[48,3840]{1,0:T(8,128)(2,1)} %get-tuple-element.180), channel_id=1, source_target_pairs={{0,8},{1,9},{2,10},{3,11},{4,12},{5,13},{6,14},{7,15},{8,0},{9,1},... | collective-permute-start | bytes 1105928 | tf_op jit(solution)/shard_map/ppermute | solution.py:347
  310.1 24.2 %collective-permute-start.40 = (bf16[48,3840]{1,0:T(8,128)(2,1)}, bf16[48,3840]{1,0:T(8,128)(2,1)}, u32[]{:S(2)}, u32[]{:S(2)}) collective-permute-start(bf16[48,3840]{1,0:T(8,128)(2,1)} %get-tuple-element.181), channel_id=1, source_target_pairs={{0,12},{1,13},{2,14},{3,15},{4,8},{5,9},{6,10},{7,11},{8,4},{9,5},... | collective-permute-start | bytes 1105928 | tf_op jit(solution)/shard_map/ppermute | solution.py:347
  323.1 20.8 %collective-permute-start.37 = (bf16[4,48,2304]{2,1,0:T(8,128)(2,1)}, bf16[4,48,2304]{2,1,0:T(8,128)(2,1)}, u32[]{:S(2)}, u32[]{:S(2)}) collective-permute-start(bf16[4,48,2304]{2,1,0:T(8,128)(2,1)} %get-tuple-element.187), channel_id=1, source_target_pairs={{0,2},{1,3},{2,0},{3,1},{4,6},{5,7},{6,4},{7,5},{8,10},{9,11},{10,... | collective-permute-start | bytes 2654216 | tf_op jit(solution)/shard_map/ppermute | solution.py:347
  350.0 4.4 %collective-permute-start.42 = (f32[24,768]{1,0:T(8,128)S(1)}, f32[24,768]{1,0:T(8,128)S(1)}, u32[]{:S(2)}, u32[]{:S(2)}) collective-permute-start(f32[24,768]{1,0:T(8,128)S(1)} %add.240), channel_id=1, source_target_pairs={{0,2},{1,3},{2,0},{3,1},{4,6},{5,7},{6,4},{7,5},{8,10},{9,11},{10,... | collective-permute-start | bytes 221192 | tf_op jit(solution)/shard_map/ppermute | solution.py:951
  353.5 14.7 %collective-permute-start.50 = (bf16[48,3840]{1,0:T(8,128)(2,1)S(1)}, bf16[48,3840]{1,0:T(8,128)(2,1)S(1)}, u32[]{:S(2)}, u32[]{:S(2)}) collective-permute-start(bf16[48,3840]{1,0:T(8,128)(2,1)S(1)} %add_convert_fusion.4), channel_id=1, source_target_pairs={{0,16},{16,0},{1,17},{17,1},{2,18},{18,2},{3,19},{19,3},{4,20},{20... | collective-permute-start | bytes 1105928 | tf_op jit(solution)/shard_map/ppermute | solution.py:957
  354.4 4.4 %collective-permute-start.43 = (f32[24,768]{1,0:T(8,128)S(1)}, f32[24,768]{1,0:T(8,128)S(1)}, u32[]{:S(2)}, u32[]{:S(2)}) collective-permute-start(f32[24,768]{1,0:T(8,128)S(1)} %add.241), channel_id=1, source_target_pairs={{0,4},{1,5},{2,6},{3,7},{4,0},{5,1},{6,2},{7,3},{8,12},{9,13},{10,... | collective-permute-start | bytes 221192 | tf_op jit(solution)/shard_map/ppermute | solution.py:951
  358.8 8.0 %collective-permute-start.44 = (f32[24,768]{1,0:T(8,128)S(1)}, f32[24,768]{1,0:T(8,128)S(1)}, u32[]{:S(2)}, u32[]{:S(2)}) collective-permute-start(f32[24,768]{1,0:T(8,128)S(1)} %add.242), channel_id=1, source_target_pairs={{0,8},{1,9},{2,10},{3,11},{4,12},{5,13},{6,14},{7,15},{8,0},{9,1},... | collective-permute-start | bytes 221192 | tf_op jit(solution)/shard_map/ppermute | solution.py:951
  362.4 9.9 %collective-permute-start.46 = (bf16[48,2304]{1,0:T(8,128)(2,1)}, bf16[48,2304]{1,0:T(8,128)(2,1)S(1)}, u32[]{:S(2)}, u32[]{:S(2)}) collective-permute-start(bf16[48,2304]{1,0:T(8,128)(2,1)} %get-tuple-element.200), channel_id=1, source_target_pairs={{0,4},{1,5},{2,6},{3,7},{4,0},{5,1},{6,2},{7,3},{8,12},{9,13},{10,... | collective-permute-start | bytes 663560 | tf_op jit(solution)/shard_map/ppermute | solution.py:347
  363.5 18.0 %collective-permute-start.47 = (bf16[48,2304]{1,0:T(8,128)(2,1)}, bf16[48,2304]{1,0:T(8,128)(2,1)S(1)}, u32[]{:S(2)}, u32[]{:S(2)}) collective-permute-start(bf16[48,2304]{1,0:T(8,128)(2,1)} %get-tuple-element.201), channel_id=1, source_target_pairs={{0,8},{1,9},{2,10},{3,11},{4,12},{5,13},{6,14},{7,15},{8,0},{9,1},... | collective-permute-start | bytes 663560 | tf_op jit(solution)/shard_map/ppermute | solution.py:347
  364.5 17.0 %collective-permute-start.48 = (bf16[48,2304]{1,0:T(8,128)(2,1)}, bf16[48,2304]{1,0:T(8,128)(2,1)S(1)}, u32[]{:S(2)}, u32[]{:S(2)}) collective-permute-start(bf16[48,2304]{1,0:T(8,128)(2,1)} %get-tuple-element.202), channel_id=1, source_target_pairs={{0,12},{1,13},{2,14},{3,15},{4,8},{5,9},{6,10},{7,11},{8,4},{9,5},... | collective-permute-start | bytes 663560 | tf_op jit(solution)/shard_map/ppermute | solution.py:347
  381.6 6.0 %collective-permute-start.49 = (bf16[48,2304]{1,0:T(8,128)(2,1)S(1)}, bf16[48,2304]{1,0:T(8,128)(2,1)S(1)}, u32[]{:S(2)}, u32[]{:S(2)}) collective-permute-start(bf16[48,2304]{1,0:T(8,128)(2,1)S(1)} %add_convert_fusion.7), channel_id=1, source_target_pairs={{0,16},{16,0},{1,17},{17,1},{2,18},{18,2},{3,19},{19,3},{4,20},{20... | collective-permute-start | bytes 663560 | tf_op jit(solution)/shard_map/ppermute | solution.py:957
  (57 other events, 740.6 us)

commit v7 on v6

--- a/solution.py
+++ b/solution.py
@@ -95,10 +95,6 @@
     return lax.dot_general(
         left_side, right_side, (((1,), (1,)), ((), ())), preferred_element_type=f32
     )
-
-
-def column_sum(values):
-    return jnp.sum(values, axis=0, keepdims=True, dtype=f32)
 
 
 def iota(shape, axis):
@@ -355,25 +351,45 @@
     return (slot & 3) * 4 + (slot >> 2) * 2
 
 
-def place_kernel(groups, place, *refs):
-    for copy in start_rows(place, groups, refs[:-2], refs[-2], refs[-1]):
+def project_kernel(groups, place, mixed_ref, bias_ref, *refs):
+    *pieces, query_ref, both_ref, weight_ref, sems = refs
+    width = mixed_ref.shape[1]
+    tokens = query_ref.shape[0]
+    for copy in start_rows(place, groups, pieces, weight_ref, sems):
         copy.wait()
-
-
-def place_rows(place, groups, pieces, shape):
+    own = mixed_ref[pl.ds(pl.multiple_of(place[1] * tokens, 16), tokens), :]
+    queries = jnp.dot(own, weight_ref[:, :width], preferred_element_type=f32) + bias_ref[:, :width]
+    query_ref[...] = (queries.astype(bf16).astype(f32) * 0.125).astype(bf16)
+    for part in range(2):
+        rows = pl.ds(part * tokens, tokens)
+        for column in (1, 2):
+            at = slice(column * width, (column + 1) * width)
+            out = slice((column - 1) * width, column * width)
+            values = jnp.dot(mixed_ref[rows, :], weight_ref[:, at], preferred_element_type=f32)
+            both_ref[rows, out] = (values + bias_ref[:, at]).astype(bf16)
+
+
+def project(place, mixed, biases, groups, pieces):
+    rows, width = mixed.shape
+    vmem = pl.BlockSpec(memory_space=pltpu.VMEM)
     return pl.pallas_call(
-        functools.partial(place_kernel, groups),
+        functools.partial(project_kernel, groups),
         grid_spec=pltpu.PrefetchScalarGridSpec(
             num_scalar_prefetch=1,
             grid=(),
-            in_specs=any_specs(len(pieces)),
-            out_specs=pl.BlockSpec(memory_space=pltpu.VMEM),
+            in_specs=[vmem] * 2 + any_specs(len(pieces)),
+            out_specs=[vmem] * 3,
             scratch_shapes=[pltpu.SemaphoreType.DMA((32,))],
         ),
-        out_shape=jax.ShapeDtypeStruct(shape, bf16),
+        out_shape=[
+            jax.ShapeDtypeStruct((rows // 2, width), bf16),
+            jax.ShapeDtypeStruct((rows, 2 * width), bf16),
+            jax.ShapeDtypeStruct((width, 3 * width), bf16),
+        ],
         cost_estimate=small_cost,
-        name="place_rows",
-    )(place, *pieces)
+        compiler_params=pltpu.CompilerParams(vmem_limit_bytes=16 << 20),
+        name="project",
+    )(place, mixed, biases, *pieces)
 
 
 def column_parts(shard):
@@ -548,6 +564,7 @@
             jax.ShapeDtypeStruct((tokens, hidden_width), f32),
         ],
         cost_estimate=small_cost,
+        compiler_params=pltpu.CompilerParams(vmem_limit_bytes=28 << 20),
         name="up_forward",
     )(place, context, mixed, vectors, bias_up, *pieces)
 
@@ -599,6 +616,7 @@
             jax.ShapeDtypeStruct((8, width), f32),
         ],
         cost_estimate=small_cost,
+        compiler_params=pltpu.CompilerParams(vmem_limit_bytes=24 << 20),
         name="down_forward",
     )(place, active, unit, vectors, grads, *pieces)
 
@@ -694,51 +712,31 @@
             jax.ShapeDtypeStruct((8, width), f32),
         ],
         cost_estimate=small_cost,
+        compiler_params=pltpu.CompilerParams(vmem_limit_bytes=32 << 20),
         name="ffn_back",
     )(place, low, slope, total, unit, scale, vectors, *pieces_rest, *pieces_down)
 
 
-def grad_rows_kernel(place, *refs):
-    *inputs, h_ref, keep_ref, send_ref = refs
-    rows = keep_ref.shape[1]
-    both = jnp.concatenate([ref[0] for ref in inputs], axis=0)
-    product = jnp.dot(both, h_ref[...], preferred_element_type=f32).astype(bf16)
-    for index in range(2):
-        keep_ref[index] = product[index * rows : (index + 1) * rows]
-        send_ref[index] = product[(index + 2) * rows : (index + 3) * rows]
-
-
-def grad_by_rows(inputs_t, grads, place):
+def grad_rows_kernel(x_ref, h_ref, out_ref):
+    out_ref[...] = jnp.dot(x_ref[...], h_ref[...], preferred_element_type=f32).astype(bf16)
+
+
+def grad_rows(inputs_t, grads):
     width, tokens = inputs_t.shape
     columns = grads.shape[1]
-    rows = width // 16
-    inputs_t = inputs_t.reshape(16, rows, tokens)
-    half = jax.ShapeDtypeStruct((8, rows, columns), bf16)
-    out = pl.BlockSpec((2, rows, columns), lambda step, place: (step, 0, 0))
-
-    def input_spec(index):
-        return pl.BlockSpec(
-            (1, rows, tokens),
-            lambda step, place: (
-                place[0] ^ (slot_mask(2 * step + (index & 1)) + (index >> 1)),
-                0,
-                0,
-            ),
-        )
-
     return pl.pallas_call(
         grad_rows_kernel,
-        grid_spec=pltpu.PrefetchScalarGridSpec(
-            num_scalar_prefetch=1,
-            grid=(4,),
-            in_specs=[input_spec(index) for index in range(4)]
-            + [pl.BlockSpec((tokens, columns), lambda step, place: (0, 0))],
-            out_specs=[out, out],
-        ),
-        out_shape=[half, half],
+        grid=(4,),
+        in_specs=[
+            pl.BlockSpec((width // 4, tokens), lambda step: (step, 0)),
+            pl.BlockSpec((tokens, columns), lambda step: (0, 0)),
+        ],
+        out_specs=pl.BlockSpec((width // 4, columns), lambda step: (step, 0)),
+        out_shape=jax.ShapeDtypeStruct((width, columns), bf16),
         cost_estimate=small_cost,
+        compiler_params=pltpu.CompilerParams(vmem_limit_bytes=12 << 20),
         name="grad_rows",
-    )(place, *[inputs_t] * 4, grads)
+    )(inputs_t, grads)
 
 
 def grad_columns_kernel(parts, place, *refs):
@@ -804,6 +802,7 @@
         ),
         out_shape=[half, half],
         cost_estimate=small_cost,
+        compiler_params=pltpu.CompilerParams(vmem_limit_bytes=16 << 20),
         name="grad_columns",
     )(place, *operands)
 
@@ -838,8 +837,77 @@
         ),
         out_shape=jax.ShapeDtypeStruct((tokens, width), dtype),
         cost_estimate=small_cost,
+        compiler_params=pltpu.CompilerParams(vmem_limit_bytes=16 << 20),
         name="input_back",
     )(place, *operands)
+
+
+def back_rows(values, mask):
+    return jnp.where(mask, pltpu.roll(values, dilation, 0), 0.0)
+
+
+def ahead_rows(values, mask):
+    return jnp.where(mask, pltpu.roll(values, values.shape[0] - dilation, 0), 0.0)
+
+
+def tap_sums(grads, inputs, ahead, back):
+    terms = (grads * back_rows(inputs, back), grads * inputs, grads * ahead_rows(inputs, ahead), grads)
+    return [jnp.sum(term, axis=0, keepdims=True) for term in terms]
+
+
+def small_sums_kernel(
+    own_ref, other_ref, x_ref, x_other_ref, mask_ref, gq_ref, gv_ref, one_ref, two_ref, up_ref, table_ref, out_ref
+):
+    width = own_ref.shape[1]
+    mask = mask_ref[...] > 0.0
+    own = tap_sums(own_ref[...], x_ref[...].astype(f32), mask[:, 0:1], mask[:, 1:2])
+    other = tap_sums(
+        other_ref[...].astype(f32), x_other_ref[...].astype(f32), mask[:, 2:3], mask[:, 3:4]
+    )
+    rows = [a + b for a, b in zip(own, other)]
+    for ref in (gq_ref, gv_ref):
+        rows.append(jnp.sum(ref[...].astype(f32), axis=0, keepdims=True))
+    rows.append(jnp.zeros((2, width), f32))
+    out_ref[0:8] = jnp.concatenate(rows, axis=0)
+    out_ref[8:16] = one_ref[...]
+    out_ref[16:24] = two_ref[...]
+    count = up_ref.shape[1] // width
+    for index in range(count):
+        out_ref[24 + index : 25 + index] = up_ref[:, index * width : (index + 1) * width]
+    for index in range(3 * HEADS):
+        row, lane = 28 + index // 6, index % 6 * LANES
+        table = table_ref[index // 3]
+        out_ref[row : row + 1, lane : lane + LANES] = table[index % 3 : index % 3 + 1]
+    out_ref[34:40] = jnp.zeros((6, width), f32)
+
+
+def small_sums(*operands):
+    return pl.pallas_call(
+        small_sums_kernel,
+        out_shape=jax.ShapeDtypeStruct((40, operands[0].shape[1]), f32),
+        cost_estimate=small_cost,
+        compiler_params=pltpu.CompilerParams(vmem_limit_bytes=24 << 20),
+        name="small_sums",
+    )(*operands)
+
+
+def state_back_kernel(own_ref, other_ref, mask_ref, tap_ref, out_ref):
+    grads = own_ref[...] + other_ref[...].astype(f32)
+    mask = mask_ref[...] > 0.0
+    total = grads + tap_ref[1:2] * grads
+    total = total + tap_ref[0:1] * ahead_rows(grads, mask[:, 0:1])
+    total = total + tap_ref[2:3] * back_rows(grads, mask[:, 1:2])
+    out_ref[...] = total.astype(bf16)
+
+
+def state_back(own, other, masks, taps):
+    return pl.pallas_call(
+        state_back_kernel,
+        out_shape=jax.ShapeDtypeStruct(own.shape, bf16),
+        cost_estimate=small_cost,
+        compiler_params=pltpu.CompilerParams(vmem_limit_bytes=20 << 20),
+        name="state_back",
+    )(own, other, masks, taps)
 
 
 def first_half_kernel(place, keep_near, part_near, keep_far, part_far, held_ref, out_ref):
@@ -862,6 +930,7 @@
             jax.ShapeDtypeStruct(half_shape, bf16),
         ],
         cost_estimate=small_cost,
+        compiler_params=pltpu.CompilerParams(vmem_limit_bytes=12 << 20),
         name="halve",
     )(place, keep, partner, keep, partner)
 
@@ -901,6 +970,7 @@
         out_shape=[jax.ShapeDtypeStruct((rows, width), f32)]
         + [jax.ShapeDtypeStruct((rows, width), bf16)] * 3,
         cost_estimate=small_cost,
+        compiler_params=pltpu.CompilerParams(vmem_limit_bytes=12 << 20),
         name="column_sends",
     )(held, across)
     return own, sends
@@ -999,6 +1069,7 @@
         column_qkv = column_of(half_columns(pack_qkv, is_text))
         parts_near = column_parts(after(half_columns(pack_rest[:, :split], is_text), column_qkv))
         pieces_qkv = half_pieces(column_qkv)
+        w_down = after(w_down, column_qkv)
         column_near = jnp.stack([after(part, pieces_qkv[0]) for part in parts_near])
         parts_far = column_parts(after(pack_rest[:, split:], column_near))
         pieces_near = half_pieces(column_near)
@@ -1008,6 +1079,7 @@
     else:
         groups_qkv = (("full", 0),)
         pieces_qkv = [lax.all_gather(pack_qkv, "page", axis=0, tiled=True)]
+    full_down = lax.all_gather(w_down, "page", axis=0, tiled=True)
 
     page_ids, pos_bins, bins_x, bins_y = token_ids(segments[0], box_x[0], box_y[0])
     bounds = page_bounds(segments[0], is_text)
@@ -1030,40 +1102,44 @@
     )
     tables = jnp.pad(tables, ((0, 0), (0, 5), (0, 0)))
 
-    def mix_fn(inputs_f, weight_f, bias_f):
-        return dilated_mix(inputs_f, own_pages, weight_f, bias_f)
-
     own_states = own_low.astype(f32)
-    mixed, mix_pull = jax.vjp(mix_fn, own_states, conv_weight, conv_bias)
+    mixed = dilated_mix(own_states, own_pages, conv_weight, conv_bias)
     mixed_low = mixed.astype(bf16)
     other_pages = jnp.where(is_text, page_ids[1], page_ids[0])
     other_mixed = dilated_mix(other_low.astype(f32), other_pages, conv_weight, conv_bias)
     other_mixed = other_mixed.astype(bf16)
+    masks = jnp.pad(
+        jnp.stack(
+            [
+                own_pages == shifted(own_pages, dilation, -1),
+                own_pages == shifted(own_pages, -dilation, -1),
+                other_pages == shifted(other_pages, dilation, -1),
+                other_pages == shifted(other_pages, -dilation, -1),
+            ],
+            axis=1,
+        ).astype(f32),
+        ((0, 0), (0, LANES - 4)),
+    )
     mixed_all = jnp.concatenate(
         [jnp.where(is_text, mixed_low, other_mixed), jnp.where(is_text, other_mixed, mixed_low)],
         axis=0,
     )
     mixed_t = mixed_all.T
     if fast:
-        pieces_qkv[0] = after(pieces_qkv[0], mixed_all, mixed_t, features, tables, bounds, own_flip)
-    full_qkv = place_rows(place, groups_qkv, pieces_qkv, (d_model, pack_qkv.shape[1]))
-    full_query = full_qkv[:, :d_model]
-    full_kv = full_qkv[:, d_model:]
-    queries = ((plain_dot(mixed_low, full_query) + b_query).astype(bf16) * 0.125).astype(bf16)
-    kv_bias = jnp.concatenate([jnp.zeros_like(b_value), b_value])
-    keys_values = (plain_dot(mixed_all, full_kv) + kv_bias).astype(bf16)
+        early = (mixed_all, mixed_t, features, tables, bounds, own_flip, own_feats, masks)
+        pieces_qkv[0] = after(pieces_qkv[0], *early)
+    biases = jnp.concatenate([b_query, jnp.zeros_like(b_value), b_value])[None]
+    queries, keys_values, full_qkv = project(place, mixed_all, biases, groups_qkv, pieces_qkv)
     attend_in = queries
     if fast:
-        column_far = jnp.stack([after(part, keys_values, queries) for part in parts_far])
-        parts_down = column_parts(after(w_down, column_far))
+        column_far = jnp.stack([after(part, queries) for part in parts_far])
         across_far = exchange(column_far, 2)
         attend_in = after(queries, column_far)
     context = attend(bounds, attend_in, keys_values, features, own_feats, tables)
     if fast:
-        column_down = jnp.stack([after(part, context) for part in parts_down])
-        pieces_near[2] = after(pieces_near[2], column_down)
+        pieces_near[2] = after(pieces_near[2], context)
         pieces_near[3] = exchange(pieces_near[2], 1)
-        across_far = after(across_far, column_down)
+        across_far = after(across_far, context)
         pieces_rest = pieces_near + row_pieces(column_far, across_far)
         groups_rest = (("halves", 0), ("rows", split))
     else:
@@ -1075,31 +1151,17 @@
     unit, scale, normed_low, normed_t, active, active_t, slope = up_forward(
         place, context, mixed, vectors, b_up[None], groups_rest, pieces_rest
     )
-    if fast:
-        across_down = after(exchange(column_down, 2), active)
-        pieces_down = row_pieces(column_down, across_down)
-        groups_down = (("rows", 0),)
-    else:
-        groups_down = (("full", 0),)
-        pieces_down = [lax.all_gather(w_down, "page", axis=0, tiled=True)]
+    groups_down = (("full", 0),)
+    pieces_down = [full_down]
     output_row, grad_sum_two, grad_ffn, small_two = down_forward(
         place, active, unit, vectors, cotangent[0, 0], groups_down, pieces_down
     )
-    grad_ffn_in = grad_ffn
-    if fast:
-        keep_down, send_down = grad_by_rows(active_t, grad_ffn, place)
-        partner_down = exchange(send_down, 1)
-        context_t = after(context, send_down).T
-        partner_down = after(partner_down, context_t)
-        held_down, plane_out = halve_plane(place, keep_down, partner_down)
-        plane_down = swap(plane_out)
-        grad_ffn_in = after(grad_ffn, plane_out)
-    else:
-        shard_down = summed_rows([(active_t, grad_ffn)])
-        context_t = context.T
+    rows_down = grad_rows(active_t, grad_ffn)
+    shard_down = lax.psum_scatter(rows_down, "page", scatter_dimension=0, tiled=True)
+    context_t = context.T
     grad_hidden, grad_b_up, grad_first, grad_branch, grad_context, small_one = ffn_back(
         place,
-        grad_ffn_in,
+        after(grad_ffn, rows_down),
         slope,
         grad_sum_two,
         unit,
@@ -1112,20 +1174,12 @@
     )
     attend_in = grad_context
     if fast:
-        plane_down = after(plane_down, grad_branch)
-        held_down, across_out = halve_across(place, held_down, plane_down)
-        across_down = exchange(across_out, 2)
-        branch_in = after(grad_branch, across_out)
-        pairs = [(context_t, False, branch_in), (normed_t, False, grad_hidden)]
+        pairs = [(context_t, False, grad_branch), (normed_t, False, grad_hidden)]
         keep_rest, send_rest = grad_by_columns(pairs, place, d_model)
-        across_down = after(across_down, keep_rest)
-        partner_rest = exchange(after(send_rest, across_down), 1)
-        own_down, sends_down = column_sends(held_down, across_down)
-        arrived_down = column_arrivals(sends_down)
-        partner_rest = after(partner_rest, *sends_down)
-        held_rest, across_out = halve_across(place, keep_rest, partner_rest)
-        across_rest = exchange(across_out, 2)
-        attend_in = after(grad_context, across_out)
+        partner_rest = exchange(send_rest, 1)
+        held_rest, plane_out = halve_plane(place, keep_rest, partner_rest)
+        plane_rest = swap(plane_out)
+        attend_in = after(grad_context, plane_out)
     else:
         shard_rest = summed_rows([(context_t, grad_branch), (normed_t, grad_hidden)])
     grad_queries, grad_keys, grad_values, grad_tables = attend_back(
@@ -1133,13 +1187,10 @@
     )
     grad_keys_in, grad_queries_in = grad_keys, grad_queries
     if fast:
-        arrived_down = [after(part, grad_queries) for part in arrived_down]
-        total_down = column_total(own_down, arrived_down)
-        far_down = swap(total_down)
-        across_rest = after(across_rest, total_down)
-        own_rest, sends_rest = column_sends(held_rest, across_rest)
-        arrived_rest = column_arrivals(sends_rest)
-        grad_queries_in = after(grad_queries, *sends_rest)
+        plane_rest = after(plane_rest, grad_queries)
+        held_rest, across_out = halve_across(place, held_rest, plane_rest)
+        across_rest = exchange(across_out, 2)
+        grad_queries_in = after(grad_queries, across_out)
     pairs = [(mixed_t, True, grad_queries_in), (mixed_t, False, grad_keys), (mixed_t, False, grad_values)]
     if fast:
         keep_qkv, send_qkv = grad_by_columns(pairs, place, d_model)
@@ -1149,8 +1200,6 @@
         shard_qkv = summed_rows(
             [(mixed_low.T, grad_queries), (mixed_t, grad_keys), (mixed_t, grad_values)]
         )
-    grad_b_query = column_sum(grad_queries)
-    grad_b_value = column_sum(grad_values)
     to_other = input_back(place, full_qkv, grad_keys_in, grad_values, ())
     from_other = swap(to_other)
     grad_values_in = grad_values
@@ -1158,55 +1207,50 @@
         partner_qkv = after(partner_qkv, to_other)
         held_qkv, across_out = halve_across(place, keep_qkv, partner_qkv)
         across_qkv = exchange(across_out, 2)
-        grad_values_in = after(grad_values, across_out)
+        across_rest = after(across_rest, across_out)
+        own_rest, sends_rest = column_sends(held_rest, across_rest)
+        arrived_rest = column_arrivals(sends_rest)
+        grad_values_in = after(grad_values, *sends_rest)
     own_part = input_back(place, full_qkv, grad_keys, grad_values_in, (grad_first, grad_queries))
+    packed = small_sums(
+        own_part,
+        to_other,
+        own_low,
+        other_low,
+        masks,
+        grad_queries,
+        grad_values,
+        small_one,
+        small_two,
+        grad_b_up,
+        grad_tables,
+    )
+    packed = sum_everywhere(packed)
     if fast:
-        from_other = after(from_other, own_part)
-    grad_mixed = own_part + from_other.astype(f32)
-    grad_in, grad_conv_w, grad_conv_b = mix_pull(grad_mixed)
-
-    table_rows = grad_tables[:, :3].reshape(6, 768)
-    packed = jnp.concatenate(
-        [
-            grad_conv_w,
-            grad_conv_b[None],
-            grad_b_query,
-            grad_b_value,
-            small_one[2:3],
-            small_one[0:2],
-            small_two[2:3],
-            small_two[0:2],
-            grad_b_up.reshape(d_ff // d_model, d_model),
-            table_rows,
-            jnp.zeros((2, d_model), f32),
-        ],
-        axis=0,
-    )
+        across_qkv = after(across_qkv, packed)
+        own_qkv, sends_qkv = column_sends(held_qkv, across_qkv)
+        arrived_qkv = column_arrivals(sends_qkv)
+        from_other = after(from_other, *sends_qkv)
+    grad_in = state_back(own_part, from_other, masks, jnp.pad(conv_weight, ((0, 5), (0, 0))))
     if fast:
-        arrived_rest = [after(part, packed) for part in arrived_rest]
+        arrived_rest = [after(part, grad_in) for part in arrived_rest]
         total_rest = column_total(own_rest, arrived_rest)
         far_rest = swap(total_rest)
-        across_qkv = after(across_qkv, total_rest)
-        own_qkv, sends_qkv = column_sends(held_qkv, across_qkv)
-        arrived_qkv = column_arrivals(sends_qkv)
-        packed = after(packed, *sends_qkv)
-    packed = sum_everywhere(packed)
-    if fast:
-        arrived_qkv = [after(part, packed) for part in arrived_qkv]
+        arrived_qkv = [after(part, total_rest) for part in arrived_qkv]
         total_qkv = column_total(own_qkv, arrived_qkv)
         far_qkv = swap(total_qkv)
-    g_tables = packed[16:22].reshape(HEADS, 3, LANES)
+    g_tables = packed[28:34].reshape(HEADS, 3, LANES)
+    shard_down = shard_down.astype(f32) + swap(shard_down).astype(f32)
     if fast:
-        shard_down = jnp.where(
+        shard_rest = jnp.where(
             is_text,
-            jnp.concatenate([total_down, far_down], axis=1),
-            jnp.concatenate([far_down, total_down], axis=1),
+            jnp.concatenate([total_rest, far_rest], axis=1),
+            jnp.concatenate([far_rest, total_rest], axis=1),
         ).astype(f32)
         shard_qkv = total_qkv.astype(f32) + far_qkv.astype(f32)
-        shard_rest = total_rest.astype(f32) + far_rest.astype(f32)
     return (
         output_row[None, None],
-        grad_in.astype(bf16)[None, None],
+        grad_in[None, None],
         packed[0:3],
         packed[3],
         shard_qkv[:, :d_model],
@@ -1215,18 +1259,18 @@
         shard_qkv[:, 2 * d_model :],
         packed[5],
         shard_rest[:, :d_model],
-        packed[6],
+        packed[10],
         g_tables[:, 0, : table_pos.shape[1]],
         g_tables[:, 1, 64 : 64 + table_x.shape[1]],
         g_tables[:, 2, 64 : 64 + table_y.shape[1]],
-        packed[7],
         packed[8],
+        packed[9],
         shard_rest[:, d_model:],
-        packed[12:16].reshape(d_ff),
+        packed[24:28].reshape(d_ff),
         shard_down,
-        packed[9],
-        packed[10],
-        packed[11],
+        packed[18],
+        packed[16],
+        packed[17],
     )
 
 

time: 395 us -> 383 us (0.970)
  the two profiles are of different devices: /device:TPU:0 before, /device:TPU:8 now
where the time goes in v7:
time: 383 us; the launch traced here: 376 us
  Pallas kernels  125 us (33%)
  waiting for transfers between devices  96.1 us (25%)
  local copies, waits for them, and re-layouts  78.9 us (21%)
  starting transfers between devices  41.7 us (11%)
  other arithmetic  19.3 us (5%)
  between operations  15.4 us (4%)
    ppermute x28, waiting for transfers between devices, exchange(): return lax.ppermute(values, 'page', [(i, i ^ mask) for i in range(count)])  68.1 us
    unnamed x177, local copies, waits for them, and re-layouts  51 us
    ppermute x28, starting transfers between devices, exchange(): return lax.ppermute(values, 'page', [(i, i ^ mask) for i in range(count)])  29.9 us
    pallas_call x1, Pallas kernels, attend_back(): pl.pallas_call(attend_back_kernel, grid_spec=pltpu.PrefetchScalarGridSpec...  29.7 us
    ppermute x4, waiting for transfers between devices, sum_everywhere(): lax.ppermute(values, 'page', [(i, i ^ step) for i in range(count)])  18.8 us
    pallas_call x1, Pallas kernels, up_forward(): pl.pallas_call(functools.partial(up_kernel, groups), grid_spec=pltpu.Pref...  16.8 us
    pallas_call x1, Pallas kernels, ffn_back(): pl.pallas_call(functools.partial(ffn_back_kernel, groups, groups_down, co...  14.7 us
    pallas_call x1, Pallas kernels, attend(): pl.pallas_call(attend_kernel, grid_spec=pltpu.PrefetchScalarGridSpec(num_...  12.9 us
  transfers between devices with their start and end apart: 43, of which 19 were waited for; matrix products, arithmetic and copies ran while one was open for 13% of the time, Pallas kernels for 25%

profile of v7, /device:TPU:8, one launch (start us, length us, event | category | flops | bytes accessed | tf_op | source)
XLA Modules:
  0.0 376.4 jit_solution(85859032500963270)
XLA Ops:
  8.3 3.0 collective-permute-start.2
  33.6 2.1 collective-permute-start.8
  36.4 8.3 %collective-permute-done.4 = bf16[4,48,1152]{2,1,0:T(8,128)(2,1)S(1)} collective-permute-done((bf16[4,48,1152]{2,1,0:T(8,128)(2,1)S(1)}, bf16[4,48,1152]{2,1,0:T(8,128)(2,1)S(1)}, u32[]{:S(2)}, u32[]{:S(2)}) %collective-permute-start.4) | collective-permute-done | bytes 442400 | tf_op jit(solution)/shard_map/ppermute | solution.py:343
  45.3 3.1 collective-permute-done.9
  52.0 4.3 %collective-permute-start.13 = (bf16[48,2048]{1,0:T(8,128)(2,1)}, bf16[48,2048]{1,0:T(8,128)(2,1)S(1)}, u32[]{:S(2)}, u32[]{:S(2)}) collective-permute-start(bf16[48,2048]{1,0:T(8,128)(2,1)} %slice.152), channel_id=1, source_target_pairs={{0,8},{1,9},{2,10},{3,11},{4,12},{5,13},{6,14},{7,15},{8,0},{9,1},... | collective-permute-start | bytes 589832 | tf_op jit(solution)/shard_map/ppermute | solution.py:343
  56.6 3.1 collective-permute-start.14
  61.8 2.5 broadcast_select_fusion.1
  66.9 5.0 %project.1 = (bf16[512,768]{1,0:T(8,128)(2,1)S(1)}, bf16[1024,1536]{1,0:T(8,128)(2,1)S(1)}, bf16[768,2304]{1,0:T(8,128)(2,1)S(1)}) custom-call(s32[2]{0:T(128)S(1)} %pad_add_fusion.1.place, bf16[1024,768]{1,0:T(8,128)(2,1)S(1)} %get-tuple-element.190.mixed_ref, f32[1,2304]{1,0:T(1,128)S(1)} %broadcast_in_dim.67.bias_ref, ...), custom_call_target="tpu_custom_call" | custom-call | flops 1000 | bytes 1000 | tf_op jit(solution)/shard_map/project/pallas_call | solution.py:375
  74.4 4.8 %collective-permute-done.13 = bf16[48,2048]{1,0:T(8,128)(2,1)S(1)} collective-permute-done((bf16[48,2048]{1,0:T(8,128)(2,1)}, bf16[48,2048]{1,0:T(8,128)(2,1)S(1)}, u32[]{:S(2)}, u32[]{:S(2)}) %collective-permute-start.13) | collective-permute-done | bytes 196640 | tf_op jit(solution)/shard_map/ppermute | solution.py:343
  79.2 9.5 %collective-permute-done.14 = bf16[48,2048]{1,0:T(8,128)(2,1)S(1)} collective-permute-done((bf16[48,2048]{1,0:T(8,128)(2,1)}, bf16[48,2048]{1,0:T(8,128)(2,1)S(1)}, u32[]{:S(2)}, u32[]{:S(2)}) %collective-permute-start.14) | collective-permute-done | bytes 196640 | tf_op jit(solution)/shard_map/ppermute | solution.py:343
  88.7 1.9 pad_maximum_fusion.1.refs_4_
  92.5 12.9 %attend.1.context_ref = bf16[512,768]{1,0:T(8,128)(2,1)} custom-call(s32[48]{0:T(128)} %concatenate.72.bounds, bf16[512,768]{1,0:T(8,128)(2,1)} %copy-done.27, bf16[1024,1536]{1,0:T(8,128)(2,1)} %copy-done, bf16[1024,1536]{1,0:T(8,128)(2,1)} %copy-done, bf16[1024,128]{1,0:T(8,128)(2,1)} %copy-done.61, bf16[512,128]{1,0:T(8,128)(2,1)} %slice_select_fusion.own_feat_ref, ...), custom_call_target="tpu_custom_call" | custom-call | flops 1000 | bytes 1000 | tf_op jit(solution)/shard_map/attend/pallas_call | solution.py:269
  116.1 2.3 copy.74
  121.7 16.8 %up_forward.1 = (f32[512,768]{1,0:T(8,128)S(1)}, f32[512,128]{1,0:T(8,128)S(1)}, bf16[512,768]{1,0:T(8,128)(2,1)}, bf16[768,512]{1,0:T(8,128)(2,1)S(1)}, bf16[51...) custom-call(s32[2]{0:T(128)S(1)} %pad_add_fusion.1.place, ...), custom_call_target="tpu_custom_call" | custom-call | flops 1000 | bytes 1000 | tf_op jit(solution)/shard_map/up_forward/pallas_call | solution.py:529
  138.5 2.6 copy-done.21
  147.4 2.3 copy-done.5
  151.1 1.9 copy-done.31
  154.9 5.3 %down_forward.1 = (bf16[512,768]{1,0:T(8,128)(2,1)}, f32[512,768]{1,0:T(8,128)S(1)}, bf16[512,768]{1,0:T(8,128)(2,1)S(1)}, f32[8,768]{1,0:T(8,128)S(1)}) custom-call(s32[2]{0:T(128)S(1)} %pad_add_fusion.1.place, bf16[512,3072]{1,0:T(8,128)(2,1)S(1)} %copy-done.31, f32[512,768]{1,0:T(8,128)S(1)} %copy-done.23, f32[8,768]{1,0:T(8,128)S(1)} %copy-done.48, ...), custom_call_target="tpu_custom_call" | custom-call | flops 1000 | bytes 1000 | tf_op jit(solution)/shard_map/down_forward/pallas_call | solution.py:600
  162.0 3.1 grad_rows.1
  165.1 2.1 copy-done.7
  168.2 2.3 copy-done.6
  176.1 14.7 %ffn_back.1 = (bf16[512,3072]{1,0:T(8,128)(2,1)S(1)}, f32[1,3072]{1,0:T(1,128)S(1)}, f32[512,768]{1,0:T(8,128)S(1)}, bf16[512,768]{1,0:T(8,128)(2,1)S(1)}, bf16[...) custom-call(s32[2]{0:T(128)S(1)} %pad_add_fusion.1.place, bf16[512,768]{1,0:T(8,128)(2,1)S(1)} %copy-done.26, ...), custom_call_target="tpu_custom_call" | custom-call | flops 1000 | bytes 1000 | tf_op jit(solution)/shard_map/ffn_back/pallas_call | solution.py:677
  191.0 6.1 %grad_columns.2 = (bf16[8,48,3840]{2,1,0:T(8,128)(2,1)S(1)}, bf16[8,48,3840]{2,1,0:T(8,128)(2,1)}) custom-call(s32[2]{0:T(128)S(1)} %pad_add_fusion.1.place, bf16[768,512]{1,0:T(8,128)(2,1)S(1)} %bitcast.54, bf16[512,768]{1,0:T(8,128)(2,1)S(1)} %get-tuple-element.124.refs_1_, bf16[768,512]{1,0:T(8,128)(2,1)S(1)} %copy-done.46, ...), custom_call_target="tpu_custom_call" | custom-call | flops 1000 | bytes 1000 | tf_op jit(solution)/shard_map/grad_columns/pallas_call | solution.py:794
  198.8 5.6 %collective-permute-done.21.part_near.part_far = bf16[8,48,3840]{2,1,0:T(8,128)(2,1)} collective-permute-done((bf16[8,48,3840]{2,1,0:T(8,128)(2,1)}, bf16[8,48,3840]{2,1,0:T(8,128)(2,1)}, u32[]{:S(2)}, u32[]{:S(2)}) %collective-permute-start.21) | collective-permute-done | bytes 2949152 | tf_op jit(solution)/shard_map/ppermute | solution.py:343
  206.3 4.7 %halve.3 = (f32[8,48,1920]{2,1,0:T(8,128)S(1)}, bf16[8,48,1920]{2,1,0:T(8,128)(2,1)}) custom-call(s32[2]{0:T(128)S(1)} %pad_add_fusion.1.place, bf16[8,48,3840]{2,1,0:T(8,128)(2,1)S(1)} %copy-done.16, bf16[8,48,3840]{2,1,0:T(8,128)(2,1)} %collective-permute-done.21.part_near.part_far, bf16[8,48,3840]{2,1,0:T(8,128)(2,1)S(1)} %copy-done.16, ...), custom_call_target="tpu_custom_call" | custom-call | flops 1000 | bytes 1000 | tf_op jit(solution)/shard_map/halve/pallas_call | solution.py:920
  213.3 2.7 copy.75.refs_0_.refs_2_.refs_4_
  215.9 29.7 %attend_back.1 = (bf16[512,768]{1,0:T(8,128)(2,1)}, bf16[1024,768]{1,0:T(8,128)(2,1)}, bf16[1024,768]{1,0:T(8,128)(2,1)}, f32[12,8,128]{2,1,0:T(8,128)}) custom-call(s32[48]{0:T(128)} %concatenate.72.bounds, bf16[512,768]{1,0:T(8,128)(2,1)} %copy-done.27, bf16[1024,1536]{1,0:T(8,128)(2,1)} %copy-done, bf16[1024,1536]{1,0:T(8,128)(2,1)} %copy-done, ...), custom_call_target="tpu_custom_call" | custom-call | flops 1000 | bytes 1000 | tf_op jit(solution)/shard_map/attend_back/pallas_call | solution.py:294
  249.1 3.3 halve.4
  252.5 4.8 %grad_columns.3 = (bf16[8,48,2304]{2,1,0:T(8,128)(2,1)S(1)}, bf16[8,48,2304]{2,1,0:T(8,128)(2,1)S(1)}) custom-call(s32[2]{0:T(128)S(1)} %pad_add_fusion.1.place, bf16[768,1024]{1,0:T(8,128)(2,1)S(1)} %copy-done.4, bf16[512,768]{1,0:T(8,128)(2,1)S(1)} %copy-done.17, bf16[768,1024]{1,0:T(8,128)(2,1)S(1)} %copy-done.4, bf16[1024,768]{1,0:T(8,128)(2,1)S(1)} %copy-done.12, ...), custom_call_target="tpu_custom_call" | custom-call | flops 1000 | bytes 1000 | tf_op jit(solution)/shard_map/grad_columns/pallas_call | solution.py:794
  258.9 2.8 input_back.2.other_ref
  261.7 2.2 halve.5
  264.7 15.2 %collective-permute-done.23.across_ref = bf16[4,48,1920]{2,1,0:T(8,128)(2,1)S(1)} collective-permute-done((bf16[4,48,1920]{2,1,0:T(8,128)(2,1)S(1)}, bf16[4,48,1920]{2,1,0:T(8,128)(2,1)S(1)}, u32[]{:S(2)}, u32[]{:S(2)}) %collective-permute-start.23) | collective-permute-done | bytes 737312 | tf_op jit(solution)/shard_map/ppermute | solution.py:343
  279.9 2.4 column_sends.2
  283.1 2.6 input_back.3.own_ref
  285.7 3.7 small_sums.1
  292.2 8.8 %collective-permute-done.28 = f32[40,768]{1,0:T(8,128)S(1)} collective-permute-done((f32[40,768]{1,0:T(8,128)S(1)}, f32[40,768]{1,0:T(8,128)S(1)}, u32[]{:S(2)}, u32[]{:S(2)}) %collective-permute-start.28) | collective-permute-done | bytes 122912 | tf_op jit(solution)/shard_map/ppermute | solution.py:1021
  301.1 4.9 %collective-permute-done.29 = f32[40,768]{1,0:T(8,128)S(1)} collective-permute-done((f32[40,768]{1,0:T(8,128)S(1)}, f32[40,768]{1,0:T(8,128)S(1)}, u32[]{:S(2)}, u32[]{:S(2)}) %collective-permute-start.29) | collective-permute-done | bytes 122912 | tf_op jit(solution)/shard_map/ppermute | solution.py:1021
  306.0 2.4 collective-permute-start.30
  308.4 4.6 %collective-permute-done.30 = f32[40,768]{1,0:T(8,128)S(1)} collective-permute-done((f32[40,768]{1,0:T(8,128)S(1)}, f32[40,768]{1,0:T(8,128)S(1)}, u32[]{:S(2)}, u32[]{:S(2)}) %collective-permute-start.30) | collective-permute-done | bytes 122912 | tf_op jit(solution)/shard_map/ppermute | solution.py:1021
  313.3 2.2 collective-permute-start.33
  321.7 3.1 column_sends.3
  327.2 2.0 collective-permute-done.34
  329.2 4.0 %collective-permute-done.35 = bf16[48,1920]{1,0:T(8,128)(2,1)} collective-permute-done((bf16[48,1920]{1,0:T(8,128)(2,1)}, bf16[48,1920]{1,0:T(8,128)(2,1)}, u32[]{:S(2)}, u32[]{:S(2)}) %collective-permute-start.35) | collective-permute-done | bytes 184352 | tf_op jit(solution)/shard_map/ppermute | solution.py:343
  340.8 2.0 collective-permute-start.36
  346.3 3.0 collective-permute-done.32
  349.3 7.3 %collective-permute-done.36 = bf16[48,2304]{1,0:T(8,128)(2,1)S(1)} collective-permute-done((bf16[48,2304]{1,0:T(8,128)(2,1)S(1)}, bf16[48,2304]{1,0:T(8,128)(2,1)S(1)}, u32[]{:S(2)}, u32[]{:S(2)}) %collective-permute-start.36) | collective-permute-done | bytes 221216 | tf_op jit(solution)/shard_map/ppermute | solution.py:343
  356.6 5.3 %collective-permute-done.37 = bf16[48,2304]{1,0:T(8,128)(2,1)S(1)} collective-permute-done((bf16[48,2304]{1,0:T(8,128)(2,1)S(1)}, bf16[48,2304]{1,0:T(8,128)(2,1)S(1)}, u32[]{:S(2)}, u32[]{:S(2)}) %collective-permute-start.37) | collective-permute-done | bytes 221216 | tf_op jit(solution)/shard_map/ppermute | solution.py:343
  363.5 5.0 %collective-permute-done.38 = bf16[48,2304]{1,0:T(8,128)(2,1)S(1)} collective-permute-done((bf16[48,2304]{1,0:T(8,128)(2,1)S(1)}, bf16[48,2304]{1,0:T(8,128)(2,1)S(1)}, u32[]{:S(2)}, u32[]{:S(2)}) %collective-permute-start.38) | collective-permute-done | bytes 221216 | tf_op jit(solution)/shard_map/ppermute | solution.py:1027
  (326 shorter events, 106.6 us)
Async XLA Ops:
  7.2 140.2 %all-gather.2.cloned.1.call-start = ((), (), s32[]{:S(2)}) async-start(), calls=%async_computation.1 | async-start | bytes 5013504 | tf_op jit(solution)/shard_map/all_gather | solution.py:1082
  8.2 17.2 %collective-permute-start.1 = (bf16[48,1152]{1,0:T(8,128)(2,1)S(1)}, bf16[48,1152]{1,0:T(8,128)(2,1)S(1)}, u32[]{:S(2)}, u32[]{:S(2)}) collective-permute-start(bf16[48,1152]{1,0:T(8,128)(2,1)S(1)} %get-tuple-element.183), channel_id=1, source_target_pairs={{0,4},{1,5},{2,6},{3,7},{4,0},{5,1},{6,2},{7,3},{8,12},{9,13},{10,... | collective-permute-start | bytes 331784 | tf_op jit(solution)/shard_map/ppermute | solution.py:343
  8.3 17.1 %collective-permute-start.2 = (bf16[48,1152]{1,0:T(8,128)(2,1)S(1)}, bf16[48,1152]{1,0:T(8,128)(2,1)S(1)}, u32[]{:S(2)}, u32[]{:S(2)}) collective-permute-start(bf16[48,1152]{1,0:T(8,128)(2,1)S(1)} %get-tuple-element.183), channel_id=1, source_target_pairs={{0,8},{1,9},{2,10},{3,11},{4,12},{5,13},{6,14},{7,15},{8,0},{9,1},... | collective-permute-start | bytes 331784 | tf_op jit(solution)/shard_map/ppermute | solution.py:343
  11.4 14.1 %collective-permute-start.3 = (bf16[48,1152]{1,0:T(8,128)(2,1)S(1)}, bf16[48,1152]{1,0:T(8,128)(2,1)S(1)}, u32[]{:S(2)}, u32[]{:S(2)}) collective-permute-start(bf16[48,1152]{1,0:T(8,128)(2,1)S(1)} %get-tuple-element.183), channel_id=1, source_target_pairs={{0,12},{1,13},{2,14},{3,15},{4,8},{5,9},{6,10},{7,11},{8,4},{9,5},... | collective-permute-start | bytes 331784 | tf_op jit(solution)/shard_map/ppermute | solution.py:343
  11.8 40.2 %collective-permute-start = (bf16[512,768]{1,0:T(8,128)(2,1)}, bf16[512,768]{1,0:T(8,128)(2,1)S(1)}, u32[]{:S(2)}, u32[]{:S(2)}) collective-permute-start(bf16[512,768]{1,0:T(8,128)(2,1)} %bitcast.52), channel_id=1, source_target_pairs={{0,16},{16,0},{1,17},{17,1},{2,18},{18,2},{3,19},{19,3},{4,20},{20... | collective-permute-start | bytes 2359304 | tf_op jit(solution)/shard_map/ppermute | solution.py:1027
  26.4 317.9 %reduce-scatter.2.cloned.1.call-start = ((), (), s32[]{:S(2)}) async-start(), calls=%async_computation.2 | async-start | bytes 5013504 | tf_op jit(solution)/shard_map/reduce_scatter | solution.py:1160
  30.7 13.9 %collective-permute-start.4 = (bf16[4,48,1152]{2,1,0:T(8,128)(2,1)S(1)}, bf16[4,48,1152]{2,1,0:T(8,128)(2,1)S(1)}, u32[]{:S(2)}, u32[]{:S(2)}) collective-permute-start(bf16[4,48,1152]{2,1,0:T(8,128)(2,1)S(1)} %copy-done.63), channel_id=1, source_target_pairs={{0,2},{1,3},{2,0},{3,1},{4,6},{5,7},{6,4},{7,5},{8,10},{9,11},{10,... | collective-permute-start | bytes 1327112 | tf_op jit(solution)/shard_map/ppermute | solution.py:343
  32.2 13.1 %collective-permute-start.7 = (bf16[48,896]{1,0:T(8,128)(2,1)S(1)}, bf16[48,896]{1,0:T(8,128)(2,1)S(1)}, u32[]{:S(2)}, u32[]{:S(2)}) collective-permute-start(bf16[48,896]{1,0:T(8,128)(2,1)S(1)} %fusion.2), channel_id=1, source_target_pairs={{0,4},{1,5},{2,6},{3,7},{4,0},{5,1},{6,2},{7,3},{8,12},{9,13},{10,... | collective-permute-start | bytes 258056 | tf_op jit(solution)/shard_map/ppermute | solution.py:343
  33.6 11.7 %collective-permute-start.8 = (bf16[48,896]{1,0:T(8,128)(2,1)S(1)}, bf16[48,896]{1,0:T(8,128)(2,1)S(1)}, u32[]{:S(2)}, u32[]{:S(2)}) collective-permute-start(bf16[48,896]{1,0:T(8,128)(2,1)S(1)} %fusion.2), channel_id=1, source_target_pairs={{0,8},{1,9},{2,10},{3,11},{4,12},{5,13},{6,14},{7,15},{8,0},{9,1},... | collective-permute-start | bytes 258056 | tf_op jit(solution)/shard_map/ppermute | solution.py:343
  35.7 12.7 %collective-permute-start.9 = (bf16[48,896]{1,0:T(8,128)(2,1)S(1)}, bf16[48,896]{1,0:T(8,128)(2,1)S(1)}, u32[]{:S(2)}, u32[]{:S(2)}) collective-permute-start(bf16[48,896]{1,0:T(8,128)(2,1)S(1)} %fusion.2), channel_id=1, source_target_pairs={{0,12},{1,13},{2,14},{3,15},{4,8},{5,9},{6,10},{7,11},{8,4},{9,5},... | collective-permute-start | bytes 258056 | tf_op jit(solution)/shard_map/ppermute | solution.py:343
  44.7 17.0 %collective-permute-start.6 = (bf16[8,48,1152]{2,1,0:T(8,128)(2,1)S(1)}, bf16[8,48,1152]{2,1,0:T(8,128)(2,1)S(1)}, u32[]{:S(2)}, u32[]{:S(2)}) collective-permute-start(bf16[8,48,1152]{2,1,0:T(8,128)(2,1)S(1)} %constant_dynamic-update-slice_fusion.refs_0_), channel_id=1, source_target_pairs={{0,16},{16,0},{1,17},{17,1},{2,18},{18,2},{3,19},{19,3},{4,20},{20... | collective-permute-start | bytes 2654216 | tf_op jit(solution)/shard_map/ppermute | solution.py:1027
  45.3 21.6 %collective-permute-start.5 = (bf16[8,48,1152]{2,1,0:T(8,128)(2,1)S(1)}, bf16[8,48,1152]{2,1,0:T(8,128)(2,1)S(1)}, u32[]{:S(2)}, u32[]{:S(2)}) collective-permute-start(bf16[8,48,1152]{2,1,0:T(8,128)(2,1)S(1)} %constant_dynamic-update-slice_fusion.refs_0_), channel_id=1, source_target_pairs={{0,1},{1,0},{2,3},{3,2},{4,5},{5,4},{6,7},{7,6},{8,9},{9,8},{10,11... | collective-permute-start | bytes 2654216 | tf_op jit(solution)/shard_map/ppermute | solution.py:343
  49.1 7.4 %collective-permute-start.10 = (bf16[4,48,896]{2,1,0:T(8,128)(2,1)S(1)}, bf16[4,48,896]{2,1,0:T(8,128)(2,1)S(1)}, u32[]{:S(2)}, u32[]{:S(2)}) collective-permute-start(bf16[4,48,896]{2,1,0:T(8,128)(2,1)S(1)} %pad_maximum_fusion.3), channel_id=1, source_target_pairs={{0,2},{1,3},{2,0},{3,1},{4,6},{5,7},{6,4},{7,5},{8,10},{9,11},{10,... | collective-permute-start | bytes 1032200 | tf_op jit(solution)/shard_map/ppermute | solution.py:343
  51.9 22.6 %collective-permute-start.12 = (bf16[48,2048]{1,0:T(8,128)(2,1)}, bf16[48,2048]{1,0:T(8,128)(2,1)S(1)}, u32[]{:S(2)}, u32[]{:S(2)}) collective-permute-start(bf16[48,2048]{1,0:T(8,128)(2,1)} %slice.152), channel_id=1, source_target_pairs={{0,4},{1,5},{2,6},{3,7},{4,0},{5,1},{6,2},{7,3},{8,12},{9,13},{10,... | collective-permute-start | bytes 589832 | tf_op jit(solution)/shard_map/ppermute | solution.py:343
  52.0 27.2 %collective-permute-start.13 = (bf16[48,2048]{1,0:T(8,128)(2,1)}, bf16[48,2048]{1,0:T(8,128)(2,1)S(1)}, u32[]{:S(2)}, u32[]{:S(2)}) collective-permute-start(bf16[48,2048]{1,0:T(8,128)(2,1)} %slice.152), channel_id=1, source_target_pairs={{0,8},{1,9},{2,10},{3,11},{4,12},{5,13},{6,14},{7,15},{8,0},{9,1},... | collective-permute-start | bytes 589832 | tf_op jit(solution)/shard_map/ppermute | solution.py:343
  56.6 32.1 %collective-permute-start.14 = (bf16[48,2048]{1,0:T(8,128)(2,1)}, bf16[48,2048]{1,0:T(8,128)(2,1)S(1)}, u32[]{:S(2)}, u32[]{:S(2)}) collective-permute-start(bf16[48,2048]{1,0:T(8,128)(2,1)} %slice.152), channel_id=1, source_target_pairs={{0,12},{1,13},{2,14},{3,15},{4,8},{5,9},{6,10},{7,11},{8,4},{9,5},... | collective-permute-start | bytes 589832 | tf_op jit(solution)/shard_map/ppermute | solution.py:343
  61.7 5.1 %collective-permute-start.11 = (bf16[8,48,1152]{2,1,0:T(8,128)(2,1)S(1)}, bf16[8,48,1152]{2,1,0:T(8,128)(2,1)S(1)}, u32[]{:S(2)}, u32[]{:S(2)}) collective-permute-start(bf16[8,48,1152]{2,1,0:T(8,128)(2,1)S(1)} %collective-permute-done.6.refs_2_), channel_id=1, source_target_pairs={{0,1},{1,0},{2,3},{3,2},{4,5},{5,4},{6,7},{7,6},{8,9},{9,8},{10,11... | collective-permute-start | bytes 2654216 | tf_op jit(solution)/shard_map/ppermute | solution.py:343
  90.6 14.7 %collective-permute-start.19 = (bf16[4,48,2048]{2,1,0:T(8,128)(2,1)}, bf16[4,48,2048]{2,1,0:T(8,128)(2,1)}, u32[]{:S(2)}, u32[]{:S(2)}) collective-permute-start(bf16[4,48,2048]{2,1,0:T(8,128)(2,1)} %pad_maximum_fusion.1.refs_4_), channel_id=1, source_target_pairs={{0,2},{1,3},{2,0},{3,1},{4,6},{5,7},{6,4},{7,5},{8,10},{9,11},{10,... | collective-permute-start | bytes 2359304 | tf_op jit(solution)/shard_map/ppermute | solution.py:343
  91.1 14.9 %collective-permute-start.16 = (bf16[8,48,896]{2,1,0:T(8,128)(2,1)}, bf16[8,48,896]{2,1,0:T(8,128)(2,1)}, u32[]{:S(2)}, u32[]{:S(2)}) collective-permute-start(bf16[8,48,896]{2,1,0:T(8,128)(2,1)} %constant_dynamic-update-slice_fusion.5.refs_0_), channel_id=1, source_target_pairs={{0,16},{16,0},{1,17},{17,1},{2,18},{18,2},{3,19},{19,3},{4,20},{20... | collective-permute-start | bytes 2064392 | tf_op jit(solution)/shard_map/ppermute | solution.py:1027
  92.5 25.9 %collective-permute-start.18 = (bf16[4,48,2048]{2,1,0:T(8,128)(2,1)}, bf16[4,48,2048]{2,1,0:T(8,128)(2,1)}, u32[]{:S(2)}, u32[]{:S(2)}) collective-permute-start(bf16[4,48,2048]{2,1,0:T(8,128)(2,1)} %pad_maximum_fusion.1.refs_4_), channel_id=1, source_target_pairs={{0,1},{1,0},{2,3},{3,2},{4,5},{5,4},{6,7},{7,6},{8,9},{9,8},{10,11... | collective-permute-start | bytes 2359304 | tf_op jit(solution)/shard_map/ppermute | solution.py:343
  105.4 13.0 %collective-permute-start.20 = (bf16[4,48,2048]{2,1,0:T(8,128)(2,1)}, bf16[4,48,2048]{2,1,0:T(8,128)(2,1)}, u32[]{:S(2)}, u32[]{:S(2)}) collective-permute-start(bf16[4,48,2048]{2,1,0:T(8,128)(2,1)} %collective-permute-done.19.refs_6_), channel_id=1, source_target_pairs={{0,1},{1,0},{2,3},{3,2},{4,5},{5,4},{6,7},{7,6},{8,9},{9,8},{10,11... | collective-permute-start | bytes 2359304 | tf_op jit(solution)/shard_map/ppermute | solution.py:343
  106.0 12.4 %collective-permute-start.15 = (bf16[8,48,896]{2,1,0:T(8,128)(2,1)}, bf16[8,48,896]{2,1,0:T(8,128)(2,1)}, u32[]{:S(2)}, u32[]{:S(2)}) collective-permute-start(bf16[8,48,896]{2,1,0:T(8,128)(2,1)} %constant_dynamic-update-slice_fusion.5.refs_0_), channel_id=1, source_target_pairs={{0,1},{1,0},{2,3},{3,2},{4,5},{5,4},{6,7},{7,6},{8,9},{9,8},{10,11... | collective-permute-start | bytes 2064392 | tf_op jit(solution)/shard_map/ppermute | solution.py:343
  106.0 12.4 %collective-permute-start.17 = (bf16[8,48,896]{2,1,0:T(8,128)(2,1)}, bf16[8,48,896]{2,1,0:T(8,128)(2,1)}, u32[]{:S(2)}, u32[]{:S(2)}) collective-permute-start(bf16[8,48,896]{2,1,0:T(8,128)(2,1)} %collective-permute-done.16.refs_2_), channel_id=1, source_target_pairs={{0,1},{1,0},{2,3},{3,2},{4,5},{5,4},{6,7},{7,6},{8,9},{9,8},{10,11... | collective-permute-start | bytes 2064392 | tf_op jit(solution)/shard_map/ppermute | solution.py:343
  176.1 14.8 %copy-start.46 = (bf16[768,512]{1,0:T(8,128)(2,1)S(1)}, bf16[768,512]{1,0:T(8,128)(2,1)}, u32[]{:S(2)}) copy-start(bf16[768,512]{1,0:T(8,128)(2,1)} %copy-done.45) | copy-start | bytes 2359300
  198.7 5.7 %collective-permute-start.21 = (bf16[8,48,3840]{2,1,0:T(8,128)(2,1)}, bf16[8,48,3840]{2,1,0:T(8,128)(2,1)}, u32[]{:S(2)}, u32[]{:S(2)}) collective-permute-start(bf16[8,48,3840]{2,1,0:T(8,128)(2,1)} %get-tuple-element.128), channel_id=1, source_target_pairs={{0,1},{1,0},{2,3},{3,2},{4,5},{5,4},{6,7},{7,6},{8,9},{9,8},{10,11... | collective-permute-start | bytes 8847368 | tf_op jit(solution)/shard_map/ppermute | solution.py:343
  212.6 34.6 %collective-permute-start.22 = (bf16[8,48,1920]{2,1,0:T(8,128)(2,1)}, bf16[8,48,1920]{2,1,0:T(8,128)(2,1)}, u32[]{:S(2)}, u32[]{:S(2)}) collective-permute-start(bf16[8,48,1920]{2,1,0:T(8,128)(2,1)} %get-tuple-element.129), channel_id=1, source_target_pairs={{0,16},{16,0},{1,17},{17,1},{2,18},{18,2},{3,19},{19,3},{4,20},{20... | collective-permute-start | bytes 4423688 | tf_op jit(solution)/shard_map/ppermute | solution.py:1027
  257.3 4.5 %collective-permute-start.24 = (bf16[8,48,2304]{2,1,0:T(8,128)(2,1)S(1)}, bf16[8,48,2304]{2,1,0:T(8,128)(2,1)S(1)}, u32[]{:S(2)}, u32[]{:S(2)}) collective-permute-start(bf16[8,48,2304]{2,1,0:T(8,128)(2,1)S(1)} %get-tuple-element.140), channel_id=1, source_target_pairs={{0,1},{1,0},{2,3},{3,2},{4,5},{5,4},{6,7},{7,6},{8,9},{9,8},{10,11... | collective-permute-start | bytes 5308424 | tf_op jit(solution)/shard_map/ppermute | solution.py:343
  257.3 22.5 %collective-permute-start.23 = (bf16[4,48,1920]{2,1,0:T(8,128)(2,1)S(1)}, bf16[4,48,1920]{2,1,0:T(8,128)(2,1)S(1)}, u32[]{:S(2)}, u32[]{:S(2)}) collective-permute-start(bf16[4,48,1920]{2,1,0:T(8,128)(2,1)S(1)} %get-tuple-element.137), channel_id=1, source_target_pairs={{0,2},{1,3},{2,0},{3,1},{4,6},{5,7},{6,4},{7,5},{8,10},{9,11},{10,... | collective-permute-start | bytes 2211848 | tf_op jit(solution)/shard_map/ppermute | solution.py:343
  263.9 21.7 %copy-start.35 = (f32[4,48,2304]{2,1,0:T(8,128)}, f32[4,48,2304]{2,1,0:T(8,128)S(1)}, u32[]{:S(2)}) copy-start(f32[4,48,2304]{2,1,0:T(8,128)S(1)} %get-tuple-element.150.held_ref) | copy-start | bytes 5308420
  263.9 19.1 %copy-start.38 = (f32[512,768]{1,0:T(8,128)S(1)}, f32[512,768]{1,0:T(8,128)}, u32[]{:S(2)}) copy-start(f32[512,768]{1,0:T(8,128)} %copy-done.37) | copy-start | bytes 4718596
  263.9 56.3 %collective-permute-start.26 = (bf16[4,48,2304]{2,1,0:T(8,128)(2,1)}, bf16[4,48,2304]{2,1,0:T(8,128)(2,1)}, u32[]{:S(2)}, u32[]{:S(2)}) collective-permute-start(bf16[4,48,2304]{2,1,0:T(8,128)(2,1)} %get-tuple-element.144), channel_id=1, source_target_pairs={{0,2},{1,3},{2,0},{3,1},{4,6},{5,7},{6,4},{7,5},{8,10},{9,11},{10,... | collective-permute-start | bytes 2654216 | tf_op jit(solution)/shard_map/ppermute | solution.py:343
  285.7 33.8 %copy-start.73 = (f32[3,768]{1,0:T(4,128)S(1)}, f32[3,768]{1,0:T(4,128)}, u32[]{:S(2)}) copy-start(f32[3,768]{1,0:T(4,128)} %param.30) | copy-start | bytes 27652
  289.4 1.4 collective-permute-start.27
  289.5 35.3 %collective-permute-start.25 = (bf16[512,768]{1,0:T(8,128)(2,1)}, bf16[512,768]{1,0:T(8,128)(2,1)S(1)}, u32[]{:S(2)}, u32[]{:S(2)}) collective-permute-start(bf16[512,768]{1,0:T(8,128)(2,1)} %input_back.2.other_ref), channel_id=1, source_target_pairs={{0,16},{16,0},{1,17},{17,1},{2,18},{18,2},{3,19},{19,3},{4,20},{20... | collective-permute-start | bytes 2359304 | tf_op jit(solution)/shard_map/ppermute | solution.py:1027
  290.8 10.1 %collective-permute-start.28 = (f32[40,768]{1,0:T(8,128)S(1)}, f32[40,768]{1,0:T(8,128)S(1)}, u32[]{:S(2)}, u32[]{:S(2)}) collective-permute-start(f32[40,768]{1,0:T(8,128)S(1)} %add.193), channel_id=1, source_target_pairs={{0,2},{1,3},{2,0},{3,1},{4,6},{5,7},{6,4},{7,5},{8,10},{9,11},{10,... | collective-permute-start | bytes 368648 | tf_op jit(solution)/shard_map/ppermute | solution.py:1021
  301.0 5.0 %collective-permute-start.29 = (f32[40,768]{1,0:T(8,128)S(1)}, f32[40,768]{1,0:T(8,128)S(1)}, u32[]{:S(2)}, u32[]{:S(2)}) collective-permute-start(f32[40,768]{1,0:T(8,128)S(1)} %add.194), channel_id=1, source_target_pairs={{0,4},{1,5},{2,6},{3,7},{4,0},{5,1},{6,2},{7,3},{8,12},{9,13},{10,... | collective-permute-start | bytes 368648 | tf_op jit(solution)/shard_map/ppermute | solution.py:1021
  306.0 7.0 %collective-permute-start.30 = (f32[40,768]{1,0:T(8,128)S(1)}, f32[40,768]{1,0:T(8,128)S(1)}, u32[]{:S(2)}, u32[]{:S(2)}) collective-permute-start(f32[40,768]{1,0:T(8,128)S(1)} %add.195), channel_id=1, source_target_pairs={{0,8},{1,9},{2,10},{3,11},{4,12},{5,13},{6,14},{7,15},{8,0},{9,1},... | collective-permute-start | bytes 368648 | tf_op jit(solution)/shard_map/ppermute | solution.py:1021
  313.0 4.9 %collective-permute-start.31 = (f32[40,768]{1,0:T(8,128)S(1)}, f32[40,768]{1,0:T(8,128)S(1)}, u32[]{:S(2)}, u32[]{:S(2)}) collective-permute-start(f32[40,768]{1,0:T(8,128)S(1)} %add.196), channel_id=1, source_target_pairs={{0,16},{16,0},{1,17},{17,1},{2,18},{18,2},{3,19},{19,3},{4,20},{20... | collective-permute-start | bytes 368648 | tf_op jit(solution)/shard_map/ppermute | solution.py:1027
  313.3 13.9 %collective-permute-start.33 = (bf16[48,1920]{1,0:T(8,128)(2,1)}, bf16[48,1920]{1,0:T(8,128)(2,1)}, u32[]{:S(2)}, u32[]{:S(2)}) collective-permute-start(bf16[48,1920]{1,0:T(8,128)(2,1)} %get-tuple-element.146), channel_id=1, source_target_pairs={{0,4},{1,5},{2,6},{3,7},{4,0},{5,1},{6,2},{7,3},{8,12},{9,13},{10,... | collective-permute-start | bytes 552968 | tf_op jit(solution)/shard_map/ppermute | solution.py:343
  315.5 13.7 %collective-permute-start.34 = (bf16[48,1920]{1,0:T(8,128)(2,1)}, bf16[48,1920]{1,0:T(8,128)(2,1)}, u32[]{:S(2)}, u32[]{:S(2)}) collective-permute-start(bf16[48,1920]{1,0:T(8,128)(2,1)} %get-tuple-element.147), channel_id=1, source_target_pairs={{0,8},{1,9},{2,10},{3,11},{4,12},{5,13},{6,14},{7,15},{8,0},{9,1},... | collective-permute-start | bytes 552968 | tf_op jit(solution)/shard_map/ppermute | solution.py:343
  317.9 15.2 %collective-permute-start.35 = (bf16[48,1920]{1,0:T(8,128)(2,1)}, bf16[48,1920]{1,0:T(8,128)(2,1)}, u32[]{:S(2)}, u32[]{:S(2)}) collective-permute-start(bf16[48,1920]{1,0:T(8,128)(2,1)} %get-tuple-element.148), channel_id=1, source_target_pairs={{0,12},{1,13},{2,14},{3,15},{4,8},{5,9},{6,10},{7,11},{8,4},{9,5},... | collective-permute-start | bytes 552968 | tf_op jit(solution)/shard_map/ppermute | solution.py:343
  334.3 10.4 %collective-permute-start.39 = (bf16[48,1920]{1,0:T(8,128)(2,1)S(1)}, bf16[48,1920]{1,0:T(8,128)(2,1)S(1)}, u32[]{:S(2)}, u32[]{:S(2)}) collective-permute-start(bf16[48,1920]{1,0:T(8,128)(2,1)S(1)} %add_convert_fusion.4), channel_id=1, source_target_pairs={{0,16},{16,0},{1,17},{17,1},{2,18},{18,2},{3,19},{19,3},{4,20},{20... | collective-permute-start | bytes 552968 | tf_op jit(solution)/shard_map/ppermute | solution.py:1027
  340.8 8.6 %collective-permute-start.32 = (bf16[48,2304]{1,0:T(8,128)(2,1)}, bf16[48,2304]{1,0:T(8,128)(2,1)S(1)}, u32[]{:S(2)}, u32[]{:S(2)}) collective-permute-start(bf16[48,2304]{1,0:T(8,128)(2,1)} %copy-done.60), channel_id=1, source_target_pairs={{0,4},{1,5},{2,6},{3,7},{4,0},{5,1},{6,2},{7,3},{8,12},{9,13},{10,... | collective-permute-start | bytes 663560 | tf_op jit(solution)/shard_map/ppermute | solution.py:343
  340.8 15.8 %collective-permute-start.36 = (bf16[48,2304]{1,0:T(8,128)(2,1)S(1)}, bf16[48,2304]{1,0:T(8,128)(2,1)S(1)}, u32[]{:S(2)}, u32[]{:S(2)}) collective-permute-start(bf16[48,2304]{1,0:T(8,128)(2,1)S(1)} %get-tuple-element.157), channel_id=1, source_target_pairs={{0,8},{1,9},{2,10},{3,11},{4,12},{5,13},{6,14},{7,15},{8,0},{9,1},... | collective-permute-start | bytes 663560 | tf_op jit(solution)/shard_map/ppermute | solution.py:343
  342.8 19.1 %collective-permute-start.37 = (bf16[48,2304]{1,0:T(8,128)(2,1)S(1)}, bf16[48,2304]{1,0:T(8,128)(2,1)S(1)}, u32[]{:S(2)}, u32[]{:S(2)}) collective-permute-start(bf16[48,2304]{1,0:T(8,128)(2,1)S(1)} %get-tuple-element.158), channel_id=1, source_target_pairs={{0,12},{1,13},{2,14},{3,15},{4,8},{5,9},{6,10},{7,11},{8,4},{9,5},... | collective-permute-start | bytes 663560 | tf_op jit(solution)/shard_map/ppermute | solution.py:343
  344.3 18.3 %collective-permute-start.40 = (bf16[192,768]{1,0:T(8,128)(2,1)}, bf16[192,768]{1,0:T(8,128)(2,1)S(1)}, u32[]{:S(2)}, u32[]{:S(2)}) collective-permute-start(bf16[192,768]{1,0:T(8,128)(2,1)} %reduce-scatter.2.cloned.1.call-done), channel_id=1, source_target_pairs={{0,16},{16,0},{1,17},{17,1},{2,18},{18,2},{3,19},{19,3},{4,20},{20... | collective-permute-start | bytes 884744 | tf_op jit(solution)/shard_map/ppermute | solution.py:1027
  344.8 17.8 %copy-start.70 = (bf16[192,768]{1,0:T(8,128)(2,1)S(1)}, bf16[192,768]{1,0:T(8,128)(2,1)}, u32[]{:S(2)}) copy-start(bf16[192,768]{1,0:T(8,128)(2,1)} %reduce-scatter.2.cloned.1.call-done) | copy-start | bytes 884740
  362.0 6.4 %collective-permute-start.38 = (bf16[48,2304]{1,0:T(8,128)(2,1)S(1)}, bf16[48,2304]{1,0:T(8,128)(2,1)S(1)}, u32[]{:S(2)}, u32[]{:S(2)}) collective-permute-start(bf16[48,2304]{1,0:T(8,128)(2,1)S(1)} %add_convert_fusion.3), channel_id=1, source_target_pairs={{0,16},{16,0},{1,17},{17,1},{2,18},{18,2},{3,19},{19,3},{4,20},{20... | collective-permute-start | bytes 663560 | tf_op jit(solution)/shard_map/ppermute | solution.py:1027
  (78 other events, 316.2 us)
Sparse Core Ops, SparseCore 0:
  26.5 63.7 all-gather.1
  198.9 77.7 reduce-scatter.1

commit v8 on v7

--- a/solution.py
+++ b/solution.py
@@ -499,7 +499,7 @@
         active = active.astype(bf16)
         active_ref[...] = active
         active_t_ref[...] = active.T
-        slope_ref[...] = slope
+        slope_ref[...] = slope.astype(bf16)
 
     @pl.when(step == 0)
     def _():
@@ -561,10 +561,9 @@
             jax.ShapeDtypeStruct((width, tokens), bf16),
             jax.ShapeDtypeStruct((tokens, hidden_width), bf16),
             jax.ShapeDtypeStruct((hidden_width, tokens), bf16),
-            jax.ShapeDtypeStruct((tokens, hidden_width), f32),
+            jax.ShapeDtypeStruct((tokens, hidden_width), bf16),
         ],
         cost_estimate=small_cost,
-        compiler_params=pltpu.CompilerParams(vmem_limit_bytes=28 << 20),
         name="up_forward",
     )(place, context, mixed, vectors, bias_up, *pieces)
 
@@ -616,7 +615,6 @@
             jax.ShapeDtypeStruct((8, width), f32),
         ],
         cost_estimate=small_cost,
-        compiler_params=pltpu.CompilerParams(vmem_limit_bytes=24 << 20),
         name="down_forward",
     )(place, active, unit, vectors, grads, *pieces)
 
@@ -643,7 +641,7 @@
     bias = jnp.zeros((1, tile), f32)
     for part in range(2):
         rows = pl.ds(part * half, half)
-        grads = (dot_right_t(low_ref[rows, :], rows_down) * slope_ref[rows, :]).astype(bf16)
+        grads = (dot_right_t(low_ref[rows, :], rows_down) * slope_ref[rows, :].astype(f32)).astype(bf16)
         hidden_ref[rows, :] = grads
         bias = bias + jnp.sum(grads.astype(f32), axis=0, keepdims=True)
         total[rows, :] += dot_right_t(grads, columns)
@@ -712,7 +710,6 @@
             jax.ShapeDtypeStruct((8, width), f32),
         ],
         cost_estimate=small_cost,
-        compiler_params=pltpu.CompilerParams(vmem_limit_bytes=32 << 20),
         name="ffn_back",
     )(place, low, slope, total, unit, scale, vectors, *pieces_rest, *pieces_down)
 
@@ -1011,16 +1008,8 @@
     return jnp.concatenate([aligned(own_low), own_low, own_high, aligned(low), low, high])
 
 
-def sum_everywhere(values):
-    count = lax.axis_size("page")
-    if count & (count - 1):
-        values = lax.psum(values, "page")
-    else:
-        step = 1
-        while step < count:
-            values = values + lax.ppermute(values, "page", [(i, i ^ step) for i in range(count)])
-            step = step * 2
-    return values + swap(values)
+def both_sum(values, mask):
+    return values + exchange(values, mask)
 
 
 def swap(values):
@@ -1069,10 +1058,10 @@
         column_qkv = column_of(half_columns(pack_qkv, is_text))
         parts_near = column_parts(after(half_columns(pack_rest[:, :split], is_text), column_qkv))
         pieces_qkv = half_pieces(column_qkv)
-        w_down = after(w_down, column_qkv)
         column_near = jnp.stack([after(part, pieces_qkv[0]) for part in parts_near])
         parts_far = column_parts(after(pack_rest[:, split:], column_near))
         pieces_near = half_pieces(column_near)
+        w_down = after(w_down, pieces_near[0])
         pieces_qkv[2] = after(pieces_qkv[2], pieces_near[0])
         pieces_qkv[3] = exchange(pieces_qkv[2], 1)
         groups_qkv = (("halves", 0),)
@@ -1125,10 +1114,16 @@
         axis=0,
     )
     mixed_t = mixed_all.T
+    vectors = jnp.stack(
+        [b_out, gain_one, bias_one, b_down, gain_two, bias_two, jnp.zeros_like(b_out), b_out]
+    )
+    biases = jnp.concatenate([b_query, jnp.zeros_like(b_value), b_value])[None]
+    taps = jnp.pad(conv_weight, ((0, 5), (0, 0)))
+    bias_up = b_up[None]
     if fast:
         early = (mixed_all, mixed_t, features, tables, bounds, own_flip, own_feats, masks)
+        early += (vectors, biases, taps, bias_up)
         pieces_qkv[0] = after(pieces_qkv[0], *early)
-    biases = jnp.concatenate([b_query, jnp.zeros_like(b_value), b_value])[None]
     queries, keys_values, full_qkv = project(place, mixed_all, biases, groups_qkv, pieces_qkv)
     attend_in = queries
     if fast:
@@ -1145,11 +1140,8 @@
     else:
         pieces_rest = [lax.all_gather(pack_rest, "page", axis=0, tiled=True)]
         groups_rest = (("full", 0),)
-    vectors = jnp.stack(
-        [b_out, gain_one, bias_one, b_down, gain_two, bias_two, jnp.zeros_like(b_out), b_out]
-    )
     unit, scale, normed_low, normed_t, active, active_t, slope = up_forward(
-        place, context, mixed, vectors, b_up[None], groups_rest, pieces_rest
+        place, context, mixed, vectors, bias_up, groups_rest, pieces_rest
     )
     groups_down = (("full", 0),)
     pieces_down = [full_down]
@@ -1190,13 +1182,16 @@
         plane_rest = after(plane_rest, grad_queries)
         held_rest, across_out = halve_across(place, held_rest, plane_rest)
         across_rest = exchange(across_out, 2)
-        grad_queries_in = after(grad_queries, across_out)
+        shard_down = after(shard_down, grad_queries)
+        shard_down = shard_down.astype(f32) + swap(shard_down).astype(f32)
+        grad_queries_in = after(grad_queries, across_out, shard_down)
     pairs = [(mixed_t, True, grad_queries_in), (mixed_t, False, grad_keys), (mixed_t, False, grad_values)]
     if fast:
         keep_qkv, send_qkv = grad_by_columns(pairs, place, d_model)
         partner_qkv = exchange(send_qkv, 1)
         grad_keys_in = after(grad_keys, send_qkv)
     else:
+        shard_down = shard_down.astype(f32) + swap(shard_down).astype(f32)
         shard_qkv = summed_rows(
             [(mixed_low.T, grad_queries), (mixed_t, grad_keys), (mixed_t, grad_values)]
         )
@@ -1207,10 +1202,7 @@
         partner_qkv = after(partner_qkv, to_other)
         held_qkv, across_out = halve_across(place, keep_qkv, partner_qkv)
         across_qkv = exchange(across_out, 2)
-        across_rest = after(across_rest, across_out)
-        own_rest, sends_rest = column_sends(held_rest, across_rest)
-        arrived_rest = column_arrivals(sends_rest)
-        grad_values_in = after(grad_values, *sends_rest)
+        grad_values_in = after(grad_values, across_out)
     own_part = input_back(place, full_qkv, grad_keys, grad_values_in, (grad_first, grad_queries))
     packed = small_sums(
         own_part,
@@ -1225,22 +1217,30 @@
         grad_b_up,
         grad_tables,
     )
-    packed = sum_everywhere(packed)
     if fast:
+        packed = both_sum(packed, 1)
+        across_rest = after(across_rest, packed)
+        own_rest, sends_rest = column_sends(held_rest, across_rest)
+        arrived_rest = column_arrivals(sends_rest)
+        packed = both_sum(after(packed, *sends_rest), 2)
         across_qkv = after(across_qkv, packed)
         own_qkv, sends_qkv = column_sends(held_qkv, across_qkv)
         arrived_qkv = column_arrivals(sends_qkv)
         from_other = after(from_other, *sends_qkv)
-    grad_in = state_back(own_part, from_other, masks, jnp.pad(conv_weight, ((0, 5), (0, 0))))
+    else:
+        packed = lax.psum(packed, ("mod", "page"))
+    grad_in = state_back(own_part, from_other, masks, taps)
     if fast:
         arrived_rest = [after(part, grad_in) for part in arrived_rest]
         total_rest = column_total(own_rest, arrived_rest)
         far_rest = swap(total_rest)
-        arrived_qkv = [after(part, total_rest) for part in arrived_qkv]
+        packed = after(packed, total_rest)
+        packed = packed + swap(packed)
+        arrived_qkv = [after(part, packed) for part in arrived_qkv]
         total_qkv = column_total(own_qkv, arrived_qkv)
         far_qkv = swap(total_qkv)
+        packed = both_sum(both_sum(after(packed, total_qkv), 4), 8)
     g_tables = packed[28:34].reshape(HEADS, 3, LANES)
-    shard_down = shard_down.astype(f32) + swap(shard_down).astype(f32)
     if fast:
         shard_rest = jnp.where(
             is_text,

time: 383 us -> 346 us (0.903)
  the two profiles are of different devices: /device:TPU:8 before, /device:TPU:0 now
where the time goes in v8:
time: 346 us; the launch traced here: 341 us
  Pallas kernels  128 us (37%)
  waiting for transfers between devices  98.2 us (28%)
  starting transfers between devices  48.1 us (14%)
  local copies, waits for them, and re-layouts  35.9 us (10%)
  between operations  15.5 us (4%)
  other arithmetic  15.3 us (4%)
    ppermute x32, waiting for transfers between devices, exchange(): return lax.ppermute(values, 'page', [(i, i ^ mask) for i in range(count)])  73.5 us
    ppermute x32, starting transfers between devices, exchange(): return lax.ppermute(values, 'page', [(i, i ^ mask) for i in range(count)])  38.3 us
    pallas_call x1, Pallas kernels, attend_back(): pl.pallas_call(attend_back_kernel, grid_spec=pltpu.PrefetchScalarGridSpec...  29.6 us
    unnamed x113, local copies, waits for them, and re-layouts  22.3 us
    ppermute x9, waiting for transfers between devices, swap(): return lax.ppermute(values, 'mod', [(0, 1), (1, 0)])  22.2 us
    pallas_call x1, Pallas kernels, up_forward(): pl.pallas_call(functools.partial(up_kernel, groups), grid_spec=pltpu.Pref...  19.9 us
    pallas_call x1, Pallas kernels, ffn_back(): pl.pallas_call(functools.partial(ffn_back_kernel, groups, groups_down, co...  19.3 us
    pallas_call x1, Pallas kernels, attend(): pl.pallas_call(attend_kernel, grid_spec=pltpu.PrefetchScalarGridSpec(num_...  13 us
  transfers between devices with their start and end apart: 43, of which 20 were waited for; matrix products, arithmetic and copies ran while one was open for 7% of the time, Pallas kernels for 32%

profile of v8, /device:TPU:0, one launch (start us, length us, event | category | flops | bytes accessed | tf_op | source)
XLA Modules:
  0.0 340.5 jit_solution(13710885637607009176)
XLA Ops:
  8.2 5.1 %collective-permute-start.3 = (bf16[48,1152]{1,0:T(8,128)(2,1)S(1)}, bf16[48,1152]{1,0:T(8,128)(2,1)S(1)}, u32[]{:S(2)}, u32[]{:S(2)}) collective-permute-start(bf16[48,1152]{1,0:T(8,128)(2,1)S(1)} %get-tuple-element.191), channel_id=1, source_target_pairs={{0,12},{1,13},{2,14},{3,15},{4,8},{5,9},{6,10},{7,11},{8,4},{9,5},... | collective-permute-start | bytes 331784 | tf_op jit(solution)/shard_map/ppermute | solution.py:343
  15.0 2.4 collective-permute-done.3
  17.3 5.3 %collective-permute-done.2 = bf16[48,1152]{1,0:T(8,128)(2,1)S(1)} collective-permute-done((bf16[48,1152]{1,0:T(8,128)(2,1)S(1)}, bf16[48,1152]{1,0:T(8,128)(2,1)S(1)}, u32[]{:S(2)}, u32[]{:S(2)}) %collective-permute-start.2) | collective-permute-done | bytes 110624 | tf_op jit(solution)/shard_map/ppermute | solution.py:343
  22.8 2.5 collective-permute-start.9
  25.3 1.9 collective-permute-start.7
  28.8 8.8 %collective-permute-done.4 = bf16[4,48,1152]{2,1,0:T(8,128)(2,1)S(1)} collective-permute-done((bf16[4,48,1152]{2,1,0:T(8,128)(2,1)S(1)}, bf16[4,48,1152]{2,1,0:T(8,128)(2,1)S(1)}, u32[]{:S(2)}, u32[]{:S(2)}) %collective-permute-start.4) | collective-permute-done | bytes 442400 | tf_op jit(solution)/shard_map/ppermute | solution.py:343
  42.1 3.9 %collective-permute-done.10 = bf16[4,48,896]{2,1,0:T(8,128)(2,1)S(1)} collective-permute-done((bf16[4,48,896]{2,1,0:T(8,128)(2,1)S(1)}, bf16[4,48,896]{2,1,0:T(8,128)(2,1)S(1)}, u32[]{:S(2)}, u32[]{:S(2)}) %collective-permute-start.10) | collective-permute-done | bytes 344096 | tf_op jit(solution)/shard_map/ppermute | solution.py:343
  57.8 2.2 collective-permute-start.14
  60.0 2.2 collective-permute-start.12
  62.2 5.2 %collective-permute-done.x_other_ref = bf16[512,768]{1,0:T(8,128)(2,1)S(1)} collective-permute-done((bf16[512,768]{1,0:T(8,128)(2,1)S(1)}, bf16[512,768]{1,0:T(8,128)(2,1)S(1)}, u32[]{:S(2)}, u32[]{:S(2)}) %collective-permute-start) | collective-permute-done | bytes 786464 | tf_op jit(solution)/shard_map/ppermute | solution.py:1016
  67.6 14.1 %collective-permute-done.6.refs_2_ = bf16[8,48,1152]{2,1,0:T(8,128)(2,1)S(1)} collective-permute-done((bf16[8,48,1152]{2,1,0:T(8,128)(2,1)S(1)}, bf16[8,48,1152]{2,1,0:T(8,128)(2,1)S(1)}, u32[]{:S(2)}, u32[]{:S(2)}) %collective-permute-start.6) | collective-permute-done | bytes 884768 | tf_op jit(solution)/shard_map/ppermute | solution.py:1016
  81.8 2.5 broadcast_select_fusion.1
  86.9 5.1 %project.1 = (bf16[512,768]{1,0:T(8,128)(2,1)S(1)}, bf16[1024,1536]{1,0:T(8,128)(2,1)S(1)}, bf16[768,2304]{1,0:T(8,128)(2,1)S(1)}) custom-call(s32[2]{0:T(128)S(1)} %pad_add_fusion.1.place, bf16[1024,768]{1,0:T(8,128)(2,1)S(1)} %get-tuple-element.198.mixed_ref, f32[1,2304]{1,0:T(1,128)S(1)} %broadcast_in_dim.67.bias_ref, ...), custom_call_target="tpu_custom_call" | custom-call | flops 1000 | bytes 1000 | tf_op jit(solution)/shard_map/project/pallas_call | solution.py:375
  94.7 1.9 pad_maximum_fusion.1.refs_4_
  99.8 13.0 %attend.1.context_ref = bf16[512,768]{1,0:T(8,128)(2,1)} custom-call(s32[48]{0:T(128)} %concatenate.72.bounds, bf16[512,768]{1,0:T(8,128)(2,1)} %copy-done.13, bf16[1024,1536]{1,0:T(8,128)(2,1)} %copy-done, bf16[1024,1536]{1,0:T(8,128)(2,1)} %copy-done, bf16[1024,128]{1,0:T(8,128)(2,1)} %copy-done.31, bf16[512,128]{1,0:T(8,128)(2,1)} %slice_select_fusion.own_feat_ref, ...), custom_call_target="tpu_custom_call" | custom-call | flops 1000 | bytes 1000 | tf_op jit(solution)/shard_map/attend/pallas_call | solution.py:269
  112.8 4.6 %collective-permute-done.19.refs_6_ = bf16[4,48,2048]{2,1,0:T(8,128)(2,1)} collective-permute-done((bf16[4,48,2048]{2,1,0:T(8,128)(2,1)}, bf16[4,48,2048]{2,1,0:T(8,128)(2,1)}, u32[]{:S(2)}, u32[]{:S(2)}) %collective-permute-start.19) | collective-permute-done | bytes 786464 | tf_op jit(solution)/shard_map/ppermute | solution.py:343
  117.9 3.1 collective-permute-done.15.refs_1_
  122.0 19.9 %up_forward.1 = (f32[512,768]{1,0:T(8,128)}, f32[512,128]{1,0:T(8,128)}, bf16[512,768]{1,0:T(8,128)(2,1)}, bf16[768,512]{1,0:T(8,128)(2,1)}, bf16[512,3072]{1,0:...) custom-call(s32[2]{0:T(128)} %copy-done.24, bf16[512,768]{1,0:T(8,128)(2,1)} %attend.1.context_ref, ...), custom_call_target="tpu_custom_call" | custom-call | flops 1000 | bytes 1000 | tf_op jit(solution)/shard_map/up_forward/pallas_call | solution.py:529
  141.9 10.7 %down_forward.1 = (bf16[512,768]{1,0:T(8,128)(2,1)}, f32[512,768]{1,0:T(8,128)}, bf16[512,768]{1,0:T(8,128)(2,1)}, f32[8,768]{1,0:T(8,128)}) custom-call(s32[2]{0:T(128)} %copy-done.24, bf16[512,3072]{1,0:T(8,128)(2,1)} %get-tuple-element.116.active_ref, f32[512,768]{1,0:T(8,128)} %get-tuple-element.117.unit_ref, f32[8,768]{1,0:T(8,128)} %stack.142.vec_ref, ...), custom_call_target="tpu_custom_call" | custom-call | flops 1000 | bytes 1000 | tf_op jit(solution)/shard_map/down_forward/pallas_call | solution.py:599
  153.8 1.9 copy-done.14
  155.6 3.1 grad_rows.1
  158.8 2.2 copy-done.5
  161.0 2.3 copy.74
  163.4 19.3 %ffn_back.1 = (bf16[512,3072]{1,0:T(8,128)(2,1)}, f32[1,3072]{1,0:T(1,128)}, f32[512,768]{1,0:T(8,128)}, bf16[512,768]{1,0:T(8,128)(2,1)}, bf16[512,768]{1,0:T(8,128)(2,1)}, /*index=5*/f32[8,768]{1,0:T(8,128)}) custom-call(s32[2]{0:T(128)} %copy-done.24, bf16[512,768]{1,0:T(8,128)(2,1)} %get-tuple-element.122.h_ref.low_ref, ...), custom_call_target="tpu_custom_call" | custom-call | flops 1000 | bytes 1000 | tf_op jit(solution)/shard_map/ffn_back/pallas_call | solution.py:675
  182.7 1.9 copy-done.15
  188.0 5.4 %grad_columns.2 = (bf16[8,48,3840]{2,1,0:T(8,128)(2,1)S(1)}, bf16[8,48,3840]{2,1,0:T(8,128)(2,1)S(1)}) custom-call(s32[2]{0:T(128)S(1)} %copy-done.25, bf16[768,512]{1,0:T(8,128)(2,1)S(1)} %bitcast.54, bf16[512,768]{1,0:T(8,128)(2,1)S(1)} %copy-done.22, bf16[768,512]{1,0:T(8,128)(2,1)S(1)} %copy-done.21, bf16[512,3072]{1,0:T(8,128)(2,1)S(1)} %copy-done.15), custom_call_target="tpu_custom_call" | custom-call | flops 1000 | bytes 1000 | tf_op jit(solution)/shard_map/grad_columns/pallas_call | solution.py:791
  193.5 5.3 %collective-permute-done.21.part_near.part_far = bf16[8,48,3840]{2,1,0:T(8,128)(2,1)S(1)} collective-permute-done((bf16[8,48,3840]{2,1,0:T(8,128)(2,1)S(1)}, bf16[8,48,3840]{2,1,0:T(8,128)(2,1)S(1)}, u32[]{:S(2)}, u32[]{:S(2)}) %collective-permute-start.21) | collective-permute-done | bytes 2949152 | tf_op jit(solution)/shard_map/ppermute | solution.py:343
  198.8 2.9 halve.3
  204.7 29.6 %attend_back.1 = (bf16[512,768]{1,0:T(8,128)(2,1)}, bf16[1024,768]{1,0:T(8,128)(2,1)}, bf16[1024,768]{1,0:T(8,128)(2,1)}, f32[12,8,128]{2,1,0:T(8,128)}) custom-call(s32[48]{0:T(128)} %concatenate.72.bounds, bf16[512,768]{1,0:T(8,128)(2,1)} %copy-done.13, bf16[1024,1536]{1,0:T(8,128)(2,1)} %copy-done, bf16[1024,1536]{1,0:T(8,128)(2,1)} %copy-done, ...), custom_call_target="tpu_custom_call" | custom-call | flops 1000 | bytes 1000 | tf_op jit(solution)/shard_map/attend_back/pallas_call | solution.py:294
  234.3 2.5 reduce-scatter.2.cloned.1.call-done
  238.2 2.6 copy.75.refs_0_.refs_2_.refs_4_
  240.8 1.8 copy-done.8
  242.7 3.3 halve.4
  246.0 1.9 convert_add_fusion
  247.9 4.8 %grad_columns.3 = (bf16[8,48,2304]{2,1,0:T(8,128)(2,1)S(1)}, bf16[8,48,2304]{2,1,0:T(8,128)(2,1)S(1)}) custom-call(s32[2]{0:T(128)S(1)} %copy-done.25, bf16[768,1024]{1,0:T(8,128)(2,1)S(1)} %copy-done.4, bf16[512,768]{1,0:T(8,128)(2,1)S(1)} %copy-done.9, bf16[768,1024]{1,0:T(8,128)(2,1)S(1)} %copy-done.4, bf16[1024,768]{1,0:T(8,128)(2,1)S(1)} %copy-done.6, ...), custom_call_target="tpu_custom_call" | custom-call | flops 1000 | bytes 1000 | tf_op jit(solution)/shard_map/grad_columns/pallas_call | solution.py:791
  253.6 2.0 input_back.2.other_ref
  259.2 2.6 input_back.3.own_ref
  261.8 2.1 small_sums.1
  265.3 6.8 %collective-permute-done.28.across_ref = bf16[4,48,1920]{2,1,0:T(8,128)(2,1)S(1)} collective-permute-done((bf16[4,48,1920]{2,1,0:T(8,128)(2,1)S(1)}, bf16[4,48,1920]{2,1,0:T(8,128)(2,1)S(1)}, u32[]{:S(2)}, u32[]{:S(2)}) %collective-permute-start.28) | collective-permute-done | bytes 737312 | tf_op jit(solution)/shard_map/ppermute | solution.py:343
  273.5 1.8 collective-permute-start.32
  276.5 16.7 %collective-permute-done.29 = f32[40,768]{1,0:T(8,128)S(1)} collective-permute-done((f32[40,768]{1,0:T(8,128)S(1)}, f32[40,768]{1,0:T(8,128)S(1)}, u32[]{:S(2)}, u32[]{:S(2)}) %collective-permute-start.29) | collective-permute-done | bytes 122912 | tf_op jit(solution)/shard_map/ppermute | solution.py:343
  299.1 1.9 collective-permute-start.36
  301.0 4.1 %collective-permute-done.30 = bf16[48,1920]{1,0:T(8,128)(2,1)S(1)} collective-permute-done((bf16[48,1920]{1,0:T(8,128)(2,1)S(1)}, bf16[48,1920]{1,0:T(8,128)(2,1)S(1)}, u32[]{:S(2)}, u32[]{:S(2)}) %collective-permute-start.30) | collective-permute-done | bytes 184352 | tf_op jit(solution)/shard_map/ppermute | solution.py:343
  307.3 2.9 collective-permute-done.33
  310.2 4.6 %collective-permute-done.35 = bf16[48,2304]{1,0:T(8,128)(2,1)S(1)} collective-permute-done((bf16[48,2304]{1,0:T(8,128)(2,1)S(1)}, bf16[48,2304]{1,0:T(8,128)(2,1)S(1)}, u32[]{:S(2)}, u32[]{:S(2)}) %collective-permute-start.35) | collective-permute-done | bytes 221216 | tf_op jit(solution)/shard_map/ppermute | solution.py:343
  315.5 3.4 %collective-permute-start.37 = (f32[40,768]{1,0:T(8,128)S(1)}, f32[40,768]{1,0:T(8,128)S(1)}, u32[]{:S(2)}, u32[]{:S(2)}) collective-permute-start(f32[40,768]{1,0:T(8,128)S(1)} %add.199), channel_id=1, source_target_pairs={{0,4},{1,5},{2,6},{3,7},{4,0},{5,1},{6,2},{7,3},{8,12},{9,13},{10,... | collective-permute-start | bytes 368648 | tf_op jit(solution)/shard_map/ppermute | solution.py:343
  321.8 3.6 %collective-permute-start.38 = (f32[40,768]{1,0:T(8,128)S(1)}, f32[40,768]{1,0:T(8,128)S(1)}, u32[]{:S(2)}, u32[]{:S(2)}) collective-permute-start(f32[40,768]{1,0:T(8,128)S(1)} %add.203), channel_id=1, source_target_pairs={{0,8},{1,9},{2,10},{3,11},{4,12},{5,13},{6,14},{7,15},{8,0},{9,1},... | collective-permute-start | bytes 368648 | tf_op jit(solution)/shard_map/ppermute | solution.py:343
  326.2 3.4 collective-permute-done.38
  (261 shorter events, 64.1 us)
Async XLA Ops:
  7.2 134.7 %all-gather.2.cloned.1.call-start = ((), (), s32[]{:S(2)}) async-start(), calls=%async_computation.1 | async-start | bytes 5013504 | tf_op jit(solution)/shard_map/all_gather | solution.py:1071
  8.2 9.1 %collective-permute-start.3 = (bf16[48,1152]{1,0:T(8,128)(2,1)S(1)}, bf16[48,1152]{1,0:T(8,128)(2,1)S(1)}, u32[]{:S(2)}, u32[]{:S(2)}) collective-permute-start(bf16[48,1152]{1,0:T(8,128)(2,1)S(1)} %get-tuple-element.191), channel_id=1, source_target_pairs={{0,12},{1,13},{2,14},{3,15},{4,8},{5,9},{6,10},{7,11},{8,4},{9,5},... | collective-permute-start | bytes 331784 | tf_op jit(solution)/shard_map/ppermute | solution.py:343
  13.4 9.3 %collective-permute-start.2 = (bf16[48,1152]{1,0:T(8,128)(2,1)S(1)}, bf16[48,1152]{1,0:T(8,128)(2,1)S(1)}, u32[]{:S(2)}, u32[]{:S(2)}) collective-permute-start(bf16[48,1152]{1,0:T(8,128)(2,1)S(1)} %get-tuple-element.191), channel_id=1, source_target_pairs={{0,8},{1,9},{2,10},{3,11},{4,12},{5,13},{6,14},{7,15},{8,0},{9,1},... | collective-permute-start | bytes 331784 | tf_op jit(solution)/shard_map/ppermute | solution.py:343
  13.4 9.3 %collective-permute-start.1 = (bf16[48,1152]{1,0:T(8,128)(2,1)S(1)}, bf16[48,1152]{1,0:T(8,128)(2,1)S(1)}, u32[]{:S(2)}, u32[]{:S(2)}) collective-permute-start(bf16[48,1152]{1,0:T(8,128)(2,1)S(1)} %get-tuple-element.191), channel_id=1, source_target_pairs={{0,4},{1,5},{2,6},{3,7},{4,0},{5,1},{6,2},{7,3},{8,12},{9,13},{10,... | collective-permute-start | bytes 331784 | tf_op jit(solution)/shard_map/ppermute | solution.py:343
  22.8 15.1 %collective-permute-start.9 = (bf16[48,896]{1,0:T(8,128)(2,1)S(1)}, bf16[48,896]{1,0:T(8,128)(2,1)S(1)}, u32[]{:S(2)}, u32[]{:S(2)}) collective-permute-start(bf16[48,896]{1,0:T(8,128)(2,1)S(1)} %fusion.2), channel_id=1, source_target_pairs={{0,12},{1,13},{2,14},{3,15},{4,8},{5,9},{6,10},{7,11},{8,4},{9,5},... | collective-permute-start | bytes 258056 | tf_op jit(solution)/shard_map/ppermute | solution.py:343
  25.3 12.5 %collective-permute-start.8 = (bf16[48,896]{1,0:T(8,128)(2,1)S(1)}, bf16[48,896]{1,0:T(8,128)(2,1)S(1)}, u32[]{:S(2)}, u32[]{:S(2)}) collective-permute-start(bf16[48,896]{1,0:T(8,128)(2,1)S(1)} %fusion.2), channel_id=1, source_target_pairs={{0,8},{1,9},{2,10},{3,11},{4,12},{5,13},{6,14},{7,15},{8,0},{9,1},... | collective-permute-start | bytes 258056 | tf_op jit(solution)/shard_map/ppermute | solution.py:343
  25.3 12.6 %collective-permute-start.7 = (bf16[48,896]{1,0:T(8,128)(2,1)S(1)}, bf16[48,896]{1,0:T(8,128)(2,1)S(1)}, u32[]{:S(2)}, u32[]{:S(2)}) collective-permute-start(bf16[48,896]{1,0:T(8,128)(2,1)S(1)} %fusion.2), channel_id=1, source_target_pairs={{0,4},{1,5},{2,6},{3,7},{4,0},{5,1},{6,2},{7,3},{8,12},{9,13},{10,... | collective-permute-start | bytes 258056 | tf_op jit(solution)/shard_map/ppermute | solution.py:343
  27.2 10.4 %collective-permute-start.4 = (bf16[4,48,1152]{2,1,0:T(8,128)(2,1)S(1)}, bf16[4,48,1152]{2,1,0:T(8,128)(2,1)S(1)}, u32[]{:S(2)}, u32[]{:S(2)}) collective-permute-start(bf16[4,48,1152]{2,1,0:T(8,128)(2,1)S(1)} %pad_maximum_fusion.2), channel_id=1, source_target_pairs={{0,2},{1,3},{2,0},{3,1},{4,6},{5,7},{6,4},{7,5},{8,10},{9,11},{10,... | collective-permute-start | bytes 1327112 | tf_op jit(solution)/shard_map/ppermute | solution.py:343
  28.8 19.6 %copy-start.32 = (bf16[48,3072]{1,0:T(8,128)(2,1)S(1)}, bf16[48,3072]{1,0:T(8,128)(2,1)}, u32[]{:S(2)}) copy-start(bf16[48,3072]{1,0:T(8,128)(2,1)} %param.44) | copy-start | bytes 884740
  37.6 29.7 %copy-start.19 = (bf16[8,48,1152]{2,1,0:T(8,128)(2,1)}, bf16[8,48,1152]{2,1,0:T(8,128)(2,1)S(1)}, u32[]{:S(2)}) copy-start(bf16[8,48,1152]{2,1,0:T(8,128)(2,1)S(1)} %constant_dynamic-update-slice_fusion.refs_0_) | copy-start | bytes 2654212
  38.6 7.4 %collective-permute-start.10 = (bf16[4,48,896]{2,1,0:T(8,128)(2,1)S(1)}, bf16[4,48,896]{2,1,0:T(8,128)(2,1)S(1)}, u32[]{:S(2)}, u32[]{:S(2)}) collective-permute-start(bf16[4,48,896]{2,1,0:T(8,128)(2,1)S(1)} %pad_maximum_fusion.3), channel_id=1, source_target_pairs={{0,2},{1,3},{2,0},{3,1},{4,6},{5,7},{6,4},{7,5},{8,10},{9,11},{10,... | collective-permute-start | bytes 1032200 | tf_op jit(solution)/shard_map/ppermute | solution.py:343
  46.8 189.9 %reduce-scatter.2.cloned.1.call-start = ((), (), s32[]{:S(2)}) async-start(), calls=%async_computation.2 | async-start | bytes 5013504 | tf_op jit(solution)/shard_map/reduce_scatter | solution.py:1152
  46.8 20.5 %collective-permute-start = (bf16[512,768]{1,0:T(8,128)(2,1)S(1)}, bf16[512,768]{1,0:T(8,128)(2,1)S(1)}, u32[]{:S(2)}, u32[]{:S(2)}) collective-permute-start(bf16[512,768]{1,0:T(8,128)(2,1)S(1)} %bitcast.52), channel_id=1, source_target_pairs={{0,16},{16,0},{1,17},{17,1},{2,18},{18,2},{3,19},{19,3},{4,20},{20... | collective-permute-start | bytes 2359304 | tf_op jit(solution)/shard_map/ppermute | solution.py:1016
  52.3 34.5 %copy-start.24 = (s32[2]{0:T(128)}, s32[2]{0:T(128)S(1)}, u32[]{:S(2)}) copy-start(s32[2]{0:T(128)S(1)} %pad_add_fusion.1.place) | copy-start | bytes 28
  56.3 25.5 %collective-permute-start.6 = (bf16[8,48,1152]{2,1,0:T(8,128)(2,1)S(1)}, bf16[8,48,1152]{2,1,0:T(8,128)(2,1)S(1)}, u32[]{:S(2)}, u32[]{:S(2)}) collective-permute-start(bf16[8,48,1152]{2,1,0:T(8,128)(2,1)S(1)} %constant_dynamic-update-slice_fusion.refs_0_), channel_id=1, source_target_pairs={{0,16},{16,0},{1,17},{17,1},{2,18},{18,2},{3,19},{19,3},{4,20},{20... | collective-permute-start | bytes 2654216 | tf_op jit(solution)/shard_map/ppermute | solution.py:1016
  57.8 24.0 %copy-start.39 = (f32[768]{0:T(1024)S(1)}, f32[768]{0:T(1024)}, u32[]{:S(2)}) copy-start(f32[768]{0:T(1024)} %param.31) | copy-start | bytes 9220
  57.8 36.9 %collective-permute-start.14 = (bf16[48,2048]{1,0:T(8,128)(2,1)}, bf16[48,2048]{1,0:T(8,128)(2,1)S(1)}, u32[]{:S(2)}, u32[]{:S(2)}) collective-permute-start(bf16[48,2048]{1,0:T(8,128)(2,1)} %slice.152), channel_id=1, source_target_pairs={{0,12},{1,13},{2,14},{3,15},{4,8},{5,9},{6,10},{7,11},{8,4},{9,5},... | collective-permute-start | bytes 589832 | tf_op jit(solution)/shard_map/ppermute | solution.py:343
  60.0 34.6 %collective-permute-start.13 = (bf16[48,2048]{1,0:T(8,128)(2,1)}, bf16[48,2048]{1,0:T(8,128)(2,1)S(1)}, u32[]{:S(2)}, u32[]{:S(2)}) collective-permute-start(bf16[48,2048]{1,0:T(8,128)(2,1)} %slice.152), channel_id=1, source_target_pairs={{0,8},{1,9},{2,10},{3,11},{4,12},{5,13},{6,14},{7,15},{8,0},{9,1},... | collective-permute-start | bytes 589832 | tf_op jit(solution)/shard_map/ppermute | solution.py:343
  60.0 34.6 %collective-permute-start.12 = (bf16[48,2048]{1,0:T(8,128)(2,1)}, bf16[48,2048]{1,0:T(8,128)(2,1)S(1)}, u32[]{:S(2)}, u32[]{:S(2)}) collective-permute-start(bf16[48,2048]{1,0:T(8,128)(2,1)} %slice.152), channel_id=1, source_target_pairs={{0,4},{1,5},{2,6},{3,7},{4,0},{5,1},{6,2},{7,3},{8,12},{9,13},{10,... | collective-permute-start | bytes 589832 | tf_op jit(solution)/shard_map/ppermute | solution.py:343
  67.4 19.4 %collective-permute-start.5 = (bf16[8,48,1152]{2,1,0:T(8,128)(2,1)S(1)}, bf16[8,48,1152]{2,1,0:T(8,128)(2,1)S(1)}, u32[]{:S(2)}, u32[]{:S(2)}) collective-permute-start(bf16[8,48,1152]{2,1,0:T(8,128)(2,1)S(1)} %constant_dynamic-update-slice_fusion.refs_0_), channel_id=1, source_target_pairs={{0,1},{1,0},{2,3},{3,2},{4,5},{5,4},{6,7},{7,6},{8,9},{9,8},{10,11... | collective-permute-start | bytes 2654216 | tf_op jit(solution)/shard_map/ppermute | solution.py:343
  81.8 5.0 %collective-permute-start.11 = (bf16[8,48,1152]{2,1,0:T(8,128)(2,1)S(1)}, bf16[8,48,1152]{2,1,0:T(8,128)(2,1)S(1)}, u32[]{:S(2)}, u32[]{:S(2)}) collective-permute-start(bf16[8,48,1152]{2,1,0:T(8,128)(2,1)S(1)} %collective-permute-done.6.refs_2_), channel_id=1, source_target_pairs={{0,1},{1,0},{2,3},{3,2},{4,5},{5,4},{6,7},{7,6},{8,9},{9,8},{10,11... | collective-permute-start | bytes 2654216 | tf_op jit(solution)/shard_map/ppermute | solution.py:343
  96.6 20.8 %collective-permute-start.19 = (bf16[4,48,2048]{2,1,0:T(8,128)(2,1)}, bf16[4,48,2048]{2,1,0:T(8,128)(2,1)}, u32[]{:S(2)}, u32[]{:S(2)}) collective-permute-start(bf16[4,48,2048]{2,1,0:T(8,128)(2,1)} %pad_maximum_fusion.1.refs_4_), channel_id=1, source_target_pairs={{0,2},{1,3},{2,0},{3,1},{4,6},{5,7},{6,4},{7,5},{8,10},{9,11},{10,... | collective-permute-start | bytes 2359304 | tf_op jit(solution)/shard_map/ppermute | solution.py:343
  98.3 19.6 %collective-permute-start.16 = (bf16[8,48,896]{2,1,0:T(8,128)(2,1)}, bf16[8,48,896]{2,1,0:T(8,128)(2,1)}, u32[]{:S(2)}, u32[]{:S(2)}) collective-permute-start(bf16[8,48,896]{2,1,0:T(8,128)(2,1)} %constant_dynamic-update-slice_fusion.5.refs_0_), channel_id=1, source_target_pairs={{0,16},{16,0},{1,17},{17,1},{2,18},{18,2},{3,19},{19,3},{4,20},{20... | collective-permute-start | bytes 2064392 | tf_op jit(solution)/shard_map/ppermute | solution.py:1016
  99.8 22.2 %collective-permute-start.18 = (bf16[4,48,2048]{2,1,0:T(8,128)(2,1)}, bf16[4,48,2048]{2,1,0:T(8,128)(2,1)}, u32[]{:S(2)}, u32[]{:S(2)}) collective-permute-start(bf16[4,48,2048]{2,1,0:T(8,128)(2,1)} %pad_maximum_fusion.1.refs_4_), channel_id=1, source_target_pairs={{0,1},{1,0},{2,3},{3,2},{4,5},{5,4},{6,7},{7,6},{8,9},{9,8},{10,11... | collective-permute-start | bytes 2359304 | tf_op jit(solution)/shard_map/ppermute | solution.py:343
  117.4 4.6 %collective-permute-start.20 = (bf16[4,48,2048]{2,1,0:T(8,128)(2,1)}, bf16[4,48,2048]{2,1,0:T(8,128)(2,1)}, u32[]{:S(2)}, u32[]{:S(2)}) collective-permute-start(bf16[4,48,2048]{2,1,0:T(8,128)(2,1)} %collective-permute-done.19.refs_6_), channel_id=1, source_target_pairs={{0,1},{1,0},{2,3},{3,2},{4,5},{5,4},{6,7},{7,6},{8,9},{9,8},{10,11... | collective-permute-start | bytes 2359304 | tf_op jit(solution)/shard_map/ppermute | solution.py:343
  117.4 3.6 %collective-permute-start.15 = (bf16[8,48,896]{2,1,0:T(8,128)(2,1)}, bf16[8,48,896]{2,1,0:T(8,128)(2,1)}, u32[]{:S(2)}, u32[]{:S(2)}) collective-permute-start(bf16[8,48,896]{2,1,0:T(8,128)(2,1)} %constant_dynamic-update-slice_fusion.5.refs_0_), channel_id=1, source_target_pairs={{0,1},{1,0},{2,3},{3,2},{4,5},{5,4},{6,7},{7,6},{8,9},{9,8},{10,11... | collective-permute-start | bytes 2064392 | tf_op jit(solution)/shard_map/ppermute | solution.py:343
  117.9 4.1 %collective-permute-start.17 = (bf16[8,48,896]{2,1,0:T(8,128)(2,1)}, bf16[8,48,896]{2,1,0:T(8,128)(2,1)}, u32[]{:S(2)}, u32[]{:S(2)}) collective-permute-start(bf16[8,48,896]{2,1,0:T(8,128)(2,1)} %collective-permute-done.16.refs_2_), channel_id=1, source_target_pairs={{0,1},{1,0},{2,3},{3,2},{4,5},{5,4},{6,7},{7,6},{8,9},{9,8},{10,11... | collective-permute-start | bytes 2064392 | tf_op jit(solution)/shard_map/ppermute | solution.py:343
  193.4 5.4 %collective-permute-start.21 = (bf16[8,48,3840]{2,1,0:T(8,128)(2,1)S(1)}, bf16[8,48,3840]{2,1,0:T(8,128)(2,1)S(1)}, u32[]{:S(2)}, u32[]{:S(2)}) collective-permute-start(bf16[8,48,3840]{2,1,0:T(8,128)(2,1)S(1)} %get-tuple-element.132), channel_id=1, source_target_pairs={{0,1},{1,0},{2,3},{3,2},{4,5},{5,4},{6,7},{7,6},{8,9},{9,8},{10,11... | collective-permute-start | bytes 8847368 | tf_op jit(solution)/shard_map/ppermute | solution.py:343
  203.3 37.5 %collective-permute-start.22 = (bf16[8,48,1920]{2,1,0:T(8,128)(2,1)}, bf16[8,48,1920]{2,1,0:T(8,128)(2,1)}, u32[]{:S(2)}, u32[]{:S(2)}) collective-permute-start(bf16[8,48,1920]{2,1,0:T(8,128)(2,1)} %get-tuple-element.133), channel_id=1, source_target_pairs={{0,16},{16,0},{1,17},{17,1},{2,18},{18,2},{3,19},{19,3},{4,20},{20... | collective-permute-start | bytes 4423688 | tf_op jit(solution)/shard_map/ppermute | solution.py:1016
  236.7 9.2 %collective-permute-start.23 = (bf16[192,768]{1,0:T(8,128)(2,1)}, bf16[192,768]{1,0:T(8,128)(2,1)}, u32[]{:S(2)}, u32[]{:S(2)}) collective-permute-start(bf16[192,768]{1,0:T(8,128)(2,1)} %reduce-scatter.2.cloned.1.call-done), channel_id=1, source_target_pairs={{0,16},{16,0},{1,17},{17,1},{2,18},{18,2},{3,19},{19,3},{4,20},{20... | collective-permute-start | bytes 884744 | tf_op jit(solution)/shard_map/ppermute | solution.py:1016
  252.7 3.8 %collective-permute-start.24 = (bf16[8,48,2304]{2,1,0:T(8,128)(2,1)S(1)}, bf16[8,48,2304]{2,1,0:T(8,128)(2,1)S(1)}, u32[]{:S(2)}, u32[]{:S(2)}) collective-permute-start(bf16[8,48,2304]{2,1,0:T(8,128)(2,1)S(1)} %get-tuple-element.144), channel_id=1, source_target_pairs={{0,1},{1,0},{2,3},{3,2},{4,5},{5,4},{6,7},{7,6},{8,9},{9,8},{10,11... | collective-permute-start | bytes 5308424 | tf_op jit(solution)/shard_map/ppermute | solution.py:343
  252.8 19.4 %collective-permute-start.28 = (bf16[4,48,1920]{2,1,0:T(8,128)(2,1)S(1)}, bf16[4,48,1920]{2,1,0:T(8,128)(2,1)S(1)}, u32[]{:S(2)}, u32[]{:S(2)}) collective-permute-start(bf16[4,48,1920]{2,1,0:T(8,128)(2,1)S(1)} %get-tuple-element.140), channel_id=1, source_target_pairs={{0,2},{1,3},{2,0},{3,1},{4,6},{5,7},{6,4},{7,5},{8,10},{9,11},{10,... | collective-permute-start | bytes 2211848 | tf_op jit(solution)/shard_map/ppermute | solution.py:343
  257.7 36.5 %collective-permute-start.26 = (bf16[4,48,2304]{2,1,0:T(8,128)(2,1)S(1)}, bf16[4,48,2304]{2,1,0:T(8,128)(2,1)S(1)}, u32[]{:S(2)}, u32[]{:S(2)}) collective-permute-start(bf16[4,48,2304]{2,1,0:T(8,128)(2,1)S(1)} %get-tuple-element.148), channel_id=1, source_target_pairs={{0,2},{1,3},{2,0},{3,1},{4,6},{5,7},{6,4},{7,5},{8,10},{9,11},{10,... | collective-permute-start | bytes 2654216 | tf_op jit(solution)/shard_map/ppermute | solution.py:343
  258.5 37.5 %collective-permute-start.25 = (bf16[512,768]{1,0:T(8,128)(2,1)S(1)}, bf16[512,768]{1,0:T(8,128)(2,1)S(1)}, u32[]{:S(2)}, u32[]{:S(2)}) collective-permute-start(bf16[512,768]{1,0:T(8,128)(2,1)S(1)} %input_back.2.other_ref), channel_id=1, source_target_pairs={{0,16},{16,0},{1,17},{17,1},{2,18},{18,2},{3,19},{19,3},{4,20},{20... | collective-permute-start | bytes 2359304 | tf_op jit(solution)/shard_map/ppermute | solution.py:1016
  263.9 1.4 collective-permute-start.27
  272.7 24.7 %copy-start.23 = (f32[8,768]{1,0:T(8,128)S(1)}, f32[8,768]{1,0:T(8,128)}, u32[]{:S(2)}) copy-start(f32[8,768]{1,0:T(8,128)} %pad.39.tap_ref) | copy-start | bytes 73732
  272.7 20.6 %collective-permute-start.29 = (f32[40,768]{1,0:T(8,128)S(1)}, f32[40,768]{1,0:T(8,128)S(1)}, u32[]{:S(2)}, u32[]{:S(2)}) collective-permute-start(f32[40,768]{1,0:T(8,128)S(1)} %add.194), channel_id=1, source_target_pairs={{0,2},{1,3},{2,0},{3,1},{4,6},{5,7},{6,4},{7,5},{8,10},{9,11},{10,... | collective-permute-start | bytes 368648 | tf_op jit(solution)/shard_map/ppermute | solution.py:343
  273.5 25.6 %collective-permute-start.32 = (bf16[48,1920]{1,0:T(8,128)(2,1)S(1)}, bf16[48,1920]{1,0:T(8,128)(2,1)S(1)}, u32[]{:S(2)}, u32[]{:S(2)}) collective-permute-start(bf16[48,1920]{1,0:T(8,128)(2,1)S(1)} %get-tuple-element.159), channel_id=1, source_target_pairs={{0,12},{1,13},{2,14},{3,15},{4,8},{5,9},{6,10},{7,11},{8,4},{9,5},... | collective-permute-start | bytes 552968 | tf_op jit(solution)/shard_map/ppermute | solution.py:343
  275.3 25.7 %collective-permute-start.31 = (bf16[48,1920]{1,0:T(8,128)(2,1)S(1)}, bf16[48,1920]{1,0:T(8,128)(2,1)S(1)}, u32[]{:S(2)}, u32[]{:S(2)}) collective-permute-start(bf16[48,1920]{1,0:T(8,128)(2,1)S(1)} %get-tuple-element.158), channel_id=1, source_target_pairs={{0,8},{1,9},{2,10},{3,11},{4,12},{5,13},{6,14},{7,15},{8,0},{9,1},... | collective-permute-start | bytes 552968 | tf_op jit(solution)/shard_map/ppermute | solution.py:343
  293.3 11.8 %collective-permute-start.30 = (bf16[48,1920]{1,0:T(8,128)(2,1)S(1)}, bf16[48,1920]{1,0:T(8,128)(2,1)S(1)}, u32[]{:S(2)}, u32[]{:S(2)}) collective-permute-start(bf16[48,1920]{1,0:T(8,128)(2,1)S(1)} %get-tuple-element.157), channel_id=1, source_target_pairs={{0,4},{1,5},{2,6},{3,7},{4,0},{5,1},{6,2},{7,3},{8,12},{9,13},{10,... | collective-permute-start | bytes 552968 | tf_op jit(solution)/shard_map/ppermute | solution.py:343
  294.9 15.3 %collective-permute-start.34 = (bf16[48,2304]{1,0:T(8,128)(2,1)S(1)}, bf16[48,2304]{1,0:T(8,128)(2,1)S(1)}, u32[]{:S(2)}, u32[]{:S(2)}) collective-permute-start(bf16[48,2304]{1,0:T(8,128)(2,1)S(1)} %get-tuple-element.162), channel_id=1, source_target_pairs={{0,4},{1,5},{2,6},{3,7},{4,0},{5,1},{6,2},{7,3},{8,12},{9,13},{10,... | collective-permute-start | bytes 663560 | tf_op jit(solution)/shard_map/ppermute | solution.py:343
  296.0 18.7 %collective-permute-start.35 = (bf16[48,2304]{1,0:T(8,128)(2,1)S(1)}, bf16[48,2304]{1,0:T(8,128)(2,1)S(1)}, u32[]{:S(2)}, u32[]{:S(2)}) collective-permute-start(bf16[48,2304]{1,0:T(8,128)(2,1)S(1)} %get-tuple-element.163), channel_id=1, source_target_pairs={{0,8},{1,9},{2,10},{3,11},{4,12},{5,13},{6,14},{7,15},{8,0},{9,1},... | collective-permute-start | bytes 663560 | tf_op jit(solution)/shard_map/ppermute | solution.py:343
  299.1 15.7 %collective-permute-start.36 = (bf16[48,2304]{1,0:T(8,128)(2,1)S(1)}, bf16[48,2304]{1,0:T(8,128)(2,1)S(1)}, u32[]{:S(2)}, u32[]{:S(2)}) collective-permute-start(bf16[48,2304]{1,0:T(8,128)(2,1)S(1)} %get-tuple-element.164), channel_id=1, source_target_pairs={{0,12},{1,13},{2,14},{3,15},{4,8},{5,9},{6,10},{7,11},{8,4},{9,5},... | collective-permute-start | bytes 663560 | tf_op jit(solution)/shard_map/ppermute | solution.py:343
  305.2 4.9 %collective-permute-start.33 = (f32[40,768]{1,0:T(8,128)S(1)}, f32[40,768]{1,0:T(8,128)S(1)}, u32[]{:S(2)}, u32[]{:S(2)}) collective-permute-start(f32[40,768]{1,0:T(8,128)S(1)} %add.195), channel_id=1, source_target_pairs={{0,16},{16,0},{1,17},{17,1},{2,18},{18,2},{3,19},{19,3},{4,20},{20... | collective-permute-start | bytes 368648 | tf_op jit(solution)/shard_map/ppermute | solution.py:1016
  305.9 13.0 %collective-permute-start.40 = (bf16[48,1920]{1,0:T(8,128)(2,1)S(1)}, bf16[48,1920]{1,0:T(8,128)(2,1)S(1)}, u32[]{:S(2)}, u32[]{:S(2)}) collective-permute-start(bf16[48,1920]{1,0:T(8,128)(2,1)S(1)} %add_convert_fusion.4), channel_id=1, source_target_pairs={{0,16},{16,0},{1,17},{17,1},{2,18},{18,2},{3,19},{19,3},{4,20},{20... | collective-permute-start | bytes 552968 | tf_op jit(solution)/shard_map/ppermute | solution.py:1016
  314.9 10.5 %collective-permute-start.39 = (bf16[48,2304]{1,0:T(8,128)(2,1)S(1)}, bf16[48,2304]{1,0:T(8,128)(2,1)S(1)}, u32[]{:S(2)}, u32[]{:S(2)}) collective-permute-start(bf16[48,2304]{1,0:T(8,128)(2,1)S(1)} %add_convert_fusion.3), channel_id=1, source_target_pairs={{0,16},{16,0},{1,17},{17,1},{2,18},{18,2},{3,19},{19,3},{4,20},{20... | collective-permute-start | bytes 663560 | tf_op jit(solution)/shard_map/ppermute | solution.py:1016
  315.5 6.3 %collective-permute-start.37 = (f32[40,768]{1,0:T(8,128)S(1)}, f32[40,768]{1,0:T(8,128)S(1)}, u32[]{:S(2)}, u32[]{:S(2)}) collective-permute-start(f32[40,768]{1,0:T(8,128)S(1)} %add.199), channel_id=1, source_target_pairs={{0,4},{1,5},{2,6},{3,7},{4,0},{5,1},{6,2},{7,3},{8,12},{9,13},{10,... | collective-permute-start | bytes 368648 | tf_op jit(solution)/shard_map/ppermute | solution.py:343
  321.8 7.8 %collective-permute-start.38 = (f32[40,768]{1,0:T(8,128)S(1)}, f32[40,768]{1,0:T(8,128)S(1)}, u32[]{:S(2)}, u32[]{:S(2)}) collective-permute-start(f32[40,768]{1,0:T(8,128)S(1)} %add.203), channel_id=1, source_target_pairs={{0,8},{1,9},{2,10},{3,11},{4,12},{5,13},{6,14},{7,15},{8,0},{9,1},... | collective-permute-start | bytes 368648 | tf_op jit(solution)/shard_map/ppermute | solution.py:343
  (45 other events, 290.1 us)
Sparse Core Ops, SparseCore 0:
  46.9 65.7 all-gather.1
  161.1 75.5 reduce-scatter.1
